TPU v7x, 32 devices: a whole 2x2x4 slice. The times are simulated.
32 devices in a mesh: shot: 2 (over x), gz: 16 (over z, y, core).
Axes of the slice: x: 2, y: 2, z: 4, core: 2. Of those that a mesh axis runs over, the one named last changes fastest.
Arguments:
- source_now: float32 [256, 128, 128], P(('shot', 'gz')), parts along dimension 0, may hold values from -6 to 6
- source_before: float32 [256, 128, 128], P(('shot', 'gz')), parts along dimension 0, may hold values from -6 to 6
- receiver_now: float32 [256, 128, 128], P(('shot', 'gz')), parts along dimension 0, may hold values from -6 to 6
- receiver_before: float32 [256, 128, 128], P(('shot', 'gz')), parts along dimension 0, may hold values from -6 to 6
- speed_term: float32 [128, 128, 128], P('gz'), may hold values from 0.03 to 0.18
- saved_faces: float32 [24, 8, 128, 128], P('shot', None, 'gz'), parts along dimension 0, may hold values from -6 to 6
- face_steps: int32 [12], replicated, may hold values from 0 to 11, each once
- traces: bfloat16 [24, 128, 128], P('shot'), parts along dimension 0, may hold values from -6 to 6
- lag_offsets: int32 [8], replicated, may hold values from -8 to 8, as said below
- snap_phase: int32 [2], replicated, may hold values from 0 to 5
Outputs:
- image_out: bfloat16 [16, 128, 128, 128], P('shot', None, 'gz'), parts along dimension 0
- source_final: float32 [256, 128, 128], P(('shot', 'gz')), parts along dimension 0
- receiver_final: float32 [256, 128, 128], P(('shot', 'gz')), parts along dimension 0
There are 2 independent parts, one for each index of `shot`. A program takes and returns all parts, laid end to end along the dimension named above; an argument that names none is the same for every part. Nothing has to cross between parts.
Inputs may be any that keep to these rules, and one draw needn't show every extreme that they name: `face_steps`: each of the 12 saved slots belongs to exactly one step. `lag_offsets`: the 8 offsets are different, and both ends of the range occur.
All inputs are finite; a program needn't handle non-finite values.
Results may differ from a plain program's by a relative error of at most 0.001.
Values sent between devices are 32-bit elements; how exact they have to be, the bound alone decides.
No kernel may reach another device: no remote copies, remote signals or barrier semaphores. Data moves between devices by JAX's collectives and lax.ppermute only.
A program may use at most 64 MiB of HBM per device.

v0:
```python
import math

import jax
import jax.numpy as jnp
from jax import lax
from jax.sharding import PartitionSpec as P

LAGS = 8
LMAX = 8
SNAP_EVERY = 6
SNAPS = 2


stencil_weights = (-205.0 / 72.0, 8.0 / 5.0, -1.0 / 5.0, 8.0 / 315.0, -1.0 / 560.0)
damping = 0.25
smoothing = 16.0


def extended_2(block, sides, width):
    for axis, dim in sides:
        count = lax.axis_size(axis)
        forward = [(i, i + 1) for i in range(count - 1)]
        backward = [(target, source) for source, target in forward]
        low = lax.ppermute(
            lax.slice_in_dim(block, block.shape[dim] - width, None, axis=dim), axis, forward
        )
        high = lax.ppermute(lax.slice_in_dim(block, 0, width, axis=dim), axis, backward)
        block = jnp.concatenate([low, block, high], axis=dim)
    return block


def stencil(extended, layers):
    center = extended[:, 4 : 4 + layers]
    height = center.shape[2]
    breadth = center.shape[3]
    padded = jnp.pad(center, ((0, 0), (0, 0), (4, 4), (4, 4)))
    summed = 3.0 * stencil_weights[0] * center
    for offset in range(1, 5):
        weight = stencil_weights[offset]
        summed = summed + weight * (
            extended[:, 4 + offset : 4 + offset + layers]
            + extended[:, 4 - offset : 4 - offset + layers]
        )
        summed = summed + weight * (
            padded[:, :, 4 + offset : 4 + offset + height, 4 : 4 + breadth]
            + padded[:, :, 4 - offset : 4 - offset + height, 4 : 4 + breadth]
        )
        summed = summed + weight * (
            padded[:, :, 4 : 4 + height, 4 + offset : 4 + offset + breadth]
            + padded[:, :, 4 : 4 + height, 4 - offset : 4 - offset + breadth]
        )
    return summed


def advance(extended, center, previous, speed_term, faces_now, trace_now, top_row, layers):
    updated = 2.0 * center - previous + speed_term * stencil(extended, layers)
    breadth = updated.shape[3]
    column = lax.broadcasted_iota(jnp.int32, (8, breadth), 1)
    which = lax.broadcasted_iota(jnp.int32, (8, breadth), 0)
    target = jnp.where(which < 4, which, which + breadth - 8)
    placing = (column == target).astype(jnp.float32)
    boundary = jnp.einsum("fzy,fx->zyx", faces_now, placing, precision=lax.Precision.HIGHEST)
    x_index = lax.broadcasted_iota(jnp.int32, (1, 1, breadth), 2)
    edge_mask = (x_index < 4) | (x_index >= breadth - 4)
    source = jnp.where(edge_mask, boundary, updated[0])
    top_mask = lax.broadcasted_iota(jnp.int32, (layers, 1, 1), 0) == top_row
    receiver = updated[1] + jnp.where(top_mask, trace_now[None], 0.0)
    return jnp.stack([source, receiver])


def lag_images(snapshot, lag_offsets):
    source = snapshot[0]
    receiver = snapshot[1]
    margin = ((0, 0), (0, 0), (LMAX, LMAX))
    source_pad = jnp.pad(source, margin)
    receiver_pad = jnp.pad(receiver, margin)
    breadth = source.shape[2]
    images = []
    for lag_index in range(LAGS):
        lag_now = lag_offsets[lag_index]
        shifted_source = lax.dynamic_slice_in_dim(source_pad, LMAX - lag_now, breadth, 2)
        shifted_receiver = lax.dynamic_slice_in_dim(receiver_pad, LMAX + lag_now, breadth, 2)
        images.append(shifted_source * shifted_receiver)
    return (jnp.stack(images), source * source)


def depth_inverse(layers):
    ratio = (1.0 + 2.0 * smoothing) / (2.0 * smoothing)
    theta = math.log(ratio + math.sqrt(ratio * ratio - 1.0))
    hyper_sine = 0.5 * (math.exp(theta) - math.exp(-theta))
    scale = 1.0 / (2.0 * smoothing * hyper_sine * (1.0 - math.exp(-2.0 * (layers + 1) * theta)))
    row_index = lax.broadcasted_iota(jnp.int32, (layers, layers), 0)
    col_index = lax.broadcasted_iota(jnp.int32, (layers, layers), 1)
    apart = jnp.abs(row_index - col_index).astype(jnp.float32)
    joined = (row_index + col_index).astype(jnp.float32)
    total = float(layers)
    green = (
        jnp.exp(-theta * apart)
        - jnp.exp(-theta * (2.0 * total - joined))
        - jnp.exp(-theta * (joined + 2.0))
        + jnp.exp(-theta * (2.0 * total + 2.0 - apart))
    )
    return green * scale


def finish(raw_image, illumination):
    layers = illumination.shape[0]
    columns = illumination.reshape(layers, -1)
    inverse = depth_inverse(layers)
    smooth = jnp.dot(
        inverse, columns, precision=lax.Precision.HIGHEST, preferred_element_type=jnp.float32
    ).reshape(illumination.shape)
    return (raw_image / (smooth + damping)).astype(jnp.bfloat16)


def local(
    source_now,
    source_before,
    receiver_now,
    receiver_before,
    speed_term,
    saved_faces,
    face_steps,
    traces,
    lag_offsets,
    snap_phase,
):
    current = jnp.stack([source_now, receiver_now])
    previous = jnp.stack([source_before, receiver_before])
    layers = source_now.shape[0]
    is_top = lax.axis_index("gz") == 0
    top_row = jnp.where(is_top, 0, -1)
    raw_image = jnp.zeros((1,), jnp.float32)
    illumination = jnp.zeros((1,), jnp.float32)
    for window in range(SNAPS):
        phase_now = snap_phase[window]
        empty_snapshot = jnp.zeros_like(current)

        def one_step(local_index, carried):
            current, previous, snapshot = carried
            step_index = window * SNAP_EVERY + local_index
            extended = extended_2(current, (("gz", 1),), 4)
            faces_now = lax.dynamic_index_in_dim(
                saved_faces, face_steps[step_index], 0, keepdims=False
            )
            trace_now = lax.dynamic_index_in_dim(traces, step_index, 0, keepdims=False).astype(
                jnp.float32
            )
            updated = advance(
                extended, current, previous, speed_term, faces_now, trace_now, top_row, layers
            )
            snapshot = jnp.where(local_index == phase_now, updated, snapshot)
            return (updated, current, snapshot)

        current, previous, snapshot = lax.fori_loop(
            0, SNAP_EVERY, one_step, (current, previous, empty_snapshot)
        )
        columns_now = lax.all_to_all(snapshot, "gz", split_axis=2, concat_axis=1, tiled=True)
        raw_now, light_now = lag_images(columns_now, lag_offsets)
        if window == 0:
            raw_image = raw_now
            illumination = light_now
        else:
            raw_image = raw_image + raw_now
            illumination = illumination + light_now
    return (finish(raw_image, illumination), current[0], current[1])


def solution(mesh):
    return jax.shard_map(
        local,
        mesh=mesh,
        in_specs=(
            P(("shot", "gz"), None, None),
            P(("shot", "gz"), None, None),
            P(("shot", "gz"), None, None),
            P(("shot", "gz"), None, None),
            P("gz", None, None),
            P("shot", None, "gz", None),
            P(),
            P("shot", None, None),
            P(),
            P(),
        ),
        out_specs=(
            P("shot", None, "gz", None),
            P(("shot", "gz"), None, None),
            P(("shot", "gz"), None, None),
        ),
        check_vma=False,
    )
```

profile of v0, /device:TPU:9, one launch (start us, length us, event | category | flops | bytes accessed | tf_op | source)
XLA Modules:
  0.0 345.8 jit_solution(5449457502616833850)
XLA Ops:
  0.7 1.4 fusion.167
  3.1 1.3 pad_maximum_fusion.2
  4.5 1.3 pad_maximum_fusion.3
  5.8 135.9 %while.44 = (s32[]{:T(128)}, f32[2,8,128,128]{3,2,1,0:T(8,128)S(1)}, f32[2,8,128,128]{3,2,1,0:T(8,128)S(1)}, f32[2,8,128,128]{3,2,1,0:T(8,128)}, s32[12]{0:T(128...) while((s32[]{:T(128)}, ...), condition=%wide.region_1.2_spmd.clone, body=%wide.region_0.1_spmd.clone.sunk | while | flops 24529312 | bytes 40568852 | solution.py:155
  6.8 3.7 %collective-permute-start = (f32[2,4,128,128]{3,2,1,0:T(8,128)}, f32[2,4,128,128]{3,2,1,0:T(8,128)}, u32[]{:S(2)}, u32[]{:S(2)}) collective-permute-start(f32[2,4,128,128]{3,2,1,0:T(8,128)} %get-tuple-element.965), channel_id=1, source_target_pairs={{0,1},{1,2},{2,3},{3,4},{4,5},{5,6},{6,7},{7,8},{8,9},{9,10},{10,1... | collective-permute-start | bytes 1572872 | tf_op jit(solution)/shard_map/while/body/eval_jaxpr/ppermute | solution.py:24
  10.5 1.9 collective-permute-start.1
  16.4 6.2 %collective-permute-done = f32[2,4,128,128]{3,2,1,0:T(8,128)} collective-permute-done((f32[2,4,128,128]{3,2,1,0:T(8,128)}, f32[2,4,128,128]{3,2,1,0:T(8,128)}, u32[]{:S(2)}, u32[]{:S(2)}) %collective-permute-start) | collective-permute-done | bytes 524320 | tf_op jit(solution)/shard_map/while/body/eval_jaxpr/ppermute | solution.py:24
  24.1 2.4 fusion.183
  30.2 4.3 %collective-permute-start = (f32[2,4,128,128]{3,2,1,0:T(8,128)}, f32[2,4,128,128]{3,2,1,0:T(8,128)}, u32[]{:S(2)}, u32[]{:S(2)}) collective-permute-start(f32[2,4,128,128]{3,2,1,0:T(8,128)} %get-tuple-element.965), channel_id=1, source_target_pairs={{0,1},{1,2},{2,3},{3,4},{4,5},{5,6},{6,7},{7,8},{8,9},{9,10},{10,1... | collective-permute-start | bytes 1572872 | tf_op jit(solution)/shard_map/while/body/eval_jaxpr/ppermute | solution.py:24
  34.4 1.9 collective-permute-start.1
  40.2 6.2 %collective-permute-done = f32[2,4,128,128]{3,2,1,0:T(8,128)} collective-permute-done((f32[2,4,128,128]{3,2,1,0:T(8,128)}, f32[2,4,128,128]{3,2,1,0:T(8,128)}, u32[]{:S(2)}, u32[]{:S(2)}) %collective-permute-start) | collective-permute-done | bytes 524320 | tf_op jit(solution)/shard_map/while/body/eval_jaxpr/ppermute | solution.py:24
  46.4 1.1 constant_dynamic-update-slice_fusion.14
  47.8 2.4 fusion.183
  53.9 4.4 %collective-permute-start = (f32[2,4,128,128]{3,2,1,0:T(8,128)}, f32[2,4,128,128]{3,2,1,0:T(8,128)}, u32[]{:S(2)}, u32[]{:S(2)}) collective-permute-start(f32[2,4,128,128]{3,2,1,0:T(8,128)} %get-tuple-element.965), channel_id=1, source_target_pairs={{0,1},{1,2},{2,3},{3,4},{4,5},{5,6},{6,7},{7,8},{8,9},{9,10},{10,1... | collective-permute-start | bytes 1572872 | tf_op jit(solution)/shard_map/while/body/eval_jaxpr/ppermute | solution.py:24
  58.3 1.9 collective-permute-start.1
  64.1 6.2 %collective-permute-done = f32[2,4,128,128]{3,2,1,0:T(8,128)} collective-permute-done((f32[2,4,128,128]{3,2,1,0:T(8,128)}, f32[2,4,128,128]{3,2,1,0:T(8,128)}, u32[]{:S(2)}, u32[]{:S(2)}) %collective-permute-start) | collective-permute-done | bytes 524320 | tf_op jit(solution)/shard_map/while/body/eval_jaxpr/ppermute | solution.py:24
  71.7 2.4 fusion.183
  77.8 4.4 %collective-permute-start = (f32[2,4,128,128]{3,2,1,0:T(8,128)}, f32[2,4,128,128]{3,2,1,0:T(8,128)}, u32[]{:S(2)}, u32[]{:S(2)}) collective-permute-start(f32[2,4,128,128]{3,2,1,0:T(8,128)} %get-tuple-element.965), channel_id=1, source_target_pairs={{0,1},{1,2},{2,3},{3,4},{4,5},{5,6},{6,7},{7,8},{8,9},{9,10},{10,1... | collective-permute-start | bytes 1572872 | tf_op jit(solution)/shard_map/while/body/eval_jaxpr/ppermute | solution.py:24
  82.2 1.9 collective-permute-start.1
  88.0 4.7 %collective-permute-done = f32[2,4,128,128]{3,2,1,0:T(8,128)} collective-permute-done((f32[2,4,128,128]{3,2,1,0:T(8,128)}, f32[2,4,128,128]{3,2,1,0:T(8,128)}, u32[]{:S(2)}, u32[]{:S(2)}) %collective-permute-start) | collective-permute-done | bytes 524320 | tf_op jit(solution)/shard_map/while/body/eval_jaxpr/ppermute | solution.py:24
  94.1 2.4 fusion.183
  100.1 4.4 %collective-permute-start = (f32[2,4,128,128]{3,2,1,0:T(8,128)}, f32[2,4,128,128]{3,2,1,0:T(8,128)}, u32[]{:S(2)}, u32[]{:S(2)}) collective-permute-start(f32[2,4,128,128]{3,2,1,0:T(8,128)} %get-tuple-element.965), channel_id=1, source_target_pairs={{0,1},{1,2},{2,3},{3,4},{4,5},{5,6},{6,7},{7,8},{8,9},{9,10},{10,1... | collective-permute-start | bytes 1572872 | tf_op jit(solution)/shard_map/while/body/eval_jaxpr/ppermute | solution.py:24
  104.5 1.9 collective-permute-start.1
  110.3 3.7 %collective-permute-done = f32[2,4,128,128]{3,2,1,0:T(8,128)} collective-permute-done((f32[2,4,128,128]{3,2,1,0:T(8,128)}, f32[2,4,128,128]{3,2,1,0:T(8,128)}, u32[]{:S(2)}, u32[]{:S(2)}) %collective-permute-start) | collective-permute-done | bytes 524320 | tf_op jit(solution)/shard_map/while/body/eval_jaxpr/ppermute | solution.py:24
  115.4 2.4 fusion.183
  121.5 4.4 %collective-permute-start = (f32[2,4,128,128]{3,2,1,0:T(8,128)}, f32[2,4,128,128]{3,2,1,0:T(8,128)}, u32[]{:S(2)}, u32[]{:S(2)}) collective-permute-start(f32[2,4,128,128]{3,2,1,0:T(8,128)} %get-tuple-element.965), channel_id=1, source_target_pairs={{0,1},{1,2},{2,3},{3,4},{4,5},{5,6},{6,7},{7,8},{8,9},{9,10},{10,1... | collective-permute-start | bytes 1572872 | tf_op jit(solution)/shard_map/while/body/eval_jaxpr/ppermute | solution.py:24
  125.9 1.9 collective-permute-start.1
  131.7 3.6 %collective-permute-done = f32[2,4,128,128]{3,2,1,0:T(8,128)} collective-permute-done((f32[2,4,128,128]{3,2,1,0:T(8,128)}, f32[2,4,128,128]{3,2,1,0:T(8,128)}, u32[]{:S(2)}, u32[]{:S(2)}) %collective-permute-start) | collective-permute-done | bytes 524320 | tf_op jit(solution)/shard_map/while/body/eval_jaxpr/ppermute | solution.py:24
  135.3 1.1 constant_dynamic-update-slice_fusion.14
  136.6 2.4 fusion.183
  141.6 128.2 %while.45 = (s32[]{:T(128)}, f32[2,8,128,128]{3,2,1,0:T(8,128)S(1)}, f32[2,8,128,128]{3,2,1,0:T(8,128)S(1)}, f32[2,8,128,128]{3,2,1,0:T(8,128)}, s32[12]{0:T(128...) while((s32[]{:T(128)}, ...), condition=%wide.region_3.4_spmd.clone, body=%wide.region_2.3_spmd.clone.sunk | while | flops 24529316 | bytes 40568908 | solution.py:155
  142.7 4.4 %collective-permute-start.2 = (f32[2,4,128,128]{3,2,1,0:T(8,128)}, f32[2,4,128,128]{3,2,1,0:T(8,128)}, u32[]{:S(2)}, u32[]{:S(2)}) collective-permute-start(f32[2,4,128,128]{3,2,1,0:T(8,128)} %get-tuple-element.981), channel_id=1, source_target_pairs={{0,1},{1,2},{2,3},{3,4},{4,5},{5,6},{6,7},{7,8},{8,9},{9,10},{10,1... | collective-permute-start | bytes 1572872 | tf_op jit(solution)/shard_map/while/body/eval_jaxpr/ppermute | solution.py:24
  147.1 1.9 collective-permute-start.3
  153.0 3.6 %collective-permute-done.2 = f32[2,4,128,128]{3,2,1,0:T(8,128)} collective-permute-done((f32[2,4,128,128]{3,2,1,0:T(8,128)}, f32[2,4,128,128]{3,2,1,0:T(8,128)}, u32[]{:S(2)}, u32[]{:S(2)}) %collective-permute-start.2) | collective-permute-done | bytes 524320 | tf_op jit(solution)/shard_map/while/body/eval_jaxpr/ppermute | solution.py:24
  158.0 2.4 fusion.188
  164.1 4.4 %collective-permute-start.2 = (f32[2,4,128,128]{3,2,1,0:T(8,128)}, f32[2,4,128,128]{3,2,1,0:T(8,128)}, u32[]{:S(2)}, u32[]{:S(2)}) collective-permute-start(f32[2,4,128,128]{3,2,1,0:T(8,128)} %get-tuple-element.981), channel_id=1, source_target_pairs={{0,1},{1,2},{2,3},{3,4},{4,5},{5,6},{6,7},{7,8},{8,9},{9,10},{10,1... | collective-permute-start | bytes 1572872 | tf_op jit(solution)/shard_map/while/body/eval_jaxpr/ppermute | solution.py:24
  168.5 1.9 collective-permute-start.3
  174.4 3.6 %collective-permute-done.2 = f32[2,4,128,128]{3,2,1,0:T(8,128)} collective-permute-done((f32[2,4,128,128]{3,2,1,0:T(8,128)}, f32[2,4,128,128]{3,2,1,0:T(8,128)}, u32[]{:S(2)}, u32[]{:S(2)}) %collective-permute-start.2) | collective-permute-done | bytes 524320 | tf_op jit(solution)/shard_map/while/body/eval_jaxpr/ppermute | solution.py:24
  179.3 2.4 fusion.188
  185.4 4.4 %collective-permute-start.2 = (f32[2,4,128,128]{3,2,1,0:T(8,128)}, f32[2,4,128,128]{3,2,1,0:T(8,128)}, u32[]{:S(2)}, u32[]{:S(2)}) collective-permute-start(f32[2,4,128,128]{3,2,1,0:T(8,128)} %get-tuple-element.981), channel_id=1, source_target_pairs={{0,1},{1,2},{2,3},{3,4},{4,5},{5,6},{6,7},{7,8},{8,9},{9,10},{10,1... | collective-permute-start | bytes 1572872 | tf_op jit(solution)/shard_map/while/body/eval_jaxpr/ppermute | solution.py:24
  189.8 1.9 collective-permute-start.3
  195.7 3.6 %collective-permute-done.2 = f32[2,4,128,128]{3,2,1,0:T(8,128)} collective-permute-done((f32[2,4,128,128]{3,2,1,0:T(8,128)}, f32[2,4,128,128]{3,2,1,0:T(8,128)}, u32[]{:S(2)}, u32[]{:S(2)}) %collective-permute-start.2) | collective-permute-done | bytes 524320 | tf_op jit(solution)/shard_map/while/body/eval_jaxpr/ppermute | solution.py:24
  200.7 2.4 fusion.188
  206.8 4.4 %collective-permute-start.2 = (f32[2,4,128,128]{3,2,1,0:T(8,128)}, f32[2,4,128,128]{3,2,1,0:T(8,128)}, u32[]{:S(2)}, u32[]{:S(2)}) collective-permute-start(f32[2,4,128,128]{3,2,1,0:T(8,128)} %get-tuple-element.981), channel_id=1, source_target_pairs={{0,1},{1,2},{2,3},{3,4},{4,5},{5,6},{6,7},{7,8},{8,9},{9,10},{10,1... | collective-permute-start | bytes 1572872 | tf_op jit(solution)/shard_map/while/body/eval_jaxpr/ppermute | solution.py:24
  211.2 1.9 collective-permute-start.3
  217.1 3.6 %collective-permute-done.2 = f32[2,4,128,128]{3,2,1,0:T(8,128)} collective-permute-done((f32[2,4,128,128]{3,2,1,0:T(8,128)}, f32[2,4,128,128]{3,2,1,0:T(8,128)}, u32[]{:S(2)}, u32[]{:S(2)}) %collective-permute-start.2) | collective-permute-done | bytes 524320 | tf_op jit(solution)/shard_map/while/body/eval_jaxpr/ppermute | solution.py:24
  222.0 2.4 fusion.188
  228.1 4.4 %collective-permute-start.2 = (f32[2,4,128,128]{3,2,1,0:T(8,128)}, f32[2,4,128,128]{3,2,1,0:T(8,128)}, u32[]{:S(2)}, u32[]{:S(2)}) collective-permute-start(f32[2,4,128,128]{3,2,1,0:T(8,128)} %get-tuple-element.981), channel_id=1, source_target_pairs={{0,1},{1,2},{2,3},{3,4},{4,5},{5,6},{6,7},{7,8},{8,9},{9,10},{10,1... | collective-permute-start | bytes 1572872 | tf_op jit(solution)/shard_map/while/body/eval_jaxpr/ppermute | solution.py:24
  232.5 1.9 collective-permute-start.3
  238.4 3.6 %collective-permute-done.2 = f32[2,4,128,128]{3,2,1,0:T(8,128)} collective-permute-done((f32[2,4,128,128]{3,2,1,0:T(8,128)}, f32[2,4,128,128]{3,2,1,0:T(8,128)}, u32[]{:S(2)}, u32[]{:S(2)}) %collective-permute-start.2) | collective-permute-done | bytes 524320 | tf_op jit(solution)/shard_map/while/body/eval_jaxpr/ppermute | solution.py:24
  243.4 2.4 fusion.188
  249.5 4.4 %collective-permute-start.2 = (f32[2,4,128,128]{3,2,1,0:T(8,128)}, f32[2,4,128,128]{3,2,1,0:T(8,128)}, u32[]{:S(2)}, u32[]{:S(2)}) collective-permute-start(f32[2,4,128,128]{3,2,1,0:T(8,128)} %get-tuple-element.981), channel_id=1, source_target_pairs={{0,1},{1,2},{2,3},{3,4},{4,5},{5,6},{6,7},{7,8},{8,9},{9,10},{10,1... | collective-permute-start | bytes 1572872 | tf_op jit(solution)/shard_map/while/body/eval_jaxpr/ppermute | solution.py:24
  253.9 1.9 collective-permute-start.3
  259.8 3.6 %collective-permute-done.2 = f32[2,4,128,128]{3,2,1,0:T(8,128)} collective-permute-done((f32[2,4,128,128]{3,2,1,0:T(8,128)}, f32[2,4,128,128]{3,2,1,0:T(8,128)}, u32[]{:S(2)}, u32[]{:S(2)}) %collective-permute-start.2) | collective-permute-done | bytes 524320 | tf_op jit(solution)/shard_map/while/body/eval_jaxpr/ppermute | solution.py:24
  264.8 2.4 fusion.188
  269.8 2.9 copy.32
  272.7 8.0 %all-to-all-start.1 = ((f32[2,8,128,128]{3,1,0,2:T(8,128)}), f32[2,8,128,128]{3,1,0,2:T(8,128)S(1)}, u32[]{:S(2)}, u32[]{:S(2)}) async-start(f32[2,8,128,128]{3,1,0,2:T(8,128)} %copy.32), calls=%async_computation.1 | async-start | bytes 2097152 | tf_op jit(solution)/shard_map/all_to_all | solution.py:158
  280.7 1.6 copy.29
  282.3 23.3 %all-to-all-done.1 = f32[2,8,128,128]{3,1,0,2:T(8,128)S(1)} async-done(((f32[2,8,128,128]{3,1,0,2:T(8,128)}), f32[2,8,128,128]{3,1,0,2:T(8,128)S(1)}, u32[]{:S(2)}, u32[]{:S(2)}) %all-to-all-start.1) | async-done | bytes 1048608 | tf_op jit(solution)/shard_map/all_to_all | solution.py:158
  305.6 4.8 %all-to-all-start = ((f32[2,8,128,128]{3,1,0,2:T(8,128)}), f32[2,8,128,128]{3,1,0,2:T(8,128)S(1)}, u32[]{:S(2)}, u32[]{:S(2)}) async-start(f32[2,8,128,128]{3,1,0,2:T(8,128)} %copy.29), calls=%async_computation | async-start | bytes 2097152 | tf_op jit(solution)/shard_map/all_to_all | solution.py:158
  332.5 1.3 copy.41
  333.8 1.5 all-to-all-done
  335.7 1.5 add_bitcast_fusion
  344.0 1.8 divide_convert_fusion
  (259 shorter events, 84.2 us)
Async XLA Ops:
  0.6 5.1 %copy-start.7 = (s32[12]{0:T(128)S(1)}, s32[12]{0:T(128)}, u32[]{:S(2)}) copy-start(s32[12]{0:T(128)} %param.20) | copy-start | bytes 148
  0.6 5.1 %copy-start = (f32[8,128,128]{2,1,0:T(8,128)S(1)}, f32[8,128,128]{2,1,0:T(8,128)}, u32[]{:S(2)}) copy-start(f32[8,128,128]{2,1,0:T(8,128)} %param.18) | copy-start | bytes 1572868
  6.8 15.7 %collective-permute-start = (f32[2,4,128,128]{3,2,1,0:T(8,128)}, f32[2,4,128,128]{3,2,1,0:T(8,128)}, u32[]{:S(2)}, u32[]{:S(2)}) collective-permute-start(f32[2,4,128,128]{3,2,1,0:T(8,128)} %get-tuple-element.965), channel_id=1, source_target_pairs={{0,1},{1,2},{2,3},{3,4},{4,5},{5,6},{6,7},{7,8},{8,9},{9,10},{10,1... | collective-permute-start | bytes 1572872 | tf_op jit(solution)/shard_map/while/body/eval_jaxpr/ppermute | solution.py:24
  10.5 13.5 %collective-permute-start.1 = (f32[2,4,128,128]{3,2,1,0:T(8,128)}, f32[2,4,128,128]{3,2,1,0:T(8,128)S(1)}, u32[]{:S(2)}, u32[]{:S(2)}) collective-permute-start(f32[2,4,128,128]{3,2,1,0:T(8,128)} %get-tuple-element.968), channel_id=1, source_target_pairs={{1,0},{2,1},{3,2},{4,3},{5,4},{6,5},{7,6},{8,7},{9,8},{10,9},{11,1... | collective-permute-start | bytes 1572872 | tf_op jit(solution)/shard_map/while/body/eval_jaxpr/ppermute | solution.py:27
  26.5 1.2 copy-start.3
  28.1 1.0 copy-start.4
  30.2 16.3 %collective-permute-start = (f32[2,4,128,128]{3,2,1,0:T(8,128)}, f32[2,4,128,128]{3,2,1,0:T(8,128)}, u32[]{:S(2)}, u32[]{:S(2)}) collective-permute-start(f32[2,4,128,128]{3,2,1,0:T(8,128)} %get-tuple-element.965), channel_id=1, source_target_pairs={{0,1},{1,2},{2,3},{3,4},{4,5},{5,6},{6,7},{7,8},{8,9},{9,10},{10,1... | collective-permute-start | bytes 1572872 | tf_op jit(solution)/shard_map/while/body/eval_jaxpr/ppermute | solution.py:24
  34.4 13.4 %collective-permute-start.1 = (f32[2,4,128,128]{3,2,1,0:T(8,128)}, f32[2,4,128,128]{3,2,1,0:T(8,128)S(1)}, u32[]{:S(2)}, u32[]{:S(2)}) collective-permute-start(f32[2,4,128,128]{3,2,1,0:T(8,128)} %get-tuple-element.968), channel_id=1, source_target_pairs={{1,0},{2,1},{3,2},{4,3},{5,4},{6,5},{7,6},{8,7},{9,8},{10,9},{11,1... | collective-permute-start | bytes 1572872 | tf_op jit(solution)/shard_map/while/body/eval_jaxpr/ppermute | solution.py:27
  50.2 1.2 copy-start.3
  51.9 1.0 copy-start.4
  53.9 16.4 %collective-permute-start = (f32[2,4,128,128]{3,2,1,0:T(8,128)}, f32[2,4,128,128]{3,2,1,0:T(8,128)}, u32[]{:S(2)}, u32[]{:S(2)}) collective-permute-start(f32[2,4,128,128]{3,2,1,0:T(8,128)} %get-tuple-element.965), channel_id=1, source_target_pairs={{0,1},{1,2},{2,3},{3,4},{4,5},{5,6},{6,7},{7,8},{8,9},{9,10},{10,1... | collective-permute-start | bytes 1572872 | tf_op jit(solution)/shard_map/while/body/eval_jaxpr/ppermute | solution.py:24
  58.3 13.4 %collective-permute-start.1 = (f32[2,4,128,128]{3,2,1,0:T(8,128)}, f32[2,4,128,128]{3,2,1,0:T(8,128)S(1)}, u32[]{:S(2)}, u32[]{:S(2)}) collective-permute-start(f32[2,4,128,128]{3,2,1,0:T(8,128)} %get-tuple-element.968), channel_id=1, source_target_pairs={{1,0},{2,1},{3,2},{4,3},{5,4},{6,5},{7,6},{8,7},{9,8},{10,9},{11,1... | collective-permute-start | bytes 1572872 | tf_op jit(solution)/shard_map/while/body/eval_jaxpr/ppermute | solution.py:27
  74.1 1.2 copy-start.3
  75.7 1.0 copy-start.4
  77.8 14.9 %collective-permute-start = (f32[2,4,128,128]{3,2,1,0:T(8,128)}, f32[2,4,128,128]{3,2,1,0:T(8,128)}, u32[]{:S(2)}, u32[]{:S(2)}) collective-permute-start(f32[2,4,128,128]{3,2,1,0:T(8,128)} %get-tuple-element.965), channel_id=1, source_target_pairs={{0,1},{1,2},{2,3},{3,4},{4,5},{5,6},{6,7},{7,8},{8,9},{9,10},{10,1... | collective-permute-start | bytes 1572872 | tf_op jit(solution)/shard_map/while/body/eval_jaxpr/ppermute | solution.py:24
  82.2 11.8 %collective-permute-start.1 = (f32[2,4,128,128]{3,2,1,0:T(8,128)}, f32[2,4,128,128]{3,2,1,0:T(8,128)S(1)}, u32[]{:S(2)}, u32[]{:S(2)}) collective-permute-start(f32[2,4,128,128]{3,2,1,0:T(8,128)} %get-tuple-element.968), channel_id=1, source_target_pairs={{1,0},{2,1},{3,2},{4,3},{5,4},{6,5},{7,6},{8,7},{9,8},{10,9},{11,1... | collective-permute-start | bytes 1572872 | tf_op jit(solution)/shard_map/while/body/eval_jaxpr/ppermute | solution.py:27
  96.5 1.2 copy-start.3
  98.1 1.0 copy-start.4
  100.1 13.9 %collective-permute-start = (f32[2,4,128,128]{3,2,1,0:T(8,128)}, f32[2,4,128,128]{3,2,1,0:T(8,128)}, u32[]{:S(2)}, u32[]{:S(2)}) collective-permute-start(f32[2,4,128,128]{3,2,1,0:T(8,128)} %get-tuple-element.965), channel_id=1, source_target_pairs={{0,1},{1,2},{2,3},{3,4},{4,5},{5,6},{6,7},{7,8},{8,9},{9,10},{10,1... | collective-permute-start | bytes 1572872 | tf_op jit(solution)/shard_map/while/body/eval_jaxpr/ppermute | solution.py:24
  104.5 10.8 %collective-permute-start.1 = (f32[2,4,128,128]{3,2,1,0:T(8,128)}, f32[2,4,128,128]{3,2,1,0:T(8,128)S(1)}, u32[]{:S(2)}, u32[]{:S(2)}) collective-permute-start(f32[2,4,128,128]{3,2,1,0:T(8,128)} %get-tuple-element.968), channel_id=1, source_target_pairs={{1,0},{2,1},{3,2},{4,3},{5,4},{6,5},{7,6},{8,7},{9,8},{10,9},{11,1... | collective-permute-start | bytes 1572872 | tf_op jit(solution)/shard_map/while/body/eval_jaxpr/ppermute | solution.py:27
  117.8 1.2 copy-start.3
  119.4 1.0 copy-start.4
  121.5 13.8 %collective-permute-start = (f32[2,4,128,128]{3,2,1,0:T(8,128)}, f32[2,4,128,128]{3,2,1,0:T(8,128)}, u32[]{:S(2)}, u32[]{:S(2)}) collective-permute-start(f32[2,4,128,128]{3,2,1,0:T(8,128)} %get-tuple-element.965), channel_id=1, source_target_pairs={{0,1},{1,2},{2,3},{3,4},{4,5},{5,6},{6,7},{7,8},{8,9},{9,10},{10,1... | collective-permute-start | bytes 1572872 | tf_op jit(solution)/shard_map/while/body/eval_jaxpr/ppermute | solution.py:24
  125.9 10.7 %collective-permute-start.1 = (f32[2,4,128,128]{3,2,1,0:T(8,128)}, f32[2,4,128,128]{3,2,1,0:T(8,128)S(1)}, u32[]{:S(2)}, u32[]{:S(2)}) collective-permute-start(f32[2,4,128,128]{3,2,1,0:T(8,128)} %get-tuple-element.968), channel_id=1, source_target_pairs={{1,0},{2,1},{3,2},{4,3},{5,4},{6,5},{7,6},{8,7},{9,8},{10,9},{11,1... | collective-permute-start | bytes 1572872 | tf_op jit(solution)/shard_map/while/body/eval_jaxpr/ppermute | solution.py:27
  139.1 1.2 copy-start.3
  140.7 1.0 copy-start.4
  142.7 13.9 %collective-permute-start.2 = (f32[2,4,128,128]{3,2,1,0:T(8,128)}, f32[2,4,128,128]{3,2,1,0:T(8,128)}, u32[]{:S(2)}, u32[]{:S(2)}) collective-permute-start(f32[2,4,128,128]{3,2,1,0:T(8,128)} %get-tuple-element.981), channel_id=1, source_target_pairs={{0,1},{1,2},{2,3},{3,4},{4,5},{5,6},{6,7},{7,8},{8,9},{9,10},{10,1... | collective-permute-start | bytes 1572872 | tf_op jit(solution)/shard_map/while/body/eval_jaxpr/ppermute | solution.py:24
  147.1 10.8 %collective-permute-start.3 = (f32[2,4,128,128]{3,2,1,0:T(8,128)}, f32[2,4,128,128]{3,2,1,0:T(8,128)S(1)}, u32[]{:S(2)}, u32[]{:S(2)}) collective-permute-start(f32[2,4,128,128]{3,2,1,0:T(8,128)} %get-tuple-element.984), channel_id=1, source_target_pairs={{1,0},{2,1},{3,2},{4,3},{5,4},{6,5},{7,6},{8,7},{9,8},{10,9},{11,1... | collective-permute-start | bytes 1572872 | tf_op jit(solution)/shard_map/while/body/eval_jaxpr/ppermute | solution.py:27
  160.4 1.2 copy-start.1
  162.0 1.0 copy-start.2
  164.1 13.8 %collective-permute-start.2 = (f32[2,4,128,128]{3,2,1,0:T(8,128)}, f32[2,4,128,128]{3,2,1,0:T(8,128)}, u32[]{:S(2)}, u32[]{:S(2)}) collective-permute-start(f32[2,4,128,128]{3,2,1,0:T(8,128)} %get-tuple-element.981), channel_id=1, source_target_pairs={{0,1},{1,2},{2,3},{3,4},{4,5},{5,6},{6,7},{7,8},{8,9},{9,10},{10,1... | collective-permute-start | bytes 1572872 | tf_op jit(solution)/shard_map/while/body/eval_jaxpr/ppermute | solution.py:24
  168.5 10.8 %collective-permute-start.3 = (f32[2,4,128,128]{3,2,1,0:T(8,128)}, f32[2,4,128,128]{3,2,1,0:T(8,128)S(1)}, u32[]{:S(2)}, u32[]{:S(2)}) collective-permute-start(f32[2,4,128,128]{3,2,1,0:T(8,128)} %get-tuple-element.984), channel_id=1, source_target_pairs={{1,0},{2,1},{3,2},{4,3},{5,4},{6,5},{7,6},{8,7},{9,8},{10,9},{11,1... | collective-permute-start | bytes 1572872 | tf_op jit(solution)/shard_map/while/body/eval_jaxpr/ppermute | solution.py:27
  181.7 1.2 copy-start.1
  183.3 1.0 copy-start.2
  185.4 13.9 %collective-permute-start.2 = (f32[2,4,128,128]{3,2,1,0:T(8,128)}, f32[2,4,128,128]{3,2,1,0:T(8,128)}, u32[]{:S(2)}, u32[]{:S(2)}) collective-permute-start(f32[2,4,128,128]{3,2,1,0:T(8,128)} %get-tuple-element.981), channel_id=1, source_target_pairs={{0,1},{1,2},{2,3},{3,4},{4,5},{5,6},{6,7},{7,8},{8,9},{9,10},{10,1... | collective-permute-start | bytes 1572872 | tf_op jit(solution)/shard_map/while/body/eval_jaxpr/ppermute | solution.py:24
  189.8 10.8 %collective-permute-start.3 = (f32[2,4,128,128]{3,2,1,0:T(8,128)}, f32[2,4,128,128]{3,2,1,0:T(8,128)S(1)}, u32[]{:S(2)}, u32[]{:S(2)}) collective-permute-start(f32[2,4,128,128]{3,2,1,0:T(8,128)} %get-tuple-element.984), channel_id=1, source_target_pairs={{1,0},{2,1},{3,2},{4,3},{5,4},{6,5},{7,6},{8,7},{9,8},{10,9},{11,1... | collective-permute-start | bytes 1572872 | tf_op jit(solution)/shard_map/while/body/eval_jaxpr/ppermute | solution.py:27
  203.1 1.2 copy-start.1
  204.7 1.0 copy-start.2
  206.8 13.8 %collective-permute-start.2 = (f32[2,4,128,128]{3,2,1,0:T(8,128)}, f32[2,4,128,128]{3,2,1,0:T(8,128)}, u32[]{:S(2)}, u32[]{:S(2)}) collective-permute-start(f32[2,4,128,128]{3,2,1,0:T(8,128)} %get-tuple-element.981), channel_id=1, source_target_pairs={{0,1},{1,2},{2,3},{3,4},{4,5},{5,6},{6,7},{7,8},{8,9},{9,10},{10,1... | collective-permute-start | bytes 1572872 | tf_op jit(solution)/shard_map/while/body/eval_jaxpr/ppermute | solution.py:24
  211.2 10.8 %collective-permute-start.3 = (f32[2,4,128,128]{3,2,1,0:T(8,128)}, f32[2,4,128,128]{3,2,1,0:T(8,128)S(1)}, u32[]{:S(2)}, u32[]{:S(2)}) collective-permute-start(f32[2,4,128,128]{3,2,1,0:T(8,128)} %get-tuple-element.984), channel_id=1, source_target_pairs={{1,0},{2,1},{3,2},{4,3},{5,4},{6,5},{7,6},{8,7},{9,8},{10,9},{11,1... | collective-permute-start | bytes 1572872 | tf_op jit(solution)/shard_map/while/body/eval_jaxpr/ppermute | solution.py:27
  224.5 1.2 copy-start.1
  226.1 1.0 copy-start.2
  228.1 13.9 %collective-permute-start.2 = (f32[2,4,128,128]{3,2,1,0:T(8,128)}, f32[2,4,128,128]{3,2,1,0:T(8,128)}, u32[]{:S(2)}, u32[]{:S(2)}) collective-permute-start(f32[2,4,128,128]{3,2,1,0:T(8,128)} %get-tuple-element.981), channel_id=1, source_target_pairs={{0,1},{1,2},{2,3},{3,4},{4,5},{5,6},{6,7},{7,8},{8,9},{9,10},{10,1... | collective-permute-start | bytes 1572872 | tf_op jit(solution)/shard_map/while/body/eval_jaxpr/ppermute | solution.py:24
  232.5 10.8 %collective-permute-start.3 = (f32[2,4,128,128]{3,2,1,0:T(8,128)}, f32[2,4,128,128]{3,2,1,0:T(8,128)S(1)}, u32[]{:S(2)}, u32[]{:S(2)}) collective-permute-start(f32[2,4,128,128]{3,2,1,0:T(8,128)} %get-tuple-element.984), channel_id=1, source_target_pairs={{1,0},{2,1},{3,2},{4,3},{5,4},{6,5},{7,6},{8,7},{9,8},{10,9},{11,1... | collective-permute-start | bytes 1572872 | tf_op jit(solution)/shard_map/while/body/eval_jaxpr/ppermute | solution.py:27
  245.9 1.2 copy-start.1
  247.5 1.0 copy-start.2
  249.5 13.8 %collective-permute-start.2 = (f32[2,4,128,128]{3,2,1,0:T(8,128)}, f32[2,4,128,128]{3,2,1,0:T(8,128)}, u32[]{:S(2)}, u32[]{:S(2)}) collective-permute-start(f32[2,4,128,128]{3,2,1,0:T(8,128)} %get-tuple-element.981), channel_id=1, source_target_pairs={{0,1},{1,2},{2,3},{3,4},{4,5},{5,6},{6,7},{7,8},{8,9},{9,10},{10,1... | collective-permute-start | bytes 1572872 | tf_op jit(solution)/shard_map/while/body/eval_jaxpr/ppermute | solution.py:24
  253.9 10.8 %collective-permute-start.3 = (f32[2,4,128,128]{3,2,1,0:T(8,128)}, f32[2,4,128,128]{3,2,1,0:T(8,128)S(1)}, u32[]{:S(2)}, u32[]{:S(2)}) collective-permute-start(f32[2,4,128,128]{3,2,1,0:T(8,128)} %get-tuple-element.984), channel_id=1, source_target_pairs={{1,0},{2,1},{3,2},{4,3},{5,4},{6,5},{7,6},{8,7},{9,8},{10,9},{11,1... | collective-permute-start | bytes 1572872 | tf_op jit(solution)/shard_map/while/body/eval_jaxpr/ppermute | solution.py:27
  267.2 1.2 copy-start.1
  268.8 1.0 copy-start.2
  269.8 10.9 %copy-start.5 = (f32[2,8,128,128]{3,2,1,0:T(8,128)S(1)}, f32[2,8,128,128]{3,2,1,0:T(8,128)}, u32[]{:S(2)}) copy-start(f32[2,8,128,128]{3,2,1,0:T(8,128)} %get-tuple-element.639) | copy-start | bytes 3145732
  269.8 40.6 %copy-start.6 = (s32[8]{0:T(128)S(1)}, s32[8]{0:T(128)}, u32[]{:S(2)}) copy-start(s32[8]{0:T(128)} %param.22) | copy-start | bytes 100
  272.7 33.0 %all-to-all-start.1 = ((f32[2,8,128,128]{3,1,0,2:T(8,128)}), f32[2,8,128,128]{3,1,0,2:T(8,128)S(1)}, u32[]{:S(2)}, u32[]{:S(2)}) async-start(f32[2,8,128,128]{3,1,0,2:T(8,128)} %copy.32), calls=%async_computation.1 | async-start | bytes 2097152 | tf_op jit(solution)/shard_map/all_to_all | solution.py:158
  305.6 29.7 %all-to-all-start = ((f32[2,8,128,128]{3,1,0,2:T(8,128)}), f32[2,8,128,128]{3,1,0,2:T(8,128)S(1)}, u32[]{:S(2)}, u32[]{:S(2)}) async-start(f32[2,8,128,128]{3,1,0,2:T(8,128)} %copy.29), calls=%async_computation | async-start | bytes 2097152 | tf_op jit(solution)/shard_map/all_to_all | solution.py:158
where the time goes:
time: 349 us; the launch traced here: 346 us
  starting transfers between devices  87.6 us (25%)
  waiting for transfers between devices  77.2 us (22%)
  local copies, waits for them, and re-layouts  64.5 us (18%)
  other arithmetic  55.8 us (16%)
  loops' own time  31.6 us (9%)
  between operations  21.2 us (6%)
  matrix products  8.01 us (2%)
    ppermute x12, waiting for transfers between devices, extended_2(): lax.ppermute(lax.slice_in_dim(block, block.shape[dim] - width, None, axis...  52.2 us
    ppermute x12, starting transfers between devices, extended_2(): lax.ppermute(lax.slice_in_dim(block, block.shape[dim] - width, None, axis...  51.7 us
    while x84, local copies, waits for them, and re-layouts  33.2 us
    another operation x2, loops' own time, local(): lax.fori_loop(0, SNAP_EVERY, one_step, (current, previous, empty_snapshot))  31.6 us
    add x12, other arithmetic, advance(): updated = 2.0 * center - previous + speed_term * stencil(extended, layers)  29 us
    all_to_all x2, waiting for transfers between devices, local(): lax.all_to_all(snapshot, 'gz', split_axis=2, concat_axis=1, tiled=True)  24.8 us
    ppermute x12, starting transfers between devices, extended_2(): lax.ppermute(lax.slice_in_dim(block, 0, width, axis=dim), axis, backward)  23 us
    all_to_all x2, starting transfers between devices, local(): lax.all_to_all(snapshot, 'gz', split_axis=2, concat_axis=1, tiled=True)  12.8 us
  transfers between devices with their start and end apart: 26, of which 15 were waited for; matrix products, arithmetic and copies ran while one was open for 11% of the time, Pallas kernels for 0%

commit v1 on v0

v1 whole, which is shorter than its diff:
```python
import functools

import jax
import jax.numpy as jnp
import numpy as np
from jax import lax
from jax.experimental import pallas as pl
from jax.experimental.pallas import tpu as pltpu
from jax.sharding import PartitionSpec as P

SNAP_EVERY = 6
SNAPS = 2
REACH = 4

SCALE = 5040.0
NEAR = (8064.0, -1008.0, 128.0, -9.0)
CENTRE = -43050.0
damping = 0.25
smoothing = 16.0

VMEM = pl.BlockSpec(memory_space=pltpu.VMEM)
SMEM = pl.BlockSpec(memory_space=pltpu.SMEM)
PARAMS = pltpu.CompilerParams(vmem_limit_bytes=24 * 1024 * 1024)


def f32(*shape):
    return jax.ShapeDtypeStruct(shape, jnp.float32)


def cost(flops, bytes_accessed):
    return pl.CostEstimate(flops=int(flops), bytes_accessed=int(bytes_accessed), transcendentals=0)


def banded(size):
    apart = np.abs(np.arange(size)[:, None] - np.arange(size)[None, :])
    table = np.zeros((size, size), np.float32)
    for k, weight in enumerate(NEAR):
        table[apart == k + 1] = weight
    return table


def roles(count):
    table = np.zeros((count, 8), np.int32)
    for i in range(count):
        group, field, half = i // 4, (i // 2) % 2, i % 2
        outer = (group == 0 and half == 0) or (group == count // 4 - 1 and half == 1)
        table[i, :4] = (field, half, outer, group == 0 and half == 0 and field == 1)
    return table


def pairs_to_fields(count):
    first, second = [], []
    for base in range(0, count, 4):
        first += [(base, base), (base + 1, base + 2), (base + 2, base + 1), (base + 3, base + 3)]
        second += [(base, base + 2), (base + 1, base), (base + 2, base + 3), (base + 3, base + 1)]
    return first, second


def pairs_of_halos(count):
    within = [(i, i ^ 1) for i in range(count)]
    between = [(0, 2), (2, 0), (count - 3, count - 1), (count - 1, count - 3)]
    for group in range(count // 4 - 1):
        for field in range(2):
            low, high = 4 * group + 2 * field + 1, 4 * group + 4 + 2 * field
            between += [(low, high), (high, low)]
    return between, within


def faces_kernel(face_steps, faces, out, gathered):
    steps, layers = face_steps.shape[0], out.shape[0]
    gathered[...] = jnp.zeros_like(gathered)

    def one_layer(layer, carry):
        for step in range(steps):
            base = face_steps[step] * (8 * layers) + layer
            gathered[8 * step : 8 * step + 4] = faces[pl.ds(base + 4 * layers, 4, stride=layers), :]
            gathered[8 * step + 4 : 8 * step + 8] = faces[pl.ds(base, 4, stride=layers), :]
        out[layer] = gathered[...].T
        return carry

    lax.fori_loop(0, layers, one_layer, 0)


def place_faces(saved_faces, face_steps):
    slots, eight, layers, ny = saved_faces.shape
    return pl.pallas_call(
        faces_kernel,
        out_shape=f32(layers, ny, 128),
        in_specs=[SMEM, VMEM],
        out_specs=VMEM,
        scratch_shapes=[pltpu.VMEM((128, ny), jnp.float32)],
        compiler_params=PARAMS,
        name="faces",
    )(face_steps, saved_faces.reshape(slots * eight * layers, ny))


def merge_kernel(role, now_a, now_b, before_a, before_b, speed_a, speed_b, face_a, face_b, cur, prev, speed, face, low, high):
    layers = now_a.shape[0]
    field, half = role[0], role[1]

    def one_layer(j, carry):
        place = jnp.where(half == 0, j, 2 * layers - 1 - j)
        part = (place >= layers).astype(jnp.int32)
        q = place - part * layers

        def take(a, b, scale=None):
            def run():
                cur[REACH + j] = a[0][q]
                prev[REACH + j] = a[1][q]
                speed[j] = a[2][q] * (1.0 / SCALE)
                face[j] = a[3][q]

            return run

        pl.when(part == field)(take((now_a, before_a, speed_a, face_a), None))
        pl.when(part != field)(take((now_b, before_b, speed_b, face_b), None))
        return carry

    lax.fori_loop(0, 2 * layers, one_layer, 0)
    low[...] = cur[REACH : 2 * REACH]
    high[...] = cur[2 * layers : 2 * layers + REACH]


def merge(role, parts):
    layers, ny, nx = parts[0].shape
    slab = f32(REACH, ny, nx)
    tall = f32(2 * layers + 2 * REACH, ny, nx)
    whole = f32(2 * layers, ny, nx)
    return pl.pallas_call(
        merge_kernel,
        out_shape=(tall, tall, whole, whole, slab, slab),
        in_specs=[SMEM] + [VMEM] * 8,
        out_specs=(VMEM,) * 6,
        compiler_params=PARAMS,
        name="merge",
    )(role, *parts)


def step_layers(step, role, across, along, cur, prev, speed, face, new, first, last, skip):
    ny, nx = speed.shape[1:]
    is_source = role[0] == 0
    column = lax.broadcasted_iota(jnp.int32, (ny, nx), 1)
    edge = ((column < REACH) | (column >= nx - REACH)) & is_source

    def one_layer(j, carry):
        layer = jnp.where(j < skip[0], j, j + skip[1]) if skip else j
        e = layer + REACH
        u = cur[e]
        high = u.astype(jnp.bfloat16)
        low = (u - high.astype(jnp.float32)).astype(jnp.bfloat16)
        total = jnp.dot(
            jnp.concatenate([high, low], axis=1), across[...], preferred_element_type=jnp.float32
        ) + jnp.dot(along[...], jnp.concatenate([high, low], axis=0), preferred_element_type=jnp.float32)
        for k in range(REACH):
            total = total + NEAR[k] * (cur[e + (k + 1)] + cur[e - (k + 1)])
        total = total + CENTRE * u
        updated = 2.0 * u - prev[e] + speed[layer] * total
        placed = pltpu.roll(face[layer], (128 - 8 * step - REACH) % 128, axis=1)
        new[e] = jnp.where(edge, placed, updated)
        return carry

    lax.fori_loop(first, last, one_layer, 0)


def fill_halos(role, low, high, cur):
    layers = cur.shape[0] - 2 * REACH
    inside = role[2] == 0
    for d in range(REACH):
        cur[REACH - 1 - d] = jnp.where(inside, low[d], 0.0)
        cur[REACH + layers + d] = high[REACH - 1 - d]


def add_trace(role, trace, new):
    @pl.when(role[3] == 1)
    def _():
        new[REACH] = new[REACH] + trace[...].astype(jnp.float32)


def keep_snapshot(step, role, phase, new, snap):
    count, layers, rows, _ = snap.shape
    window = step // SNAP_EVERY

    @pl.when(phase[window] == step - window * SNAP_EVERY)
    def _():
        def one_layer(j, carry):
            place = jnp.where(role[1] == 0, j, layers - 1 - j)
            for strip in range(count):
                snap[strip, place] = new[REACH + j, strip * rows : (strip + 1) * rows, :]
            return carry

        lax.fori_loop(0, layers, one_layer, 0)


def border_kernel(step, role, across, along, low, high, trace, speed, face, cur_in, prev, cur, new, low_out, high_out):
    layers = speed.shape[0]
    fill_halos(role, low, high, cur)
    step_layers(
        step, role, across, along, cur, prev, speed, face, new, 0, 2 * REACH, (REACH, layers - 2 * REACH)
    )
    add_trace(role, trace, new)
    low_out[...] = new[REACH : 2 * REACH]
    high_out[...] = new[layers : layers + REACH]


def inner_kernel(step, has_snap, role, phase, across, along, speed, face, cur, prev, *rest):
    new, snap = rest[-2:]
    layers = speed.shape[0]
    step_layers(step, role, across, along, cur, prev, speed, face, new, REACH, layers - REACH, None)
    keep_snapshot(step, role, phase, new, snap)


def last_kernel(
    step, role, phase, across, along, low, high, trace, speed, face, cur_in, prev, snap_in, cur, new, snap, out_a, out_b
):
    layers = speed.shape[0]
    fill_halos(role, low, high, cur)
    step_layers(step, role, across, along, cur, prev, speed, face, new, 0, layers, None)
    add_trace(role, trace, new)
    keep_snapshot(step, role, phase, new, snap)
    field, half = role[0], role[1]

    def one_layer(j, carry):
        place = jnp.where(half == 0, j, layers - 1 - j)
        part = (place >= layers // 2).astype(jnp.int32)
        q = place - part * (layers // 2)

        @pl.when(part == field)
        def _():
            out_a[q] = new[REACH + j]

        @pl.when(part != field)
        def _():
            out_b[q] = new[REACH + j]

        return carry

    lax.fori_loop(0, layers, one_layer, 0)


def image_kernel(lags, sweep, first, second, out, light):
    count, layers, rows, nx = first.shape
    depth = out.shape[1]

    def where_is(d):
        block = d // layers
        return (block // 2) * 4 + block % 2, d % layers

    def down(d, carried):
        block, layer = where_is(d)
        s0, s1 = first[block, layer], second[block, layer]
        carried = (s0 * s0 + s1 * s1) * sweep[d] + carried * (smoothing * sweep[d])
        light[d] = carried
        return carried

    lax.fori_loop(0, depth, down, jnp.zeros((rows, nx), jnp.float32), unroll=4)

    column = lax.broadcasted_iota(jnp.int32, (rows, nx), 1)

    def up(i, carried):
        d = depth - 1 - i
        block, layer = where_is(d)
        smooth = light[d] + carried * (smoothing * sweep[d])
        inverse = 1.0 / (smooth + damping)
        s0, s1 = first[block, layer], second[block, layer]
        r0, r1 = first[block + 2, layer], second[block + 2, layer]
        for index in range(out.shape[0]):
            lag = lags[index]
            size = jnp.abs(lag)
            right, left = lax.rem(lag + nx, nx), lax.rem(nx - lag, nx)
            raw = pltpu.roll(s0, right, axis=1) * pltpu.roll(r0, left, axis=1) + pltpu.roll(
                s1, right, axis=1
            ) * pltpu.roll(r1, left, axis=1)
            inside = (column >= size) & (column < nx - size)
            out[index, d] = jnp.where(inside, raw * inverse, 0.0).astype(out.dtype)
        return smooth

    lax.fori_loop(0, depth, up, jnp.zeros((rows, nx), jnp.float32), unroll=2)


def sweep_table(depth):
    table, before = [], 0.0
    for _ in range(depth):
        before = 1.0 / (1.0 + 2.0 * smoothing - smoothing * smoothing * before)
        table.append(before)
    return np.array(table, np.float32)


def images(lag_offsets, first, second):
    count, layers, rows, nx = first.shape
    depth = count // 2 * layers
    lags = lag_offsets.shape[0]
    return pl.pallas_call(
        image_kernel,
        out_shape=jax.ShapeDtypeStruct((lags, depth, rows, nx), jnp.bfloat16),
        in_specs=[SMEM, SMEM, VMEM, VMEM],
        out_specs=VMEM,
        scratch_shapes=[pltpu.VMEM((depth, rows, nx), jnp.float32)],
        compiler_params=pltpu.CompilerParams(vmem_limit_bytes=40 * 1024 * 1024),
        name="images",
    )(lag_offsets, jnp.asarray(sweep_table(depth)), first, second)


def local(
    source_now,
    source_before,
    receiver_now,
    receiver_before,
    speed_term,
    saved_faces,
    face_steps,
    traces,
    lag_offsets,
    snap_phase,
):
    count = lax.axis_size("gz")
    index = lax.axis_index("gz")
    own, ny, nx = source_now.shape
    layers = 2 * own
    rows = ny // count
    steps = face_steps.shape[0]
    role = lax.dynamic_index_in_dim(jnp.asarray(roles(count)), index, 0, keepdims=False)
    first_pairs, second_pairs = pairs_to_fields(count)
    back_pairs = [(b, a) for a, b in second_pairs]
    between, within = pairs_of_halos(count)
    band_x, band_y = banded(nx), banded(ny)
    across = jnp.asarray(np.concatenate([band_x, band_x], axis=0), jnp.bfloat16)
    along = jnp.asarray(np.concatenate([band_y, band_y], axis=1), jnp.bfloat16)

    keeps = index % 2 == 0

    def regroup(a, b):
        return (
            lax.ppermute(jnp.where(keeps, a, b), "gz", first_pairs),
            lax.ppermute(jnp.where(keeps, b, a), "gz", second_pairs),
        )

    faces = place_faces(saved_faces, face_steps)
    parts = (
        *regroup(source_now, receiver_now),
        *regroup(source_before, receiver_before),
        lax.ppermute(speed_term, "gz", first_pairs),
        lax.ppermute(speed_term, "gz", second_pairs),
        lax.ppermute(faces, "gz", first_pairs),
        lax.ppermute(faces, "gz", second_pairs),
    )
    cur, prev, speed, face, low, high = merge(role, parts)

    tall = f32(layers + 2 * REACH, ny, nx)
    slab = f32(REACH, ny, nx)
    strips = f32(count, layers, rows, nx)
    plane = ny * nx
    snap = None
    gathered = []
    for step in range(steps):
        low = lax.ppermute(low, "gz", between)
        high = lax.ppermute(high, "gz", within)
        trace = traces[step]
        if step < steps - 1:
            cur, new, low, high = pl.pallas_call(
                functools.partial(border_kernel, step),
                out_shape=(tall, tall, slab, slab),
                in_specs=[SMEM] + [VMEM] * 9,
                out_specs=(VMEM,) * 4,
                input_output_aliases={8: 0, 9: 1},
                compiler_params=PARAMS,
                cost_estimate=cost(60 * 8 * plane, 4 * 40 * plane),
                name="border",
            )(role, across, along, low, high, trace, speed, face, cur, prev)
            fresh = step % SNAP_EVERY == 0
            new, snap = pl.pallas_call(
                functools.partial(inner_kernel, step, not fresh),
                out_shape=(tall, strips),
                in_specs=[SMEM, SMEM] + [VMEM] * (6 if fresh else 7),
                out_specs=(VMEM,) * 2,
                input_output_aliases={7: 0} if fresh else {7: 0, 8: 1},
                compiler_params=PARAMS,
                cost_estimate=cost(60 * (layers - 8) * plane, 4 * 40 * plane),
                name="inner",
            )(role, snap_phase, across, along, speed, face, cur, new, *(() if fresh else (snap,)))
        else:
            cur, new, snap, out_a, out_b = pl.pallas_call(
                functools.partial(last_kernel, step),
                out_shape=(tall, tall, strips, f32(own, ny, nx), f32(own, ny, nx)),
                in_specs=[SMEM, SMEM] + [VMEM] * 10,
                out_specs=(VMEM,) * 5,
                input_output_aliases={9: 0, 10: 1, 11: 2},
                compiler_params=PARAMS,
                cost_estimate=cost(60 * layers * plane, 4 * 80 * plane),
                name="last",
            )(role, snap_phase, across, along, low, high, trace, speed, face, cur, prev, snap)
        prev, cur = cur, new
        if step % SNAP_EVERY == SNAP_EVERY - 1:
            gathered.append(lax.all_to_all(snap, "gz", split_axis=0, concat_axis=0, tiled=True))

    back_a = lax.ppermute(out_a, "gz", first_pairs)
    back_b = lax.ppermute(out_b, "gz", back_pairs)
    image_out = images(lag_offsets, *gathered)
    return (image_out, jnp.where(keeps, back_a, back_b), jnp.where(keeps, back_b, back_a))


def solution(mesh):
    return jax.shard_map(
        local,
        mesh=mesh,
        in_specs=(
            P(("shot", "gz"), None, None),
            P(("shot", "gz"), None, None),
            P(("shot", "gz"), None, None),
            P(("shot", "gz"), None, None),
            P("gz", None, None),
            P("shot", None, "gz", None),
            P(),
            P("shot", None, None),
            P(),
            P(),
        ),
        out_specs=(
            P("shot", None, "gz", None),
            P(("shot", "gz"), None, None),
            P(("shot", "gz"), None, None),
        ),
        check_vma=False,
    )
```

time: 349 us -> 248 us (0.71)
  Pallas kernels: 0 us -> 70.2 us
  other arithmetic: 55.8 us -> 4.54 us
  local copies, waits for them, and re-layouts: 64.5 us -> 23.1 us
  starting transfers between devices: 87.6 us -> 51 us
  loops' own time: 31.6 us -> 0 us
  between operations: 21.2 us -> 1.13 us
  waiting for transfers between devices: 77.2 us -> 94.7 us
  matrix products: 8.01 us -> 0 us
    pallas_call x0 -> x26, Pallas kernels: none -> 70.2 us  [the longest x11 24.8 us: local(): pl.pallas_call(functools.partial(border_kernel, step), out_shape=(tall, t...]
    ppermute x24 -> x34, waiting for transfers between devices: 52.4 us -> 92.6 us  [the longest x12 55.8 us: local(): low = lax.ppermute(low, 'gz', between)]
    while x86 -> x0, local copies, waits for them, and re-layouts: 37.7 us -> none
    ppermute x24 -> x34, starting transfers between devices: 74.8 us -> 37.9 us  [the longest x2 13.3 us: regroup(): lax.ppermute(jnp.where(keeps, a, b), 'gz', first_pairs)]
    another operation x2 -> x0, loops' own time: 31.6 us -> none  [local(): lax.fori_loop(0, SNAP_EVERY, one_step, (current, previous, empty_snapshot))]
    add x24 -> x0, other arithmetic: 30.3 us -> none  [the longest x12 29 us: advance(): updated = 2.0 * center - previous + speed_term * stencil(extended, layers)]
    all_to_all x2, waiting for transfers between devices: 24.8 us -> 2.07 us  [local(): lax.all_to_all(snap, 'gz', split_axis=0, concat_axis=0, tiled=True)]
    unnamed x10 -> x76, local copies, waits for them, and re-layouts: 1.18 us -> 22.4 us
  transfers between devices with their start and end apart: 26 -> 36, of which waited for: 15 -> 21; matrix products, arithmetic and copies ran while one was open for 11% -> 2% of each run, Pallas kernels for 0% -> 15%
where the time goes in v1:
time: 248 us; the launch traced here: 245 us
  waiting for transfers between devices  94.7 us (38%)
  Pallas kernels  70.2 us (28%)
  starting transfers between devices  51 us (21%)
  local copies, waits for them, and re-layouts  23.1 us (9%)
  other arithmetic  4.54 us (2%)
    ppermute x12, waiting for transfers between devices, local(): low = lax.ppermute(low, 'gz', between)  55.8 us
    pallas_call x11, Pallas kernels, local(): pl.pallas_call(functools.partial(border_kernel, step), out_shape=(tall, t...  24.8 us
    pallas_call x11, Pallas kernels, local(): pl.pallas_call(functools.partial(inner_kernel, step, not fresh), out_shap...  23.5 us
    unnamed x76, local copies, waits for them, and re-layouts  22.4 us
    pallas_call x1, Pallas kernels, images(): pl.pallas_call(image_kernel, out_shape=jax.ShapeDtypeStruct((lags, depth,...  15 us
    ppermute x2, starting transfers between devices, regroup(): lax.ppermute(jnp.where(keeps, a, b), 'gz', first_pairs)  13.3 us
    all_to_all x2, starting transfers between devices, local(): lax.all_to_all(snap, 'gz', split_axis=0, concat_axis=0, tiled=True)  13 us
    ppermute x12, starting transfers between devices, local(): low = lax.ppermute(low, 'gz', between)  12.6 us
  transfers between devices with their start and end apart: 36, of which 21 were waited for; matrix products, arithmetic and copies ran while one was open for 2% of the time, Pallas kernels for 15%

profile of v1, /device:TPU:9, one launch (start us, length us, event | category | flops | bytes accessed | tf_op | source)
XLA Modules:
  0.0 244.6 jit_solution(16940668041034134840)
XLA Ops:
  2.3 1.4 faces.1
  4.4 3.0 %collective-permute-start.6 = (f32[8,128,128]{2,1,0:T(8,128)S(1)}, f32[8,128,128]{2,1,0:T(8,128)S(1)}, u32[]{:S(2)}, u32[]{:S(2)}) collective-permute-start(f32[8,128,128]{2,1,0:T(8,128)S(1)} %faces.1), channel_id=1, source_target_pairs={{0,0},{1,2},{2,1},{3,3},{4,4},{5,6},{6,5},{7,7},{8,8},{9,10},{10,9... | collective-permute-start | bytes 1572872 | tf_op jit(solution)/shard_map/ppermute | solution.py:343
  7.5 2.5 %collective-permute-start.4 = (f32[8,128,128]{2,1,0:T(8,128)}, f32[8,128,128]{2,1,0:T(8,128)S(1)}, u32[]{:S(2)}, u32[]{:S(2)}) collective-permute-start(f32[8,128,128]{2,1,0:T(8,128)} %param.18), channel_id=1, source_target_pairs={{0,0},{1,2},{2,1},{3,3},{4,4},{5,6},{6,5},{7,7},{8,8},{9,10},{10,9... | collective-permute-start | bytes 1572872 | tf_op jit(solution)/shard_map/ppermute | solution.py:341
  10.0 2.4 broadcast_select_fusion.4
  12.5 1.1 broadcast_select_fusion.2
  15.0 6.6 %collective-permute-start = (f32[8,128,128]{2,1,0:T(8,128)}, f32[8,128,128]{2,1,0:T(8,128)S(1)}, u32[]{:S(2)}, u32[]{:S(2)}) collective-permute-start(f32[8,128,128]{2,1,0:T(8,128)} %get-tuple-element.158), channel_id=1, source_target_pairs={{0,0},{1,2},{2,1},{3,3},{4,4},{5,6},{6,5},{7,7},{8,8},{9,10},{10,9... | collective-permute-start | bytes 1572872 | tf_op jit(solution)/shard_map/ppermute | solution.py:333
  22.5 3.0 %collective-permute-done.5.speed_b = f32[8,128,128]{2,1,0:T(8,128)S(1)} collective-permute-done((f32[8,128,128]{2,1,0:T(8,128)}, f32[8,128,128]{2,1,0:T(8,128)S(1)}, u32[]{:S(2)}, u32[]{:S(2)}) %collective-permute-start.5) | collective-permute-done | bytes 524320 | tf_op jit(solution)/shard_map/ppermute | solution.py:342
  26.3 6.6 %collective-permute-start.2 = (f32[8,128,128]{2,1,0:T(8,128)}, f32[8,128,128]{2,1,0:T(8,128)S(1)}, u32[]{:S(2)}, u32[]{:S(2)}) collective-permute-start(f32[8,128,128]{2,1,0:T(8,128)} %get-tuple-element.156), channel_id=1, source_target_pairs={{0,0},{1,2},{2,1},{3,3},{4,4},{5,6},{6,5},{7,7},{8,8},{9,10},{10,9... | collective-permute-start | bytes 1572872 | tf_op jit(solution)/shard_map/ppermute | solution.py:333
  34.5 2.3 collective-permute-done.1.now_b
  37.5 5.5 %collective-permute-done.now_a = f32[8,128,128]{2,1,0:T(8,128)S(1)} collective-permute-done((f32[8,128,128]{2,1,0:T(8,128)}, f32[8,128,128]{2,1,0:T(8,128)S(1)}, u32[]{:S(2)}, u32[]{:S(2)}) %collective-permute-start) | collective-permute-done | bytes 524320 | tf_op jit(solution)/shard_map/ppermute | solution.py:333
  43.8 4.2 %collective-permute-done.3.before_b = f32[8,128,128]{2,1,0:T(8,128)S(1)} collective-permute-done((f32[8,128,128]{2,1,0:T(8,128)}, f32[8,128,128]{2,1,0:T(8,128)S(1)}, u32[]{:S(2)}, u32[]{:S(2)}) %collective-permute-start.3) | collective-permute-done | bytes 524320 | tf_op jit(solution)/shard_map/ppermute | solution.py:334
  48.8 2.9 %collective-permute-done.2.before_a = f32[8,128,128]{2,1,0:T(8,128)S(1)} collective-permute-done((f32[8,128,128]{2,1,0:T(8,128)}, f32[8,128,128]{2,1,0:T(8,128)S(1)}, u32[]{:S(2)}, u32[]{:S(2)}) %collective-permute-start.2) | collective-permute-done | bytes 524320 | tf_op jit(solution)/shard_map/ppermute | solution.py:333
  60.8 1.2 merge.1
  62.0 1.1 collective-permute-start.8
  63.1 4.7 %collective-permute-done.8.low = f32[4,128,128]{2,1,0:T(8,128)S(1)} collective-permute-done((f32[4,128,128]{2,1,0:T(8,128)S(1)}, f32[4,128,128]{2,1,0:T(8,128)S(1)}, u32[]{:S(2)}, u32[]{:S(2)}) %collective-permute-start.8) | collective-permute-done | bytes 262176 | tf_op jit(solution)/shard_map/ppermute | solution.py:355
  67.9 2.3 border.11
  70.1 1.1 collective-permute-start.10
  71.2 2.1 inner.11
  73.4 2.6 %collective-permute-done.10.low = f32[4,128,128]{2,1,0:T(8,128)S(1)} collective-permute-done((f32[4,128,128]{2,1,0:T(8,128)S(1)}, f32[4,128,128]{2,1,0:T(8,128)S(1)}, u32[]{:S(2)}, u32[]{:S(2)}) %collective-permute-start.10) | collective-permute-done | bytes 262176 | tf_op jit(solution)/shard_map/ppermute | solution.py:355
  76.0 2.3 border.12
  78.3 1.1 collective-permute-start.12
  79.5 2.1 inner.12
  81.6 2.5 %collective-permute-done.12.low = f32[4,128,128]{2,1,0:T(8,128)S(1)} collective-permute-done((f32[4,128,128]{2,1,0:T(8,128)S(1)}, f32[4,128,128]{2,1,0:T(8,128)S(1)}, u32[]{:S(2)}, u32[]{:S(2)}) %collective-permute-start.12) | collective-permute-done | bytes 262176 | tf_op jit(solution)/shard_map/ppermute | solution.py:355
  84.1 2.3 border.13
  86.4 1.1 collective-permute-start.14
  87.9 2.3 inner.13
  90.2 2.1 collective-permute-done.14.low
  92.2 2.3 border.14
  94.5 1.1 collective-permute-start.16
  96.3 2.1 inner.14
  98.4 1.9 collective-permute-done.16.low
  100.4 2.3 border.15
  102.6 1.1 collective-permute-start.18
  104.7 2.1 inner.15
  106.9 1.6 collective-permute-done.18.low
  108.5 2.3 border.16
  110.8 2.1 inner.16
  113.9 8.4 %all-to-all-start = ((f32[16,16,8,128]{3,2,1,0:T(8,128)}), f32[16,16,8,128]{3,2,1,0:T(8,128)}, u32[]{:S(2)}, u32[]{:S(2)}) async-start(f32[16,16,8,128]{3,2,1,0:T(8,128)} %copy-done.4), calls=%async_computation | async-start | bytes 2097152 | tf_op jit(solution)/shard_map/all_to_all | solution.py:393
  122.3 1.5 collective-permute-start.20
  123.8 26.2 %collective-permute-done.20.low = f32[4,128,128]{2,1,0:T(8,128)S(1)} collective-permute-done((f32[4,128,128]{2,1,0:T(8,128)}, f32[4,128,128]{2,1,0:T(8,128)S(1)}, u32[]{:S(2)}, u32[]{:S(2)}) %collective-permute-start.20) | collective-permute-done | bytes 262176 | tf_op jit(solution)/shard_map/ppermute | solution.py:355
  150.0 1.2 copy-done.1
  151.2 1.2 copy-done.3
  152.4 2.3 border.17
  155.6 2.1 inner.17
  157.7 2.8 %collective-permute-done.22.low = f32[4,128,128]{2,1,0:T(8,128)S(1)} collective-permute-done((f32[4,128,128]{2,1,0:T(8,128)S(1)}, f32[4,128,128]{2,1,0:T(8,128)S(1)}, u32[]{:S(2)}, u32[]{:S(2)}) %collective-permute-start.22) | collective-permute-done | bytes 262176 | tf_op jit(solution)/shard_map/ppermute | solution.py:355
  160.6 2.3 border.18
  163.7 2.1 inner.18
  165.8 2.8 %collective-permute-done.24.low = f32[4,128,128]{2,1,0:T(8,128)S(1)} collective-permute-done((f32[4,128,128]{2,1,0:T(8,128)S(1)}, f32[4,128,128]{2,1,0:T(8,128)S(1)}, u32[]{:S(2)}, u32[]{:S(2)}) %collective-permute-start.24) | collective-permute-done | bytes 262176 | tf_op jit(solution)/shard_map/ppermute | solution.py:355
  168.7 2.3 border.19
  171.8 2.1 inner.19
  174.0 2.8 %collective-permute-done.26.low = f32[4,128,128]{2,1,0:T(8,128)S(1)} collective-permute-done((f32[4,128,128]{2,1,0:T(8,128)S(1)}, f32[4,128,128]{2,1,0:T(8,128)S(1)}, u32[]{:S(2)}, u32[]{:S(2)}) %collective-permute-start.26) | collective-permute-done | bytes 262176 | tf_op jit(solution)/shard_map/ppermute | solution.py:355
  176.8 2.3 border.20
  180.0 2.1 inner.20
  182.1 2.8 %collective-permute-done.28.low = f32[4,128,128]{2,1,0:T(8,128)S(1)} collective-permute-done((f32[4,128,128]{2,1,0:T(8,128)S(1)}, f32[4,128,128]{2,1,0:T(8,128)S(1)}, u32[]{:S(2)}, u32[]{:S(2)}) %collective-permute-start.28) | collective-permute-done | bytes 262176 | tf_op jit(solution)/shard_map/ppermute | solution.py:355
  184.9 2.3 border.21
  188.1 2.1 inner.21
  190.2 2.8 %collective-permute-done.30.low = f32[4,128,128]{2,1,0:T(8,128)S(1)} collective-permute-done((f32[4,128,128]{2,1,0:T(8,128)S(1)}, f32[4,128,128]{2,1,0:T(8,128)S(1)}, u32[]{:S(2)}, u32[]{:S(2)}) %collective-permute-start.30) | collective-permute-done | bytes 262176 | tf_op jit(solution)/shard_map/ppermute | solution.py:355
  193.1 4.3 %last.1 = (f32[24,128,128]{2,1,0:T(8,128)S(1)}, f32[24,128,128]{2,1,0:T(8,128)S(1)}, f32[16,16,8,128]{3,2,1,0:T(8,128)S(1)}, f32[8,128,128]{2,1,0:T(8,128)S(1)}, f32[8,128,128]{2,1,0:T(8,128)S(1)}) custom-call(s32[8]{0:T(128)S(1)} %dynamic-slice_bitcast_fusion.role, s32[2]{0:T(128)S(1)} %copy-done.25, ...), custom_call_target="tpu_custom_call", output_to_operand_aliasing={{0}: (9, {}), {1}: (10, {}), {2}: (11, {})} | custom-call | flops 15728640 | bytes 5242880 | tf_op jit(solution)/shard_map/last/pallas_call | solution.py:381
  199.9 4.7 %all-to-all-start.1 = ((f32[16,16,8,128]{3,2,1,0:T(8,128)}), f32[16,16,8,128]{3,2,1,0:T(8,128)S(1)}, u32[]{:S(2)}, u32[]{:S(2)}) async-start(f32[16,16,8,128]{3,2,1,0:T(8,128)} %copy-done.5), calls=%async_computation.1 | async-start | bytes 2097152 | tf_op jit(solution)/shard_map/all_to_all | solution.py:393
  204.6 3.4 %collective-permute-start.32 = (f32[8,128,128]{2,1,0:T(8,128)S(1)}, f32[8,128,128]{2,1,0:T(8,128)S(1)}, u32[]{:S(2)}, u32[]{:S(2)}) collective-permute-start(f32[8,128,128]{2,1,0:T(8,128)S(1)} %copy-done.32), channel_id=1, source_target_pairs={{0,0},{1,2},{2,1},{3,3},{4,4},{5,6},{6,5},{7,7},{8,8},{9,10},{10,9... | collective-permute-start | bytes 1572872 | tf_op jit(solution)/shard_map/ppermute | solution.py:395
  208.0 12.5 %collective-permute-done.32 = f32[8,128,128]{2,1,0:T(8,128)S(1)} collective-permute-done((f32[8,128,128]{2,1,0:T(8,128)S(1)}, f32[8,128,128]{2,1,0:T(8,128)S(1)}, u32[]{:S(2)}, u32[]{:S(2)}) %collective-permute-start.32) | collective-permute-done | bytes 524320 | tf_op jit(solution)/shard_map/ppermute | solution.py:395
  220.6 5.8 %collective-permute-done.33 = f32[8,128,128]{2,1,0:T(8,128)S(1)} collective-permute-done((f32[8,128,128]{2,1,0:T(8,128)S(1)}, f32[8,128,128]{2,1,0:T(8,128)S(1)}, u32[]{:S(2)}, u32[]{:S(2)}) %collective-permute-start.33) | collective-permute-done | bytes 524320 | tf_op jit(solution)/shard_map/ppermute | solution.py:396
  227.5 2.1 all-to-all-done.1.second
  229.5 15.0 %images.1 = bf16[8,128,8,128]{3,2,1,0:T(8,128)(2,1)} custom-call(s32[8]{0:T(128)S(1)} %copy-done.27, f32[128]{0:T(128)S(1)} %copy-done.28, f32[16,16,8,128]{3,2,1,0:T(8,128)} %all-to-all-done.first, f32[16,16,8,128]{3,2,1,0:T(8,128)S(1)} %all-to-all-done.1.second), custom_call_target="tpu_custom_call" | custom-call | tf_op jit(solution)/shard_map/images/pallas_call | solution.py:292
  (115 shorter events, 29.9 us)
Async XLA Ops:
  0.6 1.0 copy-start.24
  3.7 10.5 %collective-permute-start.7 = (f32[8,128,128]{2,1,0:T(8,128)S(1)}, f32[8,128,128]{2,1,0:T(8,128)S(1)}, u32[]{:S(2)}, u32[]{:S(2)}) collective-permute-start(f32[8,128,128]{2,1,0:T(8,128)S(1)} %faces.1), channel_id=1, source_target_pairs={{0,2},{1,0},{2,3},{3,1},{4,6},{5,4},{6,7},{7,5},{8,10},{9,8},{10,1... | collective-permute-start | bytes 1572872 | tf_op jit(solution)/shard_map/ppermute | solution.py:344
  4.4 17.3 %collective-permute-start.6 = (f32[8,128,128]{2,1,0:T(8,128)S(1)}, f32[8,128,128]{2,1,0:T(8,128)S(1)}, u32[]{:S(2)}, u32[]{:S(2)}) collective-permute-start(f32[8,128,128]{2,1,0:T(8,128)S(1)} %faces.1), channel_id=1, source_target_pairs={{0,0},{1,2},{2,1},{3,3},{4,4},{5,6},{6,5},{7,7},{8,8},{9,10},{10,9... | collective-permute-start | bytes 1572872 | tf_op jit(solution)/shard_map/ppermute | solution.py:343
  7.5 18.0 %collective-permute-start.5 = (f32[8,128,128]{2,1,0:T(8,128)}, f32[8,128,128]{2,1,0:T(8,128)S(1)}, u32[]{:S(2)}, u32[]{:S(2)}) collective-permute-start(f32[8,128,128]{2,1,0:T(8,128)} %param.18), channel_id=1, source_target_pairs={{0,2},{1,0},{2,3},{3,1},{4,6},{5,4},{6,7},{7,5},{8,10},{9,8},{10,1... | collective-permute-start | bytes 1572872 | tf_op jit(solution)/shard_map/ppermute | solution.py:342
  7.5 26.2 %collective-permute-start.4 = (f32[8,128,128]{2,1,0:T(8,128)}, f32[8,128,128]{2,1,0:T(8,128)S(1)}, u32[]{:S(2)}, u32[]{:S(2)}) collective-permute-start(f32[8,128,128]{2,1,0:T(8,128)} %param.18), channel_id=1, source_target_pairs={{0,0},{1,2},{2,1},{3,3},{4,4},{5,6},{6,5},{7,7},{8,8},{9,10},{10,9... | collective-permute-start | bytes 1572872 | tf_op jit(solution)/shard_map/ppermute | solution.py:341
  10.0 2.5 %copy-start.35 = (f32[8,128,128]{2,1,0:T(8,128)S(1)}, f32[8,128,128]{2,1,0:T(8,128)}, u32[]{:S(2)}) copy-start(f32[8,128,128]{2,1,0:T(8,128)} %param.17) | copy-start | bytes 1572868
  10.0 2.5 %copy-start.36 = (f32[8,128,128]{2,1,0:T(8,128)S(1)}, f32[8,128,128]{2,1,0:T(8,128)}, u32[]{:S(2)}) copy-start(f32[8,128,128]{2,1,0:T(8,128)} %param.15) | copy-start | bytes 1572868
  12.4 24.3 %collective-permute-start.1 = (f32[8,128,128]{2,1,0:T(8,128)}, f32[8,128,128]{2,1,0:T(8,128)S(1)}, u32[]{:S(2)}, u32[]{:S(2)}) collective-permute-start(f32[8,128,128]{2,1,0:T(8,128)} %get-tuple-element.157), channel_id=1, source_target_pairs={{0,2},{1,0},{2,3},{3,1},{4,6},{5,4},{6,7},{7,5},{8,10},{9,8},{10,1... | collective-permute-start | bytes 1572872 | tf_op jit(solution)/shard_map/ppermute | solution.py:334
  15.0 27.9 %collective-permute-start = (f32[8,128,128]{2,1,0:T(8,128)}, f32[8,128,128]{2,1,0:T(8,128)S(1)}, u32[]{:S(2)}, u32[]{:S(2)}) collective-permute-start(f32[8,128,128]{2,1,0:T(8,128)} %get-tuple-element.158), channel_id=1, source_target_pairs={{0,0},{1,2},{2,1},{3,3},{4,4},{5,6},{6,5},{7,7},{8,8},{9,10},{10,9... | collective-permute-start | bytes 1572872 | tf_op jit(solution)/shard_map/ppermute | solution.py:333
  22.5 25.5 %collective-permute-start.3 = (f32[8,128,128]{2,1,0:T(8,128)}, f32[8,128,128]{2,1,0:T(8,128)S(1)}, u32[]{:S(2)}, u32[]{:S(2)}) collective-permute-start(f32[8,128,128]{2,1,0:T(8,128)} %get-tuple-element.155), channel_id=1, source_target_pairs={{0,2},{1,0},{2,3},{3,1},{4,6},{5,4},{6,7},{7,5},{8,10},{9,8},{10,1... | collective-permute-start | bytes 1572872 | tf_op jit(solution)/shard_map/ppermute | solution.py:334
  25.5 0.8 copy-start.12
  26.3 25.4 %collective-permute-start.2 = (f32[8,128,128]{2,1,0:T(8,128)}, f32[8,128,128]{2,1,0:T(8,128)S(1)}, u32[]{:S(2)}, u32[]{:S(2)}) collective-permute-start(f32[8,128,128]{2,1,0:T(8,128)} %get-tuple-element.156), channel_id=1, source_target_pairs={{0,0},{1,2},{2,1},{3,3},{4,4},{5,6},{6,5},{7,7},{8,8},{9,10},{10,9... | collective-permute-start | bytes 1572872 | tf_op jit(solution)/shard_map/ppermute | solution.py:333
  33.6 34.2 %copy-start.6 = (bf16[128,256]{1,0:T(8,128)(2,1)S(1)}, bf16[128,256]{1,0:T(8,128)(2,1)}, u32[]{:S(2)}) copy-start(bf16[128,256]{1,0:T(8,128)(2,1)} %constant.33.clone.along) | copy-start | bytes 196612
  33.6 34.2 %copy-start.7 = (bf16[256,128]{1,0:T(8,128)(2,1)S(1)}, bf16[256,128]{1,0:T(8,128)(2,1)}, u32[]{:S(2)}) copy-start(bf16[256,128]{1,0:T(8,128)(2,1)} %constant.32.clone.across) | copy-start | bytes 196612
  52.5 1.0 copy-start.9
  53.5 1.0 copy-start.11
  54.5 1.0 copy-start.13
  55.6 1.0 copy-start.15
  56.6 1.0 copy-start.17
  57.7 1.0 copy-start.19
  58.7 1.0 copy-start.21
  59.8 1.0 copy-start.23
  60.8 2.3 copy-start.37
  62.0 48.8 %copy-start = (f32[16,128,128]{2,1,0:T(8,128)}, f32[16,128,128]{2,1,0:T(8,128)S(1)}, u32[]{:S(2)}) copy-start(f32[16,128,128]{2,1,0:T(8,128)S(1)} %get-tuple-element.78.speed) | copy-start | bytes 3145732
  62.0 48.8 %copy-start.2 = (f32[16,128,128]{2,1,0:T(8,128)}, f32[16,128,128]{2,1,0:T(8,128)S(1)}, u32[]{:S(2)}) copy-start(f32[16,128,128]{2,1,0:T(8,128)S(1)} %get-tuple-element.79.face) | copy-start | bytes 3145732
  62.0 5.9 %collective-permute-start.8 = (f32[4,128,128]{2,1,0:T(8,128)S(1)}, f32[4,128,128]{2,1,0:T(8,128)S(1)}, u32[]{:S(2)}, u32[]{:S(2)}) collective-permute-start(f32[4,128,128]{2,1,0:T(8,128)S(1)} %get-tuple-element.80), channel_id=1, source_target_pairs={{0,2},{2,0},{13,15},{15,13},{1,4},{4,1},{3,6},{6,3},{5,8},{8,5},{7... | collective-permute-start | bytes 786440 | tf_op jit(solution)/shard_map/ppermute | solution.py:355
  63.1 4.8 %collective-permute-start.9 = (f32[4,128,128]{2,1,0:T(8,128)S(1)}, f32[4,128,128]{2,1,0:T(8,128)S(1)}, u32[]{:S(2)}, u32[]{:S(2)}) collective-permute-start(f32[4,128,128]{2,1,0:T(8,128)S(1)} %get-tuple-element.81), channel_id=1, source_target_pairs={{0,1},{1,0},{2,3},{3,2},{4,5},{5,4},{6,7},{7,6},{8,9},{9,8},{10,11... | collective-permute-start | bytes 786440 | tf_op jit(solution)/shard_map/ppermute | solution.py:356
  67.9 3.4 %copy-start.25 = (s32[2]{0:T(128)S(1)}, s32[2]{0:T(128)}, u32[]{:S(2)}) copy-start(s32[2]{0:T(128)} %phase.23) | copy-start | bytes 28
  70.1 5.9 %collective-permute-start.10 = (f32[4,128,128]{2,1,0:T(8,128)S(1)}, f32[4,128,128]{2,1,0:T(8,128)S(1)}, u32[]{:S(2)}, u32[]{:S(2)}) collective-permute-start(f32[4,128,128]{2,1,0:T(8,128)S(1)} %get-tuple-element.84), channel_id=1, source_target_pairs={{0,2},{2,0},{13,15},{15,13},{1,4},{4,1},{3,6},{6,3},{5,8},{8,5},{7... | collective-permute-start | bytes 786440 | tf_op jit(solution)/shard_map/ppermute | solution.py:355
  71.2 4.8 %collective-permute-start.11 = (f32[4,128,128]{2,1,0:T(8,128)S(1)}, f32[4,128,128]{2,1,0:T(8,128)S(1)}, u32[]{:S(2)}, u32[]{:S(2)}) collective-permute-start(f32[4,128,128]{2,1,0:T(8,128)S(1)} %get-tuple-element.85), channel_id=1, source_target_pairs={{0,1},{1,0},{2,3},{3,2},{4,5},{5,4},{6,7},{7,6},{8,9},{9,8},{10,11... | collective-permute-start | bytes 786440 | tf_op jit(solution)/shard_map/ppermute | solution.py:356
  78.3 5.9 %collective-permute-start.12 = (f32[4,128,128]{2,1,0:T(8,128)S(1)}, f32[4,128,128]{2,1,0:T(8,128)S(1)}, u32[]{:S(2)}, u32[]{:S(2)}) collective-permute-start(f32[4,128,128]{2,1,0:T(8,128)S(1)} %get-tuple-element.89), channel_id=1, source_target_pairs={{0,2},{2,0},{13,15},{15,13},{1,4},{4,1},{3,6},{6,3},{5,8},{8,5},{7... | collective-permute-start | bytes 786440 | tf_op jit(solution)/shard_map/ppermute | solution.py:355
  79.4 4.8 %collective-permute-start.13 = (f32[4,128,128]{2,1,0:T(8,128)S(1)}, f32[4,128,128]{2,1,0:T(8,128)S(1)}, u32[]{:S(2)}, u32[]{:S(2)}) collective-permute-start(f32[4,128,128]{2,1,0:T(8,128)S(1)} %get-tuple-element.90), channel_id=1, source_target_pairs={{0,1},{1,0},{2,3},{3,2},{4,5},{5,4},{6,7},{7,6},{8,9},{9,8},{10,11... | collective-permute-start | bytes 786440 | tf_op jit(solution)/shard_map/ppermute | solution.py:356
  86.4 5.9 %collective-permute-start.14 = (f32[4,128,128]{2,1,0:T(8,128)S(1)}, f32[4,128,128]{2,1,0:T(8,128)S(1)}, u32[]{:S(2)}, u32[]{:S(2)}) collective-permute-start(f32[4,128,128]{2,1,0:T(8,128)S(1)} %get-tuple-element.95), channel_id=1, source_target_pairs={{0,2},{2,0},{13,15},{15,13},{1,4},{4,1},{3,6},{6,3},{5,8},{8,5},{7... | collective-permute-start | bytes 786440 | tf_op jit(solution)/shard_map/ppermute | solution.py:355
  87.5 4.8 %collective-permute-start.15 = (f32[4,128,128]{2,1,0:T(8,128)S(1)}, f32[4,128,128]{2,1,0:T(8,128)S(1)}, u32[]{:S(2)}, u32[]{:S(2)}) collective-permute-start(f32[4,128,128]{2,1,0:T(8,128)S(1)} %get-tuple-element.96), channel_id=1, source_target_pairs={{0,1},{1,0},{2,3},{3,2},{4,5},{5,4},{6,7},{7,6},{8,9},{9,8},{10,11... | collective-permute-start | bytes 786440 | tf_op jit(solution)/shard_map/ppermute | solution.py:356
  94.5 5.9 %collective-permute-start.16 = (f32[4,128,128]{2,1,0:T(8,128)S(1)}, f32[4,128,128]{2,1,0:T(8,128)S(1)}, u32[]{:S(2)}, u32[]{:S(2)}) collective-permute-start(f32[4,128,128]{2,1,0:T(8,128)S(1)} %get-tuple-element.101), channel_id=1, source_target_pairs={{0,2},{2,0},{13,15},{15,13},{1,4},{4,1},{3,6},{6,3},{5,8},{8,5},{7... | collective-permute-start | bytes 786440 | tf_op jit(solution)/shard_map/ppermute | solution.py:355
  95.6 4.8 %collective-permute-start.17 = (f32[4,128,128]{2,1,0:T(8,128)S(1)}, f32[4,128,128]{2,1,0:T(8,128)S(1)}, u32[]{:S(2)}, u32[]{:S(2)}) collective-permute-start(f32[4,128,128]{2,1,0:T(8,128)S(1)} %get-tuple-element.102), channel_id=1, source_target_pairs={{0,1},{1,0},{2,3},{3,2},{4,5},{5,4},{6,7},{7,6},{8,9},{9,8},{10,11... | collective-permute-start | bytes 786440 | tf_op jit(solution)/shard_map/ppermute | solution.py:356
  102.6 5.9 %collective-permute-start.18 = (f32[4,128,128]{2,1,0:T(8,128)S(1)}, f32[4,128,128]{2,1,0:T(8,128)S(1)}, u32[]{:S(2)}, u32[]{:S(2)}) collective-permute-start(f32[4,128,128]{2,1,0:T(8,128)S(1)} %get-tuple-element.107), channel_id=1, source_target_pairs={{0,2},{2,0},{13,15},{15,13},{1,4},{4,1},{3,6},{6,3},{5,8},{8,5},{7... | collective-permute-start | bytes 786440 | tf_op jit(solution)/shard_map/ppermute | solution.py:355
  103.7 4.8 %collective-permute-start.19 = (f32[4,128,128]{2,1,0:T(8,128)S(1)}, f32[4,128,128]{2,1,0:T(8,128)S(1)}, u32[]{:S(2)}, u32[]{:S(2)}) collective-permute-start(f32[4,128,128]{2,1,0:T(8,128)S(1)} %get-tuple-element.108), channel_id=1, source_target_pairs={{0,1},{1,0},{2,3},{3,2},{4,5},{5,4},{6,7},{7,6},{8,9},{9,8},{10,11... | collective-permute-start | bytes 786440 | tf_op jit(solution)/shard_map/ppermute | solution.py:356
  110.8 2.2 copy-start.33
  110.8 2.2 copy-start.34
  113.0 1.0 copy-start.4
  113.9 86.0 %all-to-all-start = ((f32[16,16,8,128]{3,2,1,0:T(8,128)}), f32[16,16,8,128]{3,2,1,0:T(8,128)}, u32[]{:S(2)}, u32[]{:S(2)}) async-start(f32[16,16,8,128]{3,2,1,0:T(8,128)} %copy-done.4), calls=%async_computation | async-start | bytes 2097152 | tf_op jit(solution)/shard_map/all_to_all | solution.py:393
  122.3 27.7 %collective-permute-start.20 = (f32[4,128,128]{2,1,0:T(8,128)}, f32[4,128,128]{2,1,0:T(8,128)S(1)}, u32[]{:S(2)}, u32[]{:S(2)}) collective-permute-start(f32[4,128,128]{2,1,0:T(8,128)} %copy-done.34), channel_id=1, source_target_pairs={{0,2},{2,0},{13,15},{15,13},{1,4},{4,1},{3,6},{6,3},{5,8},{8,5},{7... | collective-permute-start | bytes 786440 | tf_op jit(solution)/shard_map/ppermute | solution.py:355
  123.8 26.2 %collective-permute-start.21 = (f32[4,128,128]{2,1,0:T(8,128)}, f32[4,128,128]{2,1,0:T(8,128)S(1)}, u32[]{:S(2)}, u32[]{:S(2)}) collective-permute-start(f32[4,128,128]{2,1,0:T(8,128)} %copy-done.33), channel_id=1, source_target_pairs={{0,1},{1,0},{2,3},{3,2},{4,5},{5,4},{6,7},{7,6},{8,9},{9,8},{10,11... | collective-permute-start | bytes 786440 | tf_op jit(solution)/shard_map/ppermute | solution.py:356
  150.0 1.2 copy-start.1
  151.2 1.2 copy-start.3
  154.7 5.9 %collective-permute-start.22 = (f32[4,128,128]{2,1,0:T(8,128)S(1)}, f32[4,128,128]{2,1,0:T(8,128)S(1)}, u32[]{:S(2)}, u32[]{:S(2)}) collective-permute-start(f32[4,128,128]{2,1,0:T(8,128)S(1)} %get-tuple-element.120), channel_id=1, source_target_pairs={{0,2},{2,0},{13,15},{15,13},{1,4},{4,1},{3,6},{6,3},{5,8},{8,5},{7... | collective-permute-start | bytes 786440 | tf_op jit(solution)/shard_map/ppermute | solution.py:355
  155.6 5.0 %collective-permute-start.23 = (f32[4,128,128]{2,1,0:T(8,128)S(1)}, f32[4,128,128]{2,1,0:T(8,128)S(1)}, u32[]{:S(2)}, u32[]{:S(2)}) collective-permute-start(f32[4,128,128]{2,1,0:T(8,128)S(1)} %get-tuple-element.121), channel_id=1, source_target_pairs={{0,1},{1,0},{2,3},{3,2},{4,5},{5,4},{6,7},{7,6},{8,9},{9,8},{10,11... | collective-permute-start | bytes 786440 | tf_op jit(solution)/shard_map/ppermute | solution.py:356
  162.8 5.9 %collective-permute-start.24 = (f32[4,128,128]{2,1,0:T(8,128)S(1)}, f32[4,128,128]{2,1,0:T(8,128)S(1)}, u32[]{:S(2)}, u32[]{:S(2)}) collective-permute-start(f32[4,128,128]{2,1,0:T(8,128)S(1)} %get-tuple-element.125), channel_id=1, source_target_pairs={{0,2},{2,0},{13,15},{15,13},{1,4},{4,1},{3,6},{6,3},{5,8},{8,5},{7... | collective-permute-start | bytes 786440 | tf_op jit(solution)/shard_map/ppermute | solution.py:355
  163.7 5.0 %collective-permute-start.25 = (f32[4,128,128]{2,1,0:T(8,128)S(1)}, f32[4,128,128]{2,1,0:T(8,128)S(1)}, u32[]{:S(2)}, u32[]{:S(2)}) collective-permute-start(f32[4,128,128]{2,1,0:T(8,128)S(1)} %get-tuple-element.126), channel_id=1, source_target_pairs={{0,1},{1,0},{2,3},{3,2},{4,5},{5,4},{6,7},{7,6},{8,9},{9,8},{10,11... | collective-permute-start | bytes 786440 | tf_op jit(solution)/shard_map/ppermute | solution.py:356
  170.9 5.9 %collective-permute-start.26 = (f32[4,128,128]{2,1,0:T(8,128)S(1)}, f32[4,128,128]{2,1,0:T(8,128)S(1)}, u32[]{:S(2)}, u32[]{:S(2)}) collective-permute-start(f32[4,128,128]{2,1,0:T(8,128)S(1)} %get-tuple-element.131), channel_id=1, source_target_pairs={{0,2},{2,0},{13,15},{15,13},{1,4},{4,1},{3,6},{6,3},{5,8},{8,5},{7... | collective-permute-start | bytes 786440 | tf_op jit(solution)/shard_map/ppermute | solution.py:355
  171.8 5.0 %collective-permute-start.27 = (f32[4,128,128]{2,1,0:T(8,128)S(1)}, f32[4,128,128]{2,1,0:T(8,128)S(1)}, u32[]{:S(2)}, u32[]{:S(2)}) collective-permute-start(f32[4,128,128]{2,1,0:T(8,128)S(1)} %get-tuple-element.132), channel_id=1, source_target_pairs={{0,1},{1,0},{2,3},{3,2},{4,5},{5,4},{6,7},{7,6},{8,9},{9,8},{10,11... | collective-permute-start | bytes 786440 | tf_op jit(solution)/shard_map/ppermute | solution.py:356
  179.1 5.9 %collective-permute-start.28 = (f32[4,128,128]{2,1,0:T(8,128)S(1)}, f32[4,128,128]{2,1,0:T(8,128)S(1)}, u32[]{:S(2)}, u32[]{:S(2)}) collective-permute-start(f32[4,128,128]{2,1,0:T(8,128)S(1)} %get-tuple-element.137), channel_id=1, source_target_pairs={{0,2},{2,0},{13,15},{15,13},{1,4},{4,1},{3,6},{6,3},{5,8},{8,5},{7... | collective-permute-start | bytes 786440 | tf_op jit(solution)/shard_map/ppermute | solution.py:355
  180.0 5.0 %collective-permute-start.29 = (f32[4,128,128]{2,1,0:T(8,128)S(1)}, f32[4,128,128]{2,1,0:T(8,128)S(1)}, u32[]{:S(2)}, u32[]{:S(2)}) collective-permute-start(f32[4,128,128]{2,1,0:T(8,128)S(1)} %get-tuple-element.138), channel_id=1, source_target_pairs={{0,1},{1,0},{2,3},{3,2},{4,5},{5,4},{6,7},{7,6},{8,9},{9,8},{10,11... | collective-permute-start | bytes 786440 | tf_op jit(solution)/shard_map/ppermute | solution.py:356
  187.2 5.9 %collective-permute-start.30 = (f32[4,128,128]{2,1,0:T(8,128)S(1)}, f32[4,128,128]{2,1,0:T(8,128)S(1)}, u32[]{:S(2)}, u32[]{:S(2)}) collective-permute-start(f32[4,128,128]{2,1,0:T(8,128)S(1)} %get-tuple-element.143), channel_id=1, source_target_pairs={{0,2},{2,0},{13,15},{15,13},{1,4},{4,1},{3,6},{6,3},{5,8},{8,5},{7... | collective-permute-start | bytes 786440 | tf_op jit(solution)/shard_map/ppermute | solution.py:355
  188.1 5.0 %collective-permute-start.31 = (f32[4,128,128]{2,1,0:T(8,128)S(1)}, f32[4,128,128]{2,1,0:T(8,128)S(1)}, u32[]{:S(2)}, u32[]{:S(2)}) collective-permute-start(f32[4,128,128]{2,1,0:T(8,128)S(1)} %get-tuple-element.144), channel_id=1, source_target_pairs={{0,1},{1,0},{2,3},{3,2},{4,5},{5,4},{6,7},{7,6},{8,9},{9,8},{10,11... | collective-permute-start | bytes 786440 | tf_op jit(solution)/shard_map/ppermute | solution.py:356
  197.4 1.0 copy-start.5
  199.9 4.7 %copy-start.32 = (f32[8,128,128]{2,1,0:T(8,128)S(1)}, f32[8,128,128]{2,1,0:T(8,128)}, u32[]{:S(2)}) copy-start(f32[8,128,128]{2,1,0:T(8,128)} %copy-done.31) | copy-start | bytes 1572868
  199.9 8.1 %copy-start.30 = (f32[8,128,128]{2,1,0:T(8,128)S(1)}, f32[8,128,128]{2,1,0:T(8,128)}, u32[]{:S(2)}) copy-start(f32[8,128,128]{2,1,0:T(8,128)} %copy-done.29) | copy-start | bytes 1572868
  199.9 29.6 %all-to-all-start.1 = ((f32[16,16,8,128]{3,2,1,0:T(8,128)}), f32[16,16,8,128]{3,2,1,0:T(8,128)S(1)}, u32[]{:S(2)}, u32[]{:S(2)}) async-start(f32[16,16,8,128]{3,2,1,0:T(8,128)} %copy-done.5), calls=%async_computation.1 | async-start | bytes 2097152 | tf_op jit(solution)/shard_map/all_to_all | solution.py:393
  204.6 24.9 %copy-start.27 = (s32[8]{0:T(128)S(1)}, s32[8]{0:T(128)}, u32[]{:S(2)}) copy-start(s32[8]{0:T(128)} %lags.1) | copy-start | bytes 100
  204.6 24.9 %copy-start.28 = (f32[128]{0:T(128)S(1)}, f32[128]{0:T(128)}, u32[]{:S(2)}) copy-start(f32[128]{0:T(128)} %constant.34.clone.sweep) | copy-start | bytes 1540
  204.6 15.9 %collective-permute-start.32 = (f32[8,128,128]{2,1,0:T(8,128)S(1)}, f32[8,128,128]{2,1,0:T(8,128)S(1)}, u32[]{:S(2)}, u32[]{:S(2)}) collective-permute-start(f32[8,128,128]{2,1,0:T(8,128)S(1)} %copy-done.32), channel_id=1, source_target_pairs={{0,0},{1,2},{2,1},{3,3},{4,4},{5,6},{6,5},{7,7},{8,8},{9,10},{10,9... | collective-permute-start | bytes 1572872 | tf_op jit(solution)/shard_map/ppermute | solution.py:395
  208.0 18.4 %collective-permute-start.33 = (f32[8,128,128]{2,1,0:T(8,128)S(1)}, f32[8,128,128]{2,1,0:T(8,128)S(1)}, u32[]{:S(2)}, u32[]{:S(2)}) collective-permute-start(f32[8,128,128]{2,1,0:T(8,128)S(1)} %copy-done.30), channel_id=1, source_target_pairs={{2,0},{0,1},{3,2},{1,3},{6,4},{4,5},{7,6},{5,7},{10,8},{8,9},{11,1... | collective-permute-start | bytes 1572872 | tf_op jit(solution)/shard_map/ppermute | solution.py:396
  (10 other events, 7.8 us)

commit v2 on v1

v2 whole, which is shorter than its diff:
```python
import functools

import jax
import jax.numpy as jnp
import numpy as np
from jax import lax
from jax.experimental import pallas as pl
from jax.experimental.pallas import tpu as pltpu
from jax.sharding import PartitionSpec as P

SNAP_EVERY = 6
SNAPS = 2
REACH = 4
EARLY = 2

SCALE = 5040.0
NEAR = (8064.0, -1008.0, 128.0, -9.0)
CENTRE = -43050.0
damping = 0.25
smoothing = 16.0

VMEM = pl.BlockSpec(memory_space=pltpu.VMEM)
SMEM = pl.BlockSpec(memory_space=pltpu.SMEM)
ANY = pl.BlockSpec(memory_space=pl.ANY)
PARAMS = pltpu.CompilerParams(vmem_limit_bytes=24 * 1024 * 1024)


def f32(*shape):
    return jax.ShapeDtypeStruct(shape, jnp.float32)


def held(*shape):
    return pltpu.VMEM(shape, jnp.float32)


def cost(flops, bytes_accessed):
    return pl.CostEstimate(flops=int(flops), bytes_accessed=int(bytes_accessed), transcendentals=0)


def banded(size):
    apart = np.abs(np.arange(size)[:, None] - np.arange(size)[None, :])
    table = np.zeros((size, size), np.float32)
    for k, weight in enumerate(NEAR):
        table[apart == k + 1] = weight
    return table


def pairs_to_fields(count):
    first, second = [], []
    for base in range(0, count, 4):
        first += [(base, base), (base + 1, base + 2), (base + 2, base + 1), (base + 3, base + 3)]
        second += [(base, base + 2), (base + 1, base), (base + 2, base + 3), (base + 3, base + 1)]
    return first, second


def pairs_of_halos(count):
    within = [(i, i ^ 1) for i in range(count)]
    between = [(0, 2), (2, 0), (count - 3, count - 1), (count - 1, count - 3)]
    for group in range(count // 4 - 1):
        for field in range(2):
            low, high = 4 * group + 2 * field + 1, 4 * group + 4 + 2 * field
            between += [(low, high), (high, low)]
    return between, within


def my_field():
    return lax.rem(lax.axis_index("gz") // 2, 2)


def my_half():
    return lax.rem(lax.axis_index("gz"), 2)


def place_of(local, layers):
    return jnp.where(my_half() == 0, local, layers - 1 - local)


def choose_kernel(here, there, first, second, sem):
    def copies(a, b):
        return pltpu.make_async_copy(a, first, sem.at[0]), pltpu.make_async_copy(b, second, sem.at[1])

    def run(a, b):
        one, two = copies(a, b)
        one.start()
        two.start()
        one.wait()
        two.wait()

    pl.when(my_half() == 0)(lambda: run(here, there))
    pl.when(my_half() != 0)(lambda: run(there, here))


def choose(here, there, spec):
    like = jax.ShapeDtypeStruct(here.shape, here.dtype)
    return pl.pallas_call(
        choose_kernel,
        out_shape=(like, like),
        in_specs=[ANY, ANY],
        out_specs=(spec, spec),
        scratch_shapes=[pltpu.SemaphoreType.DMA((2,))],
        compiler_params=PARAMS,
        name="choose",
    )(here, there)


def prepare_kernel(face_steps, lags, faces, late, early, shifts, gathered):
    steps, layers = face_steps.shape[0], late.shape[0]
    nx = shifts.shape[1] // 2
    gathered[...] = jnp.zeros_like(gathered)

    def gather(step, layer, row):
        base = face_steps[step] * (8 * layers) + layer
        gathered[row : row + 4] = faces[pl.ds(base + 4 * layers, 4, stride=layers), :]
        gathered[row + 4 : row + 8] = faces[pl.ds(base, 4, stride=layers), :]

    for layer in range(layers):
        for step in range(EARLY):
            gather(step, layer, 8 * (EARLY * layer + step))
    early[...] = gathered[...].T

    def one_layer(layer, carry):
        for step in range(steps):
            gather(step, layer, 8 * step)
        late[layer] = gathered[...].T
        return carry

    lax.fori_loop(0, layers, one_layer, 0)

    apart = lax.broadcasted_iota(jnp.int32, (nx, nx), 1) - lax.broadcasted_iota(jnp.int32, (nx, nx), 0)
    for index in range(lags.shape[0]):
        columns = slice(index * nx, (index + 1) * nx)
        for which, lag in ((0, lags[index]), (1, -lags[index])):
            moved = jnp.where(apart == lag, 1.0, 0.0).astype(jnp.bfloat16)
            shifts[which, :nx, columns] = moved
            shifts[which, nx:, columns] = moved


def prepare(saved_faces, face_steps, lag_offsets, nx):
    slots, eight, layers, ny = saved_faces.shape
    return pl.pallas_call(
        prepare_kernel,
        out_shape=(
            f32(layers, ny, 128),
            f32(ny, 128),
            jax.ShapeDtypeStruct((2, 2 * nx, lag_offsets.shape[0] * nx), jnp.bfloat16),
        ),
        in_specs=[SMEM, SMEM, VMEM],
        out_specs=(VMEM,) * 3,
        scratch_shapes=[pltpu.VMEM((128, ny), jnp.float32)],
        compiler_params=PARAMS,
        name="prepare",
    )(face_steps, lag_offsets, saved_faces.reshape(slots * eight * layers, ny))


def for_each_part(layers, run):
    def one_layer(j, carry):
        place = place_of(j, layers)
        part = (place >= layers // 2).astype(jnp.int32)
        q = place - part * (layers // 2)
        pl.when(part == my_field())(lambda: run(j, q, 0))
        pl.when(part != my_field())(lambda: run(j, q, 1))
        return carry

    lax.fori_loop(0, layers, one_layer, 0, unroll=2)


def merge_now_kernel(now_a, now_b, cur, low, high):
    layers = 2 * now_a.shape[0]

    def run(j, q, which):
        cur[REACH + j] = (now_a, now_b)[which][q]

    for_each_part(layers, run)
    low[...] = cur[REACH : 2 * REACH]
    high[...] = cur[layers : layers + REACH]


def merge_rest_kernel(before_a, before_b, speed_a, speed_b, prev, speed):
    def run(j, q, which):
        prev[REACH + j] = (before_a, before_b)[which][q]
        speed[j] = (speed_a, speed_b)[which][q] * (1.0 / SCALE)

    for_each_part(2 * before_a.shape[0], run)


def merge_faces_kernel(face_a, face_b, face):
    def run(j, q, which):
        face[j] = (face_a, face_b)[which][q]

    for_each_part(2 * face_a.shape[0], run)


def merge(kernel, name, shapes, *parts):
    return pl.pallas_call(
        kernel,
        out_shape=shapes,
        in_specs=[VMEM] * len(parts),
        out_specs=(VMEM,) * len(shapes),
        compiler_params=PARAMS,
        name=name,
    )(*parts)


def split(u):
    high = u.astype(jnp.bfloat16)
    return high, (u - high.astype(jnp.float32)).astype(jnp.bfloat16)


def advance(step, across, along, cur, prev, speed, faces, new, local):
    layers, ny, nx = speed.shape
    column = lax.broadcasted_iota(jnp.int32, (ny, nx), 1)
    edge = ((column < REACH) | (column >= nx - REACH)) & (my_field() == 0)

    def placed(layer):
        if step >= EARLY:
            return pltpu.roll(faces[0][layer], (128 - 8 * step - REACH) % 128, axis=1)
        place = place_of(layer, layers)
        part = (place >= layers // 2).astype(jnp.int32)
        lane = 8 * (EARLY * (place - part * (layers // 2)) + step) + REACH
        held = jnp.where(part == 0, faces[0][...], faces[1][...])
        return pltpu.roll(held, lax.rem(128 - lane, 128), axis=1)

    for first in range(0, len(local), 2):
        pair = local[first : first + 2]
        inputs = [cur[REACH + layer] for layer in pair]
        halves = [split(u) for u in inputs]
        along_sum = jnp.dot(
            along[...],
            jnp.concatenate([jnp.concatenate(half, axis=0) for half in halves], axis=1),
            preferred_element_type=jnp.float32,
        )
        across_sum = jnp.dot(
            jnp.concatenate([jnp.concatenate(half, axis=1) for half in halves], axis=0),
            across[...],
            preferred_element_type=jnp.float32,
        )
        for i, layer in enumerate(pair):
            e, u = REACH + layer, inputs[i]
            total = across_sum[i * ny : (i + 1) * ny] + along_sum[:, i * nx : (i + 1) * nx]
            for k in range(REACH):
                total = total + NEAR[k] * (cur[e + (k + 1)] + cur[e - (k + 1)])
            total = total + CENTRE * u
            updated = 2.0 * u - prev[e] + speed[layer] * total
            new[e] = jnp.where(edge, placed(layer), updated)


def fill_halos(low, high, cur):
    layers = cur.shape[0] - 2 * REACH
    index = lax.axis_index("gz")
    count = lax.axis_size("gz")
    place = 2 * (index // 4) + my_half()
    inside = (place > 0) & (place < count // 2 - 1)
    for d in range(REACH):
        cur[REACH - 1 - d] = jnp.where(inside, low[d], 0.0)
        cur[REACH + layers + d] = high[REACH - 1 - d]


def add_trace(step, traces, new):
    @pl.when(lax.axis_index("gz") == 2)
    def _():
        new[REACH] = new[REACH] + traces[step].astype(jnp.float32)


def keep_snapshot(step, phase, new, snap):
    count, _, layers, rows, _ = snap.shape
    window = step // SNAP_EVERY

    @pl.when(phase[window] == step - window * SNAP_EVERY)
    def _():
        def one_layer(j, carry):
            place = place_of(j, layers)
            for strip in range(count):
                snap[strip, window, place] = new[REACH + j, strip * rows : (strip + 1) * rows, :]
            return carry

        lax.fori_loop(0, layers, one_layer, 0)


def border_layers(layers):
    return list(range(REACH)) + list(range(layers - REACH, layers))


def border_kernel(step, faces, across, along, low, high, traces, speed, *rest):
    face, (cur_in, prev, cur, new, low_out, high_out) = rest[:faces], rest[faces:]
    layers = speed.shape[0]
    fill_halos(low, high, cur)
    advance(step, across, along, cur, prev, speed, face, new, border_layers(layers))
    add_trace(step, traces, new)
    low_out[...] = new[REACH : 2 * REACH]
    high_out[...] = new[layers : layers + REACH]


def inner_kernel(step, faces, keep, phase, across, along, speed, *rest):
    face, rest = rest[:faces], rest[faces:]
    cur, prev, new = rest[0], rest[1], rest[-2] if keep else rest[-1]
    layers = speed.shape[0]
    advance(step, across, along, cur, prev, speed, face, new, list(range(REACH, layers - REACH)))
    if keep:
        keep_snapshot(step, phase, new, rest[-1])


def last_kernel(step, phase, across, along, low, high, traces, speed, face, cur_in, prev, snap_in, cur, new, snap, out_a, out_b, send):
    layers = speed.shape[0]
    fill_halos(low, high, cur)
    advance(step, across, along, cur, prev, speed, (face,), new, border_layers(layers))
    add_trace(step, traces, new)
    keep_snapshot(step, phase, new, snap)

    def run(j, q, which):
        (out_a, out_b)[which][q] = new[REACH + j]

    for_each_part(layers, run)

    def one_strip(strip, carry):
        send[strip] = snap[strip]
        return carry

    lax.fori_loop(0, snap.shape[0], one_strip, 0)


def image_kernel(shifts, gathered, out, light, stage, sem):
    _, _, layers, rows, nx = gathered.shape
    lags, depth = out.shape[:2]
    size = layers * rows
    blocks = depth // layers
    table = sweep_table(depth)

    carried = jnp.zeros((rows, nx), jnp.float32)
    for d in range(depth):
        block, layer = d // layers, d % layers
        device = (block // 2) * 4 + block % 2
        s0, s1 = gathered[device, 0, layer], gathered[device, 1, layer]
        carried = (s0 * s0 + s1 * s1) * table[d] + carried * (smoothing * table[d])
        light[d] = carried
    carried = jnp.zeros((rows, nx), jnp.float32)
    for d in reversed(range(depth)):
        carried = light[d] + carried * (smoothing * table[d])
        light[d] = 1.0 / (carried + damping)

    def put(block, slot):
        return pltpu.make_async_copy(
            stage.at[slot], out.at[:, pl.ds(block * layers, layers)], sem.at[slot]
        )

    def one_block(block, carry):
        slot = lax.rem(block, 2)
        device = (block // 2) * 4 + lax.rem(block, 2)
        pl.when(block >= 2)(lambda: put(block - 2, slot).wait())

        def both(device, window):
            return jnp.concatenate(split(gathered[device, window].reshape(size, nx)), axis=1)

        sources = [both(device, window) for window in range(SNAPS)]
        receivers = [both(device + 2, window) for window in range(SNAPS)]
        inverse = light[pl.ds(block * layers, layers)].reshape(size, nx)
        for lag in range(0, lags, 2):
            columns = slice(lag * nx, (lag + 2) * nx)
            raw = 0.0
            for window in range(SNAPS):
                raw = raw + jnp.dot(
                    sources[window], shifts[0, :, columns], preferred_element_type=jnp.float32
                ) * jnp.dot(receivers[window], shifts[1, :, columns], preferred_element_type=jnp.float32)
            for i in range(2):
                value = (raw[:, i * nx : (i + 1) * nx] * inverse).astype(stage.dtype)
                stage[slot, lag + i] = value.reshape(layers, rows, nx)
        put(block, slot).start()
        return carry

    lax.fori_loop(0, blocks, one_block, 0)
    for block in (blocks - 2, blocks - 1):
        put(block, block % 2).wait()


def sweep_table(depth):
    table, before = [], 0.0
    for _ in range(depth):
        before = 1.0 / (1.0 + 2.0 * smoothing - smoothing * smoothing * before)
        table.append(before)
    return table


def images(shifts, gathered, lags):
    count, _, layers, rows, nx = gathered.shape
    depth = count // 2 * layers
    return pl.pallas_call(
        image_kernel,
        out_shape=jax.ShapeDtypeStruct((lags, depth, rows, nx), jnp.bfloat16),
        in_specs=[VMEM, VMEM],
        out_specs=ANY,
        scratch_shapes=[
            pltpu.VMEM((depth, rows, nx), jnp.float32),
            pltpu.VMEM((2, lags, layers, rows, nx), jnp.bfloat16),
            pltpu.SemaphoreType.DMA((2,)),
        ],
        compiler_params=PARAMS,
        name="images",
    )(shifts, gathered)


def local(
    source_now,
    source_before,
    receiver_now,
    receiver_before,
    speed_term,
    saved_faces,
    face_steps,
    traces,
    lag_offsets,
    snap_phase,
):
    count = lax.axis_size("gz")
    own, ny, nx = source_now.shape
    layers = 2 * own
    rows = ny // count
    steps = face_steps.shape[0]
    first_pairs, second_pairs = pairs_to_fields(count)
    back_pairs = [(b, a) for a, b in second_pairs]
    between, within = pairs_of_halos(count)
    band_x, band_y = banded(nx), banded(ny)
    across = jnp.asarray(np.concatenate([band_x, band_x], axis=0), jnp.bfloat16)
    along = jnp.asarray(np.concatenate([band_y, band_y], axis=1), jnp.bfloat16)

    def regroup(a, b):
        return lax.ppermute(a, "gz", first_pairs), lax.ppermute(b, "gz", second_pairs)

    tall = held(layers + 2 * REACH, ny, nx)
    whole = f32(layers, ny, nx)
    slab = f32(REACH, ny, nx)
    half = f32(own, ny, nx)
    strips = held(count, SNAPS, layers, rows, nx)
    plane = ny * nx

    now = regroup(*choose(source_now, receiver_now, VMEM))
    before = regroup(*choose(source_before, receiver_before, VMEM))
    speed_parts = regroup(speed_term, speed_term)
    late, early, shifts = prepare(saved_faces, face_steps, lag_offsets, nx)
    early = regroup(early, early)
    late = regroup(late, late)
    cur, low, high = merge(merge_now_kernel, "merge_now", (tall, slab, slab), *now)
    low = lax.ppermute(low, "gz", between)
    high = lax.ppermute(high, "gz", within)
    prev, speed = merge(merge_rest_kernel, "merge_rest", (tall, whole), *before, *speed_parts)

    snap = None
    for step in range(steps):
        if step == EARLY:
            face = merge(merge_faces_kernel, "merge_faces", (whole,), *late)
        faces = tuple(face) if step >= EARLY else early
        wide = len(faces)
        if step < steps - 1:
            cur, new, low, high = pl.pallas_call(
                functools.partial(border_kernel, step, wide),
                out_shape=(tall, tall, slab, slab),
                in_specs=[VMEM] * (8 + wide),
                out_specs=(VMEM,) * 4,
                input_output_aliases={6 + wide: 0, 7 + wide: 1},
                compiler_params=PARAMS,
                cost_estimate=cost(60 * 8 * plane, 4 * 40 * plane),
                name="border",
            )(across, along, low, high, traces, speed, *faces, cur, prev)
            low = lax.ppermute(low, "gz", between)
            high = lax.ppermute(high, "gz", within)
        else:
            new = prev
        operands = (snap_phase, across, along, speed, *faces, cur, new)
        inner = functools.partial(
            pl.pallas_call,
            compiler_params=PARAMS,
            cost_estimate=cost(60 * (layers - 8) * plane, 4 * 40 * plane),
            name="inner",
        )
        if step < steps - 1:
            alias = {5 + wide: 0}
            if snap is not None:
                operands, alias = (*operands, snap), {5 + wide: 0, 6 + wide: 1}
            new, snap = inner(
                functools.partial(inner_kernel, step, wide, True),
                out_shape=(tall, strips),
                in_specs=[SMEM] + [VMEM] * (len(operands) - 1),
                out_specs=(VMEM,) * 2,
                input_output_aliases=alias,
            )(*operands)
        else:
            (new,) = inner(
                functools.partial(inner_kernel, step, wide, False, None),
                out_shape=(tall,),
                in_specs=[VMEM] * (len(operands) - 1),
                out_specs=(VMEM,),
                input_output_aliases={4 + wide: 0},
            )(*operands[1:])
            _, _, _, out_a, out_b, send = pl.pallas_call(
                functools.partial(last_kernel, step),
                out_shape=(tall, tall, strips, half, half, f32(*strips.shape)),
                in_specs=[SMEM] + [VMEM] * 10,
                out_specs=(VMEM,) * 6,
                input_output_aliases={8: 0, 9: 1, 10: 2},
                compiler_params=PARAMS,
                name="last",
            )(snap_phase, across, along, low, high, traces, speed, *faces, cur, new, snap)
        prev, cur = cur, new

    gathered = lax.all_to_all(send, "gz", split_axis=0, concat_axis=0, tiled=True)
    back_a = lax.ppermute(out_a, "gz", first_pairs)
    back_b = lax.ppermute(out_b, "gz", back_pairs)
    source_final, receiver_final = choose(back_a, back_b, ANY)
    image_out = images(shifts, gathered, lag_offsets.shape[0])
    return (image_out, source_final, receiver_final)


def solution(mesh):
    return jax.shard_map(
        local,
        mesh=mesh,
        in_specs=(
            P(("shot", "gz"), None, None),
            P(("shot", "gz"), None, None),
            P(("shot", "gz"), None, None),
            P(("shot", "gz"), None, None),
            P("gz", None, None),
            P("shot", None, "gz", None),
            P(),
            P("shot", None, None),
            P(),
            P(),
        ),
        out_specs=(
            P("shot", None, "gz", None),
            P(("shot", "gz"), None, None),
            P(("shot", "gz"), None, None),
        ),
        check_vma=False,
    )
```

time: 248 us -> 196 us (0.79)
  Pallas kernels: 70.2 us -> 33.7 us
  starting transfers between devices: 51 us -> 81.2 us
  waiting for transfers between devices: 94.7 us -> 70.6 us
  local copies, waits for them, and re-layouts: 23.1 us -> 7.08 us
  other arithmetic: 4.54 us -> 0 us
    ppermute x12, waiting for transfers between devices: 55.8 us -> 5.76 us  [local(): low = lax.ppermute(low, 'gz', between)]
    ppermute x12, starting transfers between devices: 2.21 us -> 39.3 us  [local(): high = lax.ppermute(high, 'gz', within)]
    pallas_call x24 -> x30, Pallas kernels: 50.8 us -> 26.2 us  [the longest x11 13.1 us: local(): inner(functools.partial(inner_kernel, step, wide, True), out_shape=(tall,...]
    all_to_all x2 -> x1, waiting for transfers between devices: 2.07 us -> 19.1 us  [local(): lax.all_to_all(send, 'gz', split_axis=0, concat_axis=0, tiled=True)]
    unnamed x76 -> x28, local copies, waits for them, and re-layouts: 22.4 us -> 7.08 us
    pallas_call x1, Pallas kernels: 15 us -> 5.66 us  [images(): pl.pallas_call(image_kernel, out_shape=jax.ShapeDtypeStruct((lags, depth,...]
    ppermute x8 -> x10, waiting for transfers between devices: 18.4 us -> 23 us  [the longest x5 11.6 us: regroup(): lax.ppermute(b, 'gz', second_pairs)]
    select_n x3 -> x0, other arithmetic: 4.54 us -> none  [the longest x2 3.47 us: regroup(): jnp.where(keeps, b, a)]
  transfers between devices with their start and end apart: 36 -> 37, of which waited for: 21 -> 15; matrix products, arithmetic and copies ran while one was open for 2% -> 0% of each run, Pallas kernels for 15% -> 10%
where the time goes in v2:
time: 196 us; the launch traced here: 194 us
  starting transfers between devices  81.2 us (41%)
  waiting for transfers between devices  70.6 us (36%)
  Pallas kernels  33.7 us (17%)
  local copies, waits for them, and re-layouts  7.08 us (4%)
    ppermute x12, starting transfers between devices, local(): high = lax.ppermute(high, 'gz', within)  39.3 us
    all_to_all x1, waiting for transfers between devices, local(): lax.all_to_all(send, 'gz', split_axis=0, concat_axis=0, tiled=True)  19.1 us
    ppermute x5, starting transfers between devices, regroup(): lax.ppermute(a, 'gz', first_pairs)  15.5 us
    ppermute x1, waiting for transfers between devices, local(): back_a = lax.ppermute(out_a, 'gz', first_pairs)  14.3 us
    pallas_call x11, Pallas kernels, local(): inner(functools.partial(inner_kernel, step, wide, True), out_shape=(tall,...  13.1 us
    all_to_all x1, starting transfers between devices, local(): lax.all_to_all(send, 'gz', split_axis=0, concat_axis=0, tiled=True)  12.3 us
    ppermute x5, waiting for transfers between devices, regroup(): lax.ppermute(b, 'gz', second_pairs)  11.6 us
    ppermute x5, waiting for transfers between devices, regroup(): lax.ppermute(a, 'gz', first_pairs)  11.4 us
  transfers between devices with their start and end apart: 37, of which 15 were waited for; matrix products, arithmetic and copies ran while one was open for 0% of the time, Pallas kernels for 10%

profile of v2, /device:TPU:9, one launch (start us, length us, event | category | flops | bytes accessed | tf_op | source)
XLA Modules:
  0.0 193.9 jit_solution(13769424240553058129)
XLA Ops:
  0.6 1.0 copy-done.4
  1.7 1.0 copy-done.5
  2.8 3.8 %collective-permute-start = (f32[8,128,128]{2,1,0:T(8,128)S(1)}, f32[8,128,128]{2,1,0:T(8,128)S(1)}, u32[]{:S(2)}, u32[]{:S(2)}) collective-permute-start(f32[8,128,128]{2,1,0:T(8,128)S(1)} %get-tuple-element.87), channel_id=1, source_target_pairs={{0,0},{1,2},{2,1},{3,3},{4,4},{5,6},{6,5},{7,7},{8,8},{9,10},{10,9... | collective-permute-start | bytes 1572872 | tf_op jit(solution)/shard_map/ppermute | solution.py:425
  7.1 3.4 %collective-permute-start.6 = (f32[8,128,128]{2,1,0:T(8,128)}, f32[8,128,128]{2,1,0:T(8,128)S(1)}, u32[]{:S(2)}, u32[]{:S(2)}) collective-permute-start(f32[8,128,128]{2,1,0:T(8,128)} %param.16), channel_id=1, source_target_pairs={{0,0},{1,2},{2,1},{3,3},{4,4},{5,6},{6,5},{7,7},{8,8},{9,10},{10,9... | collective-permute-start | bytes 1572872 | tf_op jit(solution)/shard_map/ppermute | solution.py:425
  10.5 1.0 copy-done.6
  11.5 1.0 copy-done.7
  12.6 2.2 %collective-permute-start.4 = (f32[8,128,128]{2,1,0:T(8,128)S(1)}, f32[8,128,128]{2,1,0:T(8,128)S(1)}, u32[]{:S(2)}, u32[]{:S(2)}) collective-permute-start(f32[8,128,128]{2,1,0:T(8,128)S(1)} %get-tuple-element.91), channel_id=1, source_target_pairs={{0,0},{1,2},{2,1},{3,3},{4,4},{5,6},{6,5},{7,7},{8,8},{9,10},{10,9... | collective-permute-start | bytes 1572872 | tf_op jit(solution)/shard_map/ppermute | solution.py:425
  14.8 3.1 %collective-permute-done.now_a = f32[8,128,128]{2,1,0:T(8,128)S(1)} collective-permute-done((f32[8,128,128]{2,1,0:T(8,128)S(1)}, f32[8,128,128]{2,1,0:T(8,128)S(1)}, u32[]{:S(2)}, u32[]{:S(2)}) %collective-permute-start) | collective-permute-done | bytes 524320 | tf_op jit(solution)/shard_map/ppermute | solution.py:425
  18.0 2.4 %collective-permute-done.1.now_b = f32[8,128,128]{2,1,0:T(8,128)S(1)} collective-permute-done((f32[8,128,128]{2,1,0:T(8,128)S(1)}, f32[8,128,128]{2,1,0:T(8,128)S(1)}, u32[]{:S(2)}, u32[]{:S(2)}) %collective-permute-start.1) | collective-permute-done | bytes 524320 | tf_op jit(solution)/shard_map/ppermute | solution.py:425
  20.7 1.6 collective-permute-start.2
  22.3 9.3 %collective-permute-done.7.speed_b = f32[8,128,128]{2,1,0:T(8,128)S(1)} collective-permute-done((f32[8,128,128]{2,1,0:T(8,128)}, f32[8,128,128]{2,1,0:T(8,128)S(1)}, u32[]{:S(2)}, u32[]{:S(2)}) %collective-permute-start.7) | collective-permute-done | bytes 524320 | tf_op jit(solution)/shard_map/ppermute | solution.py:425
  31.6 1.8 prepare.1
  33.9 6.5 %collective-permute-done.4.before_a = f32[8,128,128]{2,1,0:T(8,128)S(1)} collective-permute-done((f32[8,128,128]{2,1,0:T(8,128)S(1)}, f32[8,128,128]{2,1,0:T(8,128)S(1)}, u32[]{:S(2)}, u32[]{:S(2)}) %collective-permute-start.4) | collective-permute-done | bytes 524320 | tf_op jit(solution)/shard_map/ppermute | solution.py:425
  40.4 4.2 %collective-permute-start.8 = (f32[128,128]{1,0:T(8,128)S(1)}, f32[128,128]{1,0:T(8,128)S(1)}, u32[]{:S(2)}, u32[]{:S(2)}) collective-permute-start(f32[128,128]{1,0:T(8,128)S(1)} %get-tuple-element.94), channel_id=1, source_target_pairs={{0,0},{1,2},{2,1},{3,3},{4,4},{5,6},{6,5},{7,7},{8,8},{9,10},{10,9... | collective-permute-start | bytes 196616 | tf_op jit(solution)/shard_map/ppermute | solution.py:425
  45.2 1.9 collective-permute-start.14
  47.2 0.7 border.11
  48.3 1.9 collective-permute-start.11
  50.2 1.2 inner.12
  51.4 2.5 %collective-permute-done.10.low = f32[4,128,128]{2,1,0:T(8,128)S(1)} collective-permute-done((f32[4,128,128]{2,1,0:T(8,128)S(1)}, f32[4,128,128]{2,1,0:T(8,128)S(1)}, u32[]{:S(2)}, u32[]{:S(2)}) %collective-permute-start.10) | collective-permute-done | bytes 262176 | tf_op jit(solution)/shard_map/ppermute | solution.py:462
  53.9 0.8 border.12
  54.9 1.9 collective-permute-start.13
  56.8 1.8 collective-permute-done.14.face_a
  59.0 1.3 inner.13
  60.5 0.7 border.13
  61.5 4.5 %collective-permute-start.17 = (f32[4,128,128]{2,1,0:T(8,128)S(1)}, f32[4,128,128]{2,1,0:T(8,128)S(1)}, u32[]{:S(2)}, u32[]{:S(2)}) collective-permute-start(f32[4,128,128]{2,1,0:T(8,128)S(1)} %get-tuple-element.110), channel_id=1, source_target_pairs={{0,1},{1,0},{2,3},{3,2},{4,5},{5,4},{6,7},{7,6},{8,9},{9,8},{10,11... | collective-permute-start | bytes 786440 | tf_op jit(solution)/shard_map/ppermute | solution.py:463
  66.0 1.2 inner.14
  68.1 2.5 %collective-permute-start.18 = (f32[4,128,128]{2,1,0:T(8,128)S(1)}, f32[4,128,128]{2,1,0:T(8,128)S(1)}, u32[]{:S(2)}, u32[]{:S(2)}) collective-permute-start(f32[4,128,128]{2,1,0:T(8,128)S(1)} %get-tuple-element.115), channel_id=1, source_target_pairs={{0,2},{2,0},{13,15},{15,13},{1,4},{4,1},{3,6},{6,3},{5,8},{8,5},{7... | collective-permute-start | bytes 786440 | tf_op jit(solution)/shard_map/ppermute | solution.py:462
  70.6 2.0 %collective-permute-start.19 = (f32[4,128,128]{2,1,0:T(8,128)S(1)}, f32[4,128,128]{2,1,0:T(8,128)S(1)}, u32[]{:S(2)}, u32[]{:S(2)}) collective-permute-start(f32[4,128,128]{2,1,0:T(8,128)S(1)} %get-tuple-element.116), channel_id=1, source_target_pairs={{0,1},{1,0},{2,3},{3,2},{4,5},{5,4},{6,7},{7,6},{8,9},{9,8},{10,11... | collective-permute-start | bytes 786440 | tf_op jit(solution)/shard_map/ppermute | solution.py:463
  72.7 1.2 inner.15
  73.9 1.1 collective-permute-done.18.low
  75.0 0.7 border.15
  75.7 1.5 collective-permute-start.20
  77.2 2.6 %collective-permute-start.21 = (f32[4,128,128]{2,1,0:T(8,128)S(1)}, f32[4,128,128]{2,1,0:T(8,128)S(1)}, u32[]{:S(2)}, u32[]{:S(2)}) collective-permute-start(f32[4,128,128]{2,1,0:T(8,128)S(1)} %get-tuple-element.122), channel_id=1, source_target_pairs={{0,1},{1,0},{2,3},{3,2},{4,5},{5,4},{6,7},{7,6},{8,9},{9,8},{10,11... | collective-permute-start | bytes 786440 | tf_op jit(solution)/shard_map/ppermute | solution.py:463
  79.8 1.2 inner.16
  81.0 0.8 collective-permute-done.20.low
  82.6 1.2 collective-permute-start.22
  83.8 3.2 %collective-permute-start.23 = (f32[4,128,128]{2,1,0:T(8,128)S(1)}, f32[4,128,128]{2,1,0:T(8,128)S(1)}, u32[]{:S(2)}, u32[]{:S(2)}) collective-permute-start(f32[4,128,128]{2,1,0:T(8,128)S(1)} %get-tuple-element.128), channel_id=1, source_target_pairs={{0,1},{1,0},{2,3},{3,2},{4,5},{5,4},{6,7},{7,6},{8,9},{9,8},{10,11... | collective-permute-start | bytes 786440 | tf_op jit(solution)/shard_map/ppermute | solution.py:463
  87.0 1.2 inner.17
  88.8 0.9 border.17
  89.7 0.9 collective-permute-start.24
  90.6 3.7 %collective-permute-start.25 = (f32[4,128,128]{2,1,0:T(8,128)S(1)}, f32[4,128,128]{2,1,0:T(8,128)S(1)}, u32[]{:S(2)}, u32[]{:S(2)}) collective-permute-start(f32[4,128,128]{2,1,0:T(8,128)S(1)} %get-tuple-element.134), channel_id=1, source_target_pairs={{0,1},{1,0},{2,3},{3,2},{4,5},{5,4},{6,7},{7,6},{8,9},{9,8},{10,11... | collective-permute-start | bytes 786440 | tf_op jit(solution)/shard_map/ppermute | solution.py:463
  94.3 1.2 inner.18
  97.2 4.3 %collective-permute-start.27 = (f32[4,128,128]{2,1,0:T(8,128)S(1)}, f32[4,128,128]{2,1,0:T(8,128)S(1)}, u32[]{:S(2)}, u32[]{:S(2)}) collective-permute-start(f32[4,128,128]{2,1,0:T(8,128)S(1)} %get-tuple-element.140), channel_id=1, source_target_pairs={{0,1},{1,0},{2,3},{3,2},{4,5},{5,4},{6,7},{7,6},{8,9},{9,8},{10,11... | collective-permute-start | bytes 786440 | tf_op jit(solution)/shard_map/ppermute | solution.py:463
  101.5 1.2 inner.19
  102.8 0.7 border.19
  103.8 4.9 %collective-permute-start.29 = (f32[4,128,128]{2,1,0:T(8,128)S(1)}, f32[4,128,128]{2,1,0:T(8,128)S(1)}, u32[]{:S(2)}, u32[]{:S(2)}) collective-permute-start(f32[4,128,128]{2,1,0:T(8,128)S(1)} %get-tuple-element.146), channel_id=1, source_target_pairs={{0,1},{1,0},{2,3},{3,2},{4,5},{5,4},{6,7},{7,6},{8,9},{9,8},{10,11... | collective-permute-start | bytes 786440 | tf_op jit(solution)/shard_map/ppermute | solution.py:463
  108.7 1.2 inner.20
  109.9 0.7 border.20
  110.7 5.1 %collective-permute-start.31 = (f32[4,128,128]{2,1,0:T(8,128)S(1)}, f32[4,128,128]{2,1,0:T(8,128)S(1)}, u32[]{:S(2)}, u32[]{:S(2)}) collective-permute-start(f32[4,128,128]{2,1,0:T(8,128)S(1)} %get-tuple-element.152), channel_id=1, source_target_pairs={{0,1},{1,0},{2,3},{3,2},{4,5},{5,4},{6,7},{7,6},{8,9},{9,8},{10,11... | collective-permute-start | bytes 786440 | tf_op jit(solution)/shard_map/ppermute | solution.py:463
  115.8 1.2 inner.21
  117.1 0.7 border.21
  117.9 5.1 %collective-permute-start.33 = (f32[4,128,128]{2,1,0:T(8,128)S(1)}, f32[4,128,128]{2,1,0:T(8,128)S(1)}, u32[]{:S(2)}, u32[]{:S(2)}) collective-permute-start(f32[4,128,128]{2,1,0:T(8,128)S(1)} %get-tuple-element.158), channel_id=1, source_target_pairs={{0,1},{1,0},{2,3},{3,2},{4,5},{5,4},{6,7},{7,6},{8,9},{9,8},{10,11... | collective-permute-start | bytes 786440 | tf_op jit(solution)/shard_map/ppermute | solution.py:463
  123.0 1.2 inner.22
  124.9 1.8 last.1
  126.7 1.3 copy-done.3
  128.0 0.8 copy-done.12
  128.8 0.8 copy-done.13
  129.6 12.3 %all-to-all-start = ((f32[16,2,16,8,128]{4,3,2,1,0:T(8,128)}), f32[16,2,16,8,128]{4,3,2,1,0:T(8,128)S(1)}, u32[]{:S(2)}, u32[]{:S(2)}) async-start(f32[16,2,16,8,128]{4,3,2,1,0:T(8,128)} %copy-done.3), calls=%async_computation | async-start | bytes 4194304 | tf_op jit(solution)/shard_map/all_to_all | solution.py:503
  141.9 3.4 %collective-permute-start.34 = (f32[8,128,128]{2,1,0:T(8,128)}, f32[8,128,128]{2,1,0:T(8,128)S(1)}, u32[]{:S(2)}, u32[]{:S(2)}) collective-permute-start(f32[8,128,128]{2,1,0:T(8,128)} %copy-done.13), channel_id=1, source_target_pairs={{0,0},{1,2},{2,1},{3,3},{4,4},{5,6},{6,5},{7,7},{8,8},{9,10},{10,9... | collective-permute-start | bytes 1572872 | tf_op jit(solution)/shard_map/ppermute | solution.py:504
  145.3 14.3 %collective-permute-done.34.here = f32[8,128,128]{2,1,0:T(8,128)S(1)} collective-permute-done((f32[8,128,128]{2,1,0:T(8,128)}, f32[8,128,128]{2,1,0:T(8,128)S(1)}, u32[]{:S(2)}, u32[]{:S(2)}) %collective-permute-start.34) | collective-permute-done | bytes 524320 | tf_op jit(solution)/shard_map/ppermute | solution.py:504
  159.6 8.4 %collective-permute-done.35.there = f32[8,128,128]{2,1,0:T(8,128)S(1)} collective-permute-done((f32[8,128,128]{2,1,0:T(8,128)}, f32[8,128,128]{2,1,0:T(8,128)S(1)}, u32[]{:S(2)}, u32[]{:S(2)}) %collective-permute-start.35) | collective-permute-done | bytes 524320 | tf_op jit(solution)/shard_map/ppermute | solution.py:505
  168.0 1.0 choose.5
  169.0 19.1 %all-to-all-done.gathered = f32[16,2,16,8,128]{4,3,2,1,0:T(8,128)S(1)} async-done(((f32[16,2,16,8,128]{4,3,2,1,0:T(8,128)}), f32[16,2,16,8,128]{4,3,2,1,0:T(8,128)S(1)}, u32[]{:S(2)}, u32[]{:S(2)}) %all-to-all-start) | async-done | bytes 2097184 | tf_op jit(solution)/shard_map/all_to_all | solution.py:503
  188.0 5.7 %images.1 = bf16[8,128,8,128]{3,2,1,0:T(8,128)(2,1)} custom-call(bf16[2,256,1024]{2,1,0:T(8,128)(2,1)S(1)} %get-tuple-element.86.shifts, f32[16,2,16,8,128]{4,3,2,1,0:T(8,128)S(1)} %all-to-all-done.gathered), custom_call_target="tpu_custom_call" | custom-call | tf_op jit(solution)/shard_map/images/pallas_call | solution.py:385
  (70 shorter events, 8.8 us)
Async XLA Ops:
  0.6 1.0 copy-start.4
  1.7 1.0 copy-start.5
  2.7 28.9 %copy-start.8 = (f32[12,8,8,128]{3,2,1,0:T(8,128)S(1)}, f32[12,8,8,128]{3,2,1,0:T(8,128)}, u32[]{:S(2)}) copy-start(f32[12,8,8,128]{3,2,1,0:T(8,128)} %param.17) | copy-start | bytes 1179652
  2.7 28.9 %copy-start.10 = (s32[12]{0:T(128)S(1)}, s32[12]{0:T(128)}, u32[]{:S(2)}) copy-start(s32[12]{0:T(128)} %face_steps.1) | copy-start | bytes 148
  2.7 28.9 %copy-start.11 = (s32[8]{0:T(128)S(1)}, s32[8]{0:T(128)}, u32[]{:S(2)}) copy-start(s32[8]{0:T(128)} %lags.1) | copy-start | bytes 100
  2.8 15.1 %collective-permute-start = (f32[8,128,128]{2,1,0:T(8,128)S(1)}, f32[8,128,128]{2,1,0:T(8,128)S(1)}, u32[]{:S(2)}, u32[]{:S(2)}) collective-permute-start(f32[8,128,128]{2,1,0:T(8,128)S(1)} %get-tuple-element.87), channel_id=1, source_target_pairs={{0,0},{1,2},{2,1},{3,3},{4,4},{5,6},{6,5},{7,7},{8,8},{9,10},{10,9... | collective-permute-start | bytes 1572872 | tf_op jit(solution)/shard_map/ppermute | solution.py:425
  6.7 13.7 %collective-permute-start.1 = (f32[8,128,128]{2,1,0:T(8,128)S(1)}, f32[8,128,128]{2,1,0:T(8,128)S(1)}, u32[]{:S(2)}, u32[]{:S(2)}) collective-permute-start(f32[8,128,128]{2,1,0:T(8,128)S(1)} %get-tuple-element.88), channel_id=1, source_target_pairs={{0,2},{1,0},{2,3},{3,1},{4,6},{5,4},{6,7},{7,5},{8,10},{9,8},{10,1... | collective-permute-start | bytes 1572872 | tf_op jit(solution)/shard_map/ppermute | solution.py:425
  6.7 24.9 %collective-permute-start.7 = (f32[8,128,128]{2,1,0:T(8,128)}, f32[8,128,128]{2,1,0:T(8,128)S(1)}, u32[]{:S(2)}, u32[]{:S(2)}) collective-permute-start(f32[8,128,128]{2,1,0:T(8,128)} %param.16), channel_id=1, source_target_pairs={{0,2},{1,0},{2,3},{3,1},{4,6},{5,4},{6,7},{7,5},{8,10},{9,8},{10,1... | collective-permute-start | bytes 1572872 | tf_op jit(solution)/shard_map/ppermute | solution.py:425
  7.1 26.3 %collective-permute-start.6 = (f32[8,128,128]{2,1,0:T(8,128)}, f32[8,128,128]{2,1,0:T(8,128)S(1)}, u32[]{:S(2)}, u32[]{:S(2)}) collective-permute-start(f32[8,128,128]{2,1,0:T(8,128)} %param.16), channel_id=1, source_target_pairs={{0,0},{1,2},{2,1},{3,3},{4,4},{5,6},{6,5},{7,7},{8,8},{9,10},{10,9... | collective-permute-start | bytes 1572872 | tf_op jit(solution)/shard_map/ppermute | solution.py:425
  10.5 1.0 copy-start.6
  11.5 1.0 copy-start.7
  12.6 27.8 %collective-permute-start.4 = (f32[8,128,128]{2,1,0:T(8,128)S(1)}, f32[8,128,128]{2,1,0:T(8,128)S(1)}, u32[]{:S(2)}, u32[]{:S(2)}) collective-permute-start(f32[8,128,128]{2,1,0:T(8,128)S(1)} %get-tuple-element.91), channel_id=1, source_target_pairs={{0,0},{1,2},{2,1},{3,3},{4,4},{5,6},{6,5},{7,7},{8,8},{9,10},{10,9... | collective-permute-start | bytes 1572872 | tf_op jit(solution)/shard_map/ppermute | solution.py:425
  17.9 29.2 %copy-start = (bf16[12,128,128]{2,1,0:T(8,128)(2,1)S(1)}, bf16[12,128,128]{2,1,0:T(8,128)(2,1)}, u32[]{:S(2)}) copy-start(bf16[12,128,128]{2,1,0:T(8,128)(2,1)} %traces.23) | copy-start | bytes 1179652
  17.9 29.2 %copy-start.1 = (bf16[128,256]{1,0:T(8,128)(2,1)S(1)}, bf16[128,256]{1,0:T(8,128)(2,1)}, u32[]{:S(2)}) copy-start(bf16[128,256]{1,0:T(8,128)(2,1)} %constant.5.clone.along) | copy-start | bytes 196612
  17.9 29.2 %copy-start.2 = (bf16[256,128]{1,0:T(8,128)(2,1)S(1)}, bf16[256,128]{1,0:T(8,128)(2,1)}, u32[]{:S(2)}) copy-start(bf16[256,128]{1,0:T(8,128)(2,1)} %constant.4.clone.across) | copy-start | bytes 196612
  17.9 26.7 %collective-permute-start.5 = (f32[8,128,128]{2,1,0:T(8,128)S(1)}, f32[8,128,128]{2,1,0:T(8,128)S(1)}, u32[]{:S(2)}, u32[]{:S(2)}) collective-permute-start(f32[8,128,128]{2,1,0:T(8,128)S(1)} %get-tuple-element.92), channel_id=1, source_target_pairs={{0,2},{1,0},{2,3},{3,1},{4,6},{5,4},{6,7},{7,5},{8,10},{9,8},{10,1... | collective-permute-start | bytes 1572872 | tf_op jit(solution)/shard_map/ppermute | solution.py:425
  20.7 26.4 %collective-permute-start.2 = (f32[4,128,128]{2,1,0:T(8,128)S(1)}, f32[4,128,128]{2,1,0:T(8,128)S(1)}, u32[]{:S(2)}, u32[]{:S(2)}) collective-permute-start(f32[4,128,128]{2,1,0:T(8,128)S(1)} %get-tuple-element.89), channel_id=1, source_target_pairs={{0,2},{2,0},{13,15},{15,13},{1,4},{4,1},{3,6},{6,3},{5,8},{8,5},{7... | collective-permute-start | bytes 786440 | tf_op jit(solution)/shard_map/ppermute | solution.py:441
  31.6 15.6 %collective-permute-start.3 = (f32[4,128,128]{2,1,0:T(8,128)S(1)}, f32[4,128,128]{2,1,0:T(8,128)S(1)}, u32[]{:S(2)}, u32[]{:S(2)}) collective-permute-start(f32[4,128,128]{2,1,0:T(8,128)S(1)} %get-tuple-element.90), channel_id=1, source_target_pairs={{0,1},{1,0},{2,3},{3,2},{4,5},{5,4},{6,7},{7,6},{8,9},{9,8},{10,11... | collective-permute-start | bytes 786440 | tf_op jit(solution)/shard_map/ppermute | solution.py:442
  33.4 11.8 %collective-permute-start.9 = (f32[128,128]{1,0:T(8,128)S(1)}, f32[128,128]{1,0:T(8,128)S(1)}, u32[]{:S(2)}, u32[]{:S(2)}) collective-permute-start(f32[128,128]{1,0:T(8,128)S(1)} %get-tuple-element.94), channel_id=1, source_target_pairs={{0,2},{1,0},{2,3},{3,1},{4,6},{5,4},{6,7},{7,5},{8,10},{9,8},{10,1... | collective-permute-start | bytes 196616 | tf_op jit(solution)/shard_map/ppermute | solution.py:425
  40.4 6.7 %collective-permute-start.8 = (f32[128,128]{1,0:T(8,128)S(1)}, f32[128,128]{1,0:T(8,128)S(1)}, u32[]{:S(2)}, u32[]{:S(2)}) collective-permute-start(f32[128,128]{1,0:T(8,128)S(1)} %get-tuple-element.94), channel_id=1, source_target_pairs={{0,0},{1,2},{2,1},{3,3},{4,4},{5,6},{6,5},{7,7},{8,8},{9,10},{10,9... | collective-permute-start | bytes 196616 | tf_op jit(solution)/shard_map/ppermute | solution.py:425
  44.6 12.2 %collective-permute-start.15 = (f32[8,128,128]{2,1,0:T(8,128)S(1)}, f32[8,128,128]{2,1,0:T(8,128)S(1)}, u32[]{:S(2)}, u32[]{:S(2)}) collective-permute-start(f32[8,128,128]{2,1,0:T(8,128)S(1)} %get-tuple-element.104), channel_id=1, source_target_pairs={{0,2},{1,0},{2,3},{3,1},{4,6},{5,4},{6,7},{7,5},{8,10},{9,8},{10,1... | collective-permute-start | bytes 1572872 | tf_op jit(solution)/shard_map/ppermute | solution.py:425
  45.2 13.4 %collective-permute-start.14 = (f32[8,128,128]{2,1,0:T(8,128)S(1)}, f32[8,128,128]{2,1,0:T(8,128)S(1)}, u32[]{:S(2)}, u32[]{:S(2)}) collective-permute-start(f32[8,128,128]{2,1,0:T(8,128)S(1)} %get-tuple-element.104), channel_id=1, source_target_pairs={{0,0},{1,2},{2,1},{3,3},{4,4},{5,6},{6,5},{7,7},{8,8},{9,10},{10,9... | collective-permute-start | bytes 1572872 | tf_op jit(solution)/shard_map/ppermute | solution.py:425
  47.2 3.0 %copy-start.9 = (s32[2]{0:T(128)S(1)}, s32[2]{0:T(128)}, u32[]{:S(2)}) copy-start(s32[2]{0:T(128)} %phase.23) | copy-start | bytes 28
  47.9 5.9 %collective-permute-start.10 = (f32[4,128,128]{2,1,0:T(8,128)S(1)}, f32[4,128,128]{2,1,0:T(8,128)S(1)}, u32[]{:S(2)}, u32[]{:S(2)}) collective-permute-start(f32[4,128,128]{2,1,0:T(8,128)S(1)} %get-tuple-element.97), channel_id=1, source_target_pairs={{0,2},{2,0},{13,15},{15,13},{1,4},{4,1},{3,6},{6,3},{5,8},{8,5},{7... | collective-permute-start | bytes 786440 | tf_op jit(solution)/shard_map/ppermute | solution.py:462
  48.3 5.6 %collective-permute-start.11 = (f32[4,128,128]{2,1,0:T(8,128)S(1)}, f32[4,128,128]{2,1,0:T(8,128)S(1)}, u32[]{:S(2)}, u32[]{:S(2)}) collective-permute-start(f32[4,128,128]{2,1,0:T(8,128)S(1)} %get-tuple-element.98), channel_id=1, source_target_pairs={{0,1},{1,0},{2,3},{3,2},{4,5},{5,4},{6,7},{7,6},{8,9},{9,8},{10,11... | collective-permute-start | bytes 786440 | tf_op jit(solution)/shard_map/ppermute | solution.py:463
  54.6 5.9 %collective-permute-start.12 = (f32[4,128,128]{2,1,0:T(8,128)S(1)}, f32[4,128,128]{2,1,0:T(8,128)S(1)}, u32[]{:S(2)}, u32[]{:S(2)}) collective-permute-start(f32[4,128,128]{2,1,0:T(8,128)S(1)} %get-tuple-element.102), channel_id=1, source_target_pairs={{0,2},{2,0},{13,15},{15,13},{1,4},{4,1},{3,6},{6,3},{5,8},{8,5},{7... | collective-permute-start | bytes 786440 | tf_op jit(solution)/shard_map/ppermute | solution.py:462
  54.9 5.6 %collective-permute-start.13 = (f32[4,128,128]{2,1,0:T(8,128)S(1)}, f32[4,128,128]{2,1,0:T(8,128)S(1)}, u32[]{:S(2)}, u32[]{:S(2)}) collective-permute-start(f32[4,128,128]{2,1,0:T(8,128)S(1)} %get-tuple-element.103), channel_id=1, source_target_pairs={{0,1},{1,0},{2,3},{3,2},{4,5},{5,4},{6,7},{7,6},{8,9},{9,8},{10,11... | collective-permute-start | bytes 786440 | tf_op jit(solution)/shard_map/ppermute | solution.py:463
  61.2 6.2 %collective-permute-start.16 = (f32[4,128,128]{2,1,0:T(8,128)S(1)}, f32[4,128,128]{2,1,0:T(8,128)S(1)}, u32[]{:S(2)}, u32[]{:S(2)}) collective-permute-start(f32[4,128,128]{2,1,0:T(8,128)S(1)} %get-tuple-element.109), channel_id=1, source_target_pairs={{0,2},{2,0},{13,15},{15,13},{1,4},{4,1},{3,6},{6,3},{5,8},{8,5},{7... | collective-permute-start | bytes 786440 | tf_op jit(solution)/shard_map/ppermute | solution.py:462
  61.5 5.9 %collective-permute-start.17 = (f32[4,128,128]{2,1,0:T(8,128)S(1)}, f32[4,128,128]{2,1,0:T(8,128)S(1)}, u32[]{:S(2)}, u32[]{:S(2)}) collective-permute-start(f32[4,128,128]{2,1,0:T(8,128)S(1)} %get-tuple-element.110), channel_id=1, source_target_pairs={{0,1},{1,0},{2,3},{3,2},{4,5},{5,4},{6,7},{7,6},{8,9},{9,8},{10,11... | collective-permute-start | bytes 786440 | tf_op jit(solution)/shard_map/ppermute | solution.py:463
  68.1 6.8 %collective-permute-start.18 = (f32[4,128,128]{2,1,0:T(8,128)S(1)}, f32[4,128,128]{2,1,0:T(8,128)S(1)}, u32[]{:S(2)}, u32[]{:S(2)}) collective-permute-start(f32[4,128,128]{2,1,0:T(8,128)S(1)} %get-tuple-element.115), channel_id=1, source_target_pairs={{0,2},{2,0},{13,15},{15,13},{1,4},{4,1},{3,6},{6,3},{5,8},{8,5},{7... | collective-permute-start | bytes 786440 | tf_op jit(solution)/shard_map/ppermute | solution.py:462
  70.6 4.4 %collective-permute-start.19 = (f32[4,128,128]{2,1,0:T(8,128)S(1)}, f32[4,128,128]{2,1,0:T(8,128)S(1)}, u32[]{:S(2)}, u32[]{:S(2)}) collective-permute-start(f32[4,128,128]{2,1,0:T(8,128)S(1)} %get-tuple-element.116), channel_id=1, source_target_pairs={{0,1},{1,0},{2,3},{3,2},{4,5},{5,4},{6,7},{7,6},{8,9},{9,8},{10,11... | collective-permute-start | bytes 786440 | tf_op jit(solution)/shard_map/ppermute | solution.py:463
  75.7 6.2 %collective-permute-start.20 = (f32[4,128,128]{2,1,0:T(8,128)S(1)}, f32[4,128,128]{2,1,0:T(8,128)S(1)}, u32[]{:S(2)}, u32[]{:S(2)}) collective-permute-start(f32[4,128,128]{2,1,0:T(8,128)S(1)} %get-tuple-element.121), channel_id=1, source_target_pairs={{0,2},{2,0},{13,15},{15,13},{1,4},{4,1},{3,6},{6,3},{5,8},{8,5},{7... | collective-permute-start | bytes 786440 | tf_op jit(solution)/shard_map/ppermute | solution.py:462
  77.2 4.6 %collective-permute-start.21 = (f32[4,128,128]{2,1,0:T(8,128)S(1)}, f32[4,128,128]{2,1,0:T(8,128)S(1)}, u32[]{:S(2)}, u32[]{:S(2)}) collective-permute-start(f32[4,128,128]{2,1,0:T(8,128)S(1)} %get-tuple-element.122), channel_id=1, source_target_pairs={{0,1},{1,0},{2,3},{3,2},{4,5},{5,4},{6,7},{7,6},{8,9},{9,8},{10,11... | collective-permute-start | bytes 786440 | tf_op jit(solution)/shard_map/ppermute | solution.py:463
  82.6 6.2 %collective-permute-start.22 = (f32[4,128,128]{2,1,0:T(8,128)S(1)}, f32[4,128,128]{2,1,0:T(8,128)S(1)}, u32[]{:S(2)}, u32[]{:S(2)}) collective-permute-start(f32[4,128,128]{2,1,0:T(8,128)S(1)} %get-tuple-element.127), channel_id=1, source_target_pairs={{0,2},{2,0},{13,15},{15,13},{1,4},{4,1},{3,6},{6,3},{5,8},{8,5},{7... | collective-permute-start | bytes 786440 | tf_op jit(solution)/shard_map/ppermute | solution.py:462
  83.8 4.9 %collective-permute-start.23 = (f32[4,128,128]{2,1,0:T(8,128)S(1)}, f32[4,128,128]{2,1,0:T(8,128)S(1)}, u32[]{:S(2)}, u32[]{:S(2)}) collective-permute-start(f32[4,128,128]{2,1,0:T(8,128)S(1)} %get-tuple-element.128), channel_id=1, source_target_pairs={{0,1},{1,0},{2,3},{3,2},{4,5},{5,4},{6,7},{7,6},{8,9},{9,8},{10,11... | collective-permute-start | bytes 786440 | tf_op jit(solution)/shard_map/ppermute | solution.py:463
  89.7 6.2 %collective-permute-start.24 = (f32[4,128,128]{2,1,0:T(8,128)S(1)}, f32[4,128,128]{2,1,0:T(8,128)S(1)}, u32[]{:S(2)}, u32[]{:S(2)}) collective-permute-start(f32[4,128,128]{2,1,0:T(8,128)S(1)} %get-tuple-element.133), channel_id=1, source_target_pairs={{0,2},{2,0},{13,15},{15,13},{1,4},{4,1},{3,6},{6,3},{5,8},{8,5},{7... | collective-permute-start | bytes 786440 | tf_op jit(solution)/shard_map/ppermute | solution.py:462
  90.6 5.2 %collective-permute-start.25 = (f32[4,128,128]{2,1,0:T(8,128)S(1)}, f32[4,128,128]{2,1,0:T(8,128)S(1)}, u32[]{:S(2)}, u32[]{:S(2)}) collective-permute-start(f32[4,128,128]{2,1,0:T(8,128)S(1)} %get-tuple-element.134), channel_id=1, source_target_pairs={{0,1},{1,0},{2,3},{3,2},{4,5},{5,4},{6,7},{7,6},{8,9},{9,8},{10,11... | collective-permute-start | bytes 786440 | tf_op jit(solution)/shard_map/ppermute | solution.py:463
  96.6 6.2 %collective-permute-start.26 = (f32[4,128,128]{2,1,0:T(8,128)S(1)}, f32[4,128,128]{2,1,0:T(8,128)S(1)}, u32[]{:S(2)}, u32[]{:S(2)}) collective-permute-start(f32[4,128,128]{2,1,0:T(8,128)S(1)} %get-tuple-element.139), channel_id=1, source_target_pairs={{0,2},{2,0},{13,15},{15,13},{1,4},{4,1},{3,6},{6,3},{5,8},{8,5},{7... | collective-permute-start | bytes 786440 | tf_op jit(solution)/shard_map/ppermute | solution.py:462
  97.2 5.5 %collective-permute-start.27 = (f32[4,128,128]{2,1,0:T(8,128)S(1)}, f32[4,128,128]{2,1,0:T(8,128)S(1)}, u32[]{:S(2)}, u32[]{:S(2)}) collective-permute-start(f32[4,128,128]{2,1,0:T(8,128)S(1)} %get-tuple-element.140), channel_id=1, source_target_pairs={{0,1},{1,0},{2,3},{3,2},{4,5},{5,4},{6,7},{7,6},{8,9},{9,8},{10,11... | collective-permute-start | bytes 786440 | tf_op jit(solution)/shard_map/ppermute | solution.py:463
  103.5 6.4 %collective-permute-start.28 = (f32[4,128,128]{2,1,0:T(8,128)S(1)}, f32[4,128,128]{2,1,0:T(8,128)S(1)}, u32[]{:S(2)}, u32[]{:S(2)}) collective-permute-start(f32[4,128,128]{2,1,0:T(8,128)S(1)} %get-tuple-element.145), channel_id=1, source_target_pairs={{0,2},{2,0},{13,15},{15,13},{1,4},{4,1},{3,6},{6,3},{5,8},{8,5},{7... | collective-permute-start | bytes 786440 | tf_op jit(solution)/shard_map/ppermute | solution.py:462
  103.8 6.1 %collective-permute-start.29 = (f32[4,128,128]{2,1,0:T(8,128)S(1)}, f32[4,128,128]{2,1,0:T(8,128)S(1)}, u32[]{:S(2)}, u32[]{:S(2)}) collective-permute-start(f32[4,128,128]{2,1,0:T(8,128)S(1)} %get-tuple-element.146), channel_id=1, source_target_pairs={{0,1},{1,0},{2,3},{3,2},{4,5},{5,4},{6,7},{7,6},{8,9},{9,8},{10,11... | collective-permute-start | bytes 786440 | tf_op jit(solution)/shard_map/ppermute | solution.py:463
  110.6 6.4 %collective-permute-start.30 = (f32[4,128,128]{2,1,0:T(8,128)S(1)}, f32[4,128,128]{2,1,0:T(8,128)S(1)}, u32[]{:S(2)}, u32[]{:S(2)}) collective-permute-start(f32[4,128,128]{2,1,0:T(8,128)S(1)} %get-tuple-element.151), channel_id=1, source_target_pairs={{0,2},{2,0},{13,15},{15,13},{1,4},{4,1},{3,6},{6,3},{5,8},{8,5},{7... | collective-permute-start | bytes 786440 | tf_op jit(solution)/shard_map/ppermute | solution.py:462
  110.7 6.3 %collective-permute-start.31 = (f32[4,128,128]{2,1,0:T(8,128)S(1)}, f32[4,128,128]{2,1,0:T(8,128)S(1)}, u32[]{:S(2)}, u32[]{:S(2)}) collective-permute-start(f32[4,128,128]{2,1,0:T(8,128)S(1)} %get-tuple-element.152), channel_id=1, source_target_pairs={{0,1},{1,0},{2,3},{3,2},{4,5},{5,4},{6,7},{7,6},{8,9},{9,8},{10,11... | collective-permute-start | bytes 786440 | tf_op jit(solution)/shard_map/ppermute | solution.py:463
  117.8 7.1 %collective-permute-start.32 = (f32[4,128,128]{2,1,0:T(8,128)S(1)}, f32[4,128,128]{2,1,0:T(8,128)S(1)}, u32[]{:S(2)}, u32[]{:S(2)}) collective-permute-start(f32[4,128,128]{2,1,0:T(8,128)S(1)} %get-tuple-element.157), channel_id=1, source_target_pairs={{0,2},{2,0},{13,15},{15,13},{1,4},{4,1},{3,6},{6,3},{5,8},{8,5},{7... | collective-permute-start | bytes 786440 | tf_op jit(solution)/shard_map/ppermute | solution.py:462
  117.9 7.0 %collective-permute-start.33 = (f32[4,128,128]{2,1,0:T(8,128)S(1)}, f32[4,128,128]{2,1,0:T(8,128)S(1)}, u32[]{:S(2)}, u32[]{:S(2)}) collective-permute-start(f32[4,128,128]{2,1,0:T(8,128)S(1)} %get-tuple-element.158), channel_id=1, source_target_pairs={{0,1},{1,0},{2,3},{3,2},{4,5},{5,4},{6,7},{7,6},{8,9},{9,8},{10,11... | collective-permute-start | bytes 786440 | tf_op jit(solution)/shard_map/ppermute | solution.py:463
  126.7 1.3 copy-start.3
  128.0 0.8 copy-start.12
  128.8 0.8 copy-start.13
  129.6 58.5 %all-to-all-start = ((f32[16,2,16,8,128]{4,3,2,1,0:T(8,128)}), f32[16,2,16,8,128]{4,3,2,1,0:T(8,128)S(1)}, u32[]{:S(2)}, u32[]{:S(2)}) async-start(f32[16,2,16,8,128]{4,3,2,1,0:T(8,128)} %copy-done.3), calls=%async_computation | async-start | bytes 4194304 | tf_op jit(solution)/shard_map/all_to_all | solution.py:503
  141.9 17.7 %collective-permute-start.34 = (f32[8,128,128]{2,1,0:T(8,128)}, f32[8,128,128]{2,1,0:T(8,128)S(1)}, u32[]{:S(2)}, u32[]{:S(2)}) collective-permute-start(f32[8,128,128]{2,1,0:T(8,128)} %copy-done.13), channel_id=1, source_target_pairs={{0,0},{1,2},{2,1},{3,3},{4,4},{5,6},{6,5},{7,7},{8,8},{9,10},{10,9... | collective-permute-start | bytes 1572872 | tf_op jit(solution)/shard_map/ppermute | solution.py:504
  145.3 22.7 %collective-permute-start.35 = (f32[8,128,128]{2,1,0:T(8,128)}, f32[8,128,128]{2,1,0:T(8,128)S(1)}, u32[]{:S(2)}, u32[]{:S(2)}) collective-permute-start(f32[8,128,128]{2,1,0:T(8,128)} %copy-done.12), channel_id=1, source_target_pairs={{2,0},{0,1},{3,2},{1,3},{6,4},{4,5},{7,6},{5,7},{10,8},{8,9},{11,1... | collective-permute-start | bytes 1572872 | tf_op jit(solution)/shard_map/ppermute | solution.py:505

commit v3 on v2

--- a/solution.py
+++ b/solution.py
@@ -262,7 +262,7 @@
 
 
 def keep_snapshot(step, phase, new, snap):
-    count, _, layers, rows, _ = snap.shape
+    count, layers, rows, _ = snap.shape
     window = step // SNAP_EVERY
 
     @pl.when(phase[window] == step - window * SNAP_EVERY)
@@ -270,7 +270,7 @@
         def one_layer(j, carry):
             place = place_of(j, layers)
             for strip in range(count):
-                snap[strip, window, place] = new[REACH + j, strip * rows : (strip + 1) * rows, :]
+                snap[strip, place] = new[REACH + j, strip * rows : (strip + 1) * rows, :]
             return carry
 
         lax.fori_loop(0, layers, one_layer, 0)
@@ -318,8 +318,58 @@
     lax.fori_loop(0, snap.shape[0], one_strip, 0)
 
 
-def image_kernel(shifts, gathered, out, light, stage, sem):
-    _, _, layers, rows, nx = gathered.shape
+def spread_kernel(snap, own, *parts):
+    groups = snap.shape[0] // 4
+    group = lax.axis_index("gz") // 4
+
+    def copy(target, first):
+        def one(i, carry):
+            target[i] = snap[first + i]
+            return carry
+
+        lax.fori_loop(0, target.shape[0], one, 0)
+
+    copy(own, 4 * group)
+    pieces = len(parts) // (groups - 1)
+    for i, part in enumerate(parts):
+        other = jnp.bitwise_xor(group, i // pieces + 1)
+        copy(part, 4 * other + (i % pieces) * (4 // pieces))
+
+
+def regather_kernel(own, *refs):
+    parts, outs = refs[:-4], refs[-4:]
+    groups = outs[0].shape[0]
+    pieces = len(parts) // (groups - 1)
+    size = 4 // pieces
+    group = lax.axis_index("gz") // 4
+    mine = lax.rem(lax.axis_index("gz"), 4)
+    for which, out in enumerate(outs):
+        strip = jnp.bitwise_xor(mine, which)
+        out[group] = own[strip]
+        for i, part in enumerate(parts):
+            first = (i % pieces) * size
+
+            @pl.when((strip >= first) & (strip < first + size))
+            def _(i=i, part=part, first=first, strip=strip, out=out):
+                out[jnp.bitwise_xor(group, i // pieces + 1)] = part[strip - first]
+
+
+def collect_kernel(*refs):
+    out = refs[-1]
+    mine = lax.rem(lax.axis_index("gz"), 4)
+    for which in range(4):
+        source = jnp.bitwise_xor(mine, which)
+
+        def one(group, carry):
+            out[4 * group + source] = refs[which][group]
+            return carry
+
+        lax.fori_loop(0, refs[which].shape[0], one, 0)
+
+
+def image_kernel(shifts, *refs):
+    windows, (out, light, stage, sem) = refs[:-4], refs[-4:]
+    _, layers, rows, nx = windows[0].shape
     lags, depth = out.shape[:2]
     size = layers * rows
     blocks = depth // layers
@@ -329,8 +379,8 @@
     for d in range(depth):
         block, layer = d // layers, d % layers
         device = (block // 2) * 4 + block % 2
-        s0, s1 = gathered[device, 0, layer], gathered[device, 1, layer]
-        carried = (s0 * s0 + s1 * s1) * table[d] + carried * (smoothing * table[d])
+        squares = sum(window[device, layer] * window[device, layer] for window in windows)
+        carried = squares * table[d] + carried * (smoothing * table[d])
         light[d] = carried
     carried = jnp.zeros((rows, nx), jnp.float32)
     for d in reversed(range(depth)):
@@ -348,15 +398,15 @@
         pl.when(block >= 2)(lambda: put(block - 2, slot).wait())
 
         def both(device, window):
-            return jnp.concatenate(split(gathered[device, window].reshape(size, nx)), axis=1)
-
-        sources = [both(device, window) for window in range(SNAPS)]
-        receivers = [both(device + 2, window) for window in range(SNAPS)]
+            return jnp.concatenate(split(window[device].reshape(size, nx)), axis=1)
+
+        sources = [both(device, window) for window in windows]
+        receivers = [both(device + 2, window) for window in windows]
         inverse = light[pl.ds(block * layers, layers)].reshape(size, nx)
         for lag in range(0, lags, 2):
             columns = slice(lag * nx, (lag + 2) * nx)
             raw = 0.0
-            for window in range(SNAPS):
+            for window in range(len(windows)):
                 raw = raw + jnp.dot(
                     sources[window], shifts[0, :, columns], preferred_element_type=jnp.float32
                 ) * jnp.dot(receivers[window], shifts[1, :, columns], preferred_element_type=jnp.float32)
@@ -379,13 +429,13 @@
     return table
 
 
-def images(shifts, gathered, lags):
-    count, _, layers, rows, nx = gathered.shape
+def images(shifts, windows, lags):
+    count, layers, rows, nx = windows[0].shape
     depth = count // 2 * layers
     return pl.pallas_call(
         image_kernel,
         out_shape=jax.ShapeDtypeStruct((lags, depth, rows, nx), jnp.bfloat16),
-        in_specs=[VMEM, VMEM],
+        in_specs=[VMEM] * (1 + len(windows)),
         out_specs=ANY,
         scratch_shapes=[
             pltpu.VMEM((depth, rows, nx), jnp.float32),
@@ -394,7 +444,7 @@
         ],
         compiler_params=PARAMS,
         name="images",
-    )(shifts, gathered)
+    )(shifts, *windows)
 
 
 def local(
@@ -428,7 +478,7 @@
     whole = f32(layers, ny, nx)
     slab = f32(REACH, ny, nx)
     half = f32(own, ny, nx)
-    strips = held(count, SNAPS, layers, rows, nx)
+    strips = held(count, layers, rows, nx)
     plane = ny * nx
 
     now = regroup(*choose(source_now, receiver_now, VMEM))
@@ -436,14 +486,29 @@
     speed_parts = regroup(speed_term, speed_term)
     late, early, shifts = prepare(saved_faces, face_steps, lag_offsets, nx)
     early = regroup(early, early)
-    late = regroup(late, late)
     cur, low, high = merge(merge_now_kernel, "merge_now", (tall, slab, slab), *now)
     low = lax.ppermute(low, "gz", between)
     high = lax.ppermute(high, "gz", within)
     prev, speed = merge(merge_rest_kernel, "merge_rest", (tall, whole), *before, *speed_parts)
 
+    groups = count // 4
+    pieces = 2
+    waiting, arrived = [], []
+
     snap = None
     for step in range(steps):
+        if step % SNAP_EVERY == 0 and step:
+            own_strips, *sent = merge(
+                spread_kernel,
+                "spread",
+                (f32(4, layers, rows, nx), *[f32(4 // pieces, layers, rows, nx)] * (pieces * (groups - 1))),
+                snap,
+            )
+            waiting = [
+                (pieces_now, [(i, 4 * ((i // 4) ^ (j // pieces + 1)) + i % 4) for i in range(count)])
+                for j, pieces_now in enumerate(sent)
+            ]
+            snap = None
         if step == EARLY:
             face = merge(merge_faces_kernel, "merge_faces", (whole,), *late)
         faces = tuple(face) if step >= EARLY else early
@@ -498,13 +563,29 @@
                 compiler_params=PARAMS,
                 name="last",
             )(snap_phase, across, along, low, high, traces, speed, *faces, cur, new, snap)
+        if step == 0:
+            late, new = lax.optimization_barrier((late, new))
+            late = regroup(late, late)
+        left = steps - 1 - step
+        now_many = -(-len(waiting) // left) if left else len(waiting)
+        for payload, pairs in waiting[:now_many]:
+            payload, new = lax.optimization_barrier((payload, new))
+            arrived.append(lax.ppermute(payload, "gz", pairs))
+        waiting = waiting[now_many:]
         prev, cur = cur, new
 
-    gathered = lax.all_to_all(send, "gz", split_axis=0, concat_axis=0, tiled=True)
+    mine, *others = merge(
+        regather_kernel, "regather", (f32(groups, layers, rows, nx),) * 4, own_strips, *arrived
+    )
+    others = [
+        lax.ppermute(other, "gz", [(i, i ^ (which + 1)) for i in range(count)]) for which, other in enumerate(others)
+    ]
+    (first,) = merge(collect_kernel, "collect", (f32(count, layers, rows, nx),), mine, *others)
+    second = lax.all_to_all(send, "gz", split_axis=0, concat_axis=0, tiled=True)
     back_a = lax.ppermute(out_a, "gz", first_pairs)
     back_b = lax.ppermute(out_b, "gz", back_pairs)
     source_final, receiver_final = choose(back_a, back_b, ANY)
-    image_out = images(shifts, gathered, lag_offsets.shape[0])
+    image_out = images(shifts, (first, second), lag_offsets.shape[0])
     return (image_out, source_final, receiver_final)
 
 

time: 196 us -> 209 us (1.066)
  waiting for transfers between devices: 70.6 us -> 95.2 us
  starting transfers between devices: 81.2 us -> 71.5 us
  Pallas kernels: 33.7 us -> 36.7 us
  local copies, waits for them, and re-layouts: 7.08 us -> 4.18 us
    ppermute x0 -> x9, waiting for transfers between devices: none -> 47 us  [the longest x6 35.1 us: local(): arrived.append(lax.ppermute(payload, 'gz', pairs))]
    all_to_all x1, waiting for transfers between devices: 19.1 us -> 0.01 us  [local(): second = lax.all_to_all(send, 'gz', split_axis=0, concat_axis=0, tiled=True)]
    ppermute x12, starting transfers between devices: 39.3 us -> 24.1 us  [local(): high = lax.ppermute(high, 'gz', within)]
    ppermute x1, waiting for transfers between devices: 14.3 us -> 0.01 us  [local(): back_a = lax.ppermute(out_a, 'gz', first_pairs)]
    ppermute x12, waiting for transfers between devices: 5.76 us -> 17.8 us  [local(): low = lax.ppermute(low, 'gz', between)]
    ppermute x0 -> x9, starting transfers between devices: none -> 10.5 us  [the longest x6 7.8 us: local(): arrived.append(lax.ppermute(payload, 'gz', pairs))]
    ppermute x1, waiting for transfers between devices: 8.43 us -> 0.01 us  [local(): back_b = lax.ppermute(out_b, 'gz', back_pairs)]
    ppermute x12, starting transfers between devices: 9.82 us -> 3.37 us  [local(): low = lax.ppermute(low, 'gz', between)]
  transfers between devices with their start and end apart: 37 -> 46, of which waited for: 15 -> 24; matrix products, arithmetic and copies ran while one was open for 0% -> 0% of each run, Pallas kernels for 10% -> 10%
where the time goes in v3:
time: 209 us
  waiting for transfers between devices  95.2 us (46%)
  starting transfers between devices  71.5 us (34%)
  Pallas kernels  36.7 us (18%)
  local copies, waits for them, and re-layouts  4.18 us (2%)
    ppermute x6, waiting for transfers between devices, local(): arrived.append(lax.ppermute(payload, 'gz', pairs))  35.1 us
    ppermute x12, starting transfers between devices, local(): high = lax.ppermute(high, 'gz', within)  24.1 us
    ppermute x5, starting transfers between devices, regroup(): lax.ppermute(a, 'gz', first_pairs)  18.4 us
    ppermute x12, waiting for transfers between devices, local(): low = lax.ppermute(low, 'gz', between)  17.8 us
    ppermute x5, waiting for transfers between devices, regroup(): lax.ppermute(b, 'gz', second_pairs)  16.2 us
    ppermute x5, waiting for transfers between devices, regroup(): lax.ppermute(a, 'gz', first_pairs)  14.1 us
    pallas_call x11, Pallas kernels, local(): inner(functools.partial(inner_kernel, step, wide, True), out_shape=(tall,...  14 us
    ppermute x3, waiting for transfers between devices, local(): lax.ppermute(other, 'gz', [(i, i ^ which + 1) for i in range(count)])  11.9 us
  transfers between devices with their start and end apart: 46, of which 24 were waited for; matrix products, arithmetic and copies ran while one was open for 0% of the time, Pallas kernels for 10%

profile of v3, /device:TPU:9, one launch (start us, length us, event | category | flops | bytes accessed | tf_op | source)
XLA Modules:
  0.0 208.8 jit_solution(10710235784116041942)
XLA Ops:
  0.6 1.0 copy-done.3
  1.7 1.0 copy-done.4
  2.8 3.8 %collective-permute-start.6 = (f32[8,128,128]{2,1,0:T(8,128)S(1)}, f32[8,128,128]{2,1,0:T(8,128)S(1)}, u32[]{:S(2)}, u32[]{:S(2)}) collective-permute-start(f32[8,128,128]{2,1,0:T(8,128)S(1)} %get-tuple-element.117), channel_id=1, source_target_pairs={{0,0},{1,2},{2,1},{3,3},{4,4},{5,6},{6,5},{7,7},{8,8},{9,10},{10,9... | collective-permute-start | bytes 1572872 | tf_op jit(solution)/shard_map/ppermute | solution.py:475
  7.1 3.4 %collective-permute-start.2 = (f32[8,128,128]{2,1,0:T(8,128)}, f32[8,128,128]{2,1,0:T(8,128)S(1)}, u32[]{:S(2)}, u32[]{:S(2)}) collective-permute-start(f32[8,128,128]{2,1,0:T(8,128)} %param.16), channel_id=1, source_target_pairs={{0,0},{1,2},{2,1},{3,3},{4,4},{5,6},{6,5},{7,7},{8,8},{9,10},{10,9... | collective-permute-start | bytes 1572872 | tf_op jit(solution)/shard_map/ppermute | solution.py:475
  10.5 1.0 copy-done.5
  11.5 1.0 copy-done.6
  12.6 2.2 %collective-permute-start = (f32[8,128,128]{2,1,0:T(8,128)S(1)}, f32[8,128,128]{2,1,0:T(8,128)S(1)}, u32[]{:S(2)}, u32[]{:S(2)}) collective-permute-start(f32[8,128,128]{2,1,0:T(8,128)S(1)} %get-tuple-element.112), channel_id=1, source_target_pairs={{0,0},{1,2},{2,1},{3,3},{4,4},{5,6},{6,5},{7,7},{8,8},{9,10},{10,9... | collective-permute-start | bytes 1572872 | tf_op jit(solution)/shard_map/ppermute | solution.py:475
  14.8 3.1 %collective-permute-done.6.now_a = f32[8,128,128]{2,1,0:T(8,128)S(1)} collective-permute-done((f32[8,128,128]{2,1,0:T(8,128)S(1)}, f32[8,128,128]{2,1,0:T(8,128)S(1)}, u32[]{:S(2)}, u32[]{:S(2)}) %collective-permute-start.6) | collective-permute-done | bytes 524320 | tf_op jit(solution)/shard_map/ppermute | solution.py:475
  18.0 2.4 %collective-permute-done.7.now_b = f32[8,128,128]{2,1,0:T(8,128)S(1)} collective-permute-done((f32[8,128,128]{2,1,0:T(8,128)S(1)}, f32[8,128,128]{2,1,0:T(8,128)S(1)}, u32[]{:S(2)}, u32[]{:S(2)}) %collective-permute-start.7) | collective-permute-done | bytes 524320 | tf_op jit(solution)/shard_map/ppermute | solution.py:475
  20.7 1.6 collective-permute-start.8
  22.3 9.3 %collective-permute-done.3.speed_b = f32[8,128,128]{2,1,0:T(8,128)S(1)} collective-permute-done((f32[8,128,128]{2,1,0:T(8,128)}, f32[8,128,128]{2,1,0:T(8,128)S(1)}, u32[]{:S(2)}, u32[]{:S(2)}) %collective-permute-start.3) | collective-permute-done | bytes 524320 | tf_op jit(solution)/shard_map/ppermute | solution.py:475
  31.6 1.8 prepare.1
  33.9 6.5 %collective-permute-done.before_a = f32[8,128,128]{2,1,0:T(8,128)S(1)} collective-permute-done((f32[8,128,128]{2,1,0:T(8,128)S(1)}, f32[8,128,128]{2,1,0:T(8,128)S(1)}, u32[]{:S(2)}, u32[]{:S(2)}) %collective-permute-start) | collective-permute-done | bytes 524320 | tf_op jit(solution)/shard_map/ppermute | solution.py:475
  40.4 4.2 %collective-permute-start.4 = (f32[128,128]{1,0:T(8,128)S(1)}, f32[128,128]{1,0:T(8,128)S(1)}, u32[]{:S(2)}, u32[]{:S(2)}) collective-permute-start(f32[128,128]{1,0:T(8,128)S(1)} %get-tuple-element.116), channel_id=1, source_target_pairs={{0,0},{1,2},{2,1},{3,3},{4,4},{5,6},{6,5},{7,7},{8,8},{9,10},{10,9... | collective-permute-start | bytes 196616 | tf_op jit(solution)/shard_map/ppermute | solution.py:475
  45.1 1.4 collective-permute-done.4.rest_0_
  48.0 1.3 inner.12
  49.4 4.8 %collective-permute-start.10 = (f32[8,128,128]{2,1,0:T(8,128)S(1)}, f32[8,128,128]{2,1,0:T(8,128)S(1)}, u32[]{:S(2)}, u32[]{:S(2)}) collective-permute-start(f32[8,128,128]{2,1,0:T(8,128)S(1)} %get-tuple-element.126), channel_id=1, source_target_pairs={{0,0},{1,2},{2,1},{3,3},{4,4},{5,6},{6,5},{7,7},{8,8},{9,10},{10,9... | collective-permute-start | bytes 1572872 | tf_op jit(solution)/shard_map/ppermute | solution.py:475
  55.6 1.3 inner.13
  56.8 4.6 %collective-permute-done.11.face_b = f32[8,128,128]{2,1,0:T(8,128)S(1)} collective-permute-done((f32[8,128,128]{2,1,0:T(8,128)S(1)}, f32[8,128,128]{2,1,0:T(8,128)S(1)}, u32[]{:S(2)}, u32[]{:S(2)}) %collective-permute-start.11) | collective-permute-done | bytes 524320 | tf_op jit(solution)/shard_map/ppermute | solution.py:475
  61.4 3.1 %collective-permute-done.10.face_a = f32[8,128,128]{2,1,0:T(8,128)S(1)} collective-permute-done((f32[8,128,128]{2,1,0:T(8,128)S(1)}, f32[8,128,128]{2,1,0:T(8,128)S(1)}, u32[]{:S(2)}, u32[]{:S(2)}) %collective-permute-start.10) | collective-permute-done | bytes 524320 | tf_op jit(solution)/shard_map/ppermute | solution.py:475
  66.0 1.6 collective-permute-start.17
  67.6 1.3 inner.14
  68.9 2.7 %collective-permute-done.16.low = f32[4,128,128]{2,1,0:T(8,128)S(1)} collective-permute-done((f32[4,128,128]{2,1,0:T(8,128)S(1)}, f32[4,128,128]{2,1,0:T(8,128)S(1)}, u32[]{:S(2)}, u32[]{:S(2)}) %collective-permute-start.16) | collective-permute-done | bytes 262176 | tf_op jit(solution)/shard_map/ppermute | solution.py:527
  72.6 1.9 collective-permute-start.19
  74.6 1.3 inner.15
  75.8 2.4 %collective-permute-done.18.low = f32[4,128,128]{2,1,0:T(8,128)S(1)} collective-permute-done((f32[4,128,128]{2,1,0:T(8,128)S(1)}, f32[4,128,128]{2,1,0:T(8,128)S(1)}, u32[]{:S(2)}, u32[]{:S(2)}) %collective-permute-start.18) | collective-permute-done | bytes 262176 | tf_op jit(solution)/shard_map/ppermute | solution.py:527
  79.3 2.2 %collective-permute-start.21 = (f32[4,128,128]{2,1,0:T(8,128)S(1)}, f32[4,128,128]{2,1,0:T(8,128)S(1)}, u32[]{:S(2)}, u32[]{:S(2)}) collective-permute-start(f32[4,128,128]{2,1,0:T(8,128)S(1)} %get-tuple-element.149), channel_id=1, source_target_pairs={{0,1},{1,0},{2,3},{3,2},{4,5},{5,4},{6,7},{7,6},{8,9},{9,8},{10,11... | collective-permute-start | bytes 786440 | tf_op jit(solution)/shard_map/ppermute | solution.py:528
  81.5 1.3 inner.16
  82.8 2.4 %collective-permute-done.20.low = f32[4,128,128]{2,1,0:T(8,128)S(1)} collective-permute-done((f32[4,128,128]{2,1,0:T(8,128)S(1)}, f32[4,128,128]{2,1,0:T(8,128)S(1)}, u32[]{:S(2)}, u32[]{:S(2)}) %collective-permute-start.20) | collective-permute-done | bytes 262176 | tf_op jit(solution)/shard_map/ppermute | solution.py:527
  86.0 2.4 %collective-permute-start.23 = (f32[4,128,128]{2,1,0:T(8,128)S(1)}, f32[4,128,128]{2,1,0:T(8,128)S(1)}, u32[]{:S(2)}, u32[]{:S(2)}) collective-permute-start(f32[4,128,128]{2,1,0:T(8,128)S(1)} %get-tuple-element.161), channel_id=1, source_target_pairs={{0,1},{1,0},{2,3},{3,2},{4,5},{5,4},{6,7},{7,6},{8,9},{9,8},{10,11... | collective-permute-start | bytes 786440 | tf_op jit(solution)/shard_map/ppermute | solution.py:528
  88.4 1.4 inner.17
  89.8 2.3 %collective-permute-done.22.low = f32[4,128,128]{2,1,0:T(8,128)S(1)} collective-permute-done((f32[4,128,128]{2,1,0:T(8,128)S(1)}, f32[4,128,128]{2,1,0:T(8,128)S(1)}, u32[]{:S(2)}, u32[]{:S(2)}) %collective-permute-start.22) | collective-permute-done | bytes 262176 | tf_op jit(solution)/shard_map/ppermute | solution.py:527
  93.1 2.6 %collective-permute-start.27 = (f32[4,128,128]{2,1,0:T(8,128)S(1)}, f32[4,128,128]{2,1,0:T(8,128)S(1)}, u32[]{:S(2)}, u32[]{:S(2)}) collective-permute-start(f32[4,128,128]{2,1,0:T(8,128)S(1)} %get-tuple-element.172), channel_id=1, source_target_pairs={{0,1},{1,0},{2,3},{3,2},{4,5},{5,4},{6,7},{7,6},{8,9},{9,8},{10,11... | collective-permute-start | bytes 786440 | tf_op jit(solution)/shard_map/ppermute | solution.py:528
  95.8 1.3 inner.18
  97.1 2.2 %collective-permute-done.26.low = f32[4,128,128]{2,1,0:T(8,128)S(1)} collective-permute-done((f32[4,128,128]{2,1,0:T(8,128)S(1)}, f32[4,128,128]{2,1,0:T(8,128)S(1)}, u32[]{:S(2)}, u32[]{:S(2)}) %collective-permute-start.26) | collective-permute-done | bytes 262176 | tf_op jit(solution)/shard_map/ppermute | solution.py:527
  100.1 2.8 %collective-permute-start.30 = (f32[4,128,128]{2,1,0:T(8,128)S(1)}, f32[4,128,128]{2,1,0:T(8,128)S(1)}, u32[]{:S(2)}, u32[]{:S(2)}) collective-permute-start(f32[4,128,128]{2,1,0:T(8,128)S(1)} %get-tuple-element.181), channel_id=1, source_target_pairs={{0,1},{1,0},{2,3},{3,2},{4,5},{5,4},{6,7},{7,6},{8,9},{9,8},{10,11... | collective-permute-start | bytes 786440 | tf_op jit(solution)/shard_map/ppermute | solution.py:528
  102.9 1.3 inner.19
  104.1 2.0 collective-permute-done.29.low
  107.0 3.0 %collective-permute-start.33 = (f32[4,128,128]{2,1,0:T(8,128)S(1)}, f32[4,128,128]{2,1,0:T(8,128)S(1)}, u32[]{:S(2)}, u32[]{:S(2)}) collective-permute-start(f32[4,128,128]{2,1,0:T(8,128)S(1)} %get-tuple-element.190), channel_id=1, source_target_pairs={{0,1},{1,0},{2,3},{3,2},{4,5},{5,4},{6,7},{7,6},{8,9},{9,8},{10,11... | collective-permute-start | bytes 786440 | tf_op jit(solution)/shard_map/ppermute | solution.py:528
  110.0 1.3 inner.20
  111.2 1.8 collective-permute-done.32.low
  113.9 3.3 %collective-permute-start.36 = (f32[4,128,128]{2,1,0:T(8,128)S(1)}, f32[4,128,128]{2,1,0:T(8,128)S(1)}, u32[]{:S(2)}, u32[]{:S(2)}) collective-permute-start(f32[4,128,128]{2,1,0:T(8,128)S(1)} %get-tuple-element.199), channel_id=1, source_target_pairs={{0,1},{1,0},{2,3},{3,2},{4,5},{5,4},{6,7},{7,6},{8,9},{9,8},{10,11... | collective-permute-start | bytes 786440 | tf_op jit(solution)/shard_map/ppermute | solution.py:528
  117.2 1.3 inner.21
  118.5 1.5 collective-permute-done.35.low
  120.9 3.6 %collective-permute-start.42 = (f32[4,128,128]{2,1,0:T(8,128)S(1)}, f32[4,128,128]{2,1,0:T(8,128)S(1)}, u32[]{:S(2)}, u32[]{:S(2)}) collective-permute-start(f32[4,128,128]{2,1,0:T(8,128)S(1)} %get-tuple-element.211), channel_id=1, source_target_pairs={{0,1},{1,0},{2,3},{3,2},{4,5},{5,4},{6,7},{7,6},{8,9},{9,8},{10,11... | collective-permute-start | bytes 786440 | tf_op jit(solution)/shard_map/ppermute | solution.py:528
  124.4 1.3 inner.22
  126.9 3.1 %last.1 = (f32[24,128,128]{2,1,0:T(8,128)S(1)}, f32[24,128,128]{2,1,0:T(8,128)S(1)}, f32[16,16,8,128]{3,2,1,0:T(8,128)S(1)}, f32[8,128,128]{2,1,0:T(8,128)}, f32...) custom-call(s32[2]{0:T(128)S(1)} %copy-done.8, ...), custom_call_target="tpu_custom_call", output_to_operand_aliasing={{0}: (8, {}), {1}: (9, {}), {2}: (10, {})} | custom-call | tf_op jit(solution)/shard_map/last/pallas_call | solution.py:557
  130.0 9.9 %all-to-all-start = ((f32[16,16,8,128]{3,2,1,0:T(8,128)}), f32[16,16,8,128]{3,2,1,0:T(8,128)S(1)}, u32[]{:S(2)}, u32[]{:S(2)}) async-start(f32[16,16,8,128]{3,2,1,0:T(8,128)} %get-tuple-element.214), calls=%async_computation | async-start | bytes 2097152 | tf_op jit(solution)/shard_map/all_to_all | solution.py:584
  140.0 1.4 collective-permute-start.24
  141.4 2.1 %collective-permute-start.28 = (f32[2,16,8,128]{3,2,1,0:T(8,128)S(1)}, f32[2,16,8,128]{3,2,1,0:T(8,128)S(1)}, u32[]{:S(2)}, u32[]{:S(2)}) collective-permute-start(f32[2,16,8,128]{3,2,1,0:T(8,128)S(1)} %get-tuple-element.178), channel_id=1, source_target_pairs={{0,8},{1,9},{2,10},{3,11},{4,12},{5,13},{6,14},{7,15},{8,0},{9,1},... | collective-permute-start | bytes 393224 | tf_op jit(solution)/shard_map/ppermute | solution.py:573
  143.5 4.2 %collective-permute-start.43 = (f32[8,128,128]{2,1,0:T(8,128)}, f32[8,128,128]{2,1,0:T(8,128)S(1)}, u32[]{:S(2)}, u32[]{:S(2)}) collective-permute-start(f32[8,128,128]{2,1,0:T(8,128)} %get-tuple-element.215), channel_id=1, source_target_pairs={{0,0},{1,2},{2,1},{3,3},{4,4},{5,6},{6,5},{7,7},{8,8},{9,10},{10,9... | collective-permute-start | bytes 1572872 | tf_op jit(solution)/shard_map/ppermute | solution.py:585
  147.8 13.2 %collective-permute-done.25.refs_1_ = f32[2,16,8,128]{3,2,1,0:T(8,128)S(1)} collective-permute-done((f32[2,16,8,128]{3,2,1,0:T(8,128)S(1)}, f32[2,16,8,128]{3,2,1,0:T(8,128)S(1)}, u32[]{:S(2)}, u32[]{:S(2)}) %collective-permute-start.25) | collective-permute-done | bytes 131104 | tf_op jit(solution)/shard_map/ppermute | solution.py:573
  162.0 1.8 collective-permute-done.24.refs_0_
  163.8 2.0 collective-permute-start.34
  165.8 8.0 %collective-permute-done.28.refs_2_ = f32[2,16,8,128]{3,2,1,0:T(8,128)S(1)} collective-permute-done((f32[2,16,8,128]{3,2,1,0:T(8,128)S(1)}, f32[2,16,8,128]{3,2,1,0:T(8,128)S(1)}, u32[]{:S(2)}, u32[]{:S(2)}) %collective-permute-start.28) | collective-permute-done | bytes 131104 | tf_op jit(solution)/shard_map/ppermute | solution.py:573
  173.9 1.2 collective-permute-start.37
  175.1 1.6 collective-permute-done.31.refs_3_
  176.7 7.6 %collective-permute-done.34.refs_4_ = f32[2,16,8,128]{3,2,1,0:T(8,128)S(1)} collective-permute-done((f32[2,16,8,128]{3,2,1,0:T(8,128)S(1)}, f32[2,16,8,128]{3,2,1,0:T(8,128)S(1)}, u32[]{:S(2)}, u32[]{:S(2)}) %collective-permute-start.34) | collective-permute-done | bytes 131104 | tf_op jit(solution)/shard_map/ppermute | solution.py:573
  184.2 2.8 %collective-permute-done.37.refs_5_ = f32[2,16,8,128]{3,2,1,0:T(8,128)S(1)} collective-permute-done((f32[2,16,8,128]{3,2,1,0:T(8,128)S(1)}, f32[2,16,8,128]{3,2,1,0:T(8,128)S(1)}, u32[]{:S(2)}, u32[]{:S(2)}) %collective-permute-start.37) | collective-permute-done | bytes 131104 | tf_op jit(solution)/shard_map/ppermute | solution.py:573
  187.2 1.0 collective-permute-start.38
  188.2 1.1 collective-permute-start.39
  189.9 6.1 %collective-permute-done.39.refs_2_ = f32[4,16,8,128]{3,2,1,0:T(8,128)S(1)} collective-permute-done((f32[4,16,8,128]{3,2,1,0:T(8,128)S(1)}, f32[4,16,8,128]{3,2,1,0:T(8,128)S(1)}, u32[]{:S(2)}, u32[]{:S(2)}) %collective-permute-start.39) | collective-permute-done | bytes 262176 | tf_op jit(solution)/shard_map/ppermute | solution.py:581
  196.0 5.9 %collective-permute-done.40.refs_3_ = f32[4,16,8,128]{3,2,1,0:T(8,128)S(1)} collective-permute-done((f32[4,16,8,128]{3,2,1,0:T(8,128)S(1)}, f32[4,16,8,128]{3,2,1,0:T(8,128)S(1)}, u32[]{:S(2)}, u32[]{:S(2)}) %collective-permute-start.40) | collective-permute-done | bytes 262176 | tf_op jit(solution)/shard_map/ppermute | solution.py:581
  203.0 5.7 %images.1 = bf16[8,128,8,128]{3,2,1,0:T(8,128)(2,1)} custom-call(bf16[2,256,1024]{2,1,0:T(8,128)(2,1)S(1)} %get-tuple-element.111.shifts, f32[16,16,8,128]{3,2,1,0:T(8,128)S(1)} %collect.1.refs_0_, f32[16,16,8,128]{3,2,1,0:T(8,128)S(1)} %all-to-all-done.refs_1_), custom_call_target="tpu_custom_call" | custom-call | tf_op jit(solution)/shard_map/images/pallas_call | solution.py:435
  (85 shorter events, 18.0 us)
Async XLA Ops:
  0.6 1.0 copy-start.3
  1.7 1.0 copy-start.4
  2.7 28.9 %copy-start.7 = (f32[12,8,8,128]{3,2,1,0:T(8,128)S(1)}, f32[12,8,8,128]{3,2,1,0:T(8,128)}, u32[]{:S(2)}) copy-start(f32[12,8,8,128]{3,2,1,0:T(8,128)} %param.17) | copy-start | bytes 1179652
  2.7 28.9 %copy-start.9 = (s32[12]{0:T(128)S(1)}, s32[12]{0:T(128)}, u32[]{:S(2)}) copy-start(s32[12]{0:T(128)} %face_steps.1) | copy-start | bytes 148
  2.7 28.9 %copy-start.10 = (s32[8]{0:T(128)S(1)}, s32[8]{0:T(128)}, u32[]{:S(2)}) copy-start(s32[8]{0:T(128)} %lags.1) | copy-start | bytes 100
  2.8 15.1 %collective-permute-start.6 = (f32[8,128,128]{2,1,0:T(8,128)S(1)}, f32[8,128,128]{2,1,0:T(8,128)S(1)}, u32[]{:S(2)}, u32[]{:S(2)}) collective-permute-start(f32[8,128,128]{2,1,0:T(8,128)S(1)} %get-tuple-element.117), channel_id=1, source_target_pairs={{0,0},{1,2},{2,1},{3,3},{4,4},{5,6},{6,5},{7,7},{8,8},{9,10},{10,9... | collective-permute-start | bytes 1572872 | tf_op jit(solution)/shard_map/ppermute | solution.py:475
  6.7 13.7 %collective-permute-start.7 = (f32[8,128,128]{2,1,0:T(8,128)S(1)}, f32[8,128,128]{2,1,0:T(8,128)S(1)}, u32[]{:S(2)}, u32[]{:S(2)}) collective-permute-start(f32[8,128,128]{2,1,0:T(8,128)S(1)} %get-tuple-element.118), channel_id=1, source_target_pairs={{0,2},{1,0},{2,3},{3,1},{4,6},{5,4},{6,7},{7,5},{8,10},{9,8},{10,1... | collective-permute-start | bytes 1572872 | tf_op jit(solution)/shard_map/ppermute | solution.py:475
  6.7 24.9 %collective-permute-start.3 = (f32[8,128,128]{2,1,0:T(8,128)}, f32[8,128,128]{2,1,0:T(8,128)S(1)}, u32[]{:S(2)}, u32[]{:S(2)}) collective-permute-start(f32[8,128,128]{2,1,0:T(8,128)} %param.16), channel_id=1, source_target_pairs={{0,2},{1,0},{2,3},{3,1},{4,6},{5,4},{6,7},{7,5},{8,10},{9,8},{10,1... | collective-permute-start | bytes 1572872 | tf_op jit(solution)/shard_map/ppermute | solution.py:475
  7.1 26.3 %collective-permute-start.2 = (f32[8,128,128]{2,1,0:T(8,128)}, f32[8,128,128]{2,1,0:T(8,128)S(1)}, u32[]{:S(2)}, u32[]{:S(2)}) collective-permute-start(f32[8,128,128]{2,1,0:T(8,128)} %param.16), channel_id=1, source_target_pairs={{0,0},{1,2},{2,1},{3,3},{4,4},{5,6},{6,5},{7,7},{8,8},{9,10},{10,9... | collective-permute-start | bytes 1572872 | tf_op jit(solution)/shard_map/ppermute | solution.py:475
  10.5 1.0 copy-start.5
  11.5 1.0 copy-start.6
  12.6 27.8 %collective-permute-start = (f32[8,128,128]{2,1,0:T(8,128)S(1)}, f32[8,128,128]{2,1,0:T(8,128)S(1)}, u32[]{:S(2)}, u32[]{:S(2)}) collective-permute-start(f32[8,128,128]{2,1,0:T(8,128)S(1)} %get-tuple-element.112), channel_id=1, source_target_pairs={{0,0},{1,2},{2,1},{3,3},{4,4},{5,6},{6,5},{7,7},{8,8},{9,10},{10,9... | collective-permute-start | bytes 1572872 | tf_op jit(solution)/shard_map/ppermute | solution.py:475
  17.9 28.6 %copy-start = (bf16[12,128,128]{2,1,0:T(8,128)(2,1)S(1)}, bf16[12,128,128]{2,1,0:T(8,128)(2,1)}, u32[]{:S(2)}) copy-start(bf16[12,128,128]{2,1,0:T(8,128)(2,1)} %traces.23) | copy-start | bytes 1179652
  17.9 28.6 %copy-start.1 = (bf16[128,256]{1,0:T(8,128)(2,1)S(1)}, bf16[128,256]{1,0:T(8,128)(2,1)}, u32[]{:S(2)}) copy-start(bf16[128,256]{1,0:T(8,128)(2,1)} %constant.5.clone.along) | copy-start | bytes 196612
  17.9 28.6 %copy-start.2 = (bf16[256,128]{1,0:T(8,128)(2,1)S(1)}, bf16[256,128]{1,0:T(8,128)(2,1)}, u32[]{:S(2)}) copy-start(bf16[256,128]{1,0:T(8,128)(2,1)} %constant.4.clone.across) | copy-start | bytes 196612
  17.9 26.7 %collective-permute-start.1 = (f32[8,128,128]{2,1,0:T(8,128)S(1)}, f32[8,128,128]{2,1,0:T(8,128)S(1)}, u32[]{:S(2)}, u32[]{:S(2)}) collective-permute-start(f32[8,128,128]{2,1,0:T(8,128)S(1)} %get-tuple-element.113), channel_id=1, source_target_pairs={{0,2},{1,0},{2,3},{3,1},{4,6},{5,4},{6,7},{7,5},{8,10},{9,8},{10,1... | collective-permute-start | bytes 1572872 | tf_op jit(solution)/shard_map/ppermute | solution.py:475
  20.7 25.8 %collective-permute-start.8 = (f32[4,128,128]{2,1,0:T(8,128)S(1)}, f32[4,128,128]{2,1,0:T(8,128)S(1)}, u32[]{:S(2)}, u32[]{:S(2)}) collective-permute-start(f32[4,128,128]{2,1,0:T(8,128)S(1)} %get-tuple-element.119), channel_id=1, source_target_pairs={{0,2},{2,0},{13,15},{15,13},{1,4},{4,1},{3,6},{6,3},{5,8},{8,5},{7... | collective-permute-start | bytes 786440 | tf_op jit(solution)/shard_map/ppermute | solution.py:490
  31.6 15.0 %collective-permute-start.9 = (f32[4,128,128]{2,1,0:T(8,128)S(1)}, f32[4,128,128]{2,1,0:T(8,128)S(1)}, u32[]{:S(2)}, u32[]{:S(2)}) collective-permute-start(f32[4,128,128]{2,1,0:T(8,128)S(1)} %get-tuple-element.120), channel_id=1, source_target_pairs={{0,1},{1,0},{2,3},{3,2},{4,5},{5,4},{6,7},{7,6},{8,9},{9,8},{10,11... | collective-permute-start | bytes 786440 | tf_op jit(solution)/shard_map/ppermute | solution.py:491
  33.4 11.8 %collective-permute-start.5 = (f32[128,128]{1,0:T(8,128)S(1)}, f32[128,128]{1,0:T(8,128)S(1)}, u32[]{:S(2)}, u32[]{:S(2)}) collective-permute-start(f32[128,128]{1,0:T(8,128)S(1)} %get-tuple-element.116), channel_id=1, source_target_pairs={{0,2},{1,0},{2,3},{3,1},{4,6},{5,4},{6,7},{7,5},{8,10},{9,8},{10,1... | collective-permute-start | bytes 196616 | tf_op jit(solution)/shard_map/ppermute | solution.py:475
  40.4 6.1 %collective-permute-start.4 = (f32[128,128]{1,0:T(8,128)S(1)}, f32[128,128]{1,0:T(8,128)S(1)}, u32[]{:S(2)}, u32[]{:S(2)}) collective-permute-start(f32[128,128]{1,0:T(8,128)S(1)} %get-tuple-element.116), channel_id=1, source_target_pairs={{0,0},{1,2},{2,1},{3,3},{4,4},{5,6},{6,5},{7,7},{8,8},{9,10},{10,9... | collective-permute-start | bytes 196616 | tf_op jit(solution)/shard_map/ppermute | solution.py:475
  46.6 1.5 copy-start.8
  47.4 6.7 %collective-permute-start.12 = (f32[4,128,128]{2,1,0:T(8,128)S(1)}, f32[4,128,128]{2,1,0:T(8,128)S(1)}, u32[]{:S(2)}, u32[]{:S(2)}) collective-permute-start(f32[4,128,128]{2,1,0:T(8,128)S(1)} %get-tuple-element.127), channel_id=1, source_target_pairs={{0,2},{2,0},{13,15},{15,13},{1,4},{4,1},{3,6},{6,3},{5,8},{8,5},{7... | collective-permute-start | bytes 786440 | tf_op jit(solution)/shard_map/ppermute | solution.py:527
  47.5 6.6 %collective-permute-start.13 = (f32[4,128,128]{2,1,0:T(8,128)S(1)}, f32[4,128,128]{2,1,0:T(8,128)S(1)}, u32[]{:S(2)}, u32[]{:S(2)}) collective-permute-start(f32[4,128,128]{2,1,0:T(8,128)S(1)} %get-tuple-element.128), channel_id=1, source_target_pairs={{0,1},{1,0},{2,3},{3,2},{4,5},{5,4},{6,7},{7,6},{8,9},{9,8},{10,11... | collective-permute-start | bytes 786440 | tf_op jit(solution)/shard_map/ppermute | solution.py:528
  49.3 12.1 %collective-permute-start.11 = (f32[8,128,128]{2,1,0:T(8,128)S(1)}, f32[8,128,128]{2,1,0:T(8,128)S(1)}, u32[]{:S(2)}, u32[]{:S(2)}) collective-permute-start(f32[8,128,128]{2,1,0:T(8,128)S(1)} %get-tuple-element.126), channel_id=1, source_target_pairs={{0,2},{1,0},{2,3},{3,1},{4,6},{5,4},{6,7},{7,5},{8,10},{9,8},{10,1... | collective-permute-start | bytes 1572872 | tf_op jit(solution)/shard_map/ppermute | solution.py:475
  49.4 15.2 %collective-permute-start.10 = (f32[8,128,128]{2,1,0:T(8,128)S(1)}, f32[8,128,128]{2,1,0:T(8,128)S(1)}, u32[]{:S(2)}, u32[]{:S(2)}) collective-permute-start(f32[8,128,128]{2,1,0:T(8,128)S(1)} %get-tuple-element.126), channel_id=1, source_target_pairs={{0,0},{1,2},{2,1},{3,3},{4,4},{5,6},{6,5},{7,7},{8,8},{9,10},{10,9... | collective-permute-start | bytes 1572872 | tf_op jit(solution)/shard_map/ppermute | solution.py:475
  54.9 10.0 %collective-permute-start.14 = (f32[4,128,128]{2,1,0:T(8,128)S(1)}, f32[4,128,128]{2,1,0:T(8,128)S(1)}, u32[]{:S(2)}, u32[]{:S(2)}) collective-permute-start(f32[4,128,128]{2,1,0:T(8,128)S(1)} %get-tuple-element.130), channel_id=1, source_target_pairs={{0,2},{2,0},{13,15},{15,13},{1,4},{4,1},{3,6},{6,3},{5,8},{8,5},{7... | collective-permute-start | bytes 786440 | tf_op jit(solution)/shard_map/ppermute | solution.py:527
  55.3 9.6 %collective-permute-start.15 = (f32[4,128,128]{2,1,0:T(8,128)S(1)}, f32[4,128,128]{2,1,0:T(8,128)S(1)}, u32[]{:S(2)}, u32[]{:S(2)}) collective-permute-start(f32[4,128,128]{2,1,0:T(8,128)S(1)} %get-tuple-element.131), channel_id=1, source_target_pairs={{0,1},{1,0},{2,3},{3,2},{4,5},{5,4},{6,7},{7,6},{8,9},{9,8},{10,11... | collective-permute-start | bytes 786440 | tf_op jit(solution)/shard_map/ppermute | solution.py:528
  65.7 5.9 %collective-permute-start.16 = (f32[4,128,128]{2,1,0:T(8,128)S(1)}, f32[4,128,128]{2,1,0:T(8,128)S(1)}, u32[]{:S(2)}, u32[]{:S(2)}) collective-permute-start(f32[4,128,128]{2,1,0:T(8,128)S(1)} %get-tuple-element.136), channel_id=1, source_target_pairs={{0,2},{2,0},{13,15},{15,13},{1,4},{4,1},{3,6},{6,3},{5,8},{8,5},{7... | collective-permute-start | bytes 786440 | tf_op jit(solution)/shard_map/ppermute | solution.py:527
  66.0 5.6 %collective-permute-start.17 = (f32[4,128,128]{2,1,0:T(8,128)S(1)}, f32[4,128,128]{2,1,0:T(8,128)S(1)}, u32[]{:S(2)}, u32[]{:S(2)}) collective-permute-start(f32[4,128,128]{2,1,0:T(8,128)S(1)} %get-tuple-element.137), channel_id=1, source_target_pairs={{0,1},{1,0},{2,3},{3,2},{4,5},{5,4},{6,7},{7,6},{8,9},{9,8},{10,11... | collective-permute-start | bytes 786440 | tf_op jit(solution)/shard_map/ppermute | solution.py:528
  72.3 5.9 %collective-permute-start.18 = (f32[4,128,128]{2,1,0:T(8,128)S(1)}, f32[4,128,128]{2,1,0:T(8,128)S(1)}, u32[]{:S(2)}, u32[]{:S(2)}) collective-permute-start(f32[4,128,128]{2,1,0:T(8,128)S(1)} %get-tuple-element.142), channel_id=1, source_target_pairs={{0,2},{2,0},{13,15},{15,13},{1,4},{4,1},{3,6},{6,3},{5,8},{8,5},{7... | collective-permute-start | bytes 786440 | tf_op jit(solution)/shard_map/ppermute | solution.py:527
  72.6 5.6 %collective-permute-start.19 = (f32[4,128,128]{2,1,0:T(8,128)S(1)}, f32[4,128,128]{2,1,0:T(8,128)S(1)}, u32[]{:S(2)}, u32[]{:S(2)}) collective-permute-start(f32[4,128,128]{2,1,0:T(8,128)S(1)} %get-tuple-element.143), channel_id=1, source_target_pairs={{0,1},{1,0},{2,3},{3,2},{4,5},{5,4},{6,7},{7,6},{8,9},{9,8},{10,11... | collective-permute-start | bytes 786440 | tf_op jit(solution)/shard_map/ppermute | solution.py:528
  79.0 6.1 %collective-permute-start.20 = (f32[4,128,128]{2,1,0:T(8,128)S(1)}, f32[4,128,128]{2,1,0:T(8,128)S(1)}, u32[]{:S(2)}, u32[]{:S(2)}) collective-permute-start(f32[4,128,128]{2,1,0:T(8,128)S(1)} %get-tuple-element.148), channel_id=1, source_target_pairs={{0,2},{2,0},{13,15},{15,13},{1,4},{4,1},{3,6},{6,3},{5,8},{8,5},{7... | collective-permute-start | bytes 786440 | tf_op jit(solution)/shard_map/ppermute | solution.py:527
  79.3 5.9 %collective-permute-start.21 = (f32[4,128,128]{2,1,0:T(8,128)S(1)}, f32[4,128,128]{2,1,0:T(8,128)S(1)}, u32[]{:S(2)}, u32[]{:S(2)}) collective-permute-start(f32[4,128,128]{2,1,0:T(8,128)S(1)} %get-tuple-element.149), channel_id=1, source_target_pairs={{0,1},{1,0},{2,3},{3,2},{4,5},{5,4},{6,7},{7,6},{8,9},{9,8},{10,11... | collective-permute-start | bytes 786440 | tf_op jit(solution)/shard_map/ppermute | solution.py:528
  85.9 6.2 %collective-permute-start.22 = (f32[4,128,128]{2,1,0:T(8,128)S(1)}, f32[4,128,128]{2,1,0:T(8,128)S(1)}, u32[]{:S(2)}, u32[]{:S(2)}) collective-permute-start(f32[4,128,128]{2,1,0:T(8,128)S(1)} %get-tuple-element.160), channel_id=1, source_target_pairs={{0,2},{2,0},{13,15},{15,13},{1,4},{4,1},{3,6},{6,3},{5,8},{8,5},{7... | collective-permute-start | bytes 786440 | tf_op jit(solution)/shard_map/ppermute | solution.py:527
  86.0 6.1 %collective-permute-start.23 = (f32[4,128,128]{2,1,0:T(8,128)S(1)}, f32[4,128,128]{2,1,0:T(8,128)S(1)}, u32[]{:S(2)}, u32[]{:S(2)}) collective-permute-start(f32[4,128,128]{2,1,0:T(8,128)S(1)} %get-tuple-element.161), channel_id=1, source_target_pairs={{0,1},{1,0},{2,3},{3,2},{4,5},{5,4},{6,7},{7,6},{8,9},{9,8},{10,11... | collective-permute-start | bytes 786440 | tf_op jit(solution)/shard_map/ppermute | solution.py:528
  93.0 6.2 %collective-permute-start.26 = (f32[4,128,128]{2,1,0:T(8,128)S(1)}, f32[4,128,128]{2,1,0:T(8,128)S(1)}, u32[]{:S(2)}, u32[]{:S(2)}) collective-permute-start(f32[4,128,128]{2,1,0:T(8,128)S(1)} %get-tuple-element.171), channel_id=1, source_target_pairs={{0,2},{2,0},{13,15},{15,13},{1,4},{4,1},{3,6},{6,3},{5,8},{8,5},{7... | collective-permute-start | bytes 786440 | tf_op jit(solution)/shard_map/ppermute | solution.py:527
  93.1 6.1 %collective-permute-start.27 = (f32[4,128,128]{2,1,0:T(8,128)S(1)}, f32[4,128,128]{2,1,0:T(8,128)S(1)}, u32[]{:S(2)}, u32[]{:S(2)}) collective-permute-start(f32[4,128,128]{2,1,0:T(8,128)S(1)} %get-tuple-element.172), channel_id=1, source_target_pairs={{0,1},{1,0},{2,3},{3,2},{4,5},{5,4},{6,7},{7,6},{8,9},{9,8},{10,11... | collective-permute-start | bytes 786440 | tf_op jit(solution)/shard_map/ppermute | solution.py:528
  100.0 6.2 %collective-permute-start.29 = (f32[4,128,128]{2,1,0:T(8,128)S(1)}, f32[4,128,128]{2,1,0:T(8,128)S(1)}, u32[]{:S(2)}, u32[]{:S(2)}) collective-permute-start(f32[4,128,128]{2,1,0:T(8,128)S(1)} %get-tuple-element.180), channel_id=1, source_target_pairs={{0,2},{2,0},{13,15},{15,13},{1,4},{4,1},{3,6},{6,3},{5,8},{8,5},{7... | collective-permute-start | bytes 786440 | tf_op jit(solution)/shard_map/ppermute | solution.py:527
  100.1 6.1 %collective-permute-start.30 = (f32[4,128,128]{2,1,0:T(8,128)S(1)}, f32[4,128,128]{2,1,0:T(8,128)S(1)}, u32[]{:S(2)}, u32[]{:S(2)}) collective-permute-start(f32[4,128,128]{2,1,0:T(8,128)S(1)} %get-tuple-element.181), channel_id=1, source_target_pairs={{0,1},{1,0},{2,3},{3,2},{4,5},{5,4},{6,7},{7,6},{8,9},{9,8},{10,11... | collective-permute-start | bytes 786440 | tf_op jit(solution)/shard_map/ppermute | solution.py:528
  106.9 6.2 %collective-permute-start.32 = (f32[4,128,128]{2,1,0:T(8,128)S(1)}, f32[4,128,128]{2,1,0:T(8,128)S(1)}, u32[]{:S(2)}, u32[]{:S(2)}) collective-permute-start(f32[4,128,128]{2,1,0:T(8,128)S(1)} %get-tuple-element.189), channel_id=1, source_target_pairs={{0,2},{2,0},{13,15},{15,13},{1,4},{4,1},{3,6},{6,3},{5,8},{8,5},{7... | collective-permute-start | bytes 786440 | tf_op jit(solution)/shard_map/ppermute | solution.py:527
  107.0 6.1 %collective-permute-start.33 = (f32[4,128,128]{2,1,0:T(8,128)S(1)}, f32[4,128,128]{2,1,0:T(8,128)S(1)}, u32[]{:S(2)}, u32[]{:S(2)}) collective-permute-start(f32[4,128,128]{2,1,0:T(8,128)S(1)} %get-tuple-element.190), channel_id=1, source_target_pairs={{0,1},{1,0},{2,3},{3,2},{4,5},{5,4},{6,7},{7,6},{8,9},{9,8},{10,11... | collective-permute-start | bytes 786440 | tf_op jit(solution)/shard_map/ppermute | solution.py:528
  113.8 6.2 %collective-permute-start.35 = (f32[4,128,128]{2,1,0:T(8,128)S(1)}, f32[4,128,128]{2,1,0:T(8,128)S(1)}, u32[]{:S(2)}, u32[]{:S(2)}) collective-permute-start(f32[4,128,128]{2,1,0:T(8,128)S(1)} %get-tuple-element.198), channel_id=1, source_target_pairs={{0,2},{2,0},{13,15},{15,13},{1,4},{4,1},{3,6},{6,3},{5,8},{8,5},{7... | collective-permute-start | bytes 786440 | tf_op jit(solution)/shard_map/ppermute | solution.py:527
  113.9 6.1 %collective-permute-start.36 = (f32[4,128,128]{2,1,0:T(8,128)S(1)}, f32[4,128,128]{2,1,0:T(8,128)S(1)}, u32[]{:S(2)}, u32[]{:S(2)}) collective-permute-start(f32[4,128,128]{2,1,0:T(8,128)S(1)} %get-tuple-element.199), channel_id=1, source_target_pairs={{0,1},{1,0},{2,3},{3,2},{4,5},{5,4},{6,7},{7,6},{8,9},{9,8},{10,11... | collective-permute-start | bytes 786440 | tf_op jit(solution)/shard_map/ppermute | solution.py:528
  120.8 6.2 %collective-permute-start.41 = (f32[4,128,128]{2,1,0:T(8,128)S(1)}, f32[4,128,128]{2,1,0:T(8,128)S(1)}, u32[]{:S(2)}, u32[]{:S(2)}) collective-permute-start(f32[4,128,128]{2,1,0:T(8,128)S(1)} %get-tuple-element.210), channel_id=1, source_target_pairs={{0,2},{2,0},{13,15},{15,13},{1,4},{4,1},{3,6},{6,3},{5,8},{8,5},{7... | collective-permute-start | bytes 786440 | tf_op jit(solution)/shard_map/ppermute | solution.py:527
  120.9 6.1 %collective-permute-start.42 = (f32[4,128,128]{2,1,0:T(8,128)S(1)}, f32[4,128,128]{2,1,0:T(8,128)S(1)}, u32[]{:S(2)}, u32[]{:S(2)}) collective-permute-start(f32[4,128,128]{2,1,0:T(8,128)S(1)} %get-tuple-element.211), channel_id=1, source_target_pairs={{0,1},{1,0},{2,3},{3,2},{4,5},{5,4},{6,7},{7,6},{8,9},{9,8},{10,11... | collective-permute-start | bytes 786440 | tf_op jit(solution)/shard_map/ppermute | solution.py:528
  130.0 73.0 %all-to-all-start = ((f32[16,16,8,128]{3,2,1,0:T(8,128)}), f32[16,16,8,128]{3,2,1,0:T(8,128)S(1)}, u32[]{:S(2)}, u32[]{:S(2)}) async-start(f32[16,16,8,128]{3,2,1,0:T(8,128)} %get-tuple-element.214), calls=%async_computation | async-start | bytes 2097152 | tf_op jit(solution)/shard_map/all_to_all | solution.py:584
  139.9 21.1 %collective-permute-start.25 = (f32[2,16,8,128]{3,2,1,0:T(8,128)S(1)}, f32[2,16,8,128]{3,2,1,0:T(8,128)S(1)}, u32[]{:S(2)}, u32[]{:S(2)}) collective-permute-start(f32[2,16,8,128]{3,2,1,0:T(8,128)S(1)} %get-tuple-element.169), channel_id=1, source_target_pairs={{0,4},{1,5},{2,6},{3,7},{4,0},{5,1},{6,2},{7,3},{8,12},{9,13},{10,... | collective-permute-start | bytes 393224 | tf_op jit(solution)/shard_map/ppermute | solution.py:573
  140.0 23.8 %collective-permute-start.24 = (f32[2,16,8,128]{3,2,1,0:T(8,128)S(1)}, f32[2,16,8,128]{3,2,1,0:T(8,128)S(1)}, u32[]{:S(2)}, u32[]{:S(2)}) collective-permute-start(f32[2,16,8,128]{3,2,1,0:T(8,128)S(1)} %get-tuple-element.166), channel_id=1, source_target_pairs={{0,4},{1,5},{2,6},{3,7},{4,0},{5,1},{6,2},{7,3},{8,12},{9,13},{10,... | collective-permute-start | bytes 393224 | tf_op jit(solution)/shard_map/ppermute | solution.py:573
  141.4 32.5 %collective-permute-start.28 = (f32[2,16,8,128]{3,2,1,0:T(8,128)S(1)}, f32[2,16,8,128]{3,2,1,0:T(8,128)S(1)}, u32[]{:S(2)}, u32[]{:S(2)}) collective-permute-start(f32[2,16,8,128]{3,2,1,0:T(8,128)S(1)} %get-tuple-element.178), channel_id=1, source_target_pairs={{0,8},{1,9},{2,10},{3,11},{4,12},{5,13},{6,14},{7,15},{8,0},{9,1},... | collective-permute-start | bytes 393224 | tf_op jit(solution)/shard_map/ppermute | solution.py:573
  143.5 58.5 %collective-permute-start.43 = (f32[8,128,128]{2,1,0:T(8,128)}, f32[8,128,128]{2,1,0:T(8,128)S(1)}, u32[]{:S(2)}, u32[]{:S(2)}) collective-permute-start(f32[8,128,128]{2,1,0:T(8,128)} %get-tuple-element.215), channel_id=1, source_target_pairs={{0,0},{1,2},{2,1},{3,3},{4,4},{5,6},{6,5},{7,7},{8,8},{9,10},{10,9... | collective-permute-start | bytes 1572872 | tf_op jit(solution)/shard_map/ppermute | solution.py:585
  147.7 54.3 %collective-permute-start.44 = (f32[8,128,128]{2,1,0:T(8,128)}, f32[8,128,128]{2,1,0:T(8,128)S(1)}, u32[]{:S(2)}, u32[]{:S(2)}) collective-permute-start(f32[8,128,128]{2,1,0:T(8,128)} %get-tuple-element.216), channel_id=1, source_target_pairs={{2,0},{0,1},{3,2},{1,3},{6,4},{4,5},{7,6},{5,7},{10,8},{8,9},{11,1... | collective-permute-start | bytes 1572872 | tf_op jit(solution)/shard_map/ppermute | solution.py:586
  161.0 15.7 %collective-permute-start.31 = (f32[2,16,8,128]{3,2,1,0:T(8,128)S(1)}, f32[2,16,8,128]{3,2,1,0:T(8,128)S(1)}, u32[]{:S(2)}, u32[]{:S(2)}) collective-permute-start(f32[2,16,8,128]{3,2,1,0:T(8,128)S(1)} %get-tuple-element.187), channel_id=1, source_target_pairs={{0,8},{1,9},{2,10},{3,11},{4,12},{5,13},{6,14},{7,15},{8,0},{9,1},... | collective-permute-start | bytes 393224 | tf_op jit(solution)/shard_map/ppermute | solution.py:573
  163.8 20.4 %collective-permute-start.34 = (f32[2,16,8,128]{3,2,1,0:T(8,128)S(1)}, f32[2,16,8,128]{3,2,1,0:T(8,128)S(1)}, u32[]{:S(2)}, u32[]{:S(2)}) collective-permute-start(f32[2,16,8,128]{3,2,1,0:T(8,128)S(1)} %get-tuple-element.196), channel_id=1, source_target_pairs={{0,12},{1,13},{2,14},{3,15},{4,8},{5,9},{6,10},{7,11},{8,4},{9,5},... | collective-permute-start | bytes 393224 | tf_op jit(solution)/shard_map/ppermute | solution.py:573
  173.9 13.2 %collective-permute-start.37 = (f32[2,16,8,128]{3,2,1,0:T(8,128)S(1)}, f32[2,16,8,128]{3,2,1,0:T(8,128)S(1)}, u32[]{:S(2)}, u32[]{:S(2)}) collective-permute-start(f32[2,16,8,128]{3,2,1,0:T(8,128)S(1)} %get-tuple-element.205), channel_id=1, source_target_pairs={{0,12},{1,13},{2,14},{3,15},{4,8},{5,9},{6,10},{7,11},{8,4},{9,5},... | collective-permute-start | bytes 393224 | tf_op jit(solution)/shard_map/ppermute | solution.py:573
  187.2 2.7 %collective-permute-start.38 = (f32[4,16,8,128]{3,2,1,0:T(8,128)S(1)}, f32[4,16,8,128]{3,2,1,0:T(8,128)S(1)}, u32[]{:S(2)}, u32[]{:S(2)}) collective-permute-start(f32[4,16,8,128]{3,2,1,0:T(8,128)S(1)} %get-tuple-element.207), channel_id=1, source_target_pairs={{0,1},{1,0},{2,3},{3,2},{4,5},{5,4},{6,7},{7,6},{8,9},{9,8},{10,11... | collective-permute-start | bytes 786440 | tf_op jit(solution)/shard_map/ppermute | solution.py:581
  188.2 7.8 %collective-permute-start.39 = (f32[4,16,8,128]{3,2,1,0:T(8,128)S(1)}, f32[4,16,8,128]{3,2,1,0:T(8,128)S(1)}, u32[]{:S(2)}, u32[]{:S(2)}) collective-permute-start(f32[4,16,8,128]{3,2,1,0:T(8,128)S(1)} %get-tuple-element.208), channel_id=1, source_target_pairs={{0,2},{1,3},{2,0},{3,1},{4,6},{5,7},{6,4},{7,5},{8,10},{9,11},{10,... | collective-permute-start | bytes 786440 | tf_op jit(solution)/shard_map/ppermute | solution.py:581
  189.4 12.5 %collective-permute-start.40 = (f32[4,16,8,128]{3,2,1,0:T(8,128)S(1)}, f32[4,16,8,128]{3,2,1,0:T(8,128)S(1)}, u32[]{:S(2)}, u32[]{:S(2)}) collective-permute-start(f32[4,16,8,128]{3,2,1,0:T(8,128)S(1)} %get-tuple-element.209), channel_id=1, source_target_pairs={{0,3},{1,2},{2,1},{3,0},{4,7},{5,6},{6,5},{7,4},{8,11},{9,10},{10,... | collective-permute-start | bytes 786440 | tf_op jit(solution)/shard_map/ppermute | solution.py:581

commit v4 on v3

--- a/solution.py
+++ b/solution.py
@@ -8,10 +8,11 @@
 from jax.experimental.pallas import tpu as pltpu
 from jax.sharding import PartitionSpec as P
 
+
 SNAP_EVERY = 6
-SNAPS = 2
 REACH = 4
-EARLY = 2
+EARLY = 4
+PACKED = 2
 
 SCALE = 5040.0
 NEAR = (8064.0, -1008.0, 128.0, -9.0)
@@ -113,10 +114,11 @@
         gathered[row : row + 4] = faces[pl.ds(base + 4 * layers, 4, stride=layers), :]
         gathered[row + 4 : row + 8] = faces[pl.ds(base, 4, stride=layers), :]
 
-    for layer in range(layers):
-        for step in range(EARLY):
-            gather(step, layer, 8 * (EARLY * layer + step))
-    early[...] = gathered[...].T
+    for plane in range(EARLY // PACKED):
+        for layer in range(layers):
+            for step in range(PACKED):
+                gather(PACKED * plane + step, layer, 8 * (PACKED * layer + step))
+        early[plane] = gathered[...].T
 
     def one_layer(layer, carry):
         for step in range(steps):
@@ -141,7 +143,7 @@
         prepare_kernel,
         out_shape=(
             f32(layers, ny, 128),
-            f32(ny, 128),
+            f32(EARLY // PACKED, ny, 128),
             jax.ShapeDtypeStruct((2, 2 * nx, lag_offsets.shape[0] * nx), jnp.bfloat16),
         ),
         in_specs=[SMEM, SMEM, VMEM],
@@ -190,14 +192,9 @@
     for_each_part(2 * face_a.shape[0], run)
 
 
-def merge(kernel, name, shapes, *parts):
+def merge(kernel, shapes, *parts):
     return pl.pallas_call(
-        kernel,
-        out_shape=shapes,
-        in_specs=[VMEM] * len(parts),
-        out_specs=(VMEM,) * len(shapes),
-        compiler_params=PARAMS,
-        name=name,
+        kernel, out_shape=shapes, in_specs=[VMEM] * len(parts), out_specs=(VMEM,) * len(shapes), compiler_params=PARAMS
     )(*parts)
 
 
@@ -216,8 +213,9 @@
             return pltpu.roll(faces[0][layer], (128 - 8 * step - REACH) % 128, axis=1)
         place = place_of(layer, layers)
         part = (place >= layers // 2).astype(jnp.int32)
-        lane = 8 * (EARLY * (place - part * (layers // 2)) + step) + REACH
-        held = jnp.where(part == 0, faces[0][...], faces[1][...])
+        plane, inside = step // PACKED, step % PACKED
+        lane = 8 * (PACKED * (place - part * (layers // 2)) + inside) + REACH
+        held = jnp.where(part == 0, faces[0][plane], faces[1][plane])
         return pltpu.roll(held, lax.rem(128 - lane, 128), axis=1)
 
     for first in range(0, len(local), 2):
@@ -486,21 +484,20 @@
     speed_parts = regroup(speed_term, speed_term)
     late, early, shifts = prepare(saved_faces, face_steps, lag_offsets, nx)
     early = regroup(early, early)
-    cur, low, high = merge(merge_now_kernel, "merge_now", (tall, slab, slab), *now)
+    cur, low, high = merge(merge_now_kernel, (tall, slab, slab), *now)
     low = lax.ppermute(low, "gz", between)
     high = lax.ppermute(high, "gz", within)
-    prev, speed = merge(merge_rest_kernel, "merge_rest", (tall, whole), *before, *speed_parts)
+    prev, speed = merge(merge_rest_kernel, (tall, whole), *before, *speed_parts)
 
     groups = count // 4
-    pieces = 2
-    waiting, arrived = [], []
+    pieces = max(1, 8 // groups)
+    waiting, under_way, arrived = [], [], []
 
     snap = None
     for step in range(steps):
         if step % SNAP_EVERY == 0 and step:
             own_strips, *sent = merge(
                 spread_kernel,
-                "spread",
                 (f32(4, layers, rows, nx), *[f32(4 // pieces, layers, rows, nx)] * (pieces * (groups - 1))),
                 snap,
             )
@@ -510,11 +507,11 @@
             ]
             snap = None
         if step == EARLY:
-            face = merge(merge_faces_kernel, "merge_faces", (whole,), *late)
+            face = merge(merge_faces_kernel, (whole,), *late)
         faces = tuple(face) if step >= EARLY else early
         wide = len(faces)
         if step < steps - 1:
-            cur, new, low, high = pl.pallas_call(
+            border = pl.pallas_call(
                 functools.partial(border_kernel, step, wide),
                 out_shape=(tall, tall, slab, slab),
                 in_specs=[VMEM] * (8 + wide),
@@ -523,9 +520,12 @@
                 compiler_params=PARAMS,
                 cost_estimate=cost(60 * 8 * plane, 4 * 40 * plane),
                 name="border",
-            )(across, along, low, high, traces, speed, *faces, cur, prev)
+            )
+            cur, new, low, high = border(across, along, low, high, traces, speed, *faces, cur, prev)
             low = lax.ppermute(low, "gz", between)
             high = lax.ppermute(high, "gz", within)
+            low, *under_way = lax.optimization_barrier((low, *under_way))
+            arrived, under_way = arrived + under_way, []
         else:
             new = prev
         operands = (snap_phase, across, along, speed, *faces, cur, new)
@@ -554,7 +554,7 @@
                 out_specs=(VMEM,),
                 input_output_aliases={4 + wide: 0},
             )(*operands[1:])
-            _, _, _, out_a, out_b, send = pl.pallas_call(
+            last = pl.pallas_call(
                 functools.partial(last_kernel, step),
                 out_shape=(tall, tall, strips, half, half, f32(*strips.shape)),
                 in_specs=[SMEM] + [VMEM] * 10,
@@ -562,7 +562,8 @@
                 input_output_aliases={8: 0, 9: 1, 10: 2},
                 compiler_params=PARAMS,
                 name="last",
-            )(snap_phase, across, along, low, high, traces, speed, *faces, cur, new, snap)
+            )
+            _, _, _, out_a, out_b, send = last(snap_phase, across, along, low, high, traces, speed, *faces, cur, new, snap)
         if step == 0:
             late, new = lax.optimization_barrier((late, new))
             late = regroup(late, late)
@@ -570,17 +571,15 @@
         now_many = -(-len(waiting) // left) if left else len(waiting)
         for payload, pairs in waiting[:now_many]:
             payload, new = lax.optimization_barrier((payload, new))
-            arrived.append(lax.ppermute(payload, "gz", pairs))
+            under_way.append(lax.ppermute(payload, "gz", pairs))
         waiting = waiting[now_many:]
         prev, cur = cur, new
 
-    mine, *others = merge(
-        regather_kernel, "regather", (f32(groups, layers, rows, nx),) * 4, own_strips, *arrived
-    )
+    mine, *others = merge(regather_kernel, (f32(groups, layers, rows, nx),) * 4, own_strips, *arrived, *under_way)
     others = [
         lax.ppermute(other, "gz", [(i, i ^ (which + 1)) for i in range(count)]) for which, other in enumerate(others)
     ]
-    (first,) = merge(collect_kernel, "collect", (f32(count, layers, rows, nx),), mine, *others)
+    (first,) = merge(collect_kernel, (f32(count, layers, rows, nx),), mine, *others)
     second = lax.all_to_all(send, "gz", split_axis=0, concat_axis=0, tiled=True)
     back_a = lax.ppermute(out_a, "gz", first_pairs)
     back_b = lax.ppermute(out_b, "gz", back_pairs)

time: 209 us -> 209 us (level)
  starting transfers between devices: 71.5 us -> 66.7 us
  waiting for transfers between devices: 95.2 us -> 98.2 us
    ppermute x6, waiting for transfers between devices: 35.1 us -> 50.2 us  [local(): under_way.append(lax.ppermute(payload, 'gz', pairs))]
    ppermute x12, waiting for transfers between devices: 17.8 us -> 11.7 us  [local(): low = lax.ppermute(low, 'gz', between)]
    all_to_all x1, starting transfers between devices: 9.88 us -> 4.28 us  [local(): second = lax.all_to_all(send, 'gz', split_axis=0, concat_axis=0, tiled=True)]
    ppermute x5, waiting for transfers between devices: 16.2 us -> 11.6 us  [regroup(): lax.ppermute(b, 'gz', second_pairs)]
    ppermute x12, starting transfers between devices: 3.37 us -> 5.73 us  [local(): low = lax.ppermute(low, 'gz', between)]
    unnamed x22 -> x26, local copies, waits for them, and re-layouts: 4.18 us -> 5.77 us
  transfers between devices with their start and end apart: 46 -> 46, of which waited for: 24 -> 19; matrix products, arithmetic and copies ran while one was open for 0% -> 0% of each run, Pallas kernels for 10% -> 10%
where the time goes in v4:
time: 209 us
  waiting for transfers between devices  98.2 us (47%)
  starting transfers between devices  66.7 us (32%)
  Pallas kernels  36.8 us (18%)
  local copies, waits for them, and re-layouts  5.77 us (3%)
    ppermute x6, waiting for transfers between devices, local(): under_way.append(lax.ppermute(payload, 'gz', pairs))  50.2 us
    ppermute x12, starting transfers between devices, local(): high = lax.ppermute(high, 'gz', within)  25.3 us
    ppermute x5, starting transfers between devices, regroup(): lax.ppermute(a, 'gz', first_pairs)  18.1 us
    pallas_call x11, Pallas kernels, local(): inner(functools.partial(inner_kernel, step, wide, True), out_shape=(tall,...  14.3 us
    ppermute x5, waiting for transfers between devices, regroup(): lax.ppermute(a, 'gz', first_pairs)  12.6 us
    ppermute x3, waiting for transfers between devices, local(): lax.ppermute(other, 'gz', [(i, i ^ which + 1) for i in range(count)])  11.9 us
    ppermute x12, waiting for transfers between devices, local(): low = lax.ppermute(low, 'gz', between)  11.7 us
    ppermute x5, waiting for transfers between devices, regroup(): lax.ppermute(b, 'gz', second_pairs)  11.6 us
  transfers between devices with their start and end apart: 46, of which 19 were waited for; matrix products, arithmetic and copies ran while one was open for 0% of the time, Pallas kernels for 10%

profile of v4, /device:TPU:9, one launch (start us, length us, event | category | flops | bytes accessed | tf_op | source)
XLA Modules:
  0.0 208.8 jit_solution(8972607294684872938)
XLA Ops:
  0.6 1.0 copy-done.3
  1.7 1.0 copy-done.4
  2.8 3.8 %collective-permute-start.6 = (f32[8,128,128]{2,1,0:T(8,128)S(1)}, f32[8,128,128]{2,1,0:T(8,128)S(1)}, u32[]{:S(2)}, u32[]{:S(2)}) collective-permute-start(f32[8,128,128]{2,1,0:T(8,128)S(1)} %get-tuple-element.126), channel_id=1, source_target_pairs={{0,0},{1,2},{2,1},{3,3},{4,4},{5,6},{6,5},{7,7},{8,8},{9,10},{10,9... | collective-permute-start | bytes 1572872 | tf_op jit(solution)/shard_map/ppermute | solution.py:473
  7.1 3.4 %collective-permute-start.2 = (f32[8,128,128]{2,1,0:T(8,128)}, f32[8,128,128]{2,1,0:T(8,128)S(1)}, u32[]{:S(2)}, u32[]{:S(2)}) collective-permute-start(f32[8,128,128]{2,1,0:T(8,128)} %param.16), channel_id=1, source_target_pairs={{0,0},{1,2},{2,1},{3,3},{4,4},{5,6},{6,5},{7,7},{8,8},{9,10},{10,9... | collective-permute-start | bytes 1572872 | tf_op jit(solution)/shard_map/ppermute | solution.py:473
  10.5 1.0 copy-done.5
  11.5 1.0 copy-done.6
  12.6 2.2 %collective-permute-start = (f32[8,128,128]{2,1,0:T(8,128)S(1)}, f32[8,128,128]{2,1,0:T(8,128)S(1)}, u32[]{:S(2)}, u32[]{:S(2)}) collective-permute-start(f32[8,128,128]{2,1,0:T(8,128)S(1)} %get-tuple-element.121), channel_id=1, source_target_pairs={{0,0},{1,2},{2,1},{3,3},{4,4},{5,6},{6,5},{7,7},{8,8},{9,10},{10,9... | collective-permute-start | bytes 1572872 | tf_op jit(solution)/shard_map/ppermute | solution.py:473
  14.8 3.1 %collective-permute-done.6.now_a = f32[8,128,128]{2,1,0:T(8,128)S(1)} collective-permute-done((f32[8,128,128]{2,1,0:T(8,128)S(1)}, f32[8,128,128]{2,1,0:T(8,128)S(1)}, u32[]{:S(2)}, u32[]{:S(2)}) %collective-permute-start.6) | collective-permute-done | bytes 524320 | tf_op jit(solution)/shard_map/ppermute | solution.py:473
  18.0 2.4 %collective-permute-done.7.now_b = f32[8,128,128]{2,1,0:T(8,128)S(1)} collective-permute-done((f32[8,128,128]{2,1,0:T(8,128)S(1)}, f32[8,128,128]{2,1,0:T(8,128)S(1)}, u32[]{:S(2)}, u32[]{:S(2)}) %collective-permute-start.7) | collective-permute-done | bytes 524320 | tf_op jit(solution)/shard_map/ppermute | solution.py:473
  20.7 1.6 collective-permute-start.8
  22.3 9.3 %collective-permute-done.3.speed_b = f32[8,128,128]{2,1,0:T(8,128)S(1)} collective-permute-done((f32[8,128,128]{2,1,0:T(8,128)}, f32[8,128,128]{2,1,0:T(8,128)S(1)}, u32[]{:S(2)}, u32[]{:S(2)}) %collective-permute-start.3) | collective-permute-done | bytes 524320 | tf_op jit(solution)/shard_map/ppermute | solution.py:473
  31.6 1.8 prepare.1
  33.9 6.5 %collective-permute-done.before_a = f32[8,128,128]{2,1,0:T(8,128)S(1)} collective-permute-done((f32[8,128,128]{2,1,0:T(8,128)S(1)}, f32[8,128,128]{2,1,0:T(8,128)S(1)}, u32[]{:S(2)}, u32[]{:S(2)}) %collective-permute-start) | collective-permute-done | bytes 524320 | tf_op jit(solution)/shard_map/ppermute | solution.py:473
  40.4 4.2 %collective-permute-start.4 = (f32[2,128,128]{2,1,0:T(8,128)S(1)}, f32[2,128,128]{2,1,0:T(8,128)S(1)}, u32[]{:S(2)}, u32[]{:S(2)}) collective-permute-start(f32[2,128,128]{2,1,0:T(8,128)S(1)} %get-tuple-element.125), channel_id=1, source_target_pairs={{0,0},{1,2},{2,1},{3,3},{4,4},{5,6},{6,5},{7,7},{8,8},{9,10},{10,9... | collective-permute-start | bytes 393224 | tf_op jit(solution)/shard_map/ppermute | solution.py:473
  45.1 2.1 %collective-permute-done.4.rest_0_ = f32[2,128,128]{2,1,0:T(8,128)S(1)} collective-permute-done((f32[2,128,128]{2,1,0:T(8,128)S(1)}, f32[2,128,128]{2,1,0:T(8,128)S(1)}, u32[]{:S(2)}, u32[]{:S(2)}) %collective-permute-start.4) | collective-permute-done | bytes 131104 | tf_op jit(solution)/shard_map/ppermute | solution.py:473
  47.3 0.8 border.11
  48.8 1.3 inner.12
  50.1 3.9 %collective-permute-done.12.low = f32[4,128,128]{2,1,0:T(8,128)S(1)} collective-permute-done((f32[4,128,128]{2,1,0:T(8,128)S(1)}, f32[4,128,128]{2,1,0:T(8,128)S(1)}, u32[]{:S(2)}, u32[]{:S(2)}) %collective-permute-start.12) | collective-permute-done | bytes 262176 | tf_op jit(solution)/shard_map/ppermute | solution.py:525
  54.0 0.8 border.12
  54.9 0.8 collective-permute-start.15
  55.7 4.5 %collective-permute-start.10 = (f32[8,128,128]{2,1,0:T(8,128)S(1)}, f32[8,128,128]{2,1,0:T(8,128)S(1)}, u32[]{:S(2)}, u32[]{:S(2)}) collective-permute-start(f32[8,128,128]{2,1,0:T(8,128)S(1)} %get-tuple-element.135), channel_id=1, source_target_pairs={{0,0},{1,2},{2,1},{3,3},{4,4},{5,6},{6,5},{7,7},{8,8},{9,10},{10,9... | collective-permute-start | bytes 1572872 | tf_op jit(solution)/shard_map/ppermute | solution.py:473
  60.2 1.3 inner.13
  61.5 0.8 border.13
  63.0 1.3 inner.14
  64.3 3.9 %collective-permute-done.16.low = f32[4,128,128]{2,1,0:T(8,128)S(1)} collective-permute-done((f32[4,128,128]{2,1,0:T(8,128)S(1)}, f32[4,128,128]{2,1,0:T(8,128)S(1)}, u32[]{:S(2)}, u32[]{:S(2)}) %collective-permute-start.16) | collective-permute-done | bytes 262176 | tf_op jit(solution)/shard_map/ppermute | solution.py:525
  68.2 0.8 border.14
  69.7 0.9 collective-permute-done.10.face_a
  71.0 1.3 inner.15
  72.3 2.6 %collective-permute-done.18.low = f32[4,128,128]{2,1,0:T(8,128)S(1)} collective-permute-done((f32[4,128,128]{2,1,0:T(8,128)S(1)}, f32[4,128,128]{2,1,0:T(8,128)S(1)}, u32[]{:S(2)}, u32[]{:S(2)}) %collective-permute-start.18) | collective-permute-done | bytes 262176 | tf_op jit(solution)/shard_map/ppermute | solution.py:525
  74.9 0.8 border.15
  76.1 5.9 %collective-permute-start.21 = (f32[4,128,128]{2,1,0:T(8,128)S(1)}, f32[4,128,128]{2,1,0:T(8,128)S(1)}, u32[]{:S(2)}, u32[]{:S(2)}) collective-permute-start(f32[4,128,128]{2,1,0:T(8,128)S(1)} %get-tuple-element.158), channel_id=1, source_target_pairs={{0,1},{1,0},{2,3},{3,2},{4,5},{5,4},{6,7},{7,6},{8,9},{9,8},{10,11... | collective-permute-start | bytes 786440 | tf_op jit(solution)/shard_map/ppermute | solution.py:526
  82.0 1.4 inner.16
  84.3 4.7 %collective-permute-start.23 = (f32[4,128,128]{2,1,0:T(8,128)S(1)}, f32[4,128,128]{2,1,0:T(8,128)S(1)}, u32[]{:S(2)}, u32[]{:S(2)}) collective-permute-start(f32[4,128,128]{2,1,0:T(8,128)S(1)} %get-tuple-element.169), channel_id=1, source_target_pairs={{0,1},{1,0},{2,3},{3,2},{4,5},{5,4},{6,7},{7,6},{8,9},{9,8},{10,11... | collective-permute-start | bytes 786440 | tf_op jit(solution)/shard_map/ppermute | solution.py:526
  89.0 1.3 inner.17
  90.4 0.9 border.17
  91.4 4.8 %collective-permute-start.25 = (f32[4,128,128]{2,1,0:T(8,128)S(1)}, f32[4,128,128]{2,1,0:T(8,128)S(1)}, u32[]{:S(2)}, u32[]{:S(2)}) collective-permute-start(f32[4,128,128]{2,1,0:T(8,128)S(1)} %get-tuple-element.172), channel_id=1, source_target_pairs={{0,1},{1,0},{2,3},{3,2},{4,5},{5,4},{6,7},{7,6},{8,9},{9,8},{10,11... | collective-permute-start | bytes 786440 | tf_op jit(solution)/shard_map/ppermute | solution.py:526
  96.3 1.3 inner.18
  98.5 5.1 %collective-permute-start.29 = (f32[4,128,128]{2,1,0:T(8,128)S(1)}, f32[4,128,128]{2,1,0:T(8,128)S(1)}, u32[]{:S(2)}, u32[]{:S(2)}) collective-permute-start(f32[4,128,128]{2,1,0:T(8,128)S(1)} %get-tuple-element.186), channel_id=1, source_target_pairs={{0,1},{1,0},{2,3},{3,2},{4,5},{5,4},{6,7},{7,6},{8,9},{9,8},{10,11... | collective-permute-start | bytes 786440 | tf_op jit(solution)/shard_map/ppermute | solution.py:526
  103.5 4.6 %collective-permute-start.28 = (f32[2,16,8,128]{3,2,1,0:T(8,128)S(1)}, f32[2,16,8,128]{3,2,1,0:T(8,128)S(1)}, u32[]{:S(2)}, u32[]{:S(2)}) collective-permute-start(f32[2,16,8,128]{3,2,1,0:T(8,128)S(1)} %get-tuple-element.182), channel_id=1, source_target_pairs={{0,4},{1,5},{2,6},{3,7},{4,0},{5,1},{6,2},{7,3},{8,12},{9,13},{10,... | collective-permute-start | bytes 393224 | tf_op jit(solution)/shard_map/ppermute | solution.py:574
  108.1 1.3 inner.19
  109.4 2.6 %collective-permute-done.28.refs_1_ = f32[2,16,8,128]{3,2,1,0:T(8,128)S(1)} collective-permute-done((f32[2,16,8,128]{3,2,1,0:T(8,128)S(1)}, f32[2,16,8,128]{3,2,1,0:T(8,128)S(1)}, u32[]{:S(2)}, u32[]{:S(2)}) %collective-permute-start.28) | collective-permute-done | bytes 131104 | tf_op jit(solution)/shard_map/ppermute | solution.py:574
  112.0 2.8 %collective-permute-done.27.refs_0_ = f32[2,16,8,128]{3,2,1,0:T(8,128)S(1)} collective-permute-done((f32[2,16,8,128]{3,2,1,0:T(8,128)S(1)}, f32[2,16,8,128]{3,2,1,0:T(8,128)S(1)}, u32[]{:S(2)}, u32[]{:S(2)}) %collective-permute-start.27) | collective-permute-done | bytes 131104 | tf_op jit(solution)/shard_map/ppermute | solution.py:574
  115.7 1.6 collective-permute-start.32
  117.2 1.4 inner.20
  118.6 5.9 %collective-permute-done.31.refs_2_ = f32[2,16,8,128]{3,2,1,0:T(8,128)S(1)} collective-permute-done((f32[2,16,8,128]{3,2,1,0:T(8,128)S(1)}, f32[2,16,8,128]{3,2,1,0:T(8,128)S(1)}, u32[]{:S(2)}, u32[]{:S(2)}) %collective-permute-start.31) | collective-permute-done | bytes 131104 | tf_op jit(solution)/shard_map/ppermute | solution.py:574
  124.6 1.1 collective-permute-done.30.low
  126.4 1.3 collective-permute-start.33
  128.4 1.3 inner.21
  129.7 7.0 %collective-permute-done.34.refs_3_ = f32[2,16,8,128]{3,2,1,0:T(8,128)S(1)} collective-permute-done((f32[2,16,8,128]{3,2,1,0:T(8,128)S(1)}, f32[2,16,8,128]{3,2,1,0:T(8,128)S(1)}, u32[]{:S(2)}, u32[]{:S(2)}) %collective-permute-start.34) | collective-permute-done | bytes 131104 | tf_op jit(solution)/shard_map/ppermute | solution.py:574
  137.5 1.1 collective-permute-start.36
  138.6 1.4 collective-permute-start.42
  140.0 1.3 inner.22
  142.0 6.3 %collective-permute-done.37.refs_4_ = f32[2,16,8,128]{3,2,1,0:T(8,128)S(1)} collective-permute-done((f32[2,16,8,128]{3,2,1,0:T(8,128)S(1)}, f32[2,16,8,128]{3,2,1,0:T(8,128)S(1)}, u32[]{:S(2)}, u32[]{:S(2)}) %collective-permute-start.37) | collective-permute-done | bytes 131104 | tf_op jit(solution)/shard_map/ppermute | solution.py:574
  148.3 2.7 %last.1 = (f32[24,128,128]{2,1,0:T(8,128)S(1)}, f32[24,128,128]{2,1,0:T(8,128)S(1)}, f32[16,16,8,128]{3,2,1,0:T(8,128)S(1)}, f32[8,128,128]{2,1,0:T(8,128)S(1)},...) custom-call(s32[2]{0:T(128)S(1)} %copy-done.8, ...), custom_call_target="tpu_custom_call", output_to_operand_aliasing={{0}: (8, {}), {1}: (9, {}), {2}: (10, {})} | custom-call | tf_op jit(solution)/shard_map/last/pallas_call | solution.py:566
  152.5 4.3 %all-to-all-start = ((f32[16,16,8,128]{3,2,1,0:T(8,128)}), f32[16,16,8,128]{3,2,1,0:T(8,128)S(1)}, u32[]{:S(2)}, u32[]{:S(2)}) async-start(f32[16,16,8,128]{3,2,1,0:T(8,128)} %get-tuple-element.232), calls=%async_computation | async-start | bytes 2097152 | tf_op jit(solution)/shard_map/all_to_all | solution.py:583
  156.8 3.4 %collective-permute-start.43 = (f32[8,128,128]{2,1,0:T(8,128)}, f32[8,128,128]{2,1,0:T(8,128)S(1)}, u32[]{:S(2)}, u32[]{:S(2)}) collective-permute-start(f32[8,128,128]{2,1,0:T(8,128)} %copy-done.12), channel_id=1, source_target_pairs={{0,0},{1,2},{2,1},{3,3},{4,4},{5,6},{6,5},{7,7},{8,8},{9,10},{10,9... | collective-permute-start | bytes 1572872 | tf_op jit(solution)/shard_map/ppermute | solution.py:584
  160.2 1.2 collective-permute-start.38
  161.5 25.5 %collective-permute-done.38.refs_5_ = f32[2,16,8,128]{3,2,1,0:T(8,128)S(1)} collective-permute-done((f32[2,16,8,128]{3,2,1,0:T(8,128)S(1)}, f32[2,16,8,128]{3,2,1,0:T(8,128)S(1)}, u32[]{:S(2)}, u32[]{:S(2)}) %collective-permute-start.38) | collective-permute-done | bytes 131104 | tf_op jit(solution)/shard_map/ppermute | solution.py:574
  187.2 1.0 collective-permute-start.39
  188.2 1.2 collective-permute-start.40
  189.9 6.1 %collective-permute-done.40.refs_2_ = f32[4,16,8,128]{3,2,1,0:T(8,128)S(1)} collective-permute-done((f32[4,16,8,128]{3,2,1,0:T(8,128)S(1)}, f32[4,16,8,128]{3,2,1,0:T(8,128)S(1)}, u32[]{:S(2)}, u32[]{:S(2)}) %collective-permute-start.40) | collective-permute-done | bytes 262176 | tf_op jit(solution)/shard_map/ppermute | solution.py:580
  196.0 5.9 %collective-permute-done.41.refs_3_ = f32[4,16,8,128]{3,2,1,0:T(8,128)S(1)} collective-permute-done((f32[4,16,8,128]{3,2,1,0:T(8,128)S(1)}, f32[4,16,8,128]{3,2,1,0:T(8,128)S(1)}, u32[]{:S(2)}, u32[]{:S(2)}) %collective-permute-start.41) | collective-permute-done | bytes 262176 | tf_op jit(solution)/shard_map/ppermute | solution.py:580
  202.0 1.0 choose.5
  203.0 5.7 %images.1 = bf16[8,128,8,128]{3,2,1,0:T(8,128)(2,1)} custom-call(bf16[2,256,1024]{2,1,0:T(8,128)(2,1)S(1)} %get-tuple-element.120.shifts, f32[16,16,8,128]{3,2,1,0:T(8,128)S(1)} %shard_map.144.refs_0_, f32[16,16,8,128]{3,2,1,0:T(8,128)S(1)} %all-to-all-done.refs_1_), custom_call_target="tpu_custom_call" | custom-call | tf_op jit(solution)/shard_map/images/pallas_call | solution.py:433
  (89 shorter events, 13.0 us)
Async XLA Ops:
  0.6 1.0 copy-start.3
  1.7 1.0 copy-start.4
  2.7 28.9 %copy-start.7 = (f32[12,8,8,128]{3,2,1,0:T(8,128)S(1)}, f32[12,8,8,128]{3,2,1,0:T(8,128)}, u32[]{:S(2)}) copy-start(f32[12,8,8,128]{3,2,1,0:T(8,128)} %param.17) | copy-start | bytes 1179652
  2.7 28.9 %copy-start.9 = (s32[12]{0:T(128)S(1)}, s32[12]{0:T(128)}, u32[]{:S(2)}) copy-start(s32[12]{0:T(128)} %face_steps.1) | copy-start | bytes 148
  2.7 28.9 %copy-start.10 = (s32[8]{0:T(128)S(1)}, s32[8]{0:T(128)}, u32[]{:S(2)}) copy-start(s32[8]{0:T(128)} %lags.1) | copy-start | bytes 100
  2.8 15.1 %collective-permute-start.6 = (f32[8,128,128]{2,1,0:T(8,128)S(1)}, f32[8,128,128]{2,1,0:T(8,128)S(1)}, u32[]{:S(2)}, u32[]{:S(2)}) collective-permute-start(f32[8,128,128]{2,1,0:T(8,128)S(1)} %get-tuple-element.126), channel_id=1, source_target_pairs={{0,0},{1,2},{2,1},{3,3},{4,4},{5,6},{6,5},{7,7},{8,8},{9,10},{10,9... | collective-permute-start | bytes 1572872 | tf_op jit(solution)/shard_map/ppermute | solution.py:473
  6.7 13.7 %collective-permute-start.7 = (f32[8,128,128]{2,1,0:T(8,128)S(1)}, f32[8,128,128]{2,1,0:T(8,128)S(1)}, u32[]{:S(2)}, u32[]{:S(2)}) collective-permute-start(f32[8,128,128]{2,1,0:T(8,128)S(1)} %get-tuple-element.127), channel_id=1, source_target_pairs={{0,2},{1,0},{2,3},{3,1},{4,6},{5,4},{6,7},{7,5},{8,10},{9,8},{10,1... | collective-permute-start | bytes 1572872 | tf_op jit(solution)/shard_map/ppermute | solution.py:473
  6.7 24.9 %collective-permute-start.3 = (f32[8,128,128]{2,1,0:T(8,128)}, f32[8,128,128]{2,1,0:T(8,128)S(1)}, u32[]{:S(2)}, u32[]{:S(2)}) collective-permute-start(f32[8,128,128]{2,1,0:T(8,128)} %param.16), channel_id=1, source_target_pairs={{0,2},{1,0},{2,3},{3,1},{4,6},{5,4},{6,7},{7,5},{8,10},{9,8},{10,1... | collective-permute-start | bytes 1572872 | tf_op jit(solution)/shard_map/ppermute | solution.py:473
  7.1 26.3 %collective-permute-start.2 = (f32[8,128,128]{2,1,0:T(8,128)}, f32[8,128,128]{2,1,0:T(8,128)S(1)}, u32[]{:S(2)}, u32[]{:S(2)}) collective-permute-start(f32[8,128,128]{2,1,0:T(8,128)} %param.16), channel_id=1, source_target_pairs={{0,0},{1,2},{2,1},{3,3},{4,4},{5,6},{6,5},{7,7},{8,8},{9,10},{10,9... | collective-permute-start | bytes 1572872 | tf_op jit(solution)/shard_map/ppermute | solution.py:473
  10.5 1.0 copy-start.5
  11.5 1.0 copy-start.6
  12.6 27.8 %collective-permute-start = (f32[8,128,128]{2,1,0:T(8,128)S(1)}, f32[8,128,128]{2,1,0:T(8,128)S(1)}, u32[]{:S(2)}, u32[]{:S(2)}) collective-permute-start(f32[8,128,128]{2,1,0:T(8,128)S(1)} %get-tuple-element.121), channel_id=1, source_target_pairs={{0,0},{1,2},{2,1},{3,3},{4,4},{5,6},{6,5},{7,7},{8,8},{9,10},{10,9... | collective-permute-start | bytes 1572872 | tf_op jit(solution)/shard_map/ppermute | solution.py:473
  17.9 29.3 %copy-start = (bf16[12,128,128]{2,1,0:T(8,128)(2,1)S(1)}, bf16[12,128,128]{2,1,0:T(8,128)(2,1)}, u32[]{:S(2)}) copy-start(bf16[12,128,128]{2,1,0:T(8,128)(2,1)} %traces.23) | copy-start | bytes 1179652
  17.9 29.3 %copy-start.1 = (bf16[128,256]{1,0:T(8,128)(2,1)S(1)}, bf16[128,256]{1,0:T(8,128)(2,1)}, u32[]{:S(2)}) copy-start(bf16[128,256]{1,0:T(8,128)(2,1)} %constant.5.clone.along) | copy-start | bytes 196612
  17.9 29.3 %copy-start.2 = (bf16[256,128]{1,0:T(8,128)(2,1)S(1)}, bf16[256,128]{1,0:T(8,128)(2,1)}, u32[]{:S(2)}) copy-start(bf16[256,128]{1,0:T(8,128)(2,1)} %constant.4.clone.across) | copy-start | bytes 196612
  17.9 26.7 %collective-permute-start.1 = (f32[8,128,128]{2,1,0:T(8,128)S(1)}, f32[8,128,128]{2,1,0:T(8,128)S(1)}, u32[]{:S(2)}, u32[]{:S(2)}) collective-permute-start(f32[8,128,128]{2,1,0:T(8,128)S(1)} %get-tuple-element.122), channel_id=1, source_target_pairs={{0,2},{1,0},{2,3},{3,1},{4,6},{5,4},{6,7},{7,5},{8,10},{9,8},{10,1... | collective-permute-start | bytes 1572872 | tf_op jit(solution)/shard_map/ppermute | solution.py:473
  20.7 26.5 %collective-permute-start.8 = (f32[4,128,128]{2,1,0:T(8,128)S(1)}, f32[4,128,128]{2,1,0:T(8,128)S(1)}, u32[]{:S(2)}, u32[]{:S(2)}) collective-permute-start(f32[4,128,128]{2,1,0:T(8,128)S(1)} %get-tuple-element.128), channel_id=1, source_target_pairs={{0,2},{2,0},{13,15},{15,13},{1,4},{4,1},{3,6},{6,3},{5,8},{8,5},{7... | collective-permute-start | bytes 786440 | tf_op jit(solution)/shard_map/ppermute | solution.py:488
  31.6 15.7 %collective-permute-start.9 = (f32[4,128,128]{2,1,0:T(8,128)S(1)}, f32[4,128,128]{2,1,0:T(8,128)S(1)}, u32[]{:S(2)}, u32[]{:S(2)}) collective-permute-start(f32[4,128,128]{2,1,0:T(8,128)S(1)} %get-tuple-element.129), channel_id=1, source_target_pairs={{0,1},{1,0},{2,3},{3,2},{4,5},{5,4},{6,7},{7,6},{8,9},{9,8},{10,11... | collective-permute-start | bytes 786440 | tf_op jit(solution)/shard_map/ppermute | solution.py:489
  33.4 11.7 %collective-permute-start.5 = (f32[2,128,128]{2,1,0:T(8,128)S(1)}, f32[2,128,128]{2,1,0:T(8,128)S(1)}, u32[]{:S(2)}, u32[]{:S(2)}) collective-permute-start(f32[2,128,128]{2,1,0:T(8,128)S(1)} %get-tuple-element.125), channel_id=1, source_target_pairs={{0,2},{1,0},{2,3},{3,1},{4,6},{5,4},{6,7},{7,5},{8,10},{9,8},{10,1... | collective-permute-start | bytes 393224 | tf_op jit(solution)/shard_map/ppermute | solution.py:473
  40.4 6.9 %collective-permute-start.4 = (f32[2,128,128]{2,1,0:T(8,128)S(1)}, f32[2,128,128]{2,1,0:T(8,128)S(1)}, u32[]{:S(2)}, u32[]{:S(2)}) collective-permute-start(f32[2,128,128]{2,1,0:T(8,128)S(1)} %get-tuple-element.125), channel_id=1, source_target_pairs={{0,0},{1,2},{2,1},{3,3},{4,4},{5,6},{6,5},{7,7},{8,8},{9,10},{10,9... | collective-permute-start | bytes 393224 | tf_op jit(solution)/shard_map/ppermute | solution.py:473
  47.3 1.5 copy-start.8
  48.1 5.9 %collective-permute-start.12 = (f32[4,128,128]{2,1,0:T(8,128)S(1)}, f32[4,128,128]{2,1,0:T(8,128)S(1)}, u32[]{:S(2)}, u32[]{:S(2)}) collective-permute-start(f32[4,128,128]{2,1,0:T(8,128)S(1)} %get-tuple-element.136), channel_id=1, source_target_pairs={{0,2},{2,0},{13,15},{15,13},{1,4},{4,1},{3,6},{6,3},{5,8},{8,5},{7... | collective-permute-start | bytes 786440 | tf_op jit(solution)/shard_map/ppermute | solution.py:525
  48.2 5.8 %collective-permute-start.13 = (f32[4,128,128]{2,1,0:T(8,128)S(1)}, f32[4,128,128]{2,1,0:T(8,128)S(1)}, u32[]{:S(2)}, u32[]{:S(2)}) collective-permute-start(f32[4,128,128]{2,1,0:T(8,128)S(1)} %get-tuple-element.137), channel_id=1, source_target_pairs={{0,1},{1,0},{2,3},{3,2},{4,5},{5,4},{6,7},{7,6},{8,9},{9,8},{10,11... | collective-permute-start | bytes 786440 | tf_op jit(solution)/shard_map/ppermute | solution.py:526
  54.8 6.7 %collective-permute-start.14 = (f32[4,128,128]{2,1,0:T(8,128)S(1)}, f32[4,128,128]{2,1,0:T(8,128)S(1)}, u32[]{:S(2)}, u32[]{:S(2)}) collective-permute-start(f32[4,128,128]{2,1,0:T(8,128)S(1)} %get-tuple-element.139), channel_id=1, source_target_pairs={{0,2},{2,0},{13,15},{15,13},{1,4},{4,1},{3,6},{6,3},{5,8},{8,5},{7... | collective-permute-start | bytes 786440 | tf_op jit(solution)/shard_map/ppermute | solution.py:525
  54.9 6.6 %collective-permute-start.15 = (f32[4,128,128]{2,1,0:T(8,128)S(1)}, f32[4,128,128]{2,1,0:T(8,128)S(1)}, u32[]{:S(2)}, u32[]{:S(2)}) collective-permute-start(f32[4,128,128]{2,1,0:T(8,128)S(1)} %get-tuple-element.140), channel_id=1, source_target_pairs={{0,1},{1,0},{2,3},{3,2},{4,5},{5,4},{6,7},{7,6},{8,9},{9,8},{10,11... | collective-permute-start | bytes 786440 | tf_op jit(solution)/shard_map/ppermute | solution.py:526
  55.7 13.9 %collective-permute-start.11 = (f32[8,128,128]{2,1,0:T(8,128)S(1)}, f32[8,128,128]{2,1,0:T(8,128)S(1)}, u32[]{:S(2)}, u32[]{:S(2)}) collective-permute-start(f32[8,128,128]{2,1,0:T(8,128)S(1)} %get-tuple-element.135), channel_id=1, source_target_pairs={{0,2},{1,0},{2,3},{3,1},{4,6},{5,4},{6,7},{7,5},{8,10},{9,8},{10,1... | collective-permute-start | bytes 1572872 | tf_op jit(solution)/shard_map/ppermute | solution.py:473
  55.7 14.9 %collective-permute-start.10 = (f32[8,128,128]{2,1,0:T(8,128)S(1)}, f32[8,128,128]{2,1,0:T(8,128)S(1)}, u32[]{:S(2)}, u32[]{:S(2)}) collective-permute-start(f32[8,128,128]{2,1,0:T(8,128)S(1)} %get-tuple-element.135), channel_id=1, source_target_pairs={{0,0},{1,2},{2,1},{3,3},{4,4},{5,6},{6,5},{7,7},{8,8},{9,10},{10,9... | collective-permute-start | bytes 1572872 | tf_op jit(solution)/shard_map/ppermute | solution.py:473
  62.4 5.9 %collective-permute-start.16 = (f32[4,128,128]{2,1,0:T(8,128)S(1)}, f32[4,128,128]{2,1,0:T(8,128)S(1)}, u32[]{:S(2)}, u32[]{:S(2)}) collective-permute-start(f32[4,128,128]{2,1,0:T(8,128)S(1)} %get-tuple-element.145), channel_id=1, source_target_pairs={{0,2},{2,0},{13,15},{15,13},{1,4},{4,1},{3,6},{6,3},{5,8},{8,5},{7... | collective-permute-start | bytes 786440 | tf_op jit(solution)/shard_map/ppermute | solution.py:525
  62.8 5.4 %collective-permute-start.17 = (f32[4,128,128]{2,1,0:T(8,128)S(1)}, f32[4,128,128]{2,1,0:T(8,128)S(1)}, u32[]{:S(2)}, u32[]{:S(2)}) collective-permute-start(f32[4,128,128]{2,1,0:T(8,128)S(1)} %get-tuple-element.146), channel_id=1, source_target_pairs={{0,1},{1,0},{2,3},{3,2},{4,5},{5,4},{6,7},{7,6},{8,9},{9,8},{10,11... | collective-permute-start | bytes 786440 | tf_op jit(solution)/shard_map/ppermute | solution.py:526
  69.0 5.9 %collective-permute-start.18 = (f32[4,128,128]{2,1,0:T(8,128)S(1)}, f32[4,128,128]{2,1,0:T(8,128)S(1)}, u32[]{:S(2)}, u32[]{:S(2)}) collective-permute-start(f32[4,128,128]{2,1,0:T(8,128)S(1)} %get-tuple-element.151), channel_id=1, source_target_pairs={{0,2},{2,0},{13,15},{15,13},{1,4},{4,1},{3,6},{6,3},{5,8},{8,5},{7... | collective-permute-start | bytes 786440 | tf_op jit(solution)/shard_map/ppermute | solution.py:525
  69.5 5.4 %collective-permute-start.19 = (f32[4,128,128]{2,1,0:T(8,128)S(1)}, f32[4,128,128]{2,1,0:T(8,128)S(1)}, u32[]{:S(2)}, u32[]{:S(2)}) collective-permute-start(f32[4,128,128]{2,1,0:T(8,128)S(1)} %get-tuple-element.152), channel_id=1, source_target_pairs={{0,1},{1,0},{2,3},{3,2},{4,5},{5,4},{6,7},{7,6},{8,9},{9,8},{10,11... | collective-permute-start | bytes 786440 | tf_op jit(solution)/shard_map/ppermute | solution.py:526
  75.7 7.7 %collective-permute-start.20 = (f32[4,128,128]{2,1,0:T(8,128)S(1)}, f32[4,128,128]{2,1,0:T(8,128)S(1)}, u32[]{:S(2)}, u32[]{:S(2)}) collective-permute-start(f32[4,128,128]{2,1,0:T(8,128)S(1)} %get-tuple-element.157), channel_id=1, source_target_pairs={{0,2},{2,0},{13,15},{15,13},{1,4},{4,1},{3,6},{6,3},{5,8},{8,5},{7... | collective-permute-start | bytes 786440 | tf_op jit(solution)/shard_map/ppermute | solution.py:525
  76.1 7.3 %collective-permute-start.21 = (f32[4,128,128]{2,1,0:T(8,128)S(1)}, f32[4,128,128]{2,1,0:T(8,128)S(1)}, u32[]{:S(2)}, u32[]{:S(2)}) collective-permute-start(f32[4,128,128]{2,1,0:T(8,128)S(1)} %get-tuple-element.158), channel_id=1, source_target_pairs={{0,1},{1,0},{2,3},{3,2},{4,5},{5,4},{6,7},{7,6},{8,9},{9,8},{10,11... | collective-permute-start | bytes 786440 | tf_op jit(solution)/shard_map/ppermute | solution.py:526
  84.2 6.2 %collective-permute-start.22 = (f32[4,128,128]{2,1,0:T(8,128)S(1)}, f32[4,128,128]{2,1,0:T(8,128)S(1)}, u32[]{:S(2)}, u32[]{:S(2)}) collective-permute-start(f32[4,128,128]{2,1,0:T(8,128)S(1)} %get-tuple-element.168), channel_id=1, source_target_pairs={{0,2},{2,0},{13,15},{15,13},{1,4},{4,1},{3,6},{6,3},{5,8},{8,5},{7... | collective-permute-start | bytes 786440 | tf_op jit(solution)/shard_map/ppermute | solution.py:525
  84.3 6.1 %collective-permute-start.23 = (f32[4,128,128]{2,1,0:T(8,128)S(1)}, f32[4,128,128]{2,1,0:T(8,128)S(1)}, u32[]{:S(2)}, u32[]{:S(2)}) collective-permute-start(f32[4,128,128]{2,1,0:T(8,128)S(1)} %get-tuple-element.169), channel_id=1, source_target_pairs={{0,1},{1,0},{2,3},{3,2},{4,5},{5,4},{6,7},{7,6},{8,9},{9,8},{10,11... | collective-permute-start | bytes 786440 | tf_op jit(solution)/shard_map/ppermute | solution.py:526
  91.3 6.3 %collective-permute-start.24 = (f32[4,128,128]{2,1,0:T(8,128)S(1)}, f32[4,128,128]{2,1,0:T(8,128)S(1)}, u32[]{:S(2)}, u32[]{:S(2)}) collective-permute-start(f32[4,128,128]{2,1,0:T(8,128)S(1)} %get-tuple-element.171), channel_id=1, source_target_pairs={{0,2},{2,0},{13,15},{15,13},{1,4},{4,1},{3,6},{6,3},{5,8},{8,5},{7... | collective-permute-start | bytes 786440 | tf_op jit(solution)/shard_map/ppermute | solution.py:525
  91.4 6.2 %collective-permute-start.25 = (f32[4,128,128]{2,1,0:T(8,128)S(1)}, f32[4,128,128]{2,1,0:T(8,128)S(1)}, u32[]{:S(2)}, u32[]{:S(2)}) collective-permute-start(f32[4,128,128]{2,1,0:T(8,128)S(1)} %get-tuple-element.172), channel_id=1, source_target_pairs={{0,1},{1,0},{2,3},{3,2},{4,5},{5,4},{6,7},{7,6},{8,9},{9,8},{10,11... | collective-permute-start | bytes 786440 | tf_op jit(solution)/shard_map/ppermute | solution.py:526
  98.4 16.4 %collective-permute-start.26 = (f32[4,128,128]{2,1,0:T(8,128)S(1)}, f32[4,128,128]{2,1,0:T(8,128)S(1)}, u32[]{:S(2)}, u32[]{:S(2)}) collective-permute-start(f32[4,128,128]{2,1,0:T(8,128)S(1)} %get-tuple-element.180), channel_id=1, source_target_pairs={{0,2},{2,0},{13,15},{15,13},{1,4},{4,1},{3,6},{6,3},{5,8},{8,5},{7... | collective-permute-start | bytes 786440 | tf_op jit(solution)/shard_map/ppermute | solution.py:525
  98.5 16.3 %collective-permute-start.29 = (f32[4,128,128]{2,1,0:T(8,128)S(1)}, f32[4,128,128]{2,1,0:T(8,128)S(1)}, u32[]{:S(2)}, u32[]{:S(2)}) collective-permute-start(f32[4,128,128]{2,1,0:T(8,128)S(1)} %get-tuple-element.186), channel_id=1, source_target_pairs={{0,1},{1,0},{2,3},{3,2},{4,5},{5,4},{6,7},{7,6},{8,9},{9,8},{10,11... | collective-permute-start | bytes 786440 | tf_op jit(solution)/shard_map/ppermute | solution.py:526
  103.5 8.4 %collective-permute-start.28 = (f32[2,16,8,128]{3,2,1,0:T(8,128)S(1)}, f32[2,16,8,128]{3,2,1,0:T(8,128)S(1)}, u32[]{:S(2)}, u32[]{:S(2)}) collective-permute-start(f32[2,16,8,128]{3,2,1,0:T(8,128)S(1)} %get-tuple-element.182), channel_id=1, source_target_pairs={{0,4},{1,5},{2,6},{3,7},{4,0},{5,1},{6,2},{7,3},{8,12},{9,13},{10,... | collective-permute-start | bytes 393224 | tf_op jit(solution)/shard_map/ppermute | solution.py:574
  108.1 6.7 %collective-permute-start.27 = (f32[2,16,8,128]{3,2,1,0:T(8,128)S(1)}, f32[2,16,8,128]{3,2,1,0:T(8,128)S(1)}, u32[]{:S(2)}, u32[]{:S(2)}) collective-permute-start(f32[2,16,8,128]{3,2,1,0:T(8,128)S(1)} %get-tuple-element.181), channel_id=1, source_target_pairs={{0,4},{1,5},{2,6},{3,7},{4,0},{5,1},{6,2},{7,3},{8,12},{9,13},{10,... | collective-permute-start | bytes 393224 | tf_op jit(solution)/shard_map/ppermute | solution.py:574
  115.6 10.1 %collective-permute-start.30 = (f32[4,128,128]{2,1,0:T(8,128)S(1)}, f32[4,128,128]{2,1,0:T(8,128)S(1)}, u32[]{:S(2)}, u32[]{:S(2)}) collective-permute-start(f32[4,128,128]{2,1,0:T(8,128)S(1)} %get-tuple-element.193), channel_id=1, source_target_pairs={{0,2},{2,0},{13,15},{15,13},{1,4},{4,1},{3,6},{6,3},{5,8},{8,5},{7... | collective-permute-start | bytes 786440 | tf_op jit(solution)/shard_map/ppermute | solution.py:525
  115.7 10.0 %collective-permute-start.32 = (f32[4,128,128]{2,1,0:T(8,128)S(1)}, f32[4,128,128]{2,1,0:T(8,128)S(1)}, u32[]{:S(2)}, u32[]{:S(2)}) collective-permute-start(f32[4,128,128]{2,1,0:T(8,128)S(1)} %get-tuple-element.197), channel_id=1, source_target_pairs={{0,1},{1,0},{2,3},{3,2},{4,5},{5,4},{6,7},{7,6},{8,9},{9,8},{10,11... | collective-permute-start | bytes 786440 | tf_op jit(solution)/shard_map/ppermute | solution.py:526
  117.2 7.4 %collective-permute-start.31 = (f32[2,16,8,128]{3,2,1,0:T(8,128)S(1)}, f32[2,16,8,128]{3,2,1,0:T(8,128)S(1)}, u32[]{:S(2)}, u32[]{:S(2)}) collective-permute-start(f32[2,16,8,128]{3,2,1,0:T(8,128)S(1)} %get-tuple-element.194), channel_id=1, source_target_pairs={{0,8},{1,9},{2,10},{3,11},{4,12},{5,13},{6,14},{7,15},{8,0},{9,1},... | collective-permute-start | bytes 393224 | tf_op jit(solution)/shard_map/ppermute | solution.py:574
  126.4 10.2 %collective-permute-start.33 = (f32[4,128,128]{2,1,0:T(8,128)S(1)}, f32[4,128,128]{2,1,0:T(8,128)S(1)}, u32[]{:S(2)}, u32[]{:S(2)}) collective-permute-start(f32[4,128,128]{2,1,0:T(8,128)S(1)} %get-tuple-element.204), channel_id=1, source_target_pairs={{0,2},{2,0},{13,15},{15,13},{1,4},{4,1},{3,6},{6,3},{5,8},{8,5},{7... | collective-permute-start | bytes 786440 | tf_op jit(solution)/shard_map/ppermute | solution.py:525
  127.8 8.9 %collective-permute-start.35 = (f32[4,128,128]{2,1,0:T(8,128)S(1)}, f32[4,128,128]{2,1,0:T(8,128)S(1)}, u32[]{:S(2)}, u32[]{:S(2)}) collective-permute-start(f32[4,128,128]{2,1,0:T(8,128)S(1)} %get-tuple-element.208), channel_id=1, source_target_pairs={{0,1},{1,0},{2,3},{3,2},{4,5},{5,4},{6,7},{7,6},{8,9},{9,8},{10,11... | collective-permute-start | bytes 786440 | tf_op jit(solution)/shard_map/ppermute | solution.py:526
  128.0 8.7 %collective-permute-start.34 = (f32[2,16,8,128]{3,2,1,0:T(8,128)S(1)}, f32[2,16,8,128]{3,2,1,0:T(8,128)S(1)}, u32[]{:S(2)}, u32[]{:S(2)}) collective-permute-start(f32[2,16,8,128]{3,2,1,0:T(8,128)S(1)} %get-tuple-element.205), channel_id=1, source_target_pairs={{0,8},{1,9},{2,10},{3,11},{4,12},{5,13},{6,14},{7,15},{8,0},{9,1},... | collective-permute-start | bytes 393224 | tf_op jit(solution)/shard_map/ppermute | solution.py:574
  137.5 10.8 %collective-permute-start.36 = (f32[4,128,128]{2,1,0:T(8,128)S(1)}, f32[4,128,128]{2,1,0:T(8,128)S(1)}, u32[]{:S(2)}, u32[]{:S(2)}) collective-permute-start(f32[4,128,128]{2,1,0:T(8,128)S(1)} %get-tuple-element.215), channel_id=1, source_target_pairs={{0,2},{2,0},{13,15},{15,13},{1,4},{4,1},{3,6},{6,3},{5,8},{8,5},{7... | collective-permute-start | bytes 786440 | tf_op jit(solution)/shard_map/ppermute | solution.py:525
  138.6 9.7 %collective-permute-start.42 = (f32[4,128,128]{2,1,0:T(8,128)S(1)}, f32[4,128,128]{2,1,0:T(8,128)S(1)}, u32[]{:S(2)}, u32[]{:S(2)}) collective-permute-start(f32[4,128,128]{2,1,0:T(8,128)S(1)} %get-tuple-element.229), channel_id=1, source_target_pairs={{0,1},{1,0},{2,3},{3,2},{4,5},{5,4},{6,7},{7,6},{8,9},{9,8},{10,11... | collective-permute-start | bytes 786440 | tf_op jit(solution)/shard_map/ppermute | solution.py:526
  140.0 8.3 %collective-permute-start.37 = (f32[2,16,8,128]{3,2,1,0:T(8,128)S(1)}, f32[2,16,8,128]{3,2,1,0:T(8,128)S(1)}, u32[]{:S(2)}, u32[]{:S(2)}) collective-permute-start(f32[2,16,8,128]{3,2,1,0:T(8,128)S(1)} %get-tuple-element.216), channel_id=1, source_target_pairs={{0,12},{1,13},{2,14},{3,15},{4,8},{5,9},{6,10},{7,11},{8,4},{9,5},... | collective-permute-start | bytes 393224 | tf_op jit(solution)/shard_map/ppermute | solution.py:574
  151.0 0.8 copy-start.11
  151.7 0.8 copy-start.12
  152.5 50.4 %all-to-all-start = ((f32[16,16,8,128]{3,2,1,0:T(8,128)}), f32[16,16,8,128]{3,2,1,0:T(8,128)S(1)}, u32[]{:S(2)}, u32[]{:S(2)}) async-start(f32[16,16,8,128]{3,2,1,0:T(8,128)} %get-tuple-element.232), calls=%async_computation | async-start | bytes 2097152 | tf_op jit(solution)/shard_map/all_to_all | solution.py:583
  156.8 45.1 %collective-permute-start.43 = (f32[8,128,128]{2,1,0:T(8,128)}, f32[8,128,128]{2,1,0:T(8,128)S(1)}, u32[]{:S(2)}, u32[]{:S(2)}) collective-permute-start(f32[8,128,128]{2,1,0:T(8,128)} %copy-done.12), channel_id=1, source_target_pairs={{0,0},{1,2},{2,1},{3,3},{4,4},{5,6},{6,5},{7,7},{8,8},{9,10},{10,9... | collective-permute-start | bytes 1572872 | tf_op jit(solution)/shard_map/ppermute | solution.py:584
  160.2 41.8 %collective-permute-start.44 = (f32[8,128,128]{2,1,0:T(8,128)}, f32[8,128,128]{2,1,0:T(8,128)S(1)}, u32[]{:S(2)}, u32[]{:S(2)}) collective-permute-start(f32[8,128,128]{2,1,0:T(8,128)} %copy-done.11), channel_id=1, source_target_pairs={{2,0},{0,1},{3,2},{1,3},{6,4},{4,5},{7,6},{5,7},{10,8},{8,9},{11,1... | collective-permute-start | bytes 1572872 | tf_op jit(solution)/shard_map/ppermute | solution.py:585
  160.2 26.8 %collective-permute-start.38 = (f32[2,16,8,128]{3,2,1,0:T(8,128)S(1)}, f32[2,16,8,128]{3,2,1,0:T(8,128)S(1)}, u32[]{:S(2)}, u32[]{:S(2)}) collective-permute-start(f32[2,16,8,128]{3,2,1,0:T(8,128)S(1)} %get-tuple-element.223), channel_id=1, source_target_pairs={{0,12},{1,13},{2,14},{3,15},{4,8},{5,9},{6,10},{7,11},{8,4},{9,5},... | collective-permute-start | bytes 393224 | tf_op jit(solution)/shard_map/ppermute | solution.py:574
  187.2 2.7 %collective-permute-start.39 = (f32[4,16,8,128]{3,2,1,0:T(8,128)S(1)}, f32[4,16,8,128]{3,2,1,0:T(8,128)S(1)}, u32[]{:S(2)}, u32[]{:S(2)}) collective-permute-start(f32[4,16,8,128]{3,2,1,0:T(8,128)S(1)} %get-tuple-element.225), channel_id=1, source_target_pairs={{0,1},{1,0},{2,3},{3,2},{4,5},{5,4},{6,7},{7,6},{8,9},{9,8},{10,11... | collective-permute-start | bytes 786440 | tf_op jit(solution)/shard_map/ppermute | solution.py:580
  188.2 7.8 %collective-permute-start.40 = (f32[4,16,8,128]{3,2,1,0:T(8,128)S(1)}, f32[4,16,8,128]{3,2,1,0:T(8,128)S(1)}, u32[]{:S(2)}, u32[]{:S(2)}) collective-permute-start(f32[4,16,8,128]{3,2,1,0:T(8,128)S(1)} %get-tuple-element.226), channel_id=1, source_target_pairs={{0,2},{1,3},{2,0},{3,1},{4,6},{5,7},{6,4},{7,5},{8,10},{9,11},{10,... | collective-permute-start | bytes 786440 | tf_op jit(solution)/shard_map/ppermute | solution.py:580
  189.4 12.5 %collective-permute-start.41 = (f32[4,16,8,128]{3,2,1,0:T(8,128)S(1)}, f32[4,16,8,128]{3,2,1,0:T(8,128)S(1)}, u32[]{:S(2)}, u32[]{:S(2)}) collective-permute-start(f32[4,16,8,128]{3,2,1,0:T(8,128)S(1)} %get-tuple-element.227), channel_id=1, source_target_pairs={{0,3},{1,2},{2,1},{3,0},{4,7},{5,6},{6,5},{7,4},{8,11},{9,10},{10,... | collective-permute-start | bytes 786440 | tf_op jit(solution)/shard_map/ppermute | solution.py:580

commit v5 on v4

--- a/solution.py
+++ b/solution.py
@@ -23,6 +23,7 @@
 VMEM = pl.BlockSpec(memory_space=pltpu.VMEM)
 SMEM = pl.BlockSpec(memory_space=pltpu.SMEM)
 ANY = pl.BlockSpec(memory_space=pl.ANY)
+HBM = pl.BlockSpec(memory_space=pltpu.HBM)
 PARAMS = pltpu.CompilerParams(vmem_limit_bytes=24 * 1024 * 1024)
 
 
@@ -76,29 +77,37 @@
     return jnp.where(my_half() == 0, local, layers - 1 - local)
 
 
-def choose_kernel(here, there, first, second, sem):
-    def copies(a, b):
-        return pltpu.make_async_copy(a, first, sem.at[0]), pltpu.make_async_copy(b, second, sem.at[1])
-
-    def run(a, b):
-        one, two = copies(a, b)
-        one.start()
-        two.start()
-        one.wait()
-        two.wait()
-
+def in_order(run, here, there):
     pl.when(my_half() == 0)(lambda: run(here, there))
     pl.when(my_half() != 0)(lambda: run(there, here))
 
 
-def choose(here, there, spec):
+def copy_both(pairs, sem):
+    copies = [pltpu.make_async_copy(a, b, sem.at[i]) for i, (a, b) in enumerate(pairs)]
+    for copy in copies:
+        copy.start()
+    for copy in copies:
+        copy.wait()
+
+
+def choose_kernel(here, there, first, second, sem):
+    in_order(lambda a, b: copy_both(((a, first), (b, second)), sem), here, there)
+
+
+def choose_back_kernel(here, there, first, second, one, two, sem):
+    in_order(lambda a, b: copy_both(((a, one), (b, two)), sem), here, there)
+    copy_both(((one, first), (two, second)), sem)
+
+
+def choose(here, there, back=False):
     like = jax.ShapeDtypeStruct(here.shape, here.dtype)
+    staged = [pltpu.VMEM(here.shape, here.dtype)] * 2 if back else []
     return pl.pallas_call(
-        choose_kernel,
+        choose_back_kernel if back else choose_kernel,
         out_shape=(like, like),
-        in_specs=[ANY, ANY],
-        out_specs=(spec, spec),
-        scratch_shapes=[pltpu.SemaphoreType.DMA((2,))],
+        in_specs=[ANY if back else HBM] * 2,
+        out_specs=(ANY if back else VMEM,) * 2,
+        scratch_shapes=[*staged, pltpu.SemaphoreType.DMA((2,))],
         compiler_params=PARAMS,
         name="choose",
     )(here, there)
@@ -177,10 +186,13 @@
     high[...] = cur[layers : layers + REACH]
 
 
-def merge_rest_kernel(before_a, before_b, speed_a, speed_b, prev, speed):
+def merge_rest_kernel(shared, before_a, before_b, speed_a, speed_b, prev, speed):
+    flipped = (lax.rem(lax.axis_index("shot"), 2) == 1) & shared
+
     def run(j, q, which):
         prev[REACH + j] = (before_a, before_b)[which][q]
-        speed[j] = (speed_a, speed_b)[which][q] * (1.0 / SCALE)
+        ahead, other = (speed_a, speed_b) if which == 0 else (speed_b, speed_a)
+        speed[j] = jnp.where(flipped, other[q], ahead[q]) * (1.0 / SCALE)
 
     for_each_part(2 * before_a.shape[0], run)
 
@@ -316,53 +328,46 @@
     lax.fori_loop(0, snap.shape[0], one_strip, 0)
 
 
-def spread_kernel(snap, own, *parts):
-    groups = snap.shape[0] // 4
-    group = lax.axis_index("gz") // 4
-
-    def copy(target, first):
-        def one(i, carry):
-            target[i] = snap[first + i]
+def spread_kernel(snap, *outs):
+    mine = lax.rem(lax.axis_index("gz"), 4)
+    for which, out in enumerate(outs):
+
+        def one(group, carry):
+            out[group] = snap[4 * group + jnp.bitwise_xor(mine, which)]
             return carry
 
-        lax.fori_loop(0, target.shape[0], one, 0)
-
-    copy(own, 4 * group)
-    pieces = len(parts) // (groups - 1)
-    for i, part in enumerate(parts):
-        other = jnp.bitwise_xor(group, i // pieces + 1)
-        copy(part, 4 * other + (i % pieces) * (4 // pieces))
-
-
-def regather_kernel(own, *refs):
-    parts, outs = refs[:-4], refs[-4:]
-    groups = outs[0].shape[0]
+        lax.fori_loop(0, out.shape[0], one, 0)
+
+
+def regather_kernel(*refs):
+    held_by, (own, *parts) = refs[:4], refs[4:]
+    groups = held_by[0].shape[0]
     pieces = len(parts) // (groups - 1)
     size = 4 // pieces
     group = lax.axis_index("gz") // 4
     mine = lax.rem(lax.axis_index("gz"), 4)
-    for which, out in enumerate(outs):
-        strip = jnp.bitwise_xor(mine, which)
-        out[group] = own[strip]
+    for which, strips in enumerate(held_by):
+        source = jnp.bitwise_xor(mine, which)
+        own[source] = strips[group]
         for i, part in enumerate(parts):
             first = (i % pieces) * size
 
-            @pl.when((strip >= first) & (strip < first + size))
-            def _(i=i, part=part, first=first, strip=strip, out=out):
-                out[jnp.bitwise_xor(group, i // pieces + 1)] = part[strip - first]
-
-
-def collect_kernel(*refs):
-    out = refs[-1]
-    mine = lax.rem(lax.axis_index("gz"), 4)
-    for which in range(4):
-        source = jnp.bitwise_xor(mine, which)
-
-        def one(group, carry):
-            out[4 * group + source] = refs[which][group]
-            return carry
-
-        lax.fori_loop(0, refs[which].shape[0], one, 0)
+            @pl.when((source >= first) & (source < first + size))
+            def _(i=i, part=part, first=first, source=source, strips=strips):
+                part[source - first] = strips[jnp.bitwise_xor(group, i // pieces + 1)]
+
+
+def collect_kernel(own, *refs):
+    parts, out = refs[:-1], refs[-1]
+    pieces = len(parts) // (out.shape[0] // 4 - 1)
+    size = 4 // pieces
+    group = lax.axis_index("gz") // 4
+    for i in range(4):
+        out[4 * group + i] = own[i]
+    for i, part in enumerate(parts):
+        first = 4 * jnp.bitwise_xor(group, i // pieces + 1) + (i % pieces) * size
+        for j in range(size):
+            out[first + j] = part[j]
 
 
 def image_kernel(shifts, *refs):
@@ -479,15 +484,26 @@
     strips = held(count, layers, rows, nx)
     plane = ny * nx
 
-    now = regroup(*choose(source_now, receiver_now, VMEM))
-    before = regroup(*choose(source_before, receiver_before, VMEM))
-    speed_parts = regroup(speed_term, speed_term)
+    shots = lax.axis_size("shot")
+    shared = shots % 2 == 0
+    if shared:
+        both = [
+            (shot * count + a, shot * count + b)
+            for shot in range(shots)
+            for a, b in (first_pairs, second_pairs)[shot % 2]
+        ]
+        one = lax.ppermute(speed_term, ("shot", "gz"), both)
+        speed_parts = one, lax.ppermute(one, "shot", [(shot, shot ^ 1) for shot in range(shots)])
+    else:
+        speed_parts = regroup(speed_term, speed_term)
+    now = regroup(*choose(source_now, receiver_now))
+    before = regroup(*choose(source_before, receiver_before))
     late, early, shifts = prepare(saved_faces, face_steps, lag_offsets, nx)
     early = regroup(early, early)
     cur, low, high = merge(merge_now_kernel, (tall, slab, slab), *now)
     low = lax.ppermute(low, "gz", between)
     high = lax.ppermute(high, "gz", within)
-    prev, speed = merge(merge_rest_kernel, (tall, whole), *before, *speed_parts)
+    prev, speed = merge(functools.partial(merge_rest_kernel, shared), (tall, whole), *before, *speed_parts)
 
     groups = count // 4
     pieces = max(1, 8 // groups)
@@ -495,17 +511,6 @@
 
     snap = None
     for step in range(steps):
-        if step % SNAP_EVERY == 0 and step:
-            own_strips, *sent = merge(
-                spread_kernel,
-                (f32(4, layers, rows, nx), *[f32(4 // pieces, layers, rows, nx)] * (pieces * (groups - 1))),
-                snap,
-            )
-            waiting = [
-                (pieces_now, [(i, 4 * ((i // 4) ^ (j // pieces + 1)) + i % 4) for i in range(count)])
-                for j, pieces_now in enumerate(sent)
-            ]
-            snap = None
         if step == EARLY:
             face = merge(merge_faces_kernel, (whole,), *late)
         faces = tuple(face) if step >= EARLY else early
@@ -525,7 +530,19 @@
             low = lax.ppermute(low, "gz", between)
             high = lax.ppermute(high, "gz", within)
             low, *under_way = lax.optimization_barrier((low, *under_way))
-            arrived, under_way = arrived + under_way, []
+            if step == SNAP_EVERY:
+                own_strips, *sent = merge(
+                    regather_kernel,
+                    (f32(4, layers, rows, nx), *[f32(4 // pieces, layers, rows, nx)] * (pieces * (groups - 1))),
+                    *under_way,
+                )
+                waiting = [
+                    (part, [(i, 4 * ((i // 4) ^ (j // pieces + 1)) + i % 4) for i in range(count)])
+                    for j, part in enumerate(sent)
+                ]
+            else:
+                arrived += under_way
+            under_way = []
         else:
             new = prev
         operands = (snap_phase, across, along, speed, *faces, cur, new)
@@ -567,6 +584,14 @@
         if step == 0:
             late, new = lax.optimization_barrier((late, new))
             late = regroup(late, late)
+        if step == SNAP_EVERY - 1:
+            strip_parts = merge(spread_kernel, (f32(groups, layers, rows, nx),) * 4, snap)
+            under_way.append(strip_parts[0])
+            for which in (2, 3, 1):
+                payload, new = lax.optimization_barrier((strip_parts[which], new))
+                under_way.append(lax.ppermute(payload, "gz", [(i, i ^ which) for i in range(count)]))
+            under_way = [under_way[i] for i in (0, 3, 1, 2)]
+            snap = None
         left = steps - 1 - step
         now_many = -(-len(waiting) // left) if left else len(waiting)
         for payload, pairs in waiting[:now_many]:
@@ -575,15 +600,11 @@
         waiting = waiting[now_many:]
         prev, cur = cur, new
 
-    mine, *others = merge(regather_kernel, (f32(groups, layers, rows, nx),) * 4, own_strips, *arrived, *under_way)
-    others = [
-        lax.ppermute(other, "gz", [(i, i ^ (which + 1)) for i in range(count)]) for which, other in enumerate(others)
-    ]
-    (first,) = merge(collect_kernel, (f32(count, layers, rows, nx),), mine, *others)
+    (first,) = merge(collect_kernel, (f32(count, layers, rows, nx),), own_strips, *arrived, *under_way)
     second = lax.all_to_all(send, "gz", split_axis=0, concat_axis=0, tiled=True)
     back_a = lax.ppermute(out_a, "gz", first_pairs)
     back_b = lax.ppermute(out_b, "gz", back_pairs)
-    source_final, receiver_final = choose(back_a, back_b, ANY)
+    source_final, receiver_final = choose(back_a, back_b, back=True)
     image_out = images(shifts, (first, second), lag_offsets.shape[0])
     return (image_out, source_final, receiver_final)
 

time: 209 us -> 199 us (0.952)
  waiting for transfers between devices: 98.2 us -> 83.7 us
  local copies, waits for them, and re-layouts: 5.77 us -> 8.47 us
    ppermute x5 -> x4, waiting for transfers between devices: 11.6 us -> 0.01 us  [regroup(): lax.ppermute(b, 'gz', second_pairs)]
    ppermute x3 -> x5, waiting for transfers between devices: 11.9 us -> 5.14 us  [the longest x3 5.13 us: local(): lax.ppermute(payload, 'gz', [(i, i ^ which) for i in range(count)])]
    ppermute x5 -> x4, waiting for transfers between devices: 12.6 us -> 18.5 us  [regroup(): lax.ppermute(a, 'gz', first_pairs)]
    ppermute x5 -> x4, starting transfers between devices: 18.1 us -> 13.8 us  [regroup(): lax.ppermute(a, 'gz', first_pairs)]
    ppermute x3 -> x5, starting transfers between devices: 2.75 us -> 5.78 us  [the longest x1 3.71 us: local(): one = lax.ppermute(speed_term, ('shot', 'gz'), both)]
    unnamed x26 -> x38, local copies, waits for them, and re-layouts: 5.77 us -> 8.47 us
    ppermute x12, starting transfers between devices: 5.73 us -> 8 us  [local(): low = lax.ppermute(low, 'gz', between)]
  transfers between devices with their start and end apart: 46 -> 46, of which waited for: 19 -> 15; matrix products, arithmetic and copies ran while one was open for 0% -> 0% of each run, Pallas kernels for 10% -> 11%
where the time goes in v5:
time: 199 us; the launch traced here: 197 us
  waiting for transfers between devices  83.7 us (42%)
  starting transfers between devices  66.4 us (33%)
  Pallas kernels  37.2 us (19%)
  local copies, waits for them, and re-layouts  8.47 us (4%)
    ppermute x6, waiting for transfers between devices, local(): under_way.append(lax.ppermute(payload, 'gz', pairs))  49.6 us
    ppermute x12, starting transfers between devices, local(): high = lax.ppermute(high, 'gz', within)  25.8 us
    ppermute x4, waiting for transfers between devices, regroup(): lax.ppermute(a, 'gz', first_pairs)  18.5 us
    pallas_call x11, Pallas kernels, local(): inner(functools.partial(inner_kernel, step, wide, True), out_shape=(tall,...  14.4 us
    ppermute x4, starting transfers between devices, regroup(): lax.ppermute(a, 'gz', first_pairs)  13.8 us
    ppermute x12, waiting for transfers between devices, local(): low = lax.ppermute(low, 'gz', between)  10.5 us
    pallas_call x11, Pallas kernels, local(): border(across, along, low, high, traces, speed, *faces, cur, prev)  8.69 us
    unnamed x38, local copies, waits for them, and re-layouts  8.47 us
  transfers between devices with their start and end apart: 46, of which 15 were waited for; matrix products, arithmetic and copies ran while one was open for 0% of the time, Pallas kernels for 11%

profile of v5, /device:TPU:9, one launch (start us, length us, event | category | flops | bytes accessed | tf_op | source)
XLA Modules:
  0.0 197.3 jit_solution(17740316576473269401)
XLA Ops:
  0.6 3.7 %collective-permute-start.6 = (f32[8,128,128]{2,1,0:T(8,128)}, f32[8,128,128]{2,1,0:T(8,128)S(1)}, u32[]{:S(2)}, u32[]{:S(2)}) collective-permute-start(f32[8,128,128]{2,1,0:T(8,128)} %param.16), channel_id=1, source_target_pairs={{0,0},{1,2},{2,1},{3,3},{4,4},{5,6},{6,5},{7,7},{8,8},{9,10},{10,9... | collective-permute-start | bytes 1572872 | tf_op jit(solution)/shard_map/ppermute | solution.py:495
  4.4 1.0 copy-done.3
  5.4 1.0 copy-done.4
  6.5 2.1 %collective-permute-start = (f32[8,128,128]{2,1,0:T(8,128)S(1)}, f32[8,128,128]{2,1,0:T(8,128)S(1)}, u32[]{:S(2)}, u32[]{:S(2)}) collective-permute-start(f32[8,128,128]{2,1,0:T(8,128)S(1)} %get-tuple-element.132), channel_id=1, source_target_pairs={{0,0},{1,2},{2,1},{3,3},{4,4},{5,6},{6,5},{7,7},{8,8},{9,10},{10,9... | collective-permute-start | bytes 1572872 | tf_op jit(solution)/shard_map/ppermute | solution.py:478
  8.6 1.0 copy-done.5
  9.7 1.0 copy-done.6
  10.8 3.6 %collective-permute-start.4 = (f32[8,128,128]{2,1,0:T(8,128)S(1)}, f32[8,128,128]{2,1,0:T(8,128)S(1)}, u32[]{:S(2)}, u32[]{:S(2)}) collective-permute-start(f32[8,128,128]{2,1,0:T(8,128)S(1)} %get-tuple-element.136), channel_id=1, source_target_pairs={{0,0},{1,2},{2,1},{3,3},{4,4},{5,6},{6,5},{7,7},{8,8},{9,10},{10,9... | collective-permute-start | bytes 1572872 | tf_op jit(solution)/shard_map/ppermute | solution.py:478
  14.7 8.6 %collective-permute-done.now_a = f32[8,128,128]{2,1,0:T(8,128)S(1)} collective-permute-done((f32[8,128,128]{2,1,0:T(8,128)S(1)}, f32[8,128,128]{2,1,0:T(8,128)S(1)}, u32[]{:S(2)}, u32[]{:S(2)}) %collective-permute-start) | collective-permute-done | bytes 524320 | tf_op jit(solution)/shard_map/ppermute | solution.py:478
  23.7 1.0 collective-permute-start.2
  24.7 1.8 prepare.1
  26.5 7.3 %collective-permute-done.4.before_a = f32[8,128,128]{2,1,0:T(8,128)S(1)} collective-permute-done((f32[8,128,128]{2,1,0:T(8,128)S(1)}, f32[8,128,128]{2,1,0:T(8,128)S(1)}, u32[]{:S(2)}, u32[]{:S(2)}) %collective-permute-start.4) | collective-permute-done | bytes 524320 | tf_op jit(solution)/shard_map/ppermute | solution.py:478
  33.9 3.6 %collective-permute-start.8 = (f32[2,128,128]{2,1,0:T(8,128)S(1)}, f32[2,128,128]{2,1,0:T(8,128)S(1)}, u32[]{:S(2)}, u32[]{:S(2)}) collective-permute-start(f32[2,128,128]{2,1,0:T(8,128)S(1)} %get-tuple-element.139), channel_id=1, source_target_pairs={{0,0},{1,2},{2,1},{3,3},{4,4},{5,6},{6,5},{7,7},{8,8},{9,10},{10,9... | collective-permute-start | bytes 393224 | tf_op jit(solution)/shard_map/ppermute | solution.py:478
  38.1 2.1 %collective-permute-done.8.rest_0_ = f32[2,128,128]{2,1,0:T(8,128)S(1)} collective-permute-done((f32[2,128,128]{2,1,0:T(8,128)S(1)}, f32[2,128,128]{2,1,0:T(8,128)S(1)}, u32[]{:S(2)}, u32[]{:S(2)}) %collective-permute-start.8) | collective-permute-done | bytes 131104 | tf_op jit(solution)/shard_map/ppermute | solution.py:478
  40.2 0.8 border.11
  41.7 1.3 inner.12
  43.0 3.9 %collective-permute-done.10.low = f32[4,128,128]{2,1,0:T(8,128)S(1)} collective-permute-done((f32[4,128,128]{2,1,0:T(8,128)S(1)}, f32[4,128,128]{2,1,0:T(8,128)S(1)}, u32[]{:S(2)}, u32[]{:S(2)}) %collective-permute-start.10) | collective-permute-done | bytes 262176 | tf_op jit(solution)/shard_map/ppermute | solution.py:530
  46.9 0.8 border.12
  47.8 0.8 collective-permute-start.13
  48.6 4.5 %collective-permute-start.18 = (f32[8,128,128]{2,1,0:T(8,128)S(1)}, f32[8,128,128]{2,1,0:T(8,128)S(1)}, u32[]{:S(2)}, u32[]{:S(2)}) collective-permute-start(f32[8,128,128]{2,1,0:T(8,128)S(1)} %get-tuple-element.163), channel_id=1, source_target_pairs={{0,0},{1,2},{2,1},{3,3},{4,4},{5,6},{6,5},{7,7},{8,8},{9,10},{10,9... | collective-permute-start | bytes 1572872 | tf_op jit(solution)/shard_map/ppermute | solution.py:478
  53.1 1.3 inner.13
  54.4 0.8 border.13
  55.3 1.2 collective-permute-start.14
  56.5 1.3 inner.14
  57.7 3.4 %collective-permute-done.14.low = f32[4,128,128]{2,1,0:T(8,128)S(1)} collective-permute-done((f32[4,128,128]{2,1,0:T(8,128)S(1)}, f32[4,128,128]{2,1,0:T(8,128)S(1)}, u32[]{:S(2)}, u32[]{:S(2)}) %collective-permute-start.14) | collective-permute-done | bytes 262176 | tf_op jit(solution)/shard_map/ppermute | solution.py:530
  61.1 0.8 border.14
  61.9 1.2 collective-permute-start.16
  63.9 1.3 inner.15
  65.2 2.6 %collective-permute-done.16.low = f32[4,128,128]{2,1,0:T(8,128)S(1)} collective-permute-done((f32[4,128,128]{2,1,0:T(8,128)S(1)}, f32[4,128,128]{2,1,0:T(8,128)S(1)}, u32[]{:S(2)}, u32[]{:S(2)}) %collective-permute-start.16) | collective-permute-done | bytes 262176 | tf_op jit(solution)/shard_map/ppermute | solution.py:530
  68.6 1.2 collective-permute-start.20
  69.8 5.1 %collective-permute-start.21 = (f32[4,128,128]{2,1,0:T(8,128)S(1)}, f32[4,128,128]{2,1,0:T(8,128)S(1)}, u32[]{:S(2)}, u32[]{:S(2)}) collective-permute-start(f32[4,128,128]{2,1,0:T(8,128)S(1)} %get-tuple-element.169), channel_id=1, source_target_pairs={{0,1},{1,0},{2,3},{3,2},{4,5},{5,4},{6,7},{7,6},{8,9},{9,8},{10,11... | collective-permute-start | bytes 786440 | tf_op jit(solution)/shard_map/ppermute | solution.py:531
  74.9 1.4 inner.16
  77.2 4.7 %collective-permute-start.23 = (f32[4,128,128]{2,1,0:T(8,128)S(1)}, f32[4,128,128]{2,1,0:T(8,128)S(1)}, u32[]{:S(2)}, u32[]{:S(2)}) collective-permute-start(f32[4,128,128]{2,1,0:T(8,128)S(1)} %get-tuple-element.175), channel_id=1, source_target_pairs={{0,1},{1,0},{2,3},{3,2},{4,5},{5,4},{6,7},{7,6},{8,9},{9,8},{10,11... | collective-permute-start | bytes 786440 | tf_op jit(solution)/shard_map/ppermute | solution.py:531
  81.8 1.4 inner.17
  83.7 1.7 collective-permute-start.26
  86.2 4.9 %collective-permute-start.28 = (f32[4,128,128]{2,1,0:T(8,128)S(1)}, f32[4,128,128]{2,1,0:T(8,128)S(1)}, u32[]{:S(2)}, u32[]{:S(2)}) collective-permute-start(f32[4,128,128]{2,1,0:T(8,128)S(1)} %get-tuple-element.198), channel_id=1, source_target_pairs={{0,1},{1,0},{2,3},{3,2},{4,5},{5,4},{6,7},{7,6},{8,9},{9,8},{10,11... | collective-permute-start | bytes 786440 | tf_op jit(solution)/shard_map/ppermute | solution.py:531
  91.2 1.3 inner.18
  92.5 5.1 %collective-permute-done.26.refs_2_ = f32[4,16,8,128]{3,2,1,0:T(8,128)S(1)} collective-permute-done((f32[4,16,8,128]{3,2,1,0:T(8,128)S(1)}, f32[4,16,8,128]{3,2,1,0:T(8,128)S(1)}, u32[]{:S(2)}, u32[]{:S(2)}) %collective-permute-start.26) | collective-permute-done | bytes 262176 | tf_op jit(solution)/shard_map/ppermute | solution.py:592
  98.6 4.9 %collective-permute-start.32 = (f32[4,128,128]{2,1,0:T(8,128)S(1)}, f32[4,128,128]{2,1,0:T(8,128)S(1)}, u32[]{:S(2)}, u32[]{:S(2)}) collective-permute-start(f32[4,128,128]{2,1,0:T(8,128)S(1)} %get-tuple-element.212), channel_id=1, source_target_pairs={{0,1},{1,0},{2,3},{3,2},{4,5},{5,4},{6,7},{7,6},{8,9},{9,8},{10,11... | collective-permute-start | bytes 786440 | tf_op jit(solution)/shard_map/ppermute | solution.py:531
  103.5 4.3 %collective-permute-start.31 = (f32[2,16,8,128]{3,2,1,0:T(8,128)S(1)}, f32[2,16,8,128]{3,2,1,0:T(8,128)S(1)}, u32[]{:S(2)}, u32[]{:S(2)}) collective-permute-start(f32[2,16,8,128]{3,2,1,0:T(8,128)S(1)} %get-tuple-element.208), channel_id=1, source_target_pairs={{0,4},{1,5},{2,6},{3,7},{4,0},{5,1},{6,2},{7,3},{8,12},{9,13},{10,... | collective-permute-start | bytes 393224 | tf_op jit(solution)/shard_map/ppermute | solution.py:599
  107.8 1.3 inner.19
  109.1 2.6 %collective-permute-done.31.refs_1_ = f32[2,16,8,128]{3,2,1,0:T(8,128)S(1)} collective-permute-done((f32[2,16,8,128]{3,2,1,0:T(8,128)S(1)}, f32[2,16,8,128]{3,2,1,0:T(8,128)S(1)}, u32[]{:S(2)}, u32[]{:S(2)}) %collective-permute-start.31) | collective-permute-done | bytes 131104 | tf_op jit(solution)/shard_map/ppermute | solution.py:599
  111.7 2.8 %collective-permute-done.30.refs_0_ = f32[2,16,8,128]{3,2,1,0:T(8,128)S(1)} collective-permute-done((f32[2,16,8,128]{3,2,1,0:T(8,128)S(1)}, f32[2,16,8,128]{3,2,1,0:T(8,128)S(1)}, u32[]{:S(2)}, u32[]{:S(2)}) %collective-permute-start.30) | collective-permute-done | bytes 131104 | tf_op jit(solution)/shard_map/ppermute | solution.py:599
  115.4 1.6 collective-permute-start.35
  116.9 1.4 inner.20
  118.4 6.0 %collective-permute-done.34.refs_2_ = f32[2,16,8,128]{3,2,1,0:T(8,128)S(1)} collective-permute-done((f32[2,16,8,128]{3,2,1,0:T(8,128)S(1)}, f32[2,16,8,128]{3,2,1,0:T(8,128)S(1)}, u32[]{:S(2)}, u32[]{:S(2)}) %collective-permute-start.34) | collective-permute-done | bytes 131104 | tf_op jit(solution)/shard_map/ppermute | solution.py:599
  125.6 1.9 collective-permute-start.36
  127.5 1.2 collective-permute-start.38
  128.7 1.3 inner.21
  130.0 6.4 %collective-permute-done.37.refs_3_ = f32[2,16,8,128]{3,2,1,0:T(8,128)S(1)} collective-permute-done((f32[2,16,8,128]{3,2,1,0:T(8,128)S(1)}, f32[2,16,8,128]{3,2,1,0:T(8,128)S(1)}, u32[]{:S(2)}, u32[]{:S(2)}) %collective-permute-start.37) | collective-permute-done | bytes 131104 | tf_op jit(solution)/shard_map/ppermute | solution.py:599
  137.2 1.1 collective-permute-start.39
  138.3 2.0 collective-permute-start.42
  140.3 1.3 inner.22
  142.3 6.3 %collective-permute-done.40.refs_4_ = f32[2,16,8,128]{3,2,1,0:T(8,128)S(1)} collective-permute-done((f32[2,16,8,128]{3,2,1,0:T(8,128)S(1)}, f32[2,16,8,128]{3,2,1,0:T(8,128)S(1)}, u32[]{:S(2)}, u32[]{:S(2)}) %collective-permute-start.40) | collective-permute-done | bytes 131104 | tf_op jit(solution)/shard_map/ppermute | solution.py:599
  149.3 3.0 %last.1 = (f32[24,128,128]{2,1,0:T(8,128)S(1)}, f32[24,128,128]{2,1,0:T(8,128)S(1)}, f32[16,16,8,128]{3,2,1,0:T(8,128)S(1)}, f32[8,128,128]{2,1,0:T(8,128)}, f32...) custom-call(s32[2]{0:T(128)S(1)} %copy-done.16, ...), custom_call_target="tpu_custom_call", output_to_operand_aliasing={{0}: (8, {}), {1}: (9, {}), {2}: (10, {})} | custom-call | tf_op jit(solution)/shard_map/last/pallas_call | solution.py:583
  152.3 4.1 %all-to-all-start = ((f32[16,16,8,128]{3,2,1,0:T(8,128)}), f32[16,16,8,128]{3,2,1,0:T(8,128)S(1)}, u32[]{:S(2)}, u32[]{:S(2)}) async-start(f32[16,16,8,128]{3,2,1,0:T(8,128)} %get-tuple-element.254), calls=%async_computation | async-start | bytes 2097152 | tf_op jit(solution)/shard_map/all_to_all | solution.py:604
  156.4 3.4 %collective-permute-start.43 = (f32[8,128,128]{2,1,0:T(8,128)}, f32[8,128,128]{2,1,0:T(8,128)S(1)}, u32[]{:S(2)}, u32[]{:S(2)}) collective-permute-start(f32[8,128,128]{2,1,0:T(8,128)} %get-tuple-element.255), channel_id=1, source_target_pairs={{0,0},{1,2},{2,1},{3,3},{4,4},{5,6},{6,5},{7,7},{8,8},{9,10},{10,9... | collective-permute-start | bytes 1572872 | tf_op jit(solution)/shard_map/ppermute | solution.py:605
  159.8 1.2 collective-permute-start.41
  161.1 25.5 %collective-permute-done.41.refs_5_ = f32[2,16,8,128]{3,2,1,0:T(8,128)S(1)} collective-permute-done((f32[2,16,8,128]{3,2,1,0:T(8,128)S(1)}, f32[2,16,8,128]{3,2,1,0:T(8,128)S(1)}, u32[]{:S(2)}, u32[]{:S(2)}) %collective-permute-start.41) | collective-permute-done | bytes 131104 | tf_op jit(solution)/shard_map/ppermute | solution.py:599
  186.6 0.9 copy-done.9
  187.5 0.9 copy-done.11
  188.4 0.9 copy-done.13
  189.3 0.9 copy-done.15
  190.3 1.1 choose.5
  191.4 5.7 %images.1 = bf16[8,128,8,128]{3,2,1,0:T(8,128)(2,1)} custom-call(bf16[2,256,1024]{2,1,0:T(8,128)(2,1)S(1)} %get-tuple-element.131.shifts, f32[16,16,8,128]{3,2,1,0:T(8,128)S(1)} %shard_map.144.refs_0_, f32[16,16,8,128]{3,2,1,0:T(8,128)S(1)} %all-to-all-done.refs_1_), custom_call_target="tpu_custom_call" | custom-call | tf_op jit(solution)/shard_map/images/pallas_call | solution.py:438
  (101 shorter events, 11.2 us)
Async XLA Ops:
  0.6 13.9 %collective-permute-start.6 = (f32[8,128,128]{2,1,0:T(8,128)}, f32[8,128,128]{2,1,0:T(8,128)S(1)}, u32[]{:S(2)}, u32[]{:S(2)}) collective-permute-start(f32[8,128,128]{2,1,0:T(8,128)} %param.16), channel_id=1, source_target_pairs={{0,0},{1,2},{2,1},{3,3},{4,4},{5,6},{6,5},{7,7},{8,8},{9,10},{10,9... | collective-permute-start | bytes 1572872 | tf_op jit(solution)/shard_map/ppermute | solution.py:495
  4.3 1.0 copy-start.3
  5.4 1.0 copy-start.4
  6.4 18.3 %copy-start.7 = (f32[12,8,8,128]{3,2,1,0:T(8,128)S(1)}, f32[12,8,8,128]{3,2,1,0:T(8,128)}, u32[]{:S(2)}) copy-start(f32[12,8,8,128]{3,2,1,0:T(8,128)} %param.17) | copy-start | bytes 1179652
  6.4 18.3 %copy-start.17 = (s32[12]{0:T(128)S(1)}, s32[12]{0:T(128)}, u32[]{:S(2)}) copy-start(s32[12]{0:T(128)} %face_steps.1) | copy-start | bytes 148
  6.4 18.3 %copy-start.18 = (s32[8]{0:T(128)S(1)}, s32[8]{0:T(128)}, u32[]{:S(2)}) copy-start(s32[8]{0:T(128)} %lags.1) | copy-start | bytes 100
  6.5 16.8 %collective-permute-start = (f32[8,128,128]{2,1,0:T(8,128)S(1)}, f32[8,128,128]{2,1,0:T(8,128)S(1)}, u32[]{:S(2)}, u32[]{:S(2)}) collective-permute-start(f32[8,128,128]{2,1,0:T(8,128)S(1)} %get-tuple-element.132), channel_id=1, source_target_pairs={{0,0},{1,2},{2,1},{3,3},{4,4},{5,6},{6,5},{7,7},{8,8},{9,10},{10,9... | collective-permute-start | bytes 1572872 | tf_op jit(solution)/shard_map/ppermute | solution.py:478
  8.6 14.7 %collective-permute-start.1 = (f32[8,128,128]{2,1,0:T(8,128)S(1)}, f32[8,128,128]{2,1,0:T(8,128)S(1)}, u32[]{:S(2)}, u32[]{:S(2)}) collective-permute-start(f32[8,128,128]{2,1,0:T(8,128)S(1)} %get-tuple-element.133), channel_id=1, source_target_pairs={{0,2},{1,0},{2,3},{3,1},{4,6},{5,4},{6,7},{7,5},{8,10},{9,8},{10,1... | collective-permute-start | bytes 1572872 | tf_op jit(solution)/shard_map/ppermute | solution.py:478
  8.6 1.0 copy-start.5
  9.7 1.0 copy-start.6
  10.8 23.1 %collective-permute-start.4 = (f32[8,128,128]{2,1,0:T(8,128)S(1)}, f32[8,128,128]{2,1,0:T(8,128)S(1)}, u32[]{:S(2)}, u32[]{:S(2)}) collective-permute-start(f32[8,128,128]{2,1,0:T(8,128)S(1)} %get-tuple-element.136), channel_id=1, source_target_pairs={{0,0},{1,2},{2,1},{3,3},{4,4},{5,6},{6,5},{7,7},{8,8},{9,10},{10,9... | collective-permute-start | bytes 1572872 | tf_op jit(solution)/shard_map/ppermute | solution.py:478
  14.5 25.7 %copy-start = (bf16[12,128,128]{2,1,0:T(8,128)(2,1)S(1)}, bf16[12,128,128]{2,1,0:T(8,128)(2,1)}, u32[]{:S(2)}) copy-start(bf16[12,128,128]{2,1,0:T(8,128)(2,1)} %traces.23) | copy-start | bytes 1179652
  14.5 25.7 %copy-start.1 = (bf16[128,256]{1,0:T(8,128)(2,1)S(1)}, bf16[128,256]{1,0:T(8,128)(2,1)}, u32[]{:S(2)}) copy-start(bf16[128,256]{1,0:T(8,128)(2,1)} %constant.5.clone.along) | copy-start | bytes 196612
  14.5 25.7 %copy-start.2 = (bf16[256,128]{1,0:T(8,128)(2,1)S(1)}, bf16[256,128]{1,0:T(8,128)(2,1)}, u32[]{:S(2)}) copy-start(bf16[256,128]{1,0:T(8,128)(2,1)} %constant.4.clone.across) | copy-start | bytes 196612
  14.5 19.4 %collective-permute-start.5 = (f32[8,128,128]{2,1,0:T(8,128)S(1)}, f32[8,128,128]{2,1,0:T(8,128)S(1)}, u32[]{:S(2)}, u32[]{:S(2)}) collective-permute-start(f32[8,128,128]{2,1,0:T(8,128)S(1)} %get-tuple-element.137), channel_id=1, source_target_pairs={{0,2},{1,0},{2,3},{3,1},{4,6},{5,4},{6,7},{7,5},{8,10},{9,8},{10,1... | collective-permute-start | bytes 1572872 | tf_op jit(solution)/shard_map/ppermute | solution.py:478
  14.5 23.0 %collective-permute-start.7 = (f32[8,128,128]{2,1,0:T(8,128)S(1)}, f32[8,128,128]{2,1,0:T(8,128)S(1)}, u32[]{:S(2)}, u32[]{:S(2)}) collective-permute-start(f32[8,128,128]{2,1,0:T(8,128)S(1)} %collective-permute-done.6.speed_a), channel_id=1, source_target_pairs={{0,16},{16,0},{1,17},{17,1},{2,18},{18,2},{3,19},{19,3},{4,20},{20... | collective-permute-start | bytes 1572872 | tf_op jit(solution)/shard_map/ppermute | solution.py:496
  23.7 16.4 %collective-permute-start.2 = (f32[4,128,128]{2,1,0:T(8,128)S(1)}, f32[4,128,128]{2,1,0:T(8,128)S(1)}, u32[]{:S(2)}, u32[]{:S(2)}) collective-permute-start(f32[4,128,128]{2,1,0:T(8,128)S(1)} %get-tuple-element.134), channel_id=1, source_target_pairs={{0,2},{2,0},{13,15},{15,13},{1,4},{4,1},{3,6},{6,3},{5,8},{8,5},{7... | collective-permute-start | bytes 786440 | tf_op jit(solution)/shard_map/ppermute | solution.py:504
  24.7 15.5 %collective-permute-start.3 = (f32[4,128,128]{2,1,0:T(8,128)S(1)}, f32[4,128,128]{2,1,0:T(8,128)S(1)}, u32[]{:S(2)}, u32[]{:S(2)}) collective-permute-start(f32[4,128,128]{2,1,0:T(8,128)S(1)} %get-tuple-element.135), channel_id=1, source_target_pairs={{0,1},{1,0},{2,3},{3,2},{4,5},{5,4},{6,7},{7,6},{8,9},{9,8},{10,11... | collective-permute-start | bytes 786440 | tf_op jit(solution)/shard_map/ppermute | solution.py:505
  33.9 4.2 %collective-permute-start.9 = (f32[2,128,128]{2,1,0:T(8,128)S(1)}, f32[2,128,128]{2,1,0:T(8,128)S(1)}, u32[]{:S(2)}, u32[]{:S(2)}) collective-permute-start(f32[2,128,128]{2,1,0:T(8,128)S(1)} %get-tuple-element.139), channel_id=1, source_target_pairs={{0,2},{1,0},{2,3},{3,1},{4,6},{5,4},{6,7},{7,5},{8,10},{9,8},{10,1... | collective-permute-start | bytes 393224 | tf_op jit(solution)/shard_map/ppermute | solution.py:478
  33.9 6.3 %collective-permute-start.8 = (f32[2,128,128]{2,1,0:T(8,128)S(1)}, f32[2,128,128]{2,1,0:T(8,128)S(1)}, u32[]{:S(2)}, u32[]{:S(2)}) collective-permute-start(f32[2,128,128]{2,1,0:T(8,128)S(1)} %get-tuple-element.139), channel_id=1, source_target_pairs={{0,0},{1,2},{2,1},{3,3},{4,4},{5,6},{6,5},{7,7},{8,8},{9,10},{10,9... | collective-permute-start | bytes 393224 | tf_op jit(solution)/shard_map/ppermute | solution.py:478
  40.2 1.5 copy-start.16
  41.0 5.9 %collective-permute-start.10 = (f32[4,128,128]{2,1,0:T(8,128)S(1)}, f32[4,128,128]{2,1,0:T(8,128)S(1)}, u32[]{:S(2)}, u32[]{:S(2)}) collective-permute-start(f32[4,128,128]{2,1,0:T(8,128)S(1)} %get-tuple-element.142), channel_id=1, source_target_pairs={{0,2},{2,0},{13,15},{15,13},{1,4},{4,1},{3,6},{6,3},{5,8},{8,5},{7... | collective-permute-start | bytes 786440 | tf_op jit(solution)/shard_map/ppermute | solution.py:530
  41.1 5.8 %collective-permute-start.11 = (f32[4,128,128]{2,1,0:T(8,128)S(1)}, f32[4,128,128]{2,1,0:T(8,128)S(1)}, u32[]{:S(2)}, u32[]{:S(2)}) collective-permute-start(f32[4,128,128]{2,1,0:T(8,128)S(1)} %get-tuple-element.143), channel_id=1, source_target_pairs={{0,1},{1,0},{2,3},{3,2},{4,5},{5,4},{6,7},{7,6},{8,9},{9,8},{10,11... | collective-permute-start | bytes 786440 | tf_op jit(solution)/shard_map/ppermute | solution.py:531
  47.7 6.7 %collective-permute-start.12 = (f32[4,128,128]{2,1,0:T(8,128)S(1)}, f32[4,128,128]{2,1,0:T(8,128)S(1)}, u32[]{:S(2)}, u32[]{:S(2)}) collective-permute-start(f32[4,128,128]{2,1,0:T(8,128)S(1)} %get-tuple-element.149), channel_id=1, source_target_pairs={{0,2},{2,0},{13,15},{15,13},{1,4},{4,1},{3,6},{6,3},{5,8},{8,5},{7... | collective-permute-start | bytes 786440 | tf_op jit(solution)/shard_map/ppermute | solution.py:530
  47.8 6.6 %collective-permute-start.13 = (f32[4,128,128]{2,1,0:T(8,128)S(1)}, f32[4,128,128]{2,1,0:T(8,128)S(1)}, u32[]{:S(2)}, u32[]{:S(2)}) collective-permute-start(f32[4,128,128]{2,1,0:T(8,128)S(1)} %get-tuple-element.150), channel_id=1, source_target_pairs={{0,1},{1,0},{2,3},{3,2},{4,5},{5,4},{6,7},{7,6},{8,9},{9,8},{10,11... | collective-permute-start | bytes 786440 | tf_op jit(solution)/shard_map/ppermute | solution.py:531
  48.6 14.5 %collective-permute-start.19 = (f32[8,128,128]{2,1,0:T(8,128)S(1)}, f32[8,128,128]{2,1,0:T(8,128)S(1)}, u32[]{:S(2)}, u32[]{:S(2)}) collective-permute-start(f32[8,128,128]{2,1,0:T(8,128)S(1)} %get-tuple-element.163), channel_id=1, source_target_pairs={{0,2},{1,0},{2,3},{3,1},{4,6},{5,4},{6,7},{7,5},{8,10},{9,8},{10,1... | collective-permute-start | bytes 1572872 | tf_op jit(solution)/shard_map/ppermute | solution.py:478
  48.6 14.9 %collective-permute-start.18 = (f32[8,128,128]{2,1,0:T(8,128)S(1)}, f32[8,128,128]{2,1,0:T(8,128)S(1)}, u32[]{:S(2)}, u32[]{:S(2)}) collective-permute-start(f32[8,128,128]{2,1,0:T(8,128)S(1)} %get-tuple-element.163), channel_id=1, source_target_pairs={{0,0},{1,2},{2,1},{3,3},{4,4},{5,6},{6,5},{7,7},{8,8},{9,10},{10,9... | collective-permute-start | bytes 1572872 | tf_op jit(solution)/shard_map/ppermute | solution.py:478
  55.3 5.9 %collective-permute-start.14 = (f32[4,128,128]{2,1,0:T(8,128)S(1)}, f32[4,128,128]{2,1,0:T(8,128)S(1)}, u32[]{:S(2)}, u32[]{:S(2)}) collective-permute-start(f32[4,128,128]{2,1,0:T(8,128)S(1)} %get-tuple-element.155), channel_id=1, source_target_pairs={{0,2},{2,0},{13,15},{15,13},{1,4},{4,1},{3,6},{6,3},{5,8},{8,5},{7... | collective-permute-start | bytes 786440 | tf_op jit(solution)/shard_map/ppermute | solution.py:530
  56.5 4.7 %collective-permute-start.15 = (f32[4,128,128]{2,1,0:T(8,128)S(1)}, f32[4,128,128]{2,1,0:T(8,128)S(1)}, u32[]{:S(2)}, u32[]{:S(2)}) collective-permute-start(f32[4,128,128]{2,1,0:T(8,128)S(1)} %get-tuple-element.156), channel_id=1, source_target_pairs={{0,1},{1,0},{2,3},{3,2},{4,5},{5,4},{6,7},{7,6},{8,9},{9,8},{10,11... | collective-permute-start | bytes 786440 | tf_op jit(solution)/shard_map/ppermute | solution.py:531
  61.9 5.9 %collective-permute-start.16 = (f32[4,128,128]{2,1,0:T(8,128)S(1)}, f32[4,128,128]{2,1,0:T(8,128)S(1)}, u32[]{:S(2)}, u32[]{:S(2)}) collective-permute-start(f32[4,128,128]{2,1,0:T(8,128)S(1)} %get-tuple-element.161), channel_id=1, source_target_pairs={{0,2},{2,0},{13,15},{15,13},{1,4},{4,1},{3,6},{6,3},{5,8},{8,5},{7... | collective-permute-start | bytes 786440 | tf_op jit(solution)/shard_map/ppermute | solution.py:530
  63.1 4.7 %collective-permute-start.17 = (f32[4,128,128]{2,1,0:T(8,128)S(1)}, f32[4,128,128]{2,1,0:T(8,128)S(1)}, u32[]{:S(2)}, u32[]{:S(2)}) collective-permute-start(f32[4,128,128]{2,1,0:T(8,128)S(1)} %get-tuple-element.162), channel_id=1, source_target_pairs={{0,1},{1,0},{2,3},{3,2},{4,5},{5,4},{6,7},{7,6},{8,9},{9,8},{10,11... | collective-permute-start | bytes 786440 | tf_op jit(solution)/shard_map/ppermute | solution.py:531
  68.6 7.7 %collective-permute-start.20 = (f32[4,128,128]{2,1,0:T(8,128)S(1)}, f32[4,128,128]{2,1,0:T(8,128)S(1)}, u32[]{:S(2)}, u32[]{:S(2)}) collective-permute-start(f32[4,128,128]{2,1,0:T(8,128)S(1)} %get-tuple-element.168), channel_id=1, source_target_pairs={{0,2},{2,0},{13,15},{15,13},{1,4},{4,1},{3,6},{6,3},{5,8},{8,5},{7... | collective-permute-start | bytes 786440 | tf_op jit(solution)/shard_map/ppermute | solution.py:530
  69.8 6.5 %collective-permute-start.21 = (f32[4,128,128]{2,1,0:T(8,128)S(1)}, f32[4,128,128]{2,1,0:T(8,128)S(1)}, u32[]{:S(2)}, u32[]{:S(2)}) collective-permute-start(f32[4,128,128]{2,1,0:T(8,128)S(1)} %get-tuple-element.169), channel_id=1, source_target_pairs={{0,1},{1,0},{2,3},{3,2},{4,5},{5,4},{6,7},{7,6},{8,9},{9,8},{10,11... | collective-permute-start | bytes 786440 | tf_op jit(solution)/shard_map/ppermute | solution.py:531
  77.1 8.2 %collective-permute-start.22 = (f32[4,128,128]{2,1,0:T(8,128)S(1)}, f32[4,128,128]{2,1,0:T(8,128)S(1)}, u32[]{:S(2)}, u32[]{:S(2)}) collective-permute-start(f32[4,128,128]{2,1,0:T(8,128)S(1)} %get-tuple-element.174), channel_id=1, source_target_pairs={{0,2},{2,0},{13,15},{15,13},{1,4},{4,1},{3,6},{6,3},{5,8},{8,5},{7... | collective-permute-start | bytes 786440 | tf_op jit(solution)/shard_map/ppermute | solution.py:530
  77.2 8.2 %collective-permute-start.23 = (f32[4,128,128]{2,1,0:T(8,128)S(1)}, f32[4,128,128]{2,1,0:T(8,128)S(1)}, u32[]{:S(2)}, u32[]{:S(2)}) collective-permute-start(f32[4,128,128]{2,1,0:T(8,128)S(1)} %get-tuple-element.175), channel_id=1, source_target_pairs={{0,1},{1,0},{2,3},{3,2},{4,5},{5,4},{6,7},{7,6},{8,9},{9,8},{10,11... | collective-permute-start | bytes 786440 | tf_op jit(solution)/shard_map/ppermute | solution.py:531
  83.4 9.0 %collective-permute-start.25 = (f32[4,16,8,128]{3,2,1,0:T(8,128)S(1)}, f32[4,16,8,128]{3,2,1,0:T(8,128)S(1)}, u32[]{:S(2)}, u32[]{:S(2)}) collective-permute-start(f32[4,16,8,128]{3,2,1,0:T(8,128)S(1)} %get-tuple-element.189), channel_id=1, source_target_pairs={{0,1},{1,0},{2,3},{3,2},{4,5},{5,4},{6,7},{7,6},{8,9},{9,8},{10,11... | collective-permute-start | bytes 786440 | tf_op jit(solution)/shard_map/ppermute | solution.py:592
  83.5 9.0 %collective-permute-start.27 = (f32[4,16,8,128]{3,2,1,0:T(8,128)S(1)}, f32[4,16,8,128]{3,2,1,0:T(8,128)S(1)}, u32[]{:S(2)}, u32[]{:S(2)}) collective-permute-start(f32[4,16,8,128]{3,2,1,0:T(8,128)S(1)} %get-tuple-element.191), channel_id=1, source_target_pairs={{0,3},{1,2},{2,1},{3,0},{4,7},{5,6},{6,5},{7,4},{8,11},{9,10},{10,... | collective-permute-start | bytes 786440 | tf_op jit(solution)/shard_map/ppermute | solution.py:592
  83.7 13.9 %collective-permute-start.26 = (f32[4,16,8,128]{3,2,1,0:T(8,128)S(1)}, f32[4,16,8,128]{3,2,1,0:T(8,128)S(1)}, u32[]{:S(2)}, u32[]{:S(2)}) collective-permute-start(f32[4,16,8,128]{3,2,1,0:T(8,128)S(1)} %get-tuple-element.190), channel_id=1, source_target_pairs={{0,2},{1,3},{2,0},{3,1},{4,6},{5,7},{6,4},{7,5},{8,10},{9,11},{10,... | collective-permute-start | bytes 786440 | tf_op jit(solution)/shard_map/ppermute | solution.py:592
  86.1 11.4 %collective-permute-start.24 = (f32[4,128,128]{2,1,0:T(8,128)S(1)}, f32[4,128,128]{2,1,0:T(8,128)S(1)}, u32[]{:S(2)}, u32[]{:S(2)}) collective-permute-start(f32[4,128,128]{2,1,0:T(8,128)S(1)} %get-tuple-element.187), channel_id=1, source_target_pairs={{0,2},{2,0},{13,15},{15,13},{1,4},{4,1},{3,6},{6,3},{5,8},{8,5},{7... | collective-permute-start | bytes 786440 | tf_op jit(solution)/shard_map/ppermute | solution.py:530
  86.2 11.5 %collective-permute-start.28 = (f32[4,128,128]{2,1,0:T(8,128)S(1)}, f32[4,128,128]{2,1,0:T(8,128)S(1)}, u32[]{:S(2)}, u32[]{:S(2)}) collective-permute-start(f32[4,128,128]{2,1,0:T(8,128)S(1)} %get-tuple-element.198), channel_id=1, source_target_pairs={{0,1},{1,0},{2,3},{3,2},{4,5},{5,4},{6,7},{7,6},{8,9},{9,8},{10,11... | collective-permute-start | bytes 786440 | tf_op jit(solution)/shard_map/ppermute | solution.py:531
  98.5 16.0 %collective-permute-start.29 = (f32[4,128,128]{2,1,0:T(8,128)S(1)}, f32[4,128,128]{2,1,0:T(8,128)S(1)}, u32[]{:S(2)}, u32[]{:S(2)}) collective-permute-start(f32[4,128,128]{2,1,0:T(8,128)S(1)} %get-tuple-element.206), channel_id=1, source_target_pairs={{0,2},{2,0},{13,15},{15,13},{1,4},{4,1},{3,6},{6,3},{5,8},{8,5},{7... | collective-permute-start | bytes 786440 | tf_op jit(solution)/shard_map/ppermute | solution.py:530
  98.6 15.9 %collective-permute-start.32 = (f32[4,128,128]{2,1,0:T(8,128)S(1)}, f32[4,128,128]{2,1,0:T(8,128)S(1)}, u32[]{:S(2)}, u32[]{:S(2)}) collective-permute-start(f32[4,128,128]{2,1,0:T(8,128)S(1)} %get-tuple-element.212), channel_id=1, source_target_pairs={{0,1},{1,0},{2,3},{3,2},{4,5},{5,4},{6,7},{7,6},{8,9},{9,8},{10,11... | collective-permute-start | bytes 786440 | tf_op jit(solution)/shard_map/ppermute | solution.py:531
  103.5 8.2 %collective-permute-start.31 = (f32[2,16,8,128]{3,2,1,0:T(8,128)S(1)}, f32[2,16,8,128]{3,2,1,0:T(8,128)S(1)}, u32[]{:S(2)}, u32[]{:S(2)}) collective-permute-start(f32[2,16,8,128]{3,2,1,0:T(8,128)S(1)} %get-tuple-element.208), channel_id=1, source_target_pairs={{0,4},{1,5},{2,6},{3,7},{4,0},{5,1},{6,2},{7,3},{8,12},{9,13},{10,... | collective-permute-start | bytes 393224 | tf_op jit(solution)/shard_map/ppermute | solution.py:599
  107.8 6.7 %collective-permute-start.30 = (f32[2,16,8,128]{3,2,1,0:T(8,128)S(1)}, f32[2,16,8,128]{3,2,1,0:T(8,128)S(1)}, u32[]{:S(2)}, u32[]{:S(2)}) collective-permute-start(f32[2,16,8,128]{3,2,1,0:T(8,128)S(1)} %get-tuple-element.207), channel_id=1, source_target_pairs={{0,4},{1,5},{2,6},{3,7},{4,0},{5,1},{6,2},{7,3},{8,12},{9,13},{10,... | collective-permute-start | bytes 393224 | tf_op jit(solution)/shard_map/ppermute | solution.py:599
  114.5 0.8 copy-start.8
  115.3 9.5 %collective-permute-start.33 = (f32[4,128,128]{2,1,0:T(8,128)S(1)}, f32[4,128,128]{2,1,0:T(8,128)S(1)}, u32[]{:S(2)}, u32[]{:S(2)}) collective-permute-start(f32[4,128,128]{2,1,0:T(8,128)S(1)} %get-tuple-element.219), channel_id=1, source_target_pairs={{0,2},{2,0},{13,15},{15,13},{1,4},{4,1},{3,6},{6,3},{5,8},{8,5},{7... | collective-permute-start | bytes 786440 | tf_op jit(solution)/shard_map/ppermute | solution.py:530
  115.4 9.4 %collective-permute-start.35 = (f32[4,128,128]{2,1,0:T(8,128)S(1)}, f32[4,128,128]{2,1,0:T(8,128)S(1)}, u32[]{:S(2)}, u32[]{:S(2)}) collective-permute-start(f32[4,128,128]{2,1,0:T(8,128)S(1)} %get-tuple-element.223), channel_id=1, source_target_pairs={{0,1},{1,0},{2,3},{3,2},{4,5},{5,4},{6,7},{7,6},{8,9},{9,8},{10,11... | collective-permute-start | bytes 786440 | tf_op jit(solution)/shard_map/ppermute | solution.py:531
  116.9 7.4 %collective-permute-start.34 = (f32[2,16,8,128]{3,2,1,0:T(8,128)S(1)}, f32[2,16,8,128]{3,2,1,0:T(8,128)S(1)}, u32[]{:S(2)}, u32[]{:S(2)}) collective-permute-start(f32[2,16,8,128]{3,2,1,0:T(8,128)S(1)} %get-tuple-element.220), channel_id=1, source_target_pairs={{0,8},{1,9},{2,10},{3,11},{4,12},{5,13},{6,14},{7,15},{8,0},{9,1},... | collective-permute-start | bytes 393224 | tf_op jit(solution)/shard_map/ppermute | solution.py:599
  124.3 1.3 copy-start.10
  125.6 10.8 %collective-permute-start.36 = (f32[4,128,128]{2,1,0:T(8,128)S(1)}, f32[4,128,128]{2,1,0:T(8,128)S(1)}, u32[]{:S(2)}, u32[]{:S(2)}) collective-permute-start(f32[4,128,128]{2,1,0:T(8,128)S(1)} %get-tuple-element.230), channel_id=1, source_target_pairs={{0,2},{2,0},{13,15},{15,13},{1,4},{4,1},{3,6},{6,3},{5,8},{8,5},{7... | collective-permute-start | bytes 786440 | tf_op jit(solution)/shard_map/ppermute | solution.py:530
  127.5 8.9 %collective-permute-start.38 = (f32[4,128,128]{2,1,0:T(8,128)S(1)}, f32[4,128,128]{2,1,0:T(8,128)S(1)}, u32[]{:S(2)}, u32[]{:S(2)}) collective-permute-start(f32[4,128,128]{2,1,0:T(8,128)S(1)} %get-tuple-element.234), channel_id=1, source_target_pairs={{0,1},{1,0},{2,3},{3,2},{4,5},{5,4},{6,7},{7,6},{8,9},{9,8},{10,11... | collective-permute-start | bytes 786440 | tf_op jit(solution)/shard_map/ppermute | solution.py:531
  128.7 7.7 %collective-permute-start.37 = (f32[2,16,8,128]{3,2,1,0:T(8,128)S(1)}, f32[2,16,8,128]{3,2,1,0:T(8,128)S(1)}, u32[]{:S(2)}, u32[]{:S(2)}) collective-permute-start(f32[2,16,8,128]{3,2,1,0:T(8,128)S(1)} %get-tuple-element.231), channel_id=1, source_target_pairs={{0,8},{1,9},{2,10},{3,11},{4,12},{5,13},{6,14},{7,15},{8,0},{9,1},... | collective-permute-start | bytes 393224 | tf_op jit(solution)/shard_map/ppermute | solution.py:599
  136.4 0.8 copy-start.12
  137.2 12.1 %collective-permute-start.39 = (f32[4,128,128]{2,1,0:T(8,128)S(1)}, f32[4,128,128]{2,1,0:T(8,128)S(1)}, u32[]{:S(2)}, u32[]{:S(2)}) collective-permute-start(f32[4,128,128]{2,1,0:T(8,128)S(1)} %get-tuple-element.241), channel_id=1, source_target_pairs={{0,2},{2,0},{13,15},{15,13},{1,4},{4,1},{3,6},{6,3},{5,8},{8,5},{7... | collective-permute-start | bytes 786440 | tf_op jit(solution)/shard_map/ppermute | solution.py:530
  138.3 11.0 %collective-permute-start.42 = (f32[4,128,128]{2,1,0:T(8,128)S(1)}, f32[4,128,128]{2,1,0:T(8,128)S(1)}, u32[]{:S(2)}, u32[]{:S(2)}) collective-permute-start(f32[4,128,128]{2,1,0:T(8,128)S(1)} %get-tuple-element.251), channel_id=1, source_target_pairs={{0,1},{1,0},{2,3},{3,2},{4,5},{5,4},{6,7},{7,6},{8,9},{9,8},{10,11... | collective-permute-start | bytes 786440 | tf_op jit(solution)/shard_map/ppermute | solution.py:531
  140.3 8.3 %collective-permute-start.40 = (f32[2,16,8,128]{3,2,1,0:T(8,128)S(1)}, f32[2,16,8,128]{3,2,1,0:T(8,128)S(1)}, u32[]{:S(2)}, u32[]{:S(2)}) collective-permute-start(f32[2,16,8,128]{3,2,1,0:T(8,128)S(1)} %get-tuple-element.242), channel_id=1, source_target_pairs={{0,12},{1,13},{2,14},{3,15},{4,8},{5,9},{6,10},{7,11},{8,4},{9,5},... | collective-permute-start | bytes 393224 | tf_op jit(solution)/shard_map/ppermute | solution.py:599
  152.3 39.1 %all-to-all-start = ((f32[16,16,8,128]{3,2,1,0:T(8,128)}), f32[16,16,8,128]{3,2,1,0:T(8,128)S(1)}, u32[]{:S(2)}, u32[]{:S(2)}) async-start(f32[16,16,8,128]{3,2,1,0:T(8,128)} %get-tuple-element.254), calls=%async_computation | async-start | bytes 2097152 | tf_op jit(solution)/shard_map/all_to_all | solution.py:604
  156.4 33.9 %collective-permute-start.43 = (f32[8,128,128]{2,1,0:T(8,128)}, f32[8,128,128]{2,1,0:T(8,128)S(1)}, u32[]{:S(2)}, u32[]{:S(2)}) collective-permute-start(f32[8,128,128]{2,1,0:T(8,128)} %get-tuple-element.255), channel_id=1, source_target_pairs={{0,0},{1,2},{2,1},{3,3},{4,4},{5,6},{6,5},{7,7},{8,8},{9,10},{10,9... | collective-permute-start | bytes 1572872 | tf_op jit(solution)/shard_map/ppermute | solution.py:605
  159.8 30.5 %collective-permute-start.44 = (f32[8,128,128]{2,1,0:T(8,128)}, f32[8,128,128]{2,1,0:T(8,128)S(1)}, u32[]{:S(2)}, u32[]{:S(2)}) collective-permute-start(f32[8,128,128]{2,1,0:T(8,128)} %get-tuple-element.256), channel_id=1, source_target_pairs={{2,0},{0,1},{3,2},{1,3},{6,4},{4,5},{7,6},{5,7},{10,8},{8,9},{11,1... | collective-permute-start | bytes 1572872 | tf_op jit(solution)/shard_map/ppermute | solution.py:606
  159.8 26.8 %collective-permute-start.41 = (f32[2,16,8,128]{3,2,1,0:T(8,128)S(1)}, f32[2,16,8,128]{3,2,1,0:T(8,128)S(1)}, u32[]{:S(2)}, u32[]{:S(2)}) collective-permute-start(f32[2,16,8,128]{3,2,1,0:T(8,128)S(1)} %get-tuple-element.249), channel_id=1, source_target_pairs={{0,12},{1,13},{2,14},{3,15},{4,8},{5,9},{6,10},{7,11},{8,4},{9,5},... | collective-permute-start | bytes 393224 | tf_op jit(solution)/shard_map/ppermute | solution.py:599
  186.6 0.9 copy-start.9
  187.5 0.9 copy-start.11
  188.4 0.9 copy-start.13
  189.3 0.9 copy-start.15
  (1 other events, 0.7 us)

commit v6 on v5

--- a/solution.py
+++ b/solution.py
@@ -113,8 +113,8 @@
     )(here, there)
 
 
-def prepare_kernel(face_steps, lags, faces, late, early, shifts, gathered):
-    steps, layers = face_steps.shape[0], late.shape[0]
+def prepare_kernel(layers, face_steps, lags, faces, late, early, shifts, gathered):
+    steps = face_steps.shape[0]
     nx = shifts.shape[1] // 2
     gathered[...] = jnp.zeros_like(gathered)
 
@@ -123,19 +123,14 @@
         gathered[row : row + 4] = faces[pl.ds(base + 4 * layers, 4, stride=layers), :]
         gathered[row + 4 : row + 8] = faces[pl.ds(base, 4, stride=layers), :]
 
-    for plane in range(EARLY // PACKED):
+    for plane in range(steps // PACKED):
         for layer in range(layers):
             for step in range(PACKED):
                 gather(PACKED * plane + step, layer, 8 * (PACKED * layer + step))
-        early[plane] = gathered[...].T
-
-    def one_layer(layer, carry):
-        for step in range(steps):
-            gather(step, layer, 8 * step)
-        late[layer] = gathered[...].T
-        return carry
-
-    lax.fori_loop(0, layers, one_layer, 0)
+        if plane < EARLY // PACKED:
+            early[plane] = gathered[...].T
+        else:
+            late[plane - EARLY // PACKED] = gathered[...].T
 
     apart = lax.broadcasted_iota(jnp.int32, (nx, nx), 1) - lax.broadcasted_iota(jnp.int32, (nx, nx), 0)
     for index in range(lags.shape[0]):
@@ -148,10 +143,11 @@
 
 def prepare(saved_faces, face_steps, lag_offsets, nx):
     slots, eight, layers, ny = saved_faces.shape
+    planes = face_steps.shape[0] // PACKED
     return pl.pallas_call(
-        prepare_kernel,
+        functools.partial(prepare_kernel, layers),
         out_shape=(
-            f32(layers, ny, 128),
+            f32(planes - EARLY // PACKED, ny, 128),
             f32(EARLY // PACKED, ny, 128),
             jax.ShapeDtypeStruct((2, 2 * nx, lag_offsets.shape[0] * nx), jnp.bfloat16),
         ),
@@ -197,13 +193,6 @@
     for_each_part(2 * before_a.shape[0], run)
 
 
-def merge_faces_kernel(face_a, face_b, face):
-    def run(j, q, which):
-        face[j] = (face_a, face_b)[which][q]
-
-    for_each_part(2 * face_a.shape[0], run)
-
-
 def merge(kernel, shapes, *parts):
     return pl.pallas_call(
         kernel, out_shape=shapes, in_specs=[VMEM] * len(parts), out_specs=(VMEM,) * len(shapes), compiler_params=PARAMS
@@ -221,11 +210,9 @@
     edge = ((column < REACH) | (column >= nx - REACH)) & (my_field() == 0)
 
     def placed(layer):
-        if step >= EARLY:
-            return pltpu.roll(faces[0][layer], (128 - 8 * step - REACH) % 128, axis=1)
         place = place_of(layer, layers)
         part = (place >= layers // 2).astype(jnp.int32)
-        plane, inside = step // PACKED, step % PACKED
+        plane, inside = (step if step < EARLY else step - EARLY) // PACKED, step % PACKED
         lane = 8 * (PACKED * (place - part * (layers // 2)) + inside) + REACH
         held = jnp.where(part == 0, faces[0][plane], faces[1][plane])
         return pltpu.roll(held, lax.rem(128 - lane, 128), axis=1)
@@ -309,10 +296,12 @@
         keep_snapshot(step, phase, new, rest[-1])
 
 
-def last_kernel(step, phase, across, along, low, high, traces, speed, face, cur_in, prev, snap_in, cur, new, snap, out_a, out_b, send):
+def last_kernel(
+    step, phase, across, along, low, high, traces, speed, face_a, face_b, cur_in, prev, snap_in, cur, new, snap, out_a, out_b, send
+):
     layers = speed.shape[0]
     fill_halos(low, high, cur)
-    advance(step, across, along, cur, prev, speed, (face,), new, border_layers(layers))
+    advance(step, across, along, cur, prev, speed, (face_a, face_b), new, border_layers(layers))
     add_trace(step, traces, new)
     keep_snapshot(step, phase, new, snap)
 
@@ -511,9 +500,7 @@
 
     snap = None
     for step in range(steps):
-        if step == EARLY:
-            face = merge(merge_faces_kernel, (whole,), *late)
-        faces = tuple(face) if step >= EARLY else early
+        faces = late if step >= EARLY else early
         wide = len(faces)
         if step < steps - 1:
             border = pl.pallas_call(
@@ -529,19 +516,20 @@
             cur, new, low, high = border(across, along, low, high, traces, speed, *faces, cur, prev)
             low = lax.ppermute(low, "gz", between)
             high = lax.ppermute(high, "gz", within)
-            low, *under_way = lax.optimization_barrier((low, *under_way))
+            low, *landed = lax.optimization_barrier((low, *[array for _, array in under_way]))
             if step == SNAP_EVERY:
                 own_strips, *sent = merge(
                     regather_kernel,
                     (f32(4, layers, rows, nx), *[f32(4 // pieces, layers, rows, nx)] * (pieces * (groups - 1))),
-                    *under_way,
+                    strip_parts[0],
+                    *landed,
                 )
                 waiting = [
-                    (part, [(i, 4 * ((i // 4) ^ (j // pieces + 1)) + i % 4) for i in range(count)])
-                    for j, part in enumerate(sent)
+                    (j < pieces, j, [(i, 4 * ((i // 4) ^ (j // pieces + 1)) + i % 4) for i in range(count)])
+                    for j in range(len(sent))
                 ]
             else:
-                arrived += under_way
+                arrived += [(part, array) for (part, _), array in zip(under_way, landed)]
             under_way = []
         else:
             new = prev
@@ -574,9 +562,9 @@
             last = pl.pallas_call(
                 functools.partial(last_kernel, step),
                 out_shape=(tall, tall, strips, half, half, f32(*strips.shape)),
-                in_specs=[SMEM] + [VMEM] * 10,
+                in_specs=[SMEM] + [VMEM] * 11,
                 out_specs=(VMEM,) * 6,
-                input_output_aliases={8: 0, 9: 1, 10: 2},
+                input_output_aliases={9: 0, 10: 1, 11: 2},
                 compiler_params=PARAMS,
                 name="last",
             )
@@ -586,21 +574,24 @@
             late = regroup(late, late)
         if step == SNAP_EVERY - 1:
             strip_parts = merge(spread_kernel, (f32(groups, layers, rows, nx),) * 4, snap)
-            under_way.append(strip_parts[0])
-            for which in (2, 3, 1):
+            for which in (1, 2, 3):
                 payload, new = lax.optimization_barrier((strip_parts[which], new))
-                under_way.append(lax.ppermute(payload, "gz", [(i, i ^ which) for i in range(count)]))
-            under_way = [under_way[i] for i in (0, 3, 1, 2)]
+                under_way.append((which, lax.ppermute(payload, "gz", [(i, i ^ which) for i in range(count)])))
             snap = None
-        left = steps - 1 - step
-        now_many = -(-len(waiting) // left) if left else len(waiting)
-        for payload, pairs in waiting[:now_many]:
+        slots = max(1, steps - 2 - step)
+        far = [item for item in waiting if not item[0]]
+        near = [item for item in waiting if item[0]]
+        chosen = far[: -(-len(far) // slots)] + (near[: -(-len(near) // slots)] if step > SNAP_EVERY or not far else [])
+        waiting = [item for item in waiting if item not in chosen]
+        for _, which_part, pairs in chosen:
+            payload = sent[which_part]
             payload, new = lax.optimization_barrier((payload, new))
-            under_way.append(lax.ppermute(payload, "gz", pairs))
-        waiting = waiting[now_many:]
+            under_way.append((which_part, lax.ppermute(payload, "gz", pairs)))
         prev, cur = cur, new
 
-    (first,) = merge(collect_kernel, (f32(count, layers, rows, nx),), own_strips, *arrived, *under_way)
+    (first,) = merge(
+        collect_kernel, (f32(count, layers, rows, nx),), own_strips, *[array for _, array in sorted(arrived + under_way, key=lambda item: item[0])]
+    )
     second = lax.all_to_all(send, "gz", split_axis=0, concat_axis=0, tiled=True)
     back_a = lax.ppermute(out_a, "gz", first_pairs)
     back_b = lax.ppermute(out_b, "gz", back_pairs)

time: 199 us -> 187 us (0.940)
  waiting for transfers between devices: 83.7 us -> 76.4 us
  starting transfers between devices: 66.4 us -> 62 us
    ppermute x6, waiting for transfers between devices: 49.6 us -> 20.7 us  [local(): under_way.append((which_part, lax.ppermute(payload, 'gz', pairs)))]
    ppermute x1, waiting for transfers between devices: 0.01 us -> 7.98 us  [local(): back_a = lax.ppermute(out_a, 'gz', first_pairs)]
    ppermute x12, starting transfers between devices: 25.8 us -> 17.8 us  [local(): high = lax.ppermute(high, 'gz', within)]
    ppermute x1, waiting for transfers between devices: 0.01 us -> 5.9 us  [local(): back_b = lax.ppermute(out_b, 'gz', back_pairs)]
    ppermute x12, starting transfers between devices: 8 us -> 11 us  [local(): low = lax.ppermute(low, 'gz', between)]
    ppermute x4, waiting for transfers between devices: 18.5 us -> 21.5 us  [regroup(): lax.ppermute(a, 'gz', first_pairs)]
    ppermute x12, waiting for transfers between devices: 10.5 us -> 12.8 us  [local(): low = lax.ppermute(low, 'gz', between)]
    unnamed x38 -> x42, local copies, waits for them, and re-layouts: 8.47 us -> 8.72 us
  transfers between devices with their start and end apart: 46 -> 46, of which waited for: 15 -> 20; matrix products, arithmetic and copies ran while one was open for 0% -> 0% of each run, Pallas kernels for 11% -> 10%
where the time goes in v6:
time: 187 us; the launch traced here: 184 us
  waiting for transfers between devices  76.4 us (41%)
  starting transfers between devices  62 us (33%)
  Pallas kernels  35.8 us (19%)
  local copies, waits for them, and re-layouts  8.72 us (5%)
    ppermute x4, waiting for transfers between devices, regroup(): lax.ppermute(a, 'gz', first_pairs)  21.5 us
    ppermute x6, waiting for transfers between devices, local(): under_way.append((which_part, lax.ppermute(payload, 'gz', pairs)))  20.7 us
    ppermute x12, starting transfers between devices, local(): high = lax.ppermute(high, 'gz', within)  17.8 us
    pallas_call x11, Pallas kernels, local(): inner(functools.partial(inner_kernel, step, wide, True), out_shape=(tall,...  14.2 us
    ppermute x4, starting transfers between devices, regroup(): lax.ppermute(a, 'gz', first_pairs)  13.2 us
    ppermute x12, waiting for transfers between devices, local(): low = lax.ppermute(low, 'gz', between)  12.8 us
    ppermute x12, starting transfers between devices, local(): low = lax.ppermute(low, 'gz', between)  11 us
    unnamed x42, local copies, waits for them, and re-layouts  8.72 us
  transfers between devices with their start and end apart: 46, of which 20 were waited for; matrix products, arithmetic and copies ran while one was open for 0% of the time, Pallas kernels for 10%

profile of v6, /device:TPU:9, one launch (start us, length us, event | category | flops | bytes accessed | tf_op | source)
XLA Modules:
  0.0 184.3 jit_solution(4839403403979918612)
XLA Ops:
  0.6 3.7 %collective-permute-start.2 = (f32[8,128,128]{2,1,0:T(8,128)}, f32[8,128,128]{2,1,0:T(8,128)S(1)}, u32[]{:S(2)}, u32[]{:S(2)}) collective-permute-start(f32[8,128,128]{2,1,0:T(8,128)} %param.16), channel_id=1, source_target_pairs={{0,0},{1,2},{2,1},{3,3},{4,4},{5,6},{6,5},{7,7},{8,8},{9,10},{10,9... | collective-permute-start | bytes 1572872 | tf_op jit(solution)/shard_map/ppermute | solution.py:484
  4.4 1.0 copy-done.3
  5.4 1.0 copy-done.4
  6.5 2.1 %collective-permute-start.6 = (f32[8,128,128]{2,1,0:T(8,128)S(1)}, f32[8,128,128]{2,1,0:T(8,128)S(1)}, u32[]{:S(2)}, u32[]{:S(2)}) collective-permute-start(f32[8,128,128]{2,1,0:T(8,128)S(1)} %get-tuple-element.137), channel_id=1, source_target_pairs={{0,0},{1,2},{2,1},{3,3},{4,4},{5,6},{6,5},{7,7},{8,8},{9,10},{10,9... | collective-permute-start | bytes 1572872 | tf_op jit(solution)/shard_map/ppermute | solution.py:467
  8.6 1.0 copy-done.5
  9.7 1.0 copy-done.6
  10.8 3.6 %collective-permute-start = (f32[8,128,128]{2,1,0:T(8,128)S(1)}, f32[8,128,128]{2,1,0:T(8,128)S(1)}, u32[]{:S(2)}, u32[]{:S(2)}) collective-permute-start(f32[8,128,128]{2,1,0:T(8,128)S(1)} %get-tuple-element.132), channel_id=1, source_target_pairs={{0,0},{1,2},{2,1},{3,3},{4,4},{5,6},{6,5},{7,7},{8,8},{9,10},{10,9... | collective-permute-start | bytes 1572872 | tf_op jit(solution)/shard_map/ppermute | solution.py:467
  14.7 8.6 %collective-permute-done.6.now_a = f32[8,128,128]{2,1,0:T(8,128)S(1)} collective-permute-done((f32[8,128,128]{2,1,0:T(8,128)S(1)}, f32[8,128,128]{2,1,0:T(8,128)S(1)}, u32[]{:S(2)}, u32[]{:S(2)}) %collective-permute-start.6) | collective-permute-done | bytes 524320 | tf_op jit(solution)/shard_map/ppermute | solution.py:467
  23.7 1.0 collective-permute-start.8
  24.7 1.0 prepare.1
  25.7 8.2 %collective-permute-done.before_a = f32[8,128,128]{2,1,0:T(8,128)S(1)} collective-permute-done((f32[8,128,128]{2,1,0:T(8,128)S(1)}, f32[8,128,128]{2,1,0:T(8,128)S(1)}, u32[]{:S(2)}, u32[]{:S(2)}) %collective-permute-start) | collective-permute-done | bytes 524320 | tf_op jit(solution)/shard_map/ppermute | solution.py:467
  33.9 3.6 %collective-permute-start.4 = (f32[2,128,128]{2,1,0:T(8,128)S(1)}, f32[2,128,128]{2,1,0:T(8,128)S(1)}, u32[]{:S(2)}, u32[]{:S(2)}) collective-permute-start(f32[2,128,128]{2,1,0:T(8,128)S(1)} %get-tuple-element.136), channel_id=1, source_target_pairs={{0,0},{1,2},{2,1},{3,3},{4,4},{5,6},{6,5},{7,7},{8,8},{9,10},{10,9... | collective-permute-start | bytes 393224 | tf_op jit(solution)/shard_map/ppermute | solution.py:467
  38.1 2.1 %collective-permute-done.4.rest_0_ = f32[2,128,128]{2,1,0:T(8,128)S(1)} collective-permute-done((f32[2,128,128]{2,1,0:T(8,128)S(1)}, f32[2,128,128]{2,1,0:T(8,128)S(1)}, u32[]{:S(2)}, u32[]{:S(2)}) %collective-permute-start.4) | collective-permute-done | bytes 131104 | tf_op jit(solution)/shard_map/ppermute | solution.py:467
  40.2 0.8 border.11
  41.6 1.3 inner.12
  42.9 4.0 %collective-permute-done.12.low = f32[4,128,128]{2,1,0:T(8,128)S(1)} collective-permute-done((f32[4,128,128]{2,1,0:T(8,128)S(1)}, f32[4,128,128]{2,1,0:T(8,128)S(1)}, u32[]{:S(2)}, u32[]{:S(2)}) %collective-permute-start.12) | collective-permute-done | bytes 262176 | tf_op jit(solution)/shard_map/ppermute | solution.py:517
  47.7 0.8 collective-permute-start.15
  48.6 1.3 inner.13
  49.8 3.7 %collective-permute-done.14.low = f32[4,128,128]{2,1,0:T(8,128)S(1)} collective-permute-done((f32[4,128,128]{2,1,0:T(8,128)S(1)}, f32[4,128,128]{2,1,0:T(8,128)S(1)}, u32[]{:S(2)}, u32[]{:S(2)}) %collective-permute-start.14) | collective-permute-done | bytes 262176 | tf_op jit(solution)/shard_map/ppermute | solution.py:517
  54.4 1.1 collective-permute-start.17
  55.5 1.3 inner.14
  56.8 3.4 %collective-permute-done.16.low = f32[4,128,128]{2,1,0:T(8,128)S(1)} collective-permute-done((f32[4,128,128]{2,1,0:T(8,128)S(1)}, f32[4,128,128]{2,1,0:T(8,128)S(1)}, u32[]{:S(2)}, u32[]{:S(2)}) %collective-permute-start.16) | collective-permute-done | bytes 262176 | tf_op jit(solution)/shard_map/ppermute | solution.py:517
  61.1 1.4 collective-permute-start.11
  62.5 3.9 %collective-permute-start.10 = (f32[4,128,128]{2,1,0:T(8,128)S(1)}, f32[4,128,128]{2,1,0:T(8,128)S(1)}, u32[]{:S(2)}, u32[]{:S(2)}) collective-permute-start(f32[4,128,128]{2,1,0:T(8,128)S(1)} %get-tuple-element.146), channel_id=1, source_target_pairs={{0,0},{1,2},{2,1},{3,3},{4,4},{5,6},{6,5},{7,7},{8,8},{9,10},{10,9... | collective-permute-start | bytes 786440 | tf_op jit(solution)/shard_map/ppermute | solution.py:467
  66.5 1.3 inner.15
  68.1 2.6 %collective-permute-done.10.rest_0_.face_a = f32[4,128,128]{2,1,0:T(8,128)S(1)} collective-permute-done((f32[4,128,128]{2,1,0:T(8,128)S(1)}, f32[4,128,128]{2,1,0:T(8,128)S(1)}, u32[]{:S(2)}, u32[]{:S(2)}) %collective-permute-start.10) | collective-permute-done | bytes 262176 | tf_op jit(solution)/shard_map/ppermute | solution.py:467
  71.5 3.4 %collective-permute-start.21 = (f32[4,128,128]{2,1,0:T(8,128)S(1)}, f32[4,128,128]{2,1,0:T(8,128)S(1)}, u32[]{:S(2)}, u32[]{:S(2)}) collective-permute-start(f32[4,128,128]{2,1,0:T(8,128)S(1)} %get-tuple-element.169), channel_id=1, source_target_pairs={{0,1},{1,0},{2,3},{3,2},{4,5},{5,4},{6,7},{7,6},{8,9},{9,8},{10,11... | collective-permute-start | bytes 786440 | tf_op jit(solution)/shard_map/ppermute | solution.py:518
  74.9 1.4 inner.16
  76.3 1.3 collective-permute-done.20.low
  78.5 3.4 %collective-permute-start.23 = (f32[4,128,128]{2,1,0:T(8,128)S(1)}, f32[4,128,128]{2,1,0:T(8,128)S(1)}, u32[]{:S(2)}, u32[]{:S(2)}) collective-permute-start(f32[4,128,128]{2,1,0:T(8,128)S(1)} %get-tuple-element.180), channel_id=1, source_target_pairs={{0,1},{1,0},{2,3},{3,2},{4,5},{5,4},{6,7},{7,6},{8,9},{9,8},{10,11... | collective-permute-start | bytes 786440 | tf_op jit(solution)/shard_map/ppermute | solution.py:518
  81.8 1.4 inner.17
  83.8 1.1 collective-permute-start.26
  86.5 3.7 %collective-permute-start.28 = (f32[4,128,128]{2,1,0:T(8,128)S(1)}, f32[4,128,128]{2,1,0:T(8,128)S(1)}, u32[]{:S(2)}, u32[]{:S(2)}) collective-permute-start(f32[4,128,128]{2,1,0:T(8,128)S(1)} %get-tuple-element.197), channel_id=1, source_target_pairs={{0,1},{1,0},{2,3},{3,2},{4,5},{5,4},{6,7},{7,6},{8,9},{9,8},{10,11... | collective-permute-start | bytes 786440 | tf_op jit(solution)/shard_map/ppermute | solution.py:518
  90.2 1.3 inner.18
  91.4 0.9 collective-permute-done.27.refs_3_
  92.4 4.3 %collective-permute-done.26.refs_2_ = f32[4,16,8,128]{3,2,1,0:T(8,128)S(1)} collective-permute-done((f32[4,16,8,128]{3,2,1,0:T(8,128)S(1)}, f32[4,16,8,128]{3,2,1,0:T(8,128)S(1)}, u32[]{:S(2)}, u32[]{:S(2)}) %collective-permute-start.26) | collective-permute-done | bytes 262176 | tf_op jit(solution)/shard_map/ppermute | solution.py:579
  98.3 3.0 %collective-permute-start.31 = (f32[4,128,128]{2,1,0:T(8,128)S(1)}, f32[4,128,128]{2,1,0:T(8,128)S(1)}, u32[]{:S(2)}, u32[]{:S(2)}) collective-permute-start(f32[4,128,128]{2,1,0:T(8,128)S(1)} %get-tuple-element.206), channel_id=1, source_target_pairs={{0,1},{1,0},{2,3},{3,2},{4,5},{5,4},{6,7},{7,6},{8,9},{9,8},{10,11... | collective-permute-start | bytes 786440 | tf_op jit(solution)/shard_map/ppermute | solution.py:518
  102.0 1.3 inner.19
  103.3 4.0 %collective-permute-done.30.refs_2_ = f32[2,16,8,128]{3,2,1,0:T(8,128)S(1)} collective-permute-done((f32[2,16,8,128]{3,2,1,0:T(8,128)S(1)}, f32[2,16,8,128]{3,2,1,0:T(8,128)S(1)}, u32[]{:S(2)}, u32[]{:S(2)}) %collective-permute-start.30) | collective-permute-done | bytes 131104 | tf_op jit(solution)/shard_map/ppermute | solution.py:589
  108.1 4.8 %collective-permute-start.32 = (f32[4,128,128]{2,1,0:T(8,128)S(1)}, f32[4,128,128]{2,1,0:T(8,128)S(1)}, u32[]{:S(2)}, u32[]{:S(2)}) collective-permute-start(f32[4,128,128]{2,1,0:T(8,128)S(1)} %get-tuple-element.215), channel_id=1, source_target_pairs={{0,2},{2,0},{13,15},{15,13},{1,4},{4,1},{3,6},{6,3},{5,8},{8,5},{7... | collective-permute-start | bytes 786440 | tf_op jit(solution)/shard_map/ppermute | solution.py:517
  112.9 0.8 collective-permute-start.35
  114.5 1.4 inner.20
  115.9 4.5 %collective-permute-done.34.refs_0_ = f32[2,16,8,128]{3,2,1,0:T(8,128)S(1)} collective-permute-done((f32[2,16,8,128]{3,2,1,0:T(8,128)S(1)}, f32[2,16,8,128]{3,2,1,0:T(8,128)S(1)}, u32[]{:S(2)}, u32[]{:S(2)}) %collective-permute-start.34) | collective-permute-done | bytes 131104 | tf_op jit(solution)/shard_map/ppermute | solution.py:589
  121.7 3.2 %collective-permute-start.36 = (f32[4,128,128]{2,1,0:T(8,128)S(1)}, f32[4,128,128]{2,1,0:T(8,128)S(1)}, u32[]{:S(2)}, u32[]{:S(2)}) collective-permute-start(f32[4,128,128]{2,1,0:T(8,128)S(1)} %get-tuple-element.229), channel_id=1, source_target_pairs={{0,2},{2,0},{13,15},{15,13},{1,4},{4,1},{3,6},{6,3},{5,8},{8,5},{7... | collective-permute-start | bytes 786440 | tf_op jit(solution)/shard_map/ppermute | solution.py:517
  125.3 1.6 collective-permute-start.38
  126.8 1.3 inner.21
  128.1 6.4 %collective-permute-done.38.refs_1_ = f32[2,16,8,128]{3,2,1,0:T(8,128)S(1)} collective-permute-done((f32[2,16,8,128]{3,2,1,0:T(8,128)S(1)}, f32[2,16,8,128]{3,2,1,0:T(8,128)S(1)}, u32[]{:S(2)}, u32[]{:S(2)}) %collective-permute-start.38) | collective-permute-done | bytes 131104 | tf_op jit(solution)/shard_map/ppermute | solution.py:589
  135.3 0.8 collective-permute-start.40
  136.7 1.0 collective-permute-start.41
  137.7 1.3 inner.22
  139.7 5.3 %collective-permute-done.41.refs_5_ = f32[2,16,8,128]{3,2,1,0:T(8,128)S(1)} collective-permute-done((f32[2,16,8,128]{3,2,1,0:T(8,128)S(1)}, f32[2,16,8,128]{3,2,1,0:T(8,128)S(1)}, u32[]{:S(2)}, u32[]{:S(2)}) %collective-permute-start.41) | collective-permute-done | bytes 131104 | tf_op jit(solution)/shard_map/ppermute | solution.py:589
  145.4 3.0 %last.1 = (f32[24,128,128]{2,1,0:T(8,128)S(1)}, f32[24,128,128]{2,1,0:T(8,128)S(1)}, f32[16,16,8,128]{3,2,1,0:T(8,128)S(1)}, f32[8,128,128]{2,1,0:T(8,128)}, f32...) custom-call(s32[2]{0:T(128)S(1)} %copy-done.18, ...), custom_call_target="tpu_custom_call", output_to_operand_aliasing={{0}: (9, {}), {1}: (10, {}), {2}: (11, {})} | custom-call | tf_op jit(solution)/shard_map/last/pallas_call | solution.py:571
  148.4 5.1 %all-to-all-start = ((f32[16,16,8,128]{3,2,1,0:T(8,128)}), f32[16,16,8,128]{3,2,1,0:T(8,128)S(1)}, u32[]{:S(2)}, u32[]{:S(2)}) async-start(f32[16,16,8,128]{3,2,1,0:T(8,128)} %get-tuple-element.254), calls=%async_computation | async-start | bytes 2097152 | tf_op jit(solution)/shard_map/all_to_all | solution.py:595
  153.5 3.4 %collective-permute-start.43 = (f32[8,128,128]{2,1,0:T(8,128)}, f32[8,128,128]{2,1,0:T(8,128)S(1)}, u32[]{:S(2)}, u32[]{:S(2)}) collective-permute-start(f32[8,128,128]{2,1,0:T(8,128)} %get-tuple-element.255), channel_id=1, source_target_pairs={{0,0},{1,2},{2,1},{3,3},{4,4},{5,6},{6,5},{7,7},{8,8},{9,10},{10,9... | collective-permute-start | bytes 1572872 | tf_op jit(solution)/shard_map/ppermute | solution.py:596
  156.9 0.9 copy-done.9
  157.8 0.9 copy-done.11
  158.7 0.9 copy-done.13
  159.6 0.9 copy-done.15
  160.5 0.9 copy-done.17
  161.5 8.0 %collective-permute-done.43.here = f32[8,128,128]{2,1,0:T(8,128)S(1)} collective-permute-done((f32[8,128,128]{2,1,0:T(8,128)}, f32[8,128,128]{2,1,0:T(8,128)S(1)}, u32[]{:S(2)}, u32[]{:S(2)}) %collective-permute-start.43) | collective-permute-done | bytes 524320 | tf_op jit(solution)/shard_map/ppermute | solution.py:596
  169.5 5.9 %collective-permute-done.44.there = f32[8,128,128]{2,1,0:T(8,128)S(1)} collective-permute-done((f32[8,128,128]{2,1,0:T(8,128)}, f32[8,128,128]{2,1,0:T(8,128)S(1)}, u32[]{:S(2)}, u32[]{:S(2)}) %collective-permute-start.44) | collective-permute-done | bytes 524320 | tf_op jit(solution)/shard_map/ppermute | solution.py:597
  175.4 1.1 choose.5
  176.5 2.0 %all-to-all-done.refs_1_ = f32[16,16,8,128]{3,2,1,0:T(8,128)S(1)} async-done(((f32[16,16,8,128]{3,2,1,0:T(8,128)}), f32[16,16,8,128]{3,2,1,0:T(8,128)S(1)}, u32[]{:S(2)}, u32[]{:S(2)}) %all-to-all-start) | async-done | bytes 1048608 | tf_op jit(solution)/shard_map/all_to_all | solution.py:595
  178.4 5.7 %images.1 = bf16[8,128,8,128]{3,2,1,0:T(8,128)(2,1)} custom-call(bf16[2,256,1024]{2,1,0:T(8,128)(2,1)S(1)} %get-tuple-element.131.shifts, f32[16,16,8,128]{3,2,1,0:T(8,128)S(1)} %shard_map.143.refs_0_, f32[16,16,8,128]{3,2,1,0:T(8,128)S(1)} %all-to-all-done.refs_1_), custom_call_target="tpu_custom_call" | custom-call | tf_op jit(solution)/shard_map/images/pallas_call | solution.py:427
  (104 shorter events, 16.9 us)
Async XLA Ops:
  0.6 13.9 %collective-permute-start.2 = (f32[8,128,128]{2,1,0:T(8,128)}, f32[8,128,128]{2,1,0:T(8,128)S(1)}, u32[]{:S(2)}, u32[]{:S(2)}) collective-permute-start(f32[8,128,128]{2,1,0:T(8,128)} %param.16), channel_id=1, source_target_pairs={{0,0},{1,2},{2,1},{3,3},{4,4},{5,6},{6,5},{7,7},{8,8},{9,10},{10,9... | collective-permute-start | bytes 1572872 | tf_op jit(solution)/shard_map/ppermute | solution.py:484
  4.3 1.0 copy-start.3
  5.4 1.0 copy-start.4
  6.4 18.3 %copy-start.7 = (f32[12,8,8,128]{3,2,1,0:T(8,128)S(1)}, f32[12,8,8,128]{3,2,1,0:T(8,128)}, u32[]{:S(2)}) copy-start(f32[12,8,8,128]{3,2,1,0:T(8,128)} %param.17) | copy-start | bytes 1179652
  6.4 18.3 %copy-start.19 = (s32[12]{0:T(128)S(1)}, s32[12]{0:T(128)}, u32[]{:S(2)}) copy-start(s32[12]{0:T(128)} %face_steps.1) | copy-start | bytes 148
  6.4 18.3 %copy-start.20 = (s32[8]{0:T(128)S(1)}, s32[8]{0:T(128)}, u32[]{:S(2)}) copy-start(s32[8]{0:T(128)} %lags.1) | copy-start | bytes 100
  6.5 16.8 %collective-permute-start.6 = (f32[8,128,128]{2,1,0:T(8,128)S(1)}, f32[8,128,128]{2,1,0:T(8,128)S(1)}, u32[]{:S(2)}, u32[]{:S(2)}) collective-permute-start(f32[8,128,128]{2,1,0:T(8,128)S(1)} %get-tuple-element.137), channel_id=1, source_target_pairs={{0,0},{1,2},{2,1},{3,3},{4,4},{5,6},{6,5},{7,7},{8,8},{9,10},{10,9... | collective-permute-start | bytes 1572872 | tf_op jit(solution)/shard_map/ppermute | solution.py:467
  8.6 14.7 %collective-permute-start.7 = (f32[8,128,128]{2,1,0:T(8,128)S(1)}, f32[8,128,128]{2,1,0:T(8,128)S(1)}, u32[]{:S(2)}, u32[]{:S(2)}) collective-permute-start(f32[8,128,128]{2,1,0:T(8,128)S(1)} %get-tuple-element.138), channel_id=1, source_target_pairs={{0,2},{1,0},{2,3},{3,1},{4,6},{5,4},{6,7},{7,5},{8,10},{9,8},{10,1... | collective-permute-start | bytes 1572872 | tf_op jit(solution)/shard_map/ppermute | solution.py:467
  8.6 1.0 copy-start.5
  9.7 1.0 copy-start.6
  10.8 23.1 %collective-permute-start = (f32[8,128,128]{2,1,0:T(8,128)S(1)}, f32[8,128,128]{2,1,0:T(8,128)S(1)}, u32[]{:S(2)}, u32[]{:S(2)}) collective-permute-start(f32[8,128,128]{2,1,0:T(8,128)S(1)} %get-tuple-element.132), channel_id=1, source_target_pairs={{0,0},{1,2},{2,1},{3,3},{4,4},{5,6},{6,5},{7,7},{8,8},{9,10},{10,9... | collective-permute-start | bytes 1572872 | tf_op jit(solution)/shard_map/ppermute | solution.py:467
  14.5 25.7 %copy-start = (bf16[12,128,128]{2,1,0:T(8,128)(2,1)S(1)}, bf16[12,128,128]{2,1,0:T(8,128)(2,1)}, u32[]{:S(2)}) copy-start(bf16[12,128,128]{2,1,0:T(8,128)(2,1)} %traces.23) | copy-start | bytes 1179652
  14.5 25.7 %copy-start.1 = (bf16[128,256]{1,0:T(8,128)(2,1)S(1)}, bf16[128,256]{1,0:T(8,128)(2,1)}, u32[]{:S(2)}) copy-start(bf16[128,256]{1,0:T(8,128)(2,1)} %constant.5.clone.along) | copy-start | bytes 196612
  14.5 25.7 %copy-start.2 = (bf16[256,128]{1,0:T(8,128)(2,1)S(1)}, bf16[256,128]{1,0:T(8,128)(2,1)}, u32[]{:S(2)}) copy-start(bf16[256,128]{1,0:T(8,128)(2,1)} %constant.4.clone.across) | copy-start | bytes 196612
  14.5 19.4 %collective-permute-start.1 = (f32[8,128,128]{2,1,0:T(8,128)S(1)}, f32[8,128,128]{2,1,0:T(8,128)S(1)}, u32[]{:S(2)}, u32[]{:S(2)}) collective-permute-start(f32[8,128,128]{2,1,0:T(8,128)S(1)} %get-tuple-element.133), channel_id=1, source_target_pairs={{0,2},{1,0},{2,3},{3,1},{4,6},{5,4},{6,7},{7,5},{8,10},{9,8},{10,1... | collective-permute-start | bytes 1572872 | tf_op jit(solution)/shard_map/ppermute | solution.py:467
  14.5 23.0 %collective-permute-start.3 = (f32[8,128,128]{2,1,0:T(8,128)S(1)}, f32[8,128,128]{2,1,0:T(8,128)S(1)}, u32[]{:S(2)}, u32[]{:S(2)}) collective-permute-start(f32[8,128,128]{2,1,0:T(8,128)S(1)} %collective-permute-done.2.speed_a), channel_id=1, source_target_pairs={{0,16},{16,0},{1,17},{17,1},{2,18},{18,2},{3,19},{19,3},{4,20},{20... | collective-permute-start | bytes 1572872 | tf_op jit(solution)/shard_map/ppermute | solution.py:485
  23.7 16.4 %collective-permute-start.8 = (f32[4,128,128]{2,1,0:T(8,128)S(1)}, f32[4,128,128]{2,1,0:T(8,128)S(1)}, u32[]{:S(2)}, u32[]{:S(2)}) collective-permute-start(f32[4,128,128]{2,1,0:T(8,128)S(1)} %get-tuple-element.139), channel_id=1, source_target_pairs={{0,2},{2,0},{13,15},{15,13},{1,4},{4,1},{3,6},{6,3},{5,8},{8,5},{7... | collective-permute-start | bytes 786440 | tf_op jit(solution)/shard_map/ppermute | solution.py:493
  24.7 15.5 %collective-permute-start.9 = (f32[4,128,128]{2,1,0:T(8,128)S(1)}, f32[4,128,128]{2,1,0:T(8,128)S(1)}, u32[]{:S(2)}, u32[]{:S(2)}) collective-permute-start(f32[4,128,128]{2,1,0:T(8,128)S(1)} %get-tuple-element.140), channel_id=1, source_target_pairs={{0,1},{1,0},{2,3},{3,2},{4,5},{5,4},{6,7},{7,6},{8,9},{9,8},{10,11... | collective-permute-start | bytes 786440 | tf_op jit(solution)/shard_map/ppermute | solution.py:494
  33.9 4.2 %collective-permute-start.5 = (f32[2,128,128]{2,1,0:T(8,128)S(1)}, f32[2,128,128]{2,1,0:T(8,128)S(1)}, u32[]{:S(2)}, u32[]{:S(2)}) collective-permute-start(f32[2,128,128]{2,1,0:T(8,128)S(1)} %get-tuple-element.136), channel_id=1, source_target_pairs={{0,2},{1,0},{2,3},{3,1},{4,6},{5,4},{6,7},{7,5},{8,10},{9,8},{10,1... | collective-permute-start | bytes 393224 | tf_op jit(solution)/shard_map/ppermute | solution.py:467
  33.9 6.3 %collective-permute-start.4 = (f32[2,128,128]{2,1,0:T(8,128)S(1)}, f32[2,128,128]{2,1,0:T(8,128)S(1)}, u32[]{:S(2)}, u32[]{:S(2)}) collective-permute-start(f32[2,128,128]{2,1,0:T(8,128)S(1)} %get-tuple-element.136), channel_id=1, source_target_pairs={{0,0},{1,2},{2,1},{3,3},{4,4},{5,6},{6,5},{7,7},{8,8},{9,10},{10,9... | collective-permute-start | bytes 393224 | tf_op jit(solution)/shard_map/ppermute | solution.py:467
  40.2 1.5 copy-start.18
  41.0 5.9 %collective-permute-start.12 = (f32[4,128,128]{2,1,0:T(8,128)S(1)}, f32[4,128,128]{2,1,0:T(8,128)S(1)}, u32[]{:S(2)}, u32[]{:S(2)}) collective-permute-start(f32[4,128,128]{2,1,0:T(8,128)S(1)} %get-tuple-element.147), channel_id=1, source_target_pairs={{0,2},{2,0},{13,15},{15,13},{1,4},{4,1},{3,6},{6,3},{5,8},{8,5},{7... | collective-permute-start | bytes 786440 | tf_op jit(solution)/shard_map/ppermute | solution.py:517
  41.1 5.8 %collective-permute-start.13 = (f32[4,128,128]{2,1,0:T(8,128)S(1)}, f32[4,128,128]{2,1,0:T(8,128)S(1)}, u32[]{:S(2)}, u32[]{:S(2)}) collective-permute-start(f32[4,128,128]{2,1,0:T(8,128)S(1)} %get-tuple-element.148), channel_id=1, source_target_pairs={{0,1},{1,0},{2,3},{3,2},{4,5},{5,4},{6,7},{7,6},{8,9},{9,8},{10,11... | collective-permute-start | bytes 786440 | tf_op jit(solution)/shard_map/ppermute | solution.py:518
  47.7 5.9 %collective-permute-start.14 = (f32[4,128,128]{2,1,0:T(8,128)S(1)}, f32[4,128,128]{2,1,0:T(8,128)S(1)}, u32[]{:S(2)}, u32[]{:S(2)}) collective-permute-start(f32[4,128,128]{2,1,0:T(8,128)S(1)} %get-tuple-element.150), channel_id=1, source_target_pairs={{0,2},{2,0},{13,15},{15,13},{1,4},{4,1},{3,6},{6,3},{5,8},{8,5},{7... | collective-permute-start | bytes 786440 | tf_op jit(solution)/shard_map/ppermute | solution.py:517
  47.7 5.8 %collective-permute-start.15 = (f32[4,128,128]{2,1,0:T(8,128)S(1)}, f32[4,128,128]{2,1,0:T(8,128)S(1)}, u32[]{:S(2)}, u32[]{:S(2)}) collective-permute-start(f32[4,128,128]{2,1,0:T(8,128)S(1)} %get-tuple-element.151), channel_id=1, source_target_pairs={{0,1},{1,0},{2,3},{3,2},{4,5},{5,4},{6,7},{7,6},{8,9},{9,8},{10,11... | collective-permute-start | bytes 786440 | tf_op jit(solution)/shard_map/ppermute | solution.py:518
  54.3 5.9 %collective-permute-start.16 = (f32[4,128,128]{2,1,0:T(8,128)S(1)}, f32[4,128,128]{2,1,0:T(8,128)S(1)}, u32[]{:S(2)}, u32[]{:S(2)}) collective-permute-start(f32[4,128,128]{2,1,0:T(8,128)S(1)} %get-tuple-element.156), channel_id=1, source_target_pairs={{0,2},{2,0},{13,15},{15,13},{1,4},{4,1},{3,6},{6,3},{5,8},{8,5},{7... | collective-permute-start | bytes 786440 | tf_op jit(solution)/shard_map/ppermute | solution.py:517
  54.4 5.8 %collective-permute-start.17 = (f32[4,128,128]{2,1,0:T(8,128)S(1)}, f32[4,128,128]{2,1,0:T(8,128)S(1)}, u32[]{:S(2)}, u32[]{:S(2)}) collective-permute-start(f32[4,128,128]{2,1,0:T(8,128)S(1)} %get-tuple-element.157), channel_id=1, source_target_pairs={{0,1},{1,0},{2,3},{3,2},{4,5},{5,4},{6,7},{7,6},{8,9},{9,8},{10,11... | collective-permute-start | bytes 786440 | tf_op jit(solution)/shard_map/ppermute | solution.py:518
  61.0 6.7 %collective-permute-start.18 = (f32[4,128,128]{2,1,0:T(8,128)S(1)}, f32[4,128,128]{2,1,0:T(8,128)S(1)}, u32[]{:S(2)}, u32[]{:S(2)}) collective-permute-start(f32[4,128,128]{2,1,0:T(8,128)S(1)} %get-tuple-element.162), channel_id=1, source_target_pairs={{0,2},{2,0},{13,15},{15,13},{1,4},{4,1},{3,6},{6,3},{5,8},{8,5},{7... | collective-permute-start | bytes 786440 | tf_op jit(solution)/shard_map/ppermute | solution.py:517
  61.1 7.0 %collective-permute-start.11 = (f32[4,128,128]{2,1,0:T(8,128)S(1)}, f32[4,128,128]{2,1,0:T(8,128)S(1)}, u32[]{:S(2)}, u32[]{:S(2)}) collective-permute-start(f32[4,128,128]{2,1,0:T(8,128)S(1)} %get-tuple-element.146), channel_id=1, source_target_pairs={{0,2},{1,0},{2,3},{3,1},{4,6},{5,4},{6,7},{7,5},{8,10},{9,8},{10,1... | collective-permute-start | bytes 786440 | tf_op jit(solution)/shard_map/ppermute | solution.py:467
  62.5 8.2 %collective-permute-start.10 = (f32[4,128,128]{2,1,0:T(8,128)S(1)}, f32[4,128,128]{2,1,0:T(8,128)S(1)}, u32[]{:S(2)}, u32[]{:S(2)}) collective-permute-start(f32[4,128,128]{2,1,0:T(8,128)S(1)} %get-tuple-element.146), channel_id=1, source_target_pairs={{0,0},{1,2},{2,1},{3,3},{4,4},{5,6},{6,5},{7,7},{8,8},{9,10},{10,9... | collective-permute-start | bytes 786440 | tf_op jit(solution)/shard_map/ppermute | solution.py:467
  66.4 4.3 %collective-permute-start.19 = (f32[4,128,128]{2,1,0:T(8,128)S(1)}, f32[4,128,128]{2,1,0:T(8,128)S(1)}, u32[]{:S(2)}, u32[]{:S(2)}) collective-permute-start(f32[4,128,128]{2,1,0:T(8,128)S(1)} %get-tuple-element.163), channel_id=1, source_target_pairs={{0,1},{1,0},{2,3},{3,2},{4,5},{5,4},{6,7},{7,6},{8,9},{9,8},{10,11... | collective-permute-start | bytes 786440 | tf_op jit(solution)/shard_map/ppermute | solution.py:518
  71.5 6.2 %collective-permute-start.20 = (f32[4,128,128]{2,1,0:T(8,128)S(1)}, f32[4,128,128]{2,1,0:T(8,128)S(1)}, u32[]{:S(2)}, u32[]{:S(2)}) collective-permute-start(f32[4,128,128]{2,1,0:T(8,128)S(1)} %get-tuple-element.168), channel_id=1, source_target_pairs={{0,2},{2,0},{13,15},{15,13},{1,4},{4,1},{3,6},{6,3},{5,8},{8,5},{7... | collective-permute-start | bytes 786440 | tf_op jit(solution)/shard_map/ppermute | solution.py:517
  71.5 6.1 %collective-permute-start.21 = (f32[4,128,128]{2,1,0:T(8,128)S(1)}, f32[4,128,128]{2,1,0:T(8,128)S(1)}, u32[]{:S(2)}, u32[]{:S(2)}) collective-permute-start(f32[4,128,128]{2,1,0:T(8,128)S(1)} %get-tuple-element.169), channel_id=1, source_target_pairs={{0,1},{1,0},{2,3},{3,2},{4,5},{5,4},{6,7},{7,6},{8,9},{9,8},{10,11... | collective-permute-start | bytes 786440 | tf_op jit(solution)/shard_map/ppermute | solution.py:518
  78.4 7.2 %collective-permute-start.22 = (f32[4,128,128]{2,1,0:T(8,128)S(1)}, f32[4,128,128]{2,1,0:T(8,128)S(1)}, u32[]{:S(2)}, u32[]{:S(2)}) collective-permute-start(f32[4,128,128]{2,1,0:T(8,128)S(1)} %get-tuple-element.179), channel_id=1, source_target_pairs={{0,2},{2,0},{13,15},{15,13},{1,4},{4,1},{3,6},{6,3},{5,8},{8,5},{7... | collective-permute-start | bytes 786440 | tf_op jit(solution)/shard_map/ppermute | solution.py:517
  78.5 7.2 %collective-permute-start.23 = (f32[4,128,128]{2,1,0:T(8,128)S(1)}, f32[4,128,128]{2,1,0:T(8,128)S(1)}, u32[]{:S(2)}, u32[]{:S(2)}) collective-permute-start(f32[4,128,128]{2,1,0:T(8,128)S(1)} %get-tuple-element.180), channel_id=1, source_target_pairs={{0,1},{1,0},{2,3},{3,2},{4,5},{5,4},{6,7},{7,6},{8,9},{9,8},{10,11... | collective-permute-start | bytes 786440 | tf_op jit(solution)/shard_map/ppermute | solution.py:518
  83.4 9.0 %collective-permute-start.27 = (f32[4,16,8,128]{3,2,1,0:T(8,128)S(1)}, f32[4,16,8,128]{3,2,1,0:T(8,128)S(1)}, u32[]{:S(2)}, u32[]{:S(2)}) collective-permute-start(f32[4,16,8,128]{3,2,1,0:T(8,128)S(1)} %get-tuple-element.191), channel_id=1, source_target_pairs={{0,3},{1,2},{2,1},{3,0},{4,7},{5,6},{6,5},{7,4},{8,11},{9,10},{10,... | collective-permute-start | bytes 786440 | tf_op jit(solution)/shard_map/ppermute | solution.py:579
  83.8 12.8 %collective-permute-start.26 = (f32[4,16,8,128]{3,2,1,0:T(8,128)S(1)}, f32[4,16,8,128]{3,2,1,0:T(8,128)S(1)}, u32[]{:S(2)}, u32[]{:S(2)}) collective-permute-start(f32[4,16,8,128]{3,2,1,0:T(8,128)S(1)} %get-tuple-element.190), channel_id=1, source_target_pairs={{0,2},{1,3},{2,0},{3,1},{4,6},{5,7},{6,4},{7,5},{8,10},{9,11},{10,... | collective-permute-start | bytes 786440 | tf_op jit(solution)/shard_map/ppermute | solution.py:579
  84.8 11.8 %collective-permute-start.25 = (f32[4,16,8,128]{3,2,1,0:T(8,128)S(1)}, f32[4,16,8,128]{3,2,1,0:T(8,128)S(1)}, u32[]{:S(2)}, u32[]{:S(2)}) collective-permute-start(f32[4,16,8,128]{3,2,1,0:T(8,128)S(1)} %get-tuple-element.189), channel_id=1, source_target_pairs={{0,1},{1,0},{2,3},{3,2},{4,5},{5,4},{6,7},{7,6},{8,9},{9,8},{10,11... | collective-permute-start | bytes 786440 | tf_op jit(solution)/shard_map/ppermute | solution.py:579
  86.4 10.2 %collective-permute-start.24 = (f32[4,128,128]{2,1,0:T(8,128)S(1)}, f32[4,128,128]{2,1,0:T(8,128)S(1)}, u32[]{:S(2)}, u32[]{:S(2)}) collective-permute-start(f32[4,128,128]{2,1,0:T(8,128)S(1)} %get-tuple-element.188), channel_id=1, source_target_pairs={{0,2},{2,0},{13,15},{15,13},{1,4},{4,1},{3,6},{6,3},{5,8},{8,5},{7... | collective-permute-start | bytes 786440 | tf_op jit(solution)/shard_map/ppermute | solution.py:517
  86.5 10.3 %collective-permute-start.28 = (f32[4,128,128]{2,1,0:T(8,128)S(1)}, f32[4,128,128]{2,1,0:T(8,128)S(1)}, u32[]{:S(2)}, u32[]{:S(2)}) collective-permute-start(f32[4,128,128]{2,1,0:T(8,128)S(1)} %get-tuple-element.197), channel_id=1, source_target_pairs={{0,1},{1,0},{2,3},{3,2},{4,5},{5,4},{6,7},{7,6},{8,9},{9,8},{10,11... | collective-permute-start | bytes 786440 | tf_op jit(solution)/shard_map/ppermute | solution.py:518
  97.6 9.7 %collective-permute-start.29 = (f32[4,128,128]{2,1,0:T(8,128)S(1)}, f32[4,128,128]{2,1,0:T(8,128)S(1)}, u32[]{:S(2)}, u32[]{:S(2)}) collective-permute-start(f32[4,128,128]{2,1,0:T(8,128)S(1)} %get-tuple-element.203), channel_id=1, source_target_pairs={{0,2},{2,0},{13,15},{15,13},{1,4},{4,1},{3,6},{6,3},{5,8},{8,5},{7... | collective-permute-start | bytes 786440 | tf_op jit(solution)/shard_map/ppermute | solution.py:517
  98.3 9.0 %collective-permute-start.31 = (f32[4,128,128]{2,1,0:T(8,128)S(1)}, f32[4,128,128]{2,1,0:T(8,128)S(1)}, u32[]{:S(2)}, u32[]{:S(2)}) collective-permute-start(f32[4,128,128]{2,1,0:T(8,128)S(1)} %get-tuple-element.206), channel_id=1, source_target_pairs={{0,1},{1,0},{2,3},{3,2},{4,5},{5,4},{6,7},{7,6},{8,9},{9,8},{10,11... | collective-permute-start | bytes 786440 | tf_op jit(solution)/shard_map/ppermute | solution.py:518
  101.3 6.0 %collective-permute-start.30 = (f32[2,16,8,128]{3,2,1,0:T(8,128)S(1)}, f32[2,16,8,128]{3,2,1,0:T(8,128)S(1)}, u32[]{:S(2)}, u32[]{:S(2)}) collective-permute-start(f32[2,16,8,128]{3,2,1,0:T(8,128)S(1)} %get-tuple-element.204), channel_id=1, source_target_pairs={{0,8},{1,9},{2,10},{3,11},{4,12},{5,13},{6,14},{7,15},{8,0},{9,1},... | collective-permute-start | bytes 393224 | tf_op jit(solution)/shard_map/ppermute | solution.py:589
  108.1 12.8 %collective-permute-start.32 = (f32[4,128,128]{2,1,0:T(8,128)S(1)}, f32[4,128,128]{2,1,0:T(8,128)S(1)}, u32[]{:S(2)}, u32[]{:S(2)}) collective-permute-start(f32[4,128,128]{2,1,0:T(8,128)S(1)} %get-tuple-element.215), channel_id=1, source_target_pairs={{0,2},{2,0},{13,15},{15,13},{1,4},{4,1},{3,6},{6,3},{5,8},{8,5},{7... | collective-permute-start | bytes 786440 | tf_op jit(solution)/shard_map/ppermute | solution.py:517
  112.9 8.0 %collective-permute-start.35 = (f32[4,128,128]{2,1,0:T(8,128)S(1)}, f32[4,128,128]{2,1,0:T(8,128)S(1)}, u32[]{:S(2)}, u32[]{:S(2)}) collective-permute-start(f32[4,128,128]{2,1,0:T(8,128)S(1)} %get-tuple-element.220), channel_id=1, source_target_pairs={{0,1},{1,0},{2,3},{3,2},{4,5},{5,4},{6,7},{7,6},{8,9},{9,8},{10,11... | collective-permute-start | bytes 786440 | tf_op jit(solution)/shard_map/ppermute | solution.py:518
  113.8 6.7 %collective-permute-start.34 = (f32[2,16,8,128]{3,2,1,0:T(8,128)S(1)}, f32[2,16,8,128]{3,2,1,0:T(8,128)S(1)}, u32[]{:S(2)}, u32[]{:S(2)}) collective-permute-start(f32[2,16,8,128]{3,2,1,0:T(8,128)S(1)} %get-tuple-element.217), channel_id=1, source_target_pairs={{0,4},{1,5},{2,6},{3,7},{4,0},{5,1},{6,2},{7,3},{8,12},{9,13},{10,... | collective-permute-start | bytes 393224 | tf_op jit(solution)/shard_map/ppermute | solution.py:589
  114.5 6.4 %collective-permute-start.33 = (f32[2,16,8,128]{3,2,1,0:T(8,128)S(1)}, f32[2,16,8,128]{3,2,1,0:T(8,128)S(1)}, u32[]{:S(2)}, u32[]{:S(2)}) collective-permute-start(f32[2,16,8,128]{3,2,1,0:T(8,128)S(1)} %get-tuple-element.216), channel_id=1, source_target_pairs={{0,8},{1,9},{2,10},{3,11},{4,12},{5,13},{6,14},{7,15},{8,0},{9,1},... | collective-permute-start | bytes 393224 | tf_op jit(solution)/shard_map/ppermute | solution.py:589
  120.4 1.2 copy-start.8
  121.7 12.8 %collective-permute-start.36 = (f32[4,128,128]{2,1,0:T(8,128)S(1)}, f32[4,128,128]{2,1,0:T(8,128)S(1)}, u32[]{:S(2)}, u32[]{:S(2)}) collective-permute-start(f32[4,128,128]{2,1,0:T(8,128)S(1)} %get-tuple-element.229), channel_id=1, source_target_pairs={{0,2},{2,0},{13,15},{15,13},{1,4},{4,1},{3,6},{6,3},{5,8},{8,5},{7... | collective-permute-start | bytes 786440 | tf_op jit(solution)/shard_map/ppermute | solution.py:517
  124.9 9.6 %collective-permute-start.39 = (f32[4,128,128]{2,1,0:T(8,128)S(1)}, f32[4,128,128]{2,1,0:T(8,128)S(1)}, u32[]{:S(2)}, u32[]{:S(2)}) collective-permute-start(f32[4,128,128]{2,1,0:T(8,128)S(1)} %get-tuple-element.237), channel_id=1, source_target_pairs={{0,1},{1,0},{2,3},{3,2},{4,5},{5,4},{6,7},{7,6},{8,9},{9,8},{10,11... | collective-permute-start | bytes 786440 | tf_op jit(solution)/shard_map/ppermute | solution.py:518
  125.3 9.2 %collective-permute-start.38 = (f32[2,16,8,128]{3,2,1,0:T(8,128)S(1)}, f32[2,16,8,128]{3,2,1,0:T(8,128)S(1)}, u32[]{:S(2)}, u32[]{:S(2)}) collective-permute-start(f32[2,16,8,128]{3,2,1,0:T(8,128)S(1)} %get-tuple-element.231), channel_id=1, source_target_pairs={{0,4},{1,5},{2,6},{3,7},{4,0},{5,1},{6,2},{7,3},{8,12},{9,13},{10,... | collective-permute-start | bytes 393224 | tf_op jit(solution)/shard_map/ppermute | solution.py:589
  126.8 7.7 %collective-permute-start.37 = (f32[2,16,8,128]{3,2,1,0:T(8,128)S(1)}, f32[2,16,8,128]{3,2,1,0:T(8,128)S(1)}, u32[]{:S(2)}, u32[]{:S(2)}) collective-permute-start(f32[2,16,8,128]{3,2,1,0:T(8,128)S(1)} %get-tuple-element.230), channel_id=1, source_target_pairs={{0,12},{1,13},{2,14},{3,15},{4,8},{5,9},{6,10},{7,11},{8,4},{9,5},... | collective-permute-start | bytes 393224 | tf_op jit(solution)/shard_map/ppermute | solution.py:589
  135.3 10.1 %collective-permute-start.40 = (f32[4,128,128]{2,1,0:T(8,128)S(1)}, f32[4,128,128]{2,1,0:T(8,128)S(1)}, u32[]{:S(2)}, u32[]{:S(2)}) collective-permute-start(f32[4,128,128]{2,1,0:T(8,128)S(1)} %get-tuple-element.244), channel_id=1, source_target_pairs={{0,2},{2,0},{13,15},{15,13},{1,4},{4,1},{3,6},{6,3},{5,8},{8,5},{7... | collective-permute-start | bytes 786440 | tf_op jit(solution)/shard_map/ppermute | solution.py:517
  136.1 9.3 %collective-permute-start.42 = (f32[4,128,128]{2,1,0:T(8,128)S(1)}, f32[4,128,128]{2,1,0:T(8,128)S(1)}, u32[]{:S(2)}, u32[]{:S(2)}) collective-permute-start(f32[4,128,128]{2,1,0:T(8,128)S(1)} %get-tuple-element.248), channel_id=1, source_target_pairs={{0,1},{1,0},{2,3},{3,2},{4,5},{5,4},{6,7},{7,6},{8,9},{9,8},{10,11... | collective-permute-start | bytes 786440 | tf_op jit(solution)/shard_map/ppermute | solution.py:518
  136.7 8.3 %collective-permute-start.41 = (f32[2,16,8,128]{3,2,1,0:T(8,128)S(1)}, f32[2,16,8,128]{3,2,1,0:T(8,128)S(1)}, u32[]{:S(2)}, u32[]{:S(2)}) collective-permute-start(f32[2,16,8,128]{3,2,1,0:T(8,128)S(1)} %get-tuple-element.245), channel_id=1, source_target_pairs={{0,12},{1,13},{2,14},{3,15},{4,8},{5,9},{6,10},{7,11},{8,4},{9,5},... | collective-permute-start | bytes 393224 | tf_op jit(solution)/shard_map/ppermute | solution.py:589
  145.1 3.3 %copy-start.16 = (f32[2,16,8,128]{3,2,1,0:T(8,128)}, f32[2,16,8,128]{3,2,1,0:T(8,128)S(1)}, u32[]{:S(2)}) copy-start(f32[2,16,8,128]{3,2,1,0:T(8,128)S(1)} %collective-permute-done.41.refs_5_) | copy-start | bytes 393220
  148.4 30.0 %all-to-all-start = ((f32[16,16,8,128]{3,2,1,0:T(8,128)}), f32[16,16,8,128]{3,2,1,0:T(8,128)S(1)}, u32[]{:S(2)}, u32[]{:S(2)}) async-start(f32[16,16,8,128]{3,2,1,0:T(8,128)} %get-tuple-element.254), calls=%async_computation | async-start | bytes 2097152 | tf_op jit(solution)/shard_map/all_to_all | solution.py:595
  153.5 16.0 %collective-permute-start.43 = (f32[8,128,128]{2,1,0:T(8,128)}, f32[8,128,128]{2,1,0:T(8,128)S(1)}, u32[]{:S(2)}, u32[]{:S(2)}) collective-permute-start(f32[8,128,128]{2,1,0:T(8,128)} %get-tuple-element.255), channel_id=1, source_target_pairs={{0,0},{1,2},{2,1},{3,3},{4,4},{5,6},{6,5},{7,7},{8,8},{9,10},{10,9... | collective-permute-start | bytes 1572872 | tf_op jit(solution)/shard_map/ppermute | solution.py:596
  156.9 18.5 %collective-permute-start.44 = (f32[8,128,128]{2,1,0:T(8,128)}, f32[8,128,128]{2,1,0:T(8,128)S(1)}, u32[]{:S(2)}, u32[]{:S(2)}) collective-permute-start(f32[8,128,128]{2,1,0:T(8,128)} %get-tuple-element.256), channel_id=1, source_target_pairs={{2,0},{0,1},{3,2},{1,3},{6,4},{4,5},{7,6},{5,7},{10,8},{8,9},{11,1... | collective-permute-start | bytes 1572872 | tf_op jit(solution)/shard_map/ppermute | solution.py:597
  156.9 0.9 copy-start.9
  157.8 0.9 copy-start.11
  158.7 0.9 copy-start.13
  159.6 0.9 copy-start.15
  160.5 0.9 copy-start.17
  (3 other events, 2.5 us)

commit v7 on v6

--- a/solution.py
+++ b/solution.py
@@ -241,14 +241,17 @@
             new[e] = jnp.where(edge, placed(layer), updated)
 
 
-def fill_halos(low, high, cur):
-    layers = cur.shape[0] - 2 * REACH
+def fill_low(low, cur):
     index = lax.axis_index("gz")
-    count = lax.axis_size("gz")
     place = 2 * (index // 4) + my_half()
-    inside = (place > 0) & (place < count // 2 - 1)
+    inside = (place > 0) & (place < lax.axis_size("gz") // 2 - 1)
     for d in range(REACH):
         cur[REACH - 1 - d] = jnp.where(inside, low[d], 0.0)
+
+
+def fill_high(high, cur):
+    layers = cur.shape[0] - 2 * REACH
+    for d in range(REACH):
         cur[REACH + layers + d] = high[REACH - 1 - d]
 
 
@@ -273,17 +276,17 @@
         lax.fori_loop(0, layers, one_layer, 0)
 
 
-def border_layers(layers):
-    return list(range(REACH)) + list(range(layers - REACH, layers))
-
-
-def border_kernel(step, faces, across, along, low, high, traces, speed, *rest):
-    face, (cur_in, prev, cur, new, low_out, high_out) = rest[:faces], rest[faces:]
-    layers = speed.shape[0]
-    fill_halos(low, high, cur)
-    advance(step, across, along, cur, prev, speed, face, new, border_layers(layers))
+def lower_kernel(step, across, along, low, speed, face_a, face_b, traces, cur_in, prev, cur, new, low_out):
+    fill_low(low, cur)
+    advance(step, across, along, cur, prev, speed, (face_a, face_b), new, list(range(REACH)))
     add_trace(step, traces, new)
     low_out[...] = new[REACH : 2 * REACH]
+
+
+def upper_kernel(step, across, along, high, speed, face_a, face_b, cur_in, prev, cur, new, high_out):
+    layers = speed.shape[0]
+    fill_high(high, cur)
+    advance(step, across, along, cur, prev, speed, (face_a, face_b), new, list(range(layers - REACH, layers)))
     high_out[...] = new[layers : layers + REACH]
 
 
@@ -300,8 +303,10 @@
     step, phase, across, along, low, high, traces, speed, face_a, face_b, cur_in, prev, snap_in, cur, new, snap, out_a, out_b, send
 ):
     layers = speed.shape[0]
-    fill_halos(low, high, cur)
-    advance(step, across, along, cur, prev, speed, (face_a, face_b), new, border_layers(layers))
+    fill_low(low, cur)
+    fill_high(high, cur)
+    outer = [*range(REACH), *range(layers - REACH, layers)]
+    advance(step, across, along, cur, prev, speed, (face_a, face_b), new, outer)
     add_trace(step, traces, new)
     keep_snapshot(step, phase, new, snap)
 
@@ -503,34 +508,48 @@
         faces = late if step >= EARLY else early
         wide = len(faces)
         if step < steps - 1:
-            border = pl.pallas_call(
-                functools.partial(border_kernel, step, wide),
-                out_shape=(tall, tall, slab, slab),
-                in_specs=[VMEM] * (8 + wide),
-                out_specs=(VMEM,) * 4,
-                input_output_aliases={6 + wide: 0, 7 + wide: 1},
+            lower = pl.pallas_call(
+                functools.partial(lower_kernel, step),
+                out_shape=(tall, tall, slab),
+                in_specs=[VMEM] * 9,
+                out_specs=(VMEM,) * 3,
+                input_output_aliases={7: 0, 8: 1},
                 compiler_params=PARAMS,
-                cost_estimate=cost(60 * 8 * plane, 4 * 40 * plane),
-                name="border",
+                cost_estimate=cost(60 * 4 * plane, 4 * 20 * plane),
+                name="lower",
             )
-            cur, new, low, high = border(across, along, low, high, traces, speed, *faces, cur, prev)
+            upper = pl.pallas_call(
+                functools.partial(upper_kernel, step),
+                out_shape=(tall, tall, slab),
+                in_specs=[VMEM] * 8,
+                out_specs=(VMEM,) * 3,
+                input_output_aliases={6: 0, 7: 1},
+                compiler_params=PARAMS,
+                cost_estimate=cost(60 * 4 * plane, 4 * 20 * plane),
+                name="upper",
+            )
+            cur, new, low = lower(across, along, low, speed, *faces, traces, cur, prev)
             low = lax.ppermute(low, "gz", between)
+            cur, new, high = upper(across, along, high, speed, *faces, cur, new)
             high = lax.ppermute(high, "gz", within)
-            low, *landed = lax.optimization_barrier((low, *[array for _, array in under_way]))
-            if step == SNAP_EVERY:
+            landed = []
+            if step != SNAP_EVERY:
+                low, *landed = lax.optimization_barrier((low, *[array for _, array in under_way]))
+            if step == SNAP_EVERY + 1:
                 own_strips, *sent = merge(
                     regather_kernel,
                     (f32(4, layers, rows, nx), *[f32(4 // pieces, layers, rows, nx)] * (pieces * (groups - 1))),
                     strip_parts[0],
-                    *landed,
+                    *[array for _, array in under_way],
                 )
                 waiting = [
                     (j < pieces, j, [(i, 4 * ((i // 4) ^ (j // pieces + 1)) + i % 4) for i in range(count)])
                     for j in range(len(sent))
                 ]
-            else:
+            elif step != SNAP_EVERY:
                 arrived += [(part, array) for (part, _), array in zip(under_way, landed)]
-            under_way = []
+            if step != SNAP_EVERY:
+                under_way = []
         else:
             new = prev
         operands = (snap_phase, across, along, speed, *faces, cur, new)
@@ -578,10 +597,10 @@
                 payload, new = lax.optimization_barrier((strip_parts[which], new))
                 under_way.append((which, lax.ppermute(payload, "gz", [(i, i ^ which) for i in range(count)])))
             snap = None
-        slots = max(1, steps - 2 - step)
+        slots = max(1, steps - 1 - step)
         far = [item for item in waiting if not item[0]]
         near = [item for item in waiting if item[0]]
-        chosen = far[: -(-len(far) // slots)] + (near[: -(-len(near) // slots)] if step > SNAP_EVERY or not far else [])
+        chosen = far[: -(-len(far) // slots)] + (near[: -(-len(near) // slots)] if step > SNAP_EVERY + 1 or not far else [])
         waiting = [item for item in waiting if item not in chosen]
         for _, which_part, pairs in chosen:
             payload = sent[which_part]

time: 187 us -> 192 us (1.027)
  starting transfers between devices: 62 us -> 66.2 us
    ppermute x6, waiting for transfers between devices: 20.7 us -> 39.8 us  [local(): under_way.append((which_part, lax.ppermute(payload, 'gz', pairs)))]
    ppermute x1, waiting for transfers between devices: 7.98 us -> 0.01 us  [local(): back_a = lax.ppermute(out_a, 'gz', first_pairs)]
    ppermute x1, waiting for transfers between devices: 5.9 us -> 0.01 us  [local(): back_b = lax.ppermute(out_b, 'gz', back_pairs)]
    ppermute x12, starting transfers between devices: 17.8 us -> 22.3 us  [local(): high = lax.ppermute(high, 'gz', within)]
    ppermute x12, starting transfers between devices: 11 us -> 8.96 us  [local(): low = lax.ppermute(low, 'gz', between)]
    all_to_all x1, waiting for transfers between devices: 1.97 us -> 0.01 us  [local(): second = lax.all_to_all(send, 'gz', split_axis=0, concat_axis=0, tiled=True)]
    pallas_call x11 -> x22, Pallas kernels: 8.64 us -> 9.38 us  [the longest x11 4.88 us: local(): cur, new, low = lower(across, along, low, speed, *faces, traces, cur, prev)]
    unnamed x42 -> x38, local copies, waits for them, and re-layouts: 8.72 us -> 8.7 us
  transfers between devices with their start and end apart: 46 -> 46, of which waited for: 20 -> 16; matrix products, arithmetic and copies ran while one was open for 0% -> 0% of each run, Pallas kernels for 10% -> 15%
where the time goes in v7:
time: 192 us; the launch traced here: 190 us
  waiting for transfers between devices  77.4 us (40%)
  starting transfers between devices  66.2 us (34%)
  Pallas kernels  36.4 us (19%)
  local copies, waits for them, and re-layouts  8.7 us (5%)
    ppermute x6, waiting for transfers between devices, local(): under_way.append((which_part, lax.ppermute(payload, 'gz', pairs)))  39.8 us
    ppermute x12, starting transfers between devices, local(): high = lax.ppermute(high, 'gz', within)  22.3 us
    ppermute x4, waiting for transfers between devices, regroup(): lax.ppermute(a, 'gz', first_pairs)  21.4 us
    pallas_call x11, Pallas kernels, local(): inner(functools.partial(inner_kernel, step, wide, True), out_shape=(tall,...  14.1 us
    ppermute x4, starting transfers between devices, regroup(): lax.ppermute(a, 'gz', first_pairs)  13.2 us
    ppermute x12, waiting for transfers between devices, local(): low = lax.ppermute(low, 'gz', between)  11.3 us
    ppermute x12, starting transfers between devices, local(): low = lax.ppermute(low, 'gz', between)  8.96 us
    unnamed x38, local copies, waits for them, and re-layouts  8.7 us
  transfers between devices with their start and end apart: 46, of which 16 were waited for; matrix products, arithmetic and copies ran while one was open for 0% of the time, Pallas kernels for 15%

profile of v7, /device:TPU:9, one launch (start us, length us, event | category | flops | bytes accessed | tf_op | source)
XLA Modules:
  0.0 190.1 jit_solution(528470082105677693)
XLA Ops:
  0.6 3.7 %collective-permute-start.2 = (f32[8,128,128]{2,1,0:T(8,128)}, f32[8,128,128]{2,1,0:T(8,128)S(1)}, u32[]{:S(2)}, u32[]{:S(2)}) collective-permute-start(f32[8,128,128]{2,1,0:T(8,128)} %param.16), channel_id=1, source_target_pairs={{0,0},{1,2},{2,1},{3,3},{4,4},{5,6},{6,5},{7,7},{8,8},{9,10},{10,9... | collective-permute-start | bytes 1572872 | tf_op jit(solution)/shard_map/ppermute | solution.py:489
  4.4 1.0 copy-done.3
  5.4 1.0 copy-done.4
  6.5 2.1 %collective-permute-start.6 = (f32[8,128,128]{2,1,0:T(8,128)S(1)}, f32[8,128,128]{2,1,0:T(8,128)S(1)}, u32[]{:S(2)}, u32[]{:S(2)}) collective-permute-start(f32[8,128,128]{2,1,0:T(8,128)S(1)} %get-tuple-element.154), channel_id=1, source_target_pairs={{0,0},{1,2},{2,1},{3,3},{4,4},{5,6},{6,5},{7,7},{8,8},{9,10},{10,9... | collective-permute-start | bytes 1572872 | tf_op jit(solution)/shard_map/ppermute | solution.py:472
  8.6 1.0 copy-done.5
  9.7 1.0 copy-done.6
  10.8 3.6 %collective-permute-start = (f32[8,128,128]{2,1,0:T(8,128)S(1)}, f32[8,128,128]{2,1,0:T(8,128)S(1)}, u32[]{:S(2)}, u32[]{:S(2)}) collective-permute-start(f32[8,128,128]{2,1,0:T(8,128)S(1)} %get-tuple-element.149), channel_id=1, source_target_pairs={{0,0},{1,2},{2,1},{3,3},{4,4},{5,6},{6,5},{7,7},{8,8},{9,10},{10,9... | collective-permute-start | bytes 1572872 | tf_op jit(solution)/shard_map/ppermute | solution.py:472
  14.7 8.6 %collective-permute-done.6.now_a = f32[8,128,128]{2,1,0:T(8,128)S(1)} collective-permute-done((f32[8,128,128]{2,1,0:T(8,128)S(1)}, f32[8,128,128]{2,1,0:T(8,128)S(1)}, u32[]{:S(2)}, u32[]{:S(2)}) %collective-permute-start.6) | collective-permute-done | bytes 524320 | tf_op jit(solution)/shard_map/ppermute | solution.py:472
  23.7 1.0 collective-permute-start.9
  24.7 1.0 prepare.1
  25.7 8.2 %collective-permute-done.before_a = f32[8,128,128]{2,1,0:T(8,128)S(1)} collective-permute-done((f32[8,128,128]{2,1,0:T(8,128)S(1)}, f32[8,128,128]{2,1,0:T(8,128)S(1)}, u32[]{:S(2)}, u32[]{:S(2)}) %collective-permute-start) | collective-permute-done | bytes 524320 | tf_op jit(solution)/shard_map/ppermute | solution.py:472
  33.9 3.6 %collective-permute-start.4 = (f32[2,128,128]{2,1,0:T(8,128)S(1)}, f32[2,128,128]{2,1,0:T(8,128)S(1)}, u32[]{:S(2)}, u32[]{:S(2)}) collective-permute-start(f32[2,128,128]{2,1,0:T(8,128)S(1)} %get-tuple-element.153), channel_id=1, source_target_pairs={{0,0},{1,2},{2,1},{3,3},{4,4},{5,6},{6,5},{7,7},{8,8},{9,10},{10,9... | collective-permute-start | bytes 393224 | tf_op jit(solution)/shard_map/ppermute | solution.py:472
  38.1 2.1 %collective-permute-done.4.face_a.rest_0_ = f32[2,128,128]{2,1,0:T(8,128)S(1)} collective-permute-done((f32[2,128,128]{2,1,0:T(8,128)S(1)}, f32[2,128,128]{2,1,0:T(8,128)S(1)}, u32[]{:S(2)}, u32[]{:S(2)}) %collective-permute-start.4) | collective-permute-done | bytes 131104 | tf_op jit(solution)/shard_map/ppermute | solution.py:472
  41.7 1.3 inner.12
  43.0 3.5 %collective-permute-done.13.low = f32[4,128,128]{2,1,0:T(8,128)S(1)} collective-permute-done((f32[4,128,128]{2,1,0:T(8,128)S(1)}, f32[4,128,128]{2,1,0:T(8,128)S(1)}, u32[]{:S(2)}, u32[]{:S(2)}) %collective-permute-start.13) | collective-permute-done | bytes 262176 | tf_op jit(solution)/shard_map/ppermute | solution.py:532
  47.4 0.9 collective-permute-start.14
  48.3 1.3 inner.13
  49.6 3.2 %collective-permute-done.15.low = f32[4,128,128]{2,1,0:T(8,128)S(1)} collective-permute-done((f32[4,128,128]{2,1,0:T(8,128)S(1)}, f32[4,128,128]{2,1,0:T(8,128)S(1)}, u32[]{:S(2)}, u32[]{:S(2)}) %collective-permute-start.15) | collective-permute-done | bytes 262176 | tf_op jit(solution)/shard_map/ppermute | solution.py:532
  53.7 1.2 collective-permute-start.16
  54.9 1.3 inner.14
  56.2 2.9 %collective-permute-done.17.low = f32[4,128,128]{2,1,0:T(8,128)S(1)} collective-permute-done((f32[4,128,128]{2,1,0:T(8,128)S(1)}, f32[4,128,128]{2,1,0:T(8,128)S(1)}, u32[]{:S(2)}, u32[]{:S(2)}) %collective-permute-start.17) | collective-permute-done | bytes 262176 | tf_op jit(solution)/shard_map/ppermute | solution.py:532
  59.6 1.4 collective-permute-start.11
  61.0 3.9 %collective-permute-start.10 = (f32[4,128,128]{2,1,0:T(8,128)S(1)}, f32[4,128,128]{2,1,0:T(8,128)S(1)}, u32[]{:S(2)}, u32[]{:S(2)}) collective-permute-start(f32[4,128,128]{2,1,0:T(8,128)S(1)} %get-tuple-element.165), channel_id=1, source_target_pairs={{0,0},{1,2},{2,1},{3,3},{4,4},{5,6},{6,5},{7,7},{8,8},{9,10},{10,9... | collective-permute-start | bytes 786440 | tf_op jit(solution)/shard_map/ppermute | solution.py:472
  65.4 1.3 inner.15
  66.7 2.5 %collective-permute-done.10.face_a.rest_0_ = f32[4,128,128]{2,1,0:T(8,128)S(1)} collective-permute-done((f32[4,128,128]{2,1,0:T(8,128)S(1)}, f32[4,128,128]{2,1,0:T(8,128)S(1)}, u32[]{:S(2)}, u32[]{:S(2)}) %collective-permute-start.10) | collective-permute-done | bytes 262176 | tf_op jit(solution)/shard_map/ppermute | solution.py:472
  70.1 3.4 %collective-permute-start.20 = (f32[4,128,128]{2,1,0:T(8,128)S(1)}, f32[4,128,128]{2,1,0:T(8,128)S(1)}, u32[]{:S(2)}, u32[]{:S(2)}) collective-permute-start(f32[4,128,128]{2,1,0:T(8,128)S(1)} %get-tuple-element.195), channel_id=1, source_target_pairs={{0,1},{1,0},{2,3},{3,2},{4,5},{5,4},{6,7},{7,6},{8,9},{9,8},{10,11... | collective-permute-start | bytes 786440 | tf_op jit(solution)/shard_map/ppermute | solution.py:534
  73.5 1.4 inner.16
  74.9 0.8 collective-permute-done.21.low
  76.7 3.4 %collective-permute-start.27 = (f32[4,128,128]{2,1,0:T(8,128)S(1)}, f32[4,128,128]{2,1,0:T(8,128)S(1)}, u32[]{:S(2)}, u32[]{:S(2)}) collective-permute-start(f32[4,128,128]{2,1,0:T(8,128)S(1)} %get-tuple-element.221), channel_id=1, source_target_pairs={{0,1},{1,0},{2,3},{3,2},{4,5},{5,4},{6,7},{7,6},{8,9},{9,8},{10,11... | collective-permute-start | bytes 786440 | tf_op jit(solution)/shard_map/ppermute | solution.py:534
  80.1 1.3 inner.17
  81.5 0.8 collective-permute-done.25.low
  83.5 3.4 %collective-permute-start.29 = (f32[4,128,128]{2,1,0:T(8,128)S(1)}, f32[4,128,128]{2,1,0:T(8,128)S(1)}, u32[]{:S(2)}, u32[]{:S(2)}) collective-permute-start(f32[4,128,128]{2,1,0:T(8,128)S(1)} %get-tuple-element.230), channel_id=1, source_target_pairs={{0,1},{1,0},{2,3},{3,2},{4,5},{5,4},{6,7},{7,6},{8,9},{9,8},{10,11... | collective-permute-start | bytes 786440 | tf_op jit(solution)/shard_map/ppermute | solution.py:534
  86.9 1.4 collective-permute-start.23
  88.3 0.7 collective-permute-start.22
  89.0 1.3 inner.18
  91.2 4.1 %collective-permute-start.32 = (f32[4,128,128]{2,1,0:T(8,128)S(1)}, f32[4,128,128]{2,1,0:T(8,128)S(1)}, u32[]{:S(2)}, u32[]{:S(2)}) collective-permute-start(f32[4,128,128]{2,1,0:T(8,128)S(1)} %get-tuple-element.243), channel_id=1, source_target_pairs={{0,1},{1,0},{2,3},{3,2},{4,5},{5,4},{6,7},{7,6},{8,9},{9,8},{10,11... | collective-permute-start | bytes 786440 | tf_op jit(solution)/shard_map/ppermute | solution.py:534
  95.8 4.4 %collective-permute-done.23.refs_2_ = f32[4,16,8,128]{3,2,1,0:T(8,128)S(1)} collective-permute-done((f32[4,16,8,128]{3,2,1,0:T(8,128)S(1)}, f32[4,16,8,128]{3,2,1,0:T(8,128)S(1)}, u32[]{:S(2)}, u32[]{:S(2)}) %collective-permute-start.23) | collective-permute-done | bytes 262176 | tf_op jit(solution)/shard_map/ppermute | solution.py:598
  100.3 1.3 inner.19
  102.8 4.4 %collective-permute-start.36 = (f32[4,128,128]{2,1,0:T(8,128)S(1)}, f32[4,128,128]{2,1,0:T(8,128)S(1)}, u32[]{:S(2)}, u32[]{:S(2)}) collective-permute-start(f32[4,128,128]{2,1,0:T(8,128)S(1)} %get-tuple-element.259), channel_id=1, source_target_pairs={{0,1},{1,0},{2,3},{3,2},{4,5},{5,4},{6,7},{7,6},{8,9},{9,8},{10,11... | collective-permute-start | bytes 786440 | tf_op jit(solution)/shard_map/ppermute | solution.py:534
  107.2 1.4 inner.20
  108.6 4.5 %collective-permute-done.31.refs_2_ = f32[2,16,8,128]{3,2,1,0:T(8,128)S(1)} collective-permute-done((f32[2,16,8,128]{3,2,1,0:T(8,128)S(1)}, f32[2,16,8,128]{3,2,1,0:T(8,128)S(1)}, u32[]{:S(2)}, u32[]{:S(2)}) %collective-permute-start.31) | collective-permute-done | bytes 131104 | tf_op jit(solution)/shard_map/ppermute | solution.py:608
  113.5 3.9 %collective-permute-start.33 = (f32[4,128,128]{2,1,0:T(8,128)S(1)}, f32[4,128,128]{2,1,0:T(8,128)S(1)}, u32[]{:S(2)}, u32[]{:S(2)}) collective-permute-start(f32[4,128,128]{2,1,0:T(8,128)S(1)} %get-tuple-element.252), channel_id=1, source_target_pairs={{0,2},{2,0},{13,15},{15,13},{1,4},{4,1},{3,6},{6,3},{5,8},{8,5},{7... | collective-permute-start | bytes 786440 | tf_op jit(solution)/shard_map/ppermute | solution.py:532
  117.8 0.8 collective-permute-start.40
  118.7 0.6 collective-permute-start.35
  119.3 1.3 inner.21
  120.6 4.0 %collective-permute-done.35.refs_0_ = f32[2,16,8,128]{3,2,1,0:T(8,128)S(1)} collective-permute-done((f32[2,16,8,128]{3,2,1,0:T(8,128)S(1)}, f32[2,16,8,128]{3,2,1,0:T(8,128)S(1)}, u32[]{:S(2)}, u32[]{:S(2)}) %collective-permute-start.35) | collective-permute-done | bytes 131104 | tf_op jit(solution)/shard_map/ppermute | solution.py:608
  124.6 1.2 collective-permute-done.34.refs_3_
  126.5 3.1 %collective-permute-start.37 = (f32[4,128,128]{2,1,0:T(8,128)S(1)}, f32[4,128,128]{2,1,0:T(8,128)S(1)}, u32[]{:S(2)}, u32[]{:S(2)}) collective-permute-start(f32[4,128,128]{2,1,0:T(8,128)S(1)} %get-tuple-element.268), channel_id=1, source_target_pairs={{0,2},{2,0},{13,15},{15,13},{1,4},{4,1},{3,6},{6,3},{5,8},{8,5},{7... | collective-permute-start | bytes 786440 | tf_op jit(solution)/shard_map/ppermute | solution.py:532
  130.1 2.0 %collective-permute-start.39 = (f32[2,16,8,128]{3,2,1,0:T(8,128)S(1)}, f32[2,16,8,128]{3,2,1,0:T(8,128)S(1)}, u32[]{:S(2)}, u32[]{:S(2)}) collective-permute-start(f32[2,16,8,128]{3,2,1,0:T(8,128)S(1)} %get-tuple-element.270), channel_id=1, source_target_pairs={{0,4},{1,5},{2,6},{3,7},{4,0},{5,1},{6,2},{7,3},{8,12},{9,13},{10,... | collective-permute-start | bytes 393224 | tf_op jit(solution)/shard_map/ppermute | solution.py:608
  132.0 1.3 inner.22
  133.3 0.7 inner.23.prev
  134.0 4.6 %collective-permute-done.39.refs_1_ = f32[2,16,8,128]{3,2,1,0:T(8,128)S(1)} collective-permute-done((f32[2,16,8,128]{3,2,1,0:T(8,128)S(1)}, f32[2,16,8,128]{3,2,1,0:T(8,128)S(1)}, u32[]{:S(2)}, u32[]{:S(2)}) %collective-permute-start.39) | collective-permute-done | bytes 131104 | tf_op jit(solution)/shard_map/ppermute | solution.py:608
  138.6 0.7 copy-done.14
  139.3 3.0 %last.1 = (f32[24,128,128]{2,1,0:T(8,128)S(1)}, f32[24,128,128]{2,1,0:T(8,128)S(1)}, f32[16,16,8,128]{3,2,1,0:T(8,128)S(1)}, f32[8,128,128]{2,1,0:T(8,128)}, f32...) custom-call(s32[2]{0:T(128)S(1)} %copy-done.16, ...), custom_call_target="tpu_custom_call", output_to_operand_aliasing={{0}: (9, {}), {1}: (10, {}), {2}: (11, {})} | custom-call | tf_op jit(solution)/shard_map/last/pallas_call | solution.py:590
  142.3 6.9 %all-to-all-start = ((f32[16,16,8,128]{3,2,1,0:T(8,128)}), f32[16,16,8,128]{3,2,1,0:T(8,128)S(1)}, u32[]{:S(2)}, u32[]{:S(2)}) async-start(f32[16,16,8,128]{3,2,1,0:T(8,128)} %get-tuple-element.288), calls=%async_computation | async-start | bytes 2097152 | tf_op jit(solution)/shard_map/all_to_all | solution.py:614
  149.2 3.4 %collective-permute-start.43 = (f32[8,128,128]{2,1,0:T(8,128)}, f32[8,128,128]{2,1,0:T(8,128)S(1)}, u32[]{:S(2)}, u32[]{:S(2)}) collective-permute-start(f32[8,128,128]{2,1,0:T(8,128)} %get-tuple-element.289), channel_id=1, source_target_pairs={{0,0},{1,2},{2,1},{3,3},{4,4},{5,6},{6,5},{7,7},{8,8},{9,10},{10,9... | collective-permute-start | bytes 1572872 | tf_op jit(solution)/shard_map/ppermute | solution.py:615
  152.6 1.3 collective-permute-start.41
  153.9 25.5 %collective-permute-done.41.refs_5_ = f32[2,16,8,128]{3,2,1,0:T(8,128)S(1)} collective-permute-done((f32[2,16,8,128]{3,2,1,0:T(8,128)S(1)}, f32[2,16,8,128]{3,2,1,0:T(8,128)S(1)}, u32[]{:S(2)}, u32[]{:S(2)}) %collective-permute-start.41) | collective-permute-done | bytes 131104 | tf_op jit(solution)/shard_map/ppermute | solution.py:608
  179.4 0.9 copy-done.9
  180.3 0.9 copy-done.11
  181.3 0.9 copy-done.13
  182.2 0.9 copy-done.15
  183.2 1.1 choose.5
  184.3 5.7 %images.1 = bf16[8,128,8,128]{3,2,1,0:T(8,128)(2,1)} custom-call(bf16[2,256,1024]{2,1,0:T(8,128)(2,1)S(1)} %get-tuple-element.148.shifts, f32[16,16,8,128]{3,2,1,0:T(8,128)S(1)} %shard_map.143.refs_0_, f32[16,16,8,128]{3,2,1,0:T(8,128)S(1)} %all-to-all-done.refs_1_), custom_call_target="tpu_custom_call" | custom-call | tf_op jit(solution)/shard_map/images/pallas_call | solution.py:432
  (111 shorter events, 13.6 us)
Async XLA Ops:
  0.6 13.9 %collective-permute-start.2 = (f32[8,128,128]{2,1,0:T(8,128)}, f32[8,128,128]{2,1,0:T(8,128)S(1)}, u32[]{:S(2)}, u32[]{:S(2)}) collective-permute-start(f32[8,128,128]{2,1,0:T(8,128)} %param.16), channel_id=1, source_target_pairs={{0,0},{1,2},{2,1},{3,3},{4,4},{5,6},{6,5},{7,7},{8,8},{9,10},{10,9... | collective-permute-start | bytes 1572872 | tf_op jit(solution)/shard_map/ppermute | solution.py:489
  4.3 1.0 copy-start.3
  5.4 1.0 copy-start.4
  6.4 18.3 %copy-start.7 = (f32[12,8,8,128]{3,2,1,0:T(8,128)S(1)}, f32[12,8,8,128]{3,2,1,0:T(8,128)}, u32[]{:S(2)}) copy-start(f32[12,8,8,128]{3,2,1,0:T(8,128)} %param.17) | copy-start | bytes 1179652
  6.4 18.3 %copy-start.17 = (s32[12]{0:T(128)S(1)}, s32[12]{0:T(128)}, u32[]{:S(2)}) copy-start(s32[12]{0:T(128)} %face_steps.1) | copy-start | bytes 148
  6.4 18.3 %copy-start.18 = (s32[8]{0:T(128)S(1)}, s32[8]{0:T(128)}, u32[]{:S(2)}) copy-start(s32[8]{0:T(128)} %lags.1) | copy-start | bytes 100
  6.5 16.8 %collective-permute-start.6 = (f32[8,128,128]{2,1,0:T(8,128)S(1)}, f32[8,128,128]{2,1,0:T(8,128)S(1)}, u32[]{:S(2)}, u32[]{:S(2)}) collective-permute-start(f32[8,128,128]{2,1,0:T(8,128)S(1)} %get-tuple-element.154), channel_id=1, source_target_pairs={{0,0},{1,2},{2,1},{3,3},{4,4},{5,6},{6,5},{7,7},{8,8},{9,10},{10,9... | collective-permute-start | bytes 1572872 | tf_op jit(solution)/shard_map/ppermute | solution.py:472
  8.6 14.7 %collective-permute-start.7 = (f32[8,128,128]{2,1,0:T(8,128)S(1)}, f32[8,128,128]{2,1,0:T(8,128)S(1)}, u32[]{:S(2)}, u32[]{:S(2)}) collective-permute-start(f32[8,128,128]{2,1,0:T(8,128)S(1)} %get-tuple-element.155), channel_id=1, source_target_pairs={{0,2},{1,0},{2,3},{3,1},{4,6},{5,4},{6,7},{7,5},{8,10},{9,8},{10,1... | collective-permute-start | bytes 1572872 | tf_op jit(solution)/shard_map/ppermute | solution.py:472
  8.6 1.0 copy-start.5
  9.7 1.0 copy-start.6
  10.8 23.1 %collective-permute-start = (f32[8,128,128]{2,1,0:T(8,128)S(1)}, f32[8,128,128]{2,1,0:T(8,128)S(1)}, u32[]{:S(2)}, u32[]{:S(2)}) collective-permute-start(f32[8,128,128]{2,1,0:T(8,128)S(1)} %get-tuple-element.149), channel_id=1, source_target_pairs={{0,0},{1,2},{2,1},{3,3},{4,4},{5,6},{6,5},{7,7},{8,8},{9,10},{10,9... | collective-permute-start | bytes 1572872 | tf_op jit(solution)/shard_map/ppermute | solution.py:472
  14.5 25.7 %copy-start = (bf16[128,256]{1,0:T(8,128)(2,1)S(1)}, bf16[128,256]{1,0:T(8,128)(2,1)}, u32[]{:S(2)}) copy-start(bf16[128,256]{1,0:T(8,128)(2,1)} %constant.5.clone.along) | copy-start | bytes 196612
  14.5 25.7 %copy-start.1 = (bf16[256,128]{1,0:T(8,128)(2,1)S(1)}, bf16[256,128]{1,0:T(8,128)(2,1)}, u32[]{:S(2)}) copy-start(bf16[256,128]{1,0:T(8,128)(2,1)} %constant.4.clone.across) | copy-start | bytes 196612
  14.5 25.7 %copy-start.2 = (bf16[12,128,128]{2,1,0:T(8,128)(2,1)S(1)}, bf16[12,128,128]{2,1,0:T(8,128)(2,1)}, u32[]{:S(2)}) copy-start(bf16[12,128,128]{2,1,0:T(8,128)(2,1)} %traces.23) | copy-start | bytes 1179652
  14.5 19.4 %collective-permute-start.1 = (f32[8,128,128]{2,1,0:T(8,128)S(1)}, f32[8,128,128]{2,1,0:T(8,128)S(1)}, u32[]{:S(2)}, u32[]{:S(2)}) collective-permute-start(f32[8,128,128]{2,1,0:T(8,128)S(1)} %get-tuple-element.150), channel_id=1, source_target_pairs={{0,2},{1,0},{2,3},{3,1},{4,6},{5,4},{6,7},{7,5},{8,10},{9,8},{10,1... | collective-permute-start | bytes 1572872 | tf_op jit(solution)/shard_map/ppermute | solution.py:472
  14.5 23.0 %collective-permute-start.3 = (f32[8,128,128]{2,1,0:T(8,128)S(1)}, f32[8,128,128]{2,1,0:T(8,128)S(1)}, u32[]{:S(2)}, u32[]{:S(2)}) collective-permute-start(f32[8,128,128]{2,1,0:T(8,128)S(1)} %collective-permute-done.2.speed_a), channel_id=1, source_target_pairs={{0,16},{16,0},{1,17},{17,1},{2,18},{18,2},{3,19},{19,3},{4,20},{20... | collective-permute-start | bytes 1572872 | tf_op jit(solution)/shard_map/ppermute | solution.py:490
  23.7 16.4 %collective-permute-start.9 = (f32[4,128,128]{2,1,0:T(8,128)S(1)}, f32[4,128,128]{2,1,0:T(8,128)S(1)}, u32[]{:S(2)}, u32[]{:S(2)}) collective-permute-start(f32[4,128,128]{2,1,0:T(8,128)S(1)} %get-tuple-element.157), channel_id=1, source_target_pairs={{0,2},{2,0},{13,15},{15,13},{1,4},{4,1},{3,6},{6,3},{5,8},{8,5},{7... | collective-permute-start | bytes 786440 | tf_op jit(solution)/shard_map/ppermute | solution.py:498
  24.7 16.0 %collective-permute-start.8 = (f32[4,128,128]{2,1,0:T(8,128)S(1)}, f32[4,128,128]{2,1,0:T(8,128)S(1)}, u32[]{:S(2)}, u32[]{:S(2)}) collective-permute-start(f32[4,128,128]{2,1,0:T(8,128)S(1)} %get-tuple-element.156), channel_id=1, source_target_pairs={{0,1},{1,0},{2,3},{3,2},{4,5},{5,4},{6,7},{7,6},{8,9},{9,8},{10,11... | collective-permute-start | bytes 786440 | tf_op jit(solution)/shard_map/ppermute | solution.py:499
  33.9 4.2 %collective-permute-start.5 = (f32[2,128,128]{2,1,0:T(8,128)S(1)}, f32[2,128,128]{2,1,0:T(8,128)S(1)}, u32[]{:S(2)}, u32[]{:S(2)}) collective-permute-start(f32[2,128,128]{2,1,0:T(8,128)S(1)} %get-tuple-element.153), channel_id=1, source_target_pairs={{0,2},{1,0},{2,3},{3,1},{4,6},{5,4},{6,7},{7,5},{8,10},{9,8},{10,1... | collective-permute-start | bytes 393224 | tf_op jit(solution)/shard_map/ppermute | solution.py:472
  33.9 6.3 %collective-permute-start.4 = (f32[2,128,128]{2,1,0:T(8,128)S(1)}, f32[2,128,128]{2,1,0:T(8,128)S(1)}, u32[]{:S(2)}, u32[]{:S(2)}) collective-permute-start(f32[2,128,128]{2,1,0:T(8,128)S(1)} %get-tuple-element.153), channel_id=1, source_target_pairs={{0,0},{1,2},{2,1},{3,3},{4,4},{5,6},{6,5},{7,7},{8,8},{9,10},{10,9... | collective-permute-start | bytes 393224 | tf_op jit(solution)/shard_map/ppermute | solution.py:472
  40.6 5.9 %collective-permute-start.13 = (f32[4,128,128]{2,1,0:T(8,128)S(1)}, f32[4,128,128]{2,1,0:T(8,128)S(1)}, u32[]{:S(2)}, u32[]{:S(2)}) collective-permute-start(f32[4,128,128]{2,1,0:T(8,128)S(1)} %get-tuple-element.167), channel_id=1, source_target_pairs={{0,2},{2,0},{13,15},{15,13},{1,4},{4,1},{3,6},{6,3},{5,8},{8,5},{7... | collective-permute-start | bytes 786440 | tf_op jit(solution)/shard_map/ppermute | solution.py:532
  40.7 1.0 copy-start.16
  41.1 5.9 %collective-permute-start.12 = (f32[4,128,128]{2,1,0:T(8,128)S(1)}, f32[4,128,128]{2,1,0:T(8,128)S(1)}, u32[]{:S(2)}, u32[]{:S(2)}) collective-permute-start(f32[4,128,128]{2,1,0:T(8,128)S(1)} %get-tuple-element.166), channel_id=1, source_target_pairs={{0,1},{1,0},{2,3},{3,2},{4,5},{5,4},{6,7},{7,6},{8,9},{9,8},{10,11... | collective-permute-start | bytes 786440 | tf_op jit(solution)/shard_map/ppermute | solution.py:534
  46.9 5.9 %collective-permute-start.15 = (f32[4,128,128]{2,1,0:T(8,128)S(1)}, f32[4,128,128]{2,1,0:T(8,128)S(1)}, u32[]{:S(2)}, u32[]{:S(2)}) collective-permute-start(f32[4,128,128]{2,1,0:T(8,128)S(1)} %get-tuple-element.172), channel_id=1, source_target_pairs={{0,2},{2,0},{13,15},{15,13},{1,4},{4,1},{3,6},{6,3},{5,8},{8,5},{7... | collective-permute-start | bytes 786440 | tf_op jit(solution)/shard_map/ppermute | solution.py:532
  47.4 5.9 %collective-permute-start.14 = (f32[4,128,128]{2,1,0:T(8,128)S(1)}, f32[4,128,128]{2,1,0:T(8,128)S(1)}, u32[]{:S(2)}, u32[]{:S(2)}) collective-permute-start(f32[4,128,128]{2,1,0:T(8,128)S(1)} %get-tuple-element.171), channel_id=1, source_target_pairs={{0,1},{1,0},{2,3},{3,2},{4,5},{5,4},{6,7},{7,6},{8,9},{9,8},{10,11... | collective-permute-start | bytes 786440 | tf_op jit(solution)/shard_map/ppermute | solution.py:534
  53.2 5.9 %collective-permute-start.17 = (f32[4,128,128]{2,1,0:T(8,128)S(1)}, f32[4,128,128]{2,1,0:T(8,128)S(1)}, u32[]{:S(2)}, u32[]{:S(2)}) collective-permute-start(f32[4,128,128]{2,1,0:T(8,128)S(1)} %get-tuple-element.180), channel_id=1, source_target_pairs={{0,2},{2,0},{13,15},{15,13},{1,4},{4,1},{3,6},{6,3},{5,8},{8,5},{7... | collective-permute-start | bytes 786440 | tf_op jit(solution)/shard_map/ppermute | solution.py:532
  53.7 11.2 %collective-permute-start.16 = (f32[4,128,128]{2,1,0:T(8,128)S(1)}, f32[4,128,128]{2,1,0:T(8,128)S(1)}, u32[]{:S(2)}, u32[]{:S(2)}) collective-permute-start(f32[4,128,128]{2,1,0:T(8,128)S(1)} %get-tuple-element.179), channel_id=1, source_target_pairs={{0,1},{1,0},{2,3},{3,2},{4,5},{5,4},{6,7},{7,6},{8,9},{9,8},{10,11... | collective-permute-start | bytes 786440 | tf_op jit(solution)/shard_map/ppermute | solution.py:534
  59.5 7.2 %collective-permute-start.19 = (f32[4,128,128]{2,1,0:T(8,128)S(1)}, f32[4,128,128]{2,1,0:T(8,128)S(1)}, u32[]{:S(2)}, u32[]{:S(2)}) collective-permute-start(f32[4,128,128]{2,1,0:T(8,128)S(1)} %get-tuple-element.188), channel_id=1, source_target_pairs={{0,2},{2,0},{13,15},{15,13},{1,4},{4,1},{3,6},{6,3},{5,8},{8,5},{7... | collective-permute-start | bytes 786440 | tf_op jit(solution)/shard_map/ppermute | solution.py:532
  59.6 7.1 %collective-permute-start.11 = (f32[4,128,128]{2,1,0:T(8,128)S(1)}, f32[4,128,128]{2,1,0:T(8,128)S(1)}, u32[]{:S(2)}, u32[]{:S(2)}) collective-permute-start(f32[4,128,128]{2,1,0:T(8,128)S(1)} %get-tuple-element.165), channel_id=1, source_target_pairs={{0,2},{1,0},{2,3},{3,1},{4,6},{5,4},{6,7},{7,5},{8,10},{9,8},{10,1... | collective-permute-start | bytes 786440 | tf_op jit(solution)/shard_map/ppermute | solution.py:472
  61.0 8.2 %collective-permute-start.10 = (f32[4,128,128]{2,1,0:T(8,128)S(1)}, f32[4,128,128]{2,1,0:T(8,128)S(1)}, u32[]{:S(2)}, u32[]{:S(2)}) collective-permute-start(f32[4,128,128]{2,1,0:T(8,128)S(1)} %get-tuple-element.165), channel_id=1, source_target_pairs={{0,0},{1,2},{2,1},{3,3},{4,4},{5,6},{6,5},{7,7},{8,8},{9,10},{10,9... | collective-permute-start | bytes 786440 | tf_op jit(solution)/shard_map/ppermute | solution.py:472
  65.3 4.4 %collective-permute-start.18 = (f32[4,128,128]{2,1,0:T(8,128)S(1)}, f32[4,128,128]{2,1,0:T(8,128)S(1)}, u32[]{:S(2)}, u32[]{:S(2)}) collective-permute-start(f32[4,128,128]{2,1,0:T(8,128)S(1)} %get-tuple-element.187), channel_id=1, source_target_pairs={{0,1},{1,0},{2,3},{3,2},{4,5},{5,4},{6,7},{7,6},{8,9},{9,8},{10,11... | collective-permute-start | bytes 786440 | tf_op jit(solution)/shard_map/ppermute | solution.py:534
  69.6 6.2 %collective-permute-start.21 = (f32[4,128,128]{2,1,0:T(8,128)S(1)}, f32[4,128,128]{2,1,0:T(8,128)S(1)}, u32[]{:S(2)}, u32[]{:S(2)}) collective-permute-start(f32[4,128,128]{2,1,0:T(8,128)S(1)} %get-tuple-element.196), channel_id=1, source_target_pairs={{0,2},{2,0},{13,15},{15,13},{1,4},{4,1},{3,6},{6,3},{5,8},{8,5},{7... | collective-permute-start | bytes 786440 | tf_op jit(solution)/shard_map/ppermute | solution.py:532
  70.1 6.2 %collective-permute-start.20 = (f32[4,128,128]{2,1,0:T(8,128)S(1)}, f32[4,128,128]{2,1,0:T(8,128)S(1)}, u32[]{:S(2)}, u32[]{:S(2)}) collective-permute-start(f32[4,128,128]{2,1,0:T(8,128)S(1)} %get-tuple-element.195), channel_id=1, source_target_pairs={{0,1},{1,0},{2,3},{3,2},{4,5},{5,4},{6,7},{7,6},{8,9},{9,8},{10,11... | collective-permute-start | bytes 786440 | tf_op jit(solution)/shard_map/ppermute | solution.py:534
  76.2 6.2 %collective-permute-start.25 = (f32[4,128,128]{2,1,0:T(8,128)S(1)}, f32[4,128,128]{2,1,0:T(8,128)S(1)}, u32[]{:S(2)}, u32[]{:S(2)}) collective-permute-start(f32[4,128,128]{2,1,0:T(8,128)S(1)} %get-tuple-element.218), channel_id=1, source_target_pairs={{0,2},{2,0},{13,15},{15,13},{1,4},{4,1},{3,6},{6,3},{5,8},{8,5},{7... | collective-permute-start | bytes 786440 | tf_op jit(solution)/shard_map/ppermute | solution.py:532
  76.7 6.3 %collective-permute-start.27 = (f32[4,128,128]{2,1,0:T(8,128)S(1)}, f32[4,128,128]{2,1,0:T(8,128)S(1)}, u32[]{:S(2)}, u32[]{:S(2)}) collective-permute-start(f32[4,128,128]{2,1,0:T(8,128)S(1)} %get-tuple-element.221), channel_id=1, source_target_pairs={{0,1},{1,0},{2,3},{3,2},{4,5},{5,4},{6,7},{7,6},{8,9},{9,8},{10,11... | collective-permute-start | bytes 786440 | tf_op jit(solution)/shard_map/ppermute | solution.py:534
  83.0 7.3 %collective-permute-start.26 = (f32[4,128,128]{2,1,0:T(8,128)S(1)}, f32[4,128,128]{2,1,0:T(8,128)S(1)}, u32[]{:S(2)}, u32[]{:S(2)}) collective-permute-start(f32[4,128,128]{2,1,0:T(8,128)S(1)} %get-tuple-element.220), channel_id=1, source_target_pairs={{0,2},{2,0},{13,15},{15,13},{1,4},{4,1},{3,6},{6,3},{5,8},{8,5},{7... | collective-permute-start | bytes 786440 | tf_op jit(solution)/shard_map/ppermute | solution.py:532
  83.5 7.3 %collective-permute-start.29 = (f32[4,128,128]{2,1,0:T(8,128)S(1)}, f32[4,128,128]{2,1,0:T(8,128)S(1)}, u32[]{:S(2)}, u32[]{:S(2)}) collective-permute-start(f32[4,128,128]{2,1,0:T(8,128)S(1)} %get-tuple-element.230), channel_id=1, source_target_pairs={{0,1},{1,0},{2,3},{3,2},{4,5},{5,4},{6,7},{7,6},{8,9},{9,8},{10,11... | collective-permute-start | bytes 786440 | tf_op jit(solution)/shard_map/ppermute | solution.py:534
  86.9 8.9 %collective-permute-start.24 = (f32[4,16,8,128]{3,2,1,0:T(8,128)S(1)}, f32[4,16,8,128]{3,2,1,0:T(8,128)S(1)}, u32[]{:S(2)}, u32[]{:S(2)}) collective-permute-start(f32[4,16,8,128]{3,2,1,0:T(8,128)S(1)} %get-tuple-element.216), channel_id=1, source_target_pairs={{0,3},{1,2},{2,1},{3,0},{4,7},{5,6},{6,5},{7,4},{8,11},{9,10},{10,... | collective-permute-start | bytes 786440 | tf_op jit(solution)/shard_map/ppermute | solution.py:598
  86.9 13.3 %collective-permute-start.23 = (f32[4,16,8,128]{3,2,1,0:T(8,128)S(1)}, f32[4,16,8,128]{3,2,1,0:T(8,128)S(1)}, u32[]{:S(2)}, u32[]{:S(2)}) collective-permute-start(f32[4,16,8,128]{3,2,1,0:T(8,128)S(1)} %get-tuple-element.213), channel_id=1, source_target_pairs={{0,2},{1,3},{2,0},{3,1},{4,6},{5,7},{6,4},{7,5},{8,10},{9,11},{10,... | collective-permute-start | bytes 786440 | tf_op jit(solution)/shard_map/ppermute | solution.py:598
  88.3 11.9 %collective-permute-start.22 = (f32[4,16,8,128]{3,2,1,0:T(8,128)S(1)}, f32[4,16,8,128]{3,2,1,0:T(8,128)S(1)}, u32[]{:S(2)}, u32[]{:S(2)}) collective-permute-start(f32[4,16,8,128]{3,2,1,0:T(8,128)S(1)} %get-tuple-element.210), channel_id=1, source_target_pairs={{0,1},{1,0},{2,3},{3,2},{4,5},{5,4},{6,7},{7,6},{8,9},{9,8},{10,11... | collective-permute-start | bytes 786440 | tf_op jit(solution)/shard_map/ppermute | solution.py:598
  90.7 10.9 %collective-permute-start.28 = (f32[4,128,128]{2,1,0:T(8,128)S(1)}, f32[4,128,128]{2,1,0:T(8,128)S(1)}, u32[]{:S(2)}, u32[]{:S(2)}) collective-permute-start(f32[4,128,128]{2,1,0:T(8,128)S(1)} %get-tuple-element.227), channel_id=1, source_target_pairs={{0,2},{2,0},{13,15},{15,13},{1,4},{4,1},{3,6},{6,3},{5,8},{8,5},{7... | collective-permute-start | bytes 786440 | tf_op jit(solution)/shard_map/ppermute | solution.py:532
  91.2 11.2 %collective-permute-start.32 = (f32[4,128,128]{2,1,0:T(8,128)S(1)}, f32[4,128,128]{2,1,0:T(8,128)S(1)}, u32[]{:S(2)}, u32[]{:S(2)}) collective-permute-start(f32[4,128,128]{2,1,0:T(8,128)S(1)} %get-tuple-element.243), channel_id=1, source_target_pairs={{0,1},{1,0},{2,3},{3,2},{4,5},{5,4},{6,7},{7,6},{8,9},{9,8},{10,11... | collective-permute-start | bytes 786440 | tf_op jit(solution)/shard_map/ppermute | solution.py:534
  102.0 11.0 %collective-permute-start.30 = (f32[4,128,128]{2,1,0:T(8,128)S(1)}, f32[4,128,128]{2,1,0:T(8,128)S(1)}, u32[]{:S(2)}, u32[]{:S(2)}) collective-permute-start(f32[4,128,128]{2,1,0:T(8,128)S(1)} %get-tuple-element.238), channel_id=1, source_target_pairs={{0,2},{2,0},{13,15},{15,13},{1,4},{4,1},{3,6},{6,3},{5,8},{8,5},{7... | collective-permute-start | bytes 786440 | tf_op jit(solution)/shard_map/ppermute | solution.py:532
  102.8 14.6 %collective-permute-start.36 = (f32[4,128,128]{2,1,0:T(8,128)S(1)}, f32[4,128,128]{2,1,0:T(8,128)S(1)}, u32[]{:S(2)}, u32[]{:S(2)}) collective-permute-start(f32[4,128,128]{2,1,0:T(8,128)S(1)} %get-tuple-element.259), channel_id=1, source_target_pairs={{0,1},{1,0},{2,3},{3,2},{4,5},{5,4},{6,7},{7,6},{8,9},{9,8},{10,11... | collective-permute-start | bytes 786440 | tf_op jit(solution)/shard_map/ppermute | solution.py:534
  107.2 5.9 %collective-permute-start.31 = (f32[2,16,8,128]{3,2,1,0:T(8,128)S(1)}, f32[2,16,8,128]{3,2,1,0:T(8,128)S(1)}, u32[]{:S(2)}, u32[]{:S(2)}) collective-permute-start(f32[2,16,8,128]{3,2,1,0:T(8,128)S(1)} %get-tuple-element.239), channel_id=1, source_target_pairs={{0,8},{1,9},{2,10},{3,11},{4,12},{5,13},{6,14},{7,15},{8,0},{9,1},... | collective-permute-start | bytes 393224 | tf_op jit(solution)/shard_map/ppermute | solution.py:608
  113.5 12.3 %collective-permute-start.33 = (f32[4,128,128]{2,1,0:T(8,128)S(1)}, f32[4,128,128]{2,1,0:T(8,128)S(1)}, u32[]{:S(2)}, u32[]{:S(2)}) collective-permute-start(f32[4,128,128]{2,1,0:T(8,128)S(1)} %get-tuple-element.252), channel_id=1, source_target_pairs={{0,2},{2,0},{13,15},{15,13},{1,4},{4,1},{3,6},{6,3},{5,8},{8,5},{7... | collective-permute-start | bytes 786440 | tf_op jit(solution)/shard_map/ppermute | solution.py:532
  117.8 11.7 %collective-permute-start.40 = (f32[4,128,128]{2,1,0:T(8,128)S(1)}, f32[4,128,128]{2,1,0:T(8,128)S(1)}, u32[]{:S(2)}, u32[]{:S(2)}) collective-permute-start(f32[4,128,128]{2,1,0:T(8,128)S(1)} %get-tuple-element.276), channel_id=1, source_target_pairs={{0,1},{1,0},{2,3},{3,2},{4,5},{5,4},{6,7},{7,6},{8,9},{9,8},{10,11... | collective-permute-start | bytes 786440 | tf_op jit(solution)/shard_map/ppermute | solution.py:534
  118.7 5.9 %collective-permute-start.35 = (f32[2,16,8,128]{3,2,1,0:T(8,128)S(1)}, f32[2,16,8,128]{3,2,1,0:T(8,128)S(1)}, u32[]{:S(2)}, u32[]{:S(2)}) collective-permute-start(f32[2,16,8,128]{3,2,1,0:T(8,128)S(1)} %get-tuple-element.254), channel_id=1, source_target_pairs={{0,4},{1,5},{2,6},{3,7},{4,0},{5,1},{6,2},{7,3},{8,12},{9,13},{10,... | collective-permute-start | bytes 393224 | tf_op jit(solution)/shard_map/ppermute | solution.py:608
  119.3 6.5 %collective-permute-start.34 = (f32[2,16,8,128]{3,2,1,0:T(8,128)S(1)}, f32[2,16,8,128]{3,2,1,0:T(8,128)S(1)}, u32[]{:S(2)}, u32[]{:S(2)}) collective-permute-start(f32[2,16,8,128]{3,2,1,0:T(8,128)S(1)} %get-tuple-element.253), channel_id=1, source_target_pairs={{0,8},{1,9},{2,10},{3,11},{4,12},{5,13},{6,14},{7,15},{8,0},{9,1},... | collective-permute-start | bytes 393224 | tf_op jit(solution)/shard_map/ppermute | solution.py:608
  124.6 1.7 copy-start.8
  126.5 12.8 %collective-permute-start.37 = (f32[4,128,128]{2,1,0:T(8,128)S(1)}, f32[4,128,128]{2,1,0:T(8,128)S(1)}, u32[]{:S(2)}, u32[]{:S(2)}) collective-permute-start(f32[4,128,128]{2,1,0:T(8,128)S(1)} %get-tuple-element.268), channel_id=1, source_target_pairs={{0,2},{2,0},{13,15},{15,13},{1,4},{4,1},{3,6},{6,3},{5,8},{8,5},{7... | collective-permute-start | bytes 786440 | tf_op jit(solution)/shard_map/ppermute | solution.py:532
  130.0 9.3 %collective-permute-start.42 = (f32[4,128,128]{2,1,0:T(8,128)S(1)}, f32[4,128,128]{2,1,0:T(8,128)S(1)}, u32[]{:S(2)}, u32[]{:S(2)}) collective-permute-start(f32[4,128,128]{2,1,0:T(8,128)S(1)} %get-tuple-element.285), channel_id=1, source_target_pairs={{0,1},{1,0},{2,3},{3,2},{4,5},{5,4},{6,7},{7,6},{8,9},{9,8},{10,11... | collective-permute-start | bytes 786440 | tf_op jit(solution)/shard_map/ppermute | solution.py:534
  130.1 8.5 %collective-permute-start.39 = (f32[2,16,8,128]{3,2,1,0:T(8,128)S(1)}, f32[2,16,8,128]{3,2,1,0:T(8,128)S(1)}, u32[]{:S(2)}, u32[]{:S(2)}) collective-permute-start(f32[2,16,8,128]{3,2,1,0:T(8,128)S(1)} %get-tuple-element.270), channel_id=1, source_target_pairs={{0,4},{1,5},{2,6},{3,7},{4,0},{5,1},{6,2},{7,3},{8,12},{9,13},{10,... | collective-permute-start | bytes 393224 | tf_op jit(solution)/shard_map/ppermute | solution.py:608
  132.0 6.6 %collective-permute-start.38 = (f32[2,16,8,128]{3,2,1,0:T(8,128)S(1)}, f32[2,16,8,128]{3,2,1,0:T(8,128)S(1)}, u32[]{:S(2)}, u32[]{:S(2)}) collective-permute-start(f32[2,16,8,128]{3,2,1,0:T(8,128)S(1)} %get-tuple-element.269), channel_id=1, source_target_pairs={{0,12},{1,13},{2,14},{3,15},{4,8},{5,9},{6,10},{7,11},{8,4},{9,5},... | collective-permute-start | bytes 393224 | tf_op jit(solution)/shard_map/ppermute | solution.py:608
  138.6 3.7 %copy-start.12 = (f32[2,16,8,128]{3,2,1,0:T(8,128)}, f32[2,16,8,128]{3,2,1,0:T(8,128)S(1)}, u32[]{:S(2)}) copy-start(f32[2,16,8,128]{3,2,1,0:T(8,128)S(1)} %collective-permute-done.39.refs_1_) | copy-start | bytes 393220
  138.6 0.7 copy-start.14
  142.3 42.0 %all-to-all-start = ((f32[16,16,8,128]{3,2,1,0:T(8,128)}), f32[16,16,8,128]{3,2,1,0:T(8,128)S(1)}, u32[]{:S(2)}, u32[]{:S(2)}) async-start(f32[16,16,8,128]{3,2,1,0:T(8,128)} %get-tuple-element.288), calls=%async_computation | async-start | bytes 2097152 | tf_op jit(solution)/shard_map/all_to_all | solution.py:614
  149.2 33.9 %collective-permute-start.43 = (f32[8,128,128]{2,1,0:T(8,128)}, f32[8,128,128]{2,1,0:T(8,128)S(1)}, u32[]{:S(2)}, u32[]{:S(2)}) collective-permute-start(f32[8,128,128]{2,1,0:T(8,128)} %get-tuple-element.289), channel_id=1, source_target_pairs={{0,0},{1,2},{2,1},{3,3},{4,4},{5,6},{6,5},{7,7},{8,8},{9,10},{10,9... | collective-permute-start | bytes 1572872 | tf_op jit(solution)/shard_map/ppermute | solution.py:615
  152.6 30.6 %collective-permute-start.44 = (f32[8,128,128]{2,1,0:T(8,128)}, f32[8,128,128]{2,1,0:T(8,128)S(1)}, u32[]{:S(2)}, u32[]{:S(2)}) collective-permute-start(f32[8,128,128]{2,1,0:T(8,128)} %get-tuple-element.290), channel_id=1, source_target_pairs={{2,0},{0,1},{3,2},{1,3},{6,4},{4,5},{7,6},{5,7},{10,8},{8,9},{11,1... | collective-permute-start | bytes 1572872 | tf_op jit(solution)/shard_map/ppermute | solution.py:616
  152.6 26.8 %collective-permute-start.41 = (f32[2,16,8,128]{3,2,1,0:T(8,128)S(1)}, f32[2,16,8,128]{3,2,1,0:T(8,128)S(1)}, u32[]{:S(2)}, u32[]{:S(2)}) collective-permute-start(f32[2,16,8,128]{3,2,1,0:T(8,128)S(1)} %get-tuple-element.283), channel_id=1, source_target_pairs={{0,12},{1,13},{2,14},{3,15},{4,8},{5,9},{6,10},{7,11},{8,4},{9,5},... | collective-permute-start | bytes 393224 | tf_op jit(solution)/shard_map/ppermute | solution.py:608
  179.4 0.9 copy-start.9
  180.3 0.9 copy-start.11
  181.3 0.9 copy-start.13
  182.2 0.9 copy-start.15
  (1 other events, 0.7 us)

commit v8 on v7

--- a/solution.py
+++ b/solution.py
@@ -55,14 +55,17 @@
     return first, second
 
 
-def pairs_of_halos(count):
-    within = [(i, i ^ 1) for i in range(count)]
-    between = [(0, 2), (2, 0), (count - 3, count - 1), (count - 1, count - 3)]
-    for group in range(count // 4 - 1):
-        for field in range(2):
-            low, high = 4 * group + 2 * field + 1, 4 * group + 4 + 2 * field
-            between += [(low, high), (high, low)]
-    return between, within
+def pairs_of_halos(count, shots):
+    between = []
+    for shot in range(shots):
+        base = shot * count
+        for group in range(count // 4 - 1):
+            for field in range(2):
+                low, high = base + 4 * group + 2 * field + 1, base + 4 * group + 4 + 2 * field
+                between += [(low, high), (high, low)]
+        for end in (0, 2, count - 3, count - 1):
+            between.append((base + end, (shot ^ 1) * count + end if shots % 2 == 0 else base + (end ^ 2)))
+    return between, [(i, i ^ 1) for i in range(count)]
 
 
 def my_field():
@@ -463,7 +466,8 @@
     steps = face_steps.shape[0]
     first_pairs, second_pairs = pairs_to_fields(count)
     back_pairs = [(b, a) for a, b in second_pairs]
-    between, within = pairs_of_halos(count)
+    shots = lax.axis_size("shot")
+    between, within = pairs_of_halos(count, shots)
     band_x, band_y = banded(nx), banded(ny)
     across = jnp.asarray(np.concatenate([band_x, band_x], axis=0), jnp.bfloat16)
     along = jnp.asarray(np.concatenate([band_y, band_y], axis=1), jnp.bfloat16)
@@ -478,7 +482,6 @@
     strips = held(count, layers, rows, nx)
     plane = ny * nx
 
-    shots = lax.axis_size("shot")
     shared = shots % 2 == 0
     if shared:
         both = [
@@ -495,7 +498,7 @@
     late, early, shifts = prepare(saved_faces, face_steps, lag_offsets, nx)
     early = regroup(early, early)
     cur, low, high = merge(merge_now_kernel, (tall, slab, slab), *now)
-    low = lax.ppermute(low, "gz", between)
+    low = lax.ppermute(low, ("shot", "gz"), between)
     high = lax.ppermute(high, "gz", within)
     prev, speed = merge(functools.partial(merge_rest_kernel, shared), (tall, whole), *before, *speed_parts)
 
@@ -529,26 +532,14 @@
                 name="upper",
             )
             cur, new, low = lower(across, along, low, speed, *faces, traces, cur, prev)
-            low = lax.ppermute(low, "gz", between)
+            low = lax.ppermute(low, ("shot", "gz"), between)
             cur, new, high = upper(across, along, high, speed, *faces, cur, new)
             high = lax.ppermute(high, "gz", within)
             landed = []
-            if step != SNAP_EVERY:
+            if step not in (SNAP_EVERY, SNAP_EVERY + 1):
                 low, *landed = lax.optimization_barrier((low, *[array for _, array in under_way]))
-            if step == SNAP_EVERY + 1:
-                own_strips, *sent = merge(
-                    regather_kernel,
-                    (f32(4, layers, rows, nx), *[f32(4 // pieces, layers, rows, nx)] * (pieces * (groups - 1))),
-                    strip_parts[0],
-                    *[array for _, array in under_way],
-                )
-                waiting = [
-                    (j < pieces, j, [(i, 4 * ((i // 4) ^ (j // pieces + 1)) + i % 4) for i in range(count)])
-                    for j in range(len(sent))
-                ]
-            elif step != SNAP_EVERY:
+            if step not in (SNAP_EVERY, SNAP_EVERY + 1):
                 arrived += [(part, array) for (part, _), array in zip(under_way, landed)]
-            if step != SNAP_EVERY:
                 under_way = []
         else:
             new = prev
@@ -597,6 +588,19 @@
                 payload, new = lax.optimization_barrier((strip_parts[which], new))
                 under_way.append((which, lax.ppermute(payload, "gz", [(i, i ^ which) for i in range(count)])))
             snap = None
+        if step == SNAP_EVERY + 1:
+            *landed, new = lax.optimization_barrier((*[array for _, array in under_way], new))
+            own_strips, *sent = merge(
+                regather_kernel,
+                (f32(4, layers, rows, nx), *[f32(4 // pieces, layers, rows, nx)] * (pieces * (groups - 1))),
+                strip_parts[0],
+                *landed,
+            )
+            waiting = [
+                (j < pieces, j, [(i, 4 * ((i // 4) ^ (j // pieces + 1)) + i % 4) for i in range(count)])
+                for j in range(len(sent))
+            ]
+            under_way = []
         slots = max(1, steps - 1 - step)
         far = [item for item in waiting if not item[0]]
         near = [item for item in waiting if item[0]]

time: 192 us -> 187 us (0.974)
  starting transfers between devices: 66.2 us -> 61.4 us
    ppermute x12, starting transfers between devices: 22.3 us -> 17.4 us  [local(): high = lax.ppermute(high, 'gz', within)]
  transfers between devices with their start and end apart: 46 -> 46, of which waited for: 16 -> 17; matrix products, arithmetic and copies ran while one was open for 0% -> 0% of each run, Pallas kernels for 15% -> 15%
where the time goes in v8:
time: 187 us; the launch traced here: 186 us
  waiting for transfers between devices  78.5 us (42%)
  starting transfers between devices  61.4 us (33%)
  Pallas kernels  36.4 us (19%)
  local copies, waits for them, and re-layouts  8.67 us (5%)
    ppermute x6, waiting for transfers between devices, local(): under_way.append((which_part, lax.ppermute(payload, 'gz', pairs)))  38.8 us
    ppermute x4, waiting for transfers between devices, regroup(): lax.ppermute(a, 'gz', first_pairs)  21.4 us
    ppermute x12, starting transfers between devices, local(): high = lax.ppermute(high, 'gz', within)  17.4 us
    ppermute x4, starting transfers between devices, regroup(): lax.ppermute(a, 'gz', first_pairs)  14.1 us
    pallas_call x11, Pallas kernels, local(): inner(functools.partial(inner_kernel, step, wide, True), out_shape=(tall,...  14.1 us
    ppermute x12, waiting for transfers between devices, local(): low = lax.ppermute(low, ('shot', 'gz'), between)  12.8 us
    unnamed x38, local copies, waits for them, and re-layouts  8.67 us
    all_to_all x1, starting transfers between devices, local(): second = lax.all_to_all(send, 'gz', split_axis=0, concat_axis=0, tiled=True)  8.23 us
  transfers between devices with their start and end apart: 46, of which 17 were waited for; matrix products, arithmetic and copies ran while one was open for 0% of the time, Pallas kernels for 15%

profile of v8, /device:TPU:9, one launch (start us, length us, event | category | flops | bytes accessed | tf_op | source)
XLA Modules:
  0.0 186.4 jit_solution(14554776932213399463)
XLA Ops:
  0.6 3.7 %collective-permute-start.2 = (f32[8,128,128]{2,1,0:T(8,128)}, f32[8,128,128]{2,1,0:T(8,128)S(1)}, u32[]{:S(2)}, u32[]{:S(2)}) collective-permute-start(f32[8,128,128]{2,1,0:T(8,128)} %param.16), channel_id=1, source_target_pairs={{0,0},{1,2},{2,1},{3,3},{4,4},{5,6},{6,5},{7,7},{8,8},{9,10},{10,9... | collective-permute-start | bytes 1572872 | tf_op jit(solution)/shard_map/ppermute | solution.py:492
  4.4 1.0 copy-done.3
  5.4 1.0 copy-done.4
  6.5 2.1 %collective-permute-start.6 = (f32[8,128,128]{2,1,0:T(8,128)S(1)}, f32[8,128,128]{2,1,0:T(8,128)S(1)}, u32[]{:S(2)}, u32[]{:S(2)}) collective-permute-start(f32[8,128,128]{2,1,0:T(8,128)S(1)} %get-tuple-element.157), channel_id=1, source_target_pairs={{0,0},{1,2},{2,1},{3,3},{4,4},{5,6},{6,5},{7,7},{8,8},{9,10},{10,9... | collective-permute-start | bytes 1572872 | tf_op jit(solution)/shard_map/ppermute | solution.py:476
  8.6 1.0 copy-done.5
  9.7 1.0 copy-done.6
  10.8 3.6 %collective-permute-start = (f32[8,128,128]{2,1,0:T(8,128)S(1)}, f32[8,128,128]{2,1,0:T(8,128)S(1)}, u32[]{:S(2)}, u32[]{:S(2)}) collective-permute-start(f32[8,128,128]{2,1,0:T(8,128)S(1)} %get-tuple-element.152), channel_id=1, source_target_pairs={{0,0},{1,2},{2,1},{3,3},{4,4},{5,6},{6,5},{7,7},{8,8},{9,10},{10,9... | collective-permute-start | bytes 1572872 | tf_op jit(solution)/shard_map/ppermute | solution.py:476
  14.7 8.6 %collective-permute-done.6.now_a = f32[8,128,128]{2,1,0:T(8,128)S(1)} collective-permute-done((f32[8,128,128]{2,1,0:T(8,128)S(1)}, f32[8,128,128]{2,1,0:T(8,128)S(1)}, u32[]{:S(2)}, u32[]{:S(2)}) %collective-permute-start.6) | collective-permute-done | bytes 524320 | tf_op jit(solution)/shard_map/ppermute | solution.py:476
  23.7 1.0 collective-permute-start.9
  24.7 1.0 prepare.1
  25.7 8.2 %collective-permute-done.before_a = f32[8,128,128]{2,1,0:T(8,128)S(1)} collective-permute-done((f32[8,128,128]{2,1,0:T(8,128)S(1)}, f32[8,128,128]{2,1,0:T(8,128)S(1)}, u32[]{:S(2)}, u32[]{:S(2)}) %collective-permute-start) | collective-permute-done | bytes 524320 | tf_op jit(solution)/shard_map/ppermute | solution.py:476
  33.9 3.6 %collective-permute-start.4 = (f32[2,128,128]{2,1,0:T(8,128)S(1)}, f32[2,128,128]{2,1,0:T(8,128)S(1)}, u32[]{:S(2)}, u32[]{:S(2)}) collective-permute-start(f32[2,128,128]{2,1,0:T(8,128)S(1)} %get-tuple-element.156), channel_id=1, source_target_pairs={{0,0},{1,2},{2,1},{3,3},{4,4},{5,6},{6,5},{7,7},{8,8},{9,10},{10,9... | collective-permute-start | bytes 393224 | tf_op jit(solution)/shard_map/ppermute | solution.py:476
  38.1 2.1 %collective-permute-done.4.face_a.rest_0_ = f32[2,128,128]{2,1,0:T(8,128)S(1)} collective-permute-done((f32[2,128,128]{2,1,0:T(8,128)S(1)}, f32[2,128,128]{2,1,0:T(8,128)S(1)}, u32[]{:S(2)}, u32[]{:S(2)}) %collective-permute-start.4) | collective-permute-done | bytes 131104 | tf_op jit(solution)/shard_map/ppermute | solution.py:476
  41.7 1.3 inner.12
  43.0 3.5 %collective-permute-done.13.low = f32[4,128,128]{2,1,0:T(8,128)S(1)} collective-permute-done((f32[4,128,128]{2,1,0:T(8,128)S(1)}, f32[4,128,128]{2,1,0:T(8,128)S(1)}, u32[]{:S(2)}, u32[]{:S(2)}) %collective-permute-start.13) | collective-permute-done | bytes 262176 | tf_op jit(solution)/shard_map/ppermute | solution.py:535
  47.4 0.6 collective-permute-start.14
  48.0 1.3 inner.13
  49.3 3.5 %collective-permute-done.15.low = f32[4,128,128]{2,1,0:T(8,128)S(1)} collective-permute-done((f32[4,128,128]{2,1,0:T(8,128)S(1)}, f32[4,128,128]{2,1,0:T(8,128)S(1)}, u32[]{:S(2)}, u32[]{:S(2)}) %collective-permute-start.15) | collective-permute-done | bytes 262176 | tf_op jit(solution)/shard_map/ppermute | solution.py:535
  53.7 0.6 collective-permute-start.16
  54.3 1.3 inner.14
  55.6 3.5 %collective-permute-done.17.low = f32[4,128,128]{2,1,0:T(8,128)S(1)} collective-permute-done((f32[4,128,128]{2,1,0:T(8,128)S(1)}, f32[4,128,128]{2,1,0:T(8,128)S(1)}, u32[]{:S(2)}, u32[]{:S(2)}) %collective-permute-start.17) | collective-permute-done | bytes 262176 | tf_op jit(solution)/shard_map/ppermute | solution.py:535
  60.1 4.8 %collective-permute-start.10 = (f32[4,128,128]{2,1,0:T(8,128)S(1)}, f32[4,128,128]{2,1,0:T(8,128)S(1)}, u32[]{:S(2)}, u32[]{:S(2)}) collective-permute-start(f32[4,128,128]{2,1,0:T(8,128)S(1)} %get-tuple-element.168), channel_id=1, source_target_pairs={{0,0},{1,2},{2,1},{3,3},{4,4},{5,6},{6,5},{7,7},{8,8},{9,10},{10,9... | collective-permute-start | bytes 786440 | tf_op jit(solution)/shard_map/ppermute | solution.py:476
  65.4 1.3 inner.15
  66.7 2.5 %collective-permute-done.10.face_a.rest_0_ = f32[4,128,128]{2,1,0:T(8,128)S(1)} collective-permute-done((f32[4,128,128]{2,1,0:T(8,128)S(1)}, f32[4,128,128]{2,1,0:T(8,128)S(1)}, u32[]{:S(2)}, u32[]{:S(2)}) %collective-permute-start.10) | collective-permute-done | bytes 262176 | tf_op jit(solution)/shard_map/ppermute | solution.py:476
  70.1 3.2 %collective-permute-start.20 = (f32[4,128,128]{2,1,0:T(8,128)S(1)}, f32[4,128,128]{2,1,0:T(8,128)S(1)}, u32[]{:S(2)}, u32[]{:S(2)}) collective-permute-start(f32[4,128,128]{2,1,0:T(8,128)S(1)} %get-tuple-element.198), channel_id=1, source_target_pairs={{0,1},{1,0},{2,3},{3,2},{4,5},{5,4},{6,7},{7,6},{8,9},{9,8},{10,11... | collective-permute-start | bytes 786440 | tf_op jit(solution)/shard_map/ppermute | solution.py:537
  73.3 1.4 inner.16
  74.7 1.0 collective-permute-done.21.low
  76.7 2.9 %collective-permute-start.25 = (f32[4,128,128]{2,1,0:T(8,128)S(1)}, f32[4,128,128]{2,1,0:T(8,128)S(1)}, u32[]{:S(2)}, u32[]{:S(2)}) collective-permute-start(f32[4,128,128]{2,1,0:T(8,128)S(1)} %get-tuple-element.220), channel_id=1, source_target_pairs={{0,1},{1,0},{2,3},{3,2},{4,5},{5,4},{6,7},{7,6},{8,9},{9,8},{10,11... | collective-permute-start | bytes 786440 | tf_op jit(solution)/shard_map/ppermute | solution.py:537
  79.6 1.3 inner.17
  81.0 1.3 collective-permute-done.26.low
  83.5 2.6 %collective-permute-start.27 = (f32[4,128,128]{2,1,0:T(8,128)S(1)}, f32[4,128,128]{2,1,0:T(8,128)S(1)}, u32[]{:S(2)}, u32[]{:S(2)}) collective-permute-start(f32[4,128,128]{2,1,0:T(8,128)S(1)} %get-tuple-element.225), channel_id=1, source_target_pairs={{0,1},{1,0},{2,3},{3,2},{4,5},{5,4},{6,7},{7,6},{8,9},{9,8},{10,11... | collective-permute-start | bytes 786440 | tf_op jit(solution)/shard_map/ppermute | solution.py:537
  86.1 1.4 collective-permute-start.23
  87.5 0.7 collective-permute-start.22
  88.3 1.3 inner.18
  90.5 2.2 %collective-permute-start.32 = (f32[4,128,128]{2,1,0:T(8,128)S(1)}, f32[4,128,128]{2,1,0:T(8,128)S(1)}, u32[]{:S(2)}, u32[]{:S(2)}) collective-permute-start(f32[4,128,128]{2,1,0:T(8,128)S(1)} %get-tuple-element.249), channel_id=1, source_target_pairs={{0,1},{1,0},{2,3},{3,2},{4,5},{5,4},{6,7},{7,6},{8,9},{9,8},{10,11... | collective-permute-start | bytes 786440 | tf_op jit(solution)/shard_map/ppermute | solution.py:537
  92.7 1.3 inner.19
  94.0 1.0 collective-permute-done.24.refs_3_
  95.0 4.4 %collective-permute-done.23.refs_2_ = f32[4,16,8,128]{3,2,1,0:T(8,128)S(1)} collective-permute-done((f32[4,16,8,128]{3,2,1,0:T(8,128)S(1)}, f32[4,16,8,128]{3,2,1,0:T(8,128)S(1)}, u32[]{:S(2)}, u32[]{:S(2)}) %collective-permute-start.23) | collective-permute-done | bytes 262176 | tf_op jit(solution)/shard_map/ppermute | solution.py:589
  100.9 2.3 %collective-permute-start.36 = (f32[4,128,128]{2,1,0:T(8,128)S(1)}, f32[4,128,128]{2,1,0:T(8,128)S(1)}, u32[]{:S(2)}, u32[]{:S(2)}) collective-permute-start(f32[4,128,128]{2,1,0:T(8,128)S(1)} %get-tuple-element.265), channel_id=1, source_target_pairs={{0,1},{1,0},{2,3},{3,2},{4,5},{5,4},{6,7},{7,6},{8,9},{9,8},{10,11... | collective-permute-start | bytes 786440 | tf_op jit(solution)/shard_map/ppermute | solution.py:537
  103.2 1.4 inner.20
  104.6 4.5 %collective-permute-done.31.refs_2_ = f32[2,16,8,128]{3,2,1,0:T(8,128)S(1)} collective-permute-done((f32[2,16,8,128]{3,2,1,0:T(8,128)S(1)}, f32[2,16,8,128]{3,2,1,0:T(8,128)S(1)}, u32[]{:S(2)}, u32[]{:S(2)}) %collective-permute-start.31) | collective-permute-done | bytes 131104 | tf_op jit(solution)/shard_map/ppermute | solution.py:612
  109.6 3.0 %collective-permute-start.33 = (f32[4,128,128]{2,1,0:T(8,128)S(1)}, f32[4,128,128]{2,1,0:T(8,128)S(1)}, u32[]{:S(2)}, u32[]{:S(2)}) collective-permute-start(f32[4,128,128]{2,1,0:T(8,128)S(1)} %get-tuple-element.258), channel_id=1, source_target_pairs={{1,4},{4,1},{3,6},{6,3},{5,8},{8,5},{7,10},{10,7},{9,12},{12,9},{1... | collective-permute-start | bytes 786440 | tf_op jit(solution)/shard_map/ppermute | solution.py:535
  113.0 2.0 %collective-permute-start.40 = (f32[4,128,128]{2,1,0:T(8,128)S(1)}, f32[4,128,128]{2,1,0:T(8,128)S(1)}, u32[]{:S(2)}, u32[]{:S(2)}) collective-permute-start(f32[4,128,128]{2,1,0:T(8,128)S(1)} %get-tuple-element.282), channel_id=1, source_target_pairs={{0,1},{1,0},{2,3},{3,2},{4,5},{5,4},{6,7},{7,6},{8,9},{9,8},{10,11... | collective-permute-start | bytes 786440 | tf_op jit(solution)/shard_map/ppermute | solution.py:537
  115.0 1.1 collective-permute-start.35
  116.1 1.3 inner.21
  117.4 4.1 %collective-permute-done.35.refs_0_ = f32[2,16,8,128]{3,2,1,0:T(8,128)S(1)} collective-permute-done((f32[2,16,8,128]{3,2,1,0:T(8,128)S(1)}, f32[2,16,8,128]{3,2,1,0:T(8,128)S(1)}, u32[]{:S(2)}, u32[]{:S(2)}) %collective-permute-start.35) | collective-permute-done | bytes 131104 | tf_op jit(solution)/shard_map/ppermute | solution.py:612
  121.5 1.1 collective-permute-done.34.refs_3_
  123.2 2.7 %collective-permute-start.37 = (f32[4,128,128]{2,1,0:T(8,128)S(1)}, f32[4,128,128]{2,1,0:T(8,128)S(1)}, u32[]{:S(2)}, u32[]{:S(2)}) collective-permute-start(f32[4,128,128]{2,1,0:T(8,128)S(1)} %get-tuple-element.274), channel_id=1, source_target_pairs={{1,4},{4,1},{3,6},{6,3},{5,8},{8,5},{7,10},{10,7},{9,12},{12,9},{1... | collective-permute-start | bytes 786440 | tf_op jit(solution)/shard_map/ppermute | solution.py:535
  126.4 1.6 collective-permute-start.39
  128.0 1.3 inner.22
  129.3 0.7 inner.23.prev
  130.0 3.1 %collective-permute-done.39.refs_1_ = f32[2,16,8,128]{3,2,1,0:T(8,128)S(1)} collective-permute-done((f32[2,16,8,128]{3,2,1,0:T(8,128)S(1)}, f32[2,16,8,128]{3,2,1,0:T(8,128)S(1)}, u32[]{:S(2)}, u32[]{:S(2)}) %collective-permute-start.39) | collective-permute-done | bytes 131104 | tf_op jit(solution)/shard_map/ppermute | solution.py:612
  133.7 0.6 copy-done.14
  134.3 3.0 %last.1 = (f32[24,128,128]{2,1,0:T(8,128)S(1)}, f32[24,128,128]{2,1,0:T(8,128)S(1)}, f32[16,16,8,128]{3,2,1,0:T(8,128)S(1)}, f32[8,128,128]{2,1,0:T(8,128)}, f32...) custom-call(s32[2]{0:T(128)S(1)} %copy-done.16, ...), custom_call_target="tpu_custom_call", output_to_operand_aliasing={{0}: (9, {}), {1}: (10, {}), {2}: (11, {})} | custom-call | tf_op jit(solution)/shard_map/last/pallas_call | solution.py:581
  137.3 8.2 %all-to-all-start = ((f32[16,16,8,128]{3,2,1,0:T(8,128)}), f32[16,16,8,128]{3,2,1,0:T(8,128)S(1)}, u32[]{:S(2)}, u32[]{:S(2)}) async-start(f32[16,16,8,128]{3,2,1,0:T(8,128)} %get-tuple-element.294), calls=%async_computation | async-start | bytes 2097152 | tf_op jit(solution)/shard_map/all_to_all | solution.py:618
  145.5 3.4 %collective-permute-start.43 = (f32[8,128,128]{2,1,0:T(8,128)}, f32[8,128,128]{2,1,0:T(8,128)S(1)}, u32[]{:S(2)}, u32[]{:S(2)}) collective-permute-start(f32[8,128,128]{2,1,0:T(8,128)} %get-tuple-element.295), channel_id=1, source_target_pairs={{0,0},{1,2},{2,1},{3,3},{4,4},{5,6},{6,5},{7,7},{8,8},{9,10},{10,9... | collective-permute-start | bytes 1572872 | tf_op jit(solution)/shard_map/ppermute | solution.py:619
  148.9 1.3 collective-permute-start.41
  150.2 25.5 %collective-permute-done.41.refs_5_ = f32[2,16,8,128]{3,2,1,0:T(8,128)S(1)} collective-permute-done((f32[2,16,8,128]{3,2,1,0:T(8,128)S(1)}, f32[2,16,8,128]{3,2,1,0:T(8,128)S(1)}, u32[]{:S(2)}, u32[]{:S(2)}) %collective-permute-start.41) | collective-permute-done | bytes 131104 | tf_op jit(solution)/shard_map/ppermute | solution.py:612
  175.8 0.9 copy-done.9
  176.7 0.9 copy-done.11
  177.6 0.9 copy-done.13
  178.5 0.9 copy-done.15
  179.5 1.1 choose.5
  180.6 5.7 %images.1 = bf16[8,128,8,128]{3,2,1,0:T(8,128)(2,1)} custom-call(bf16[2,256,1024]{2,1,0:T(8,128)(2,1)S(1)} %get-tuple-element.151.shifts, f32[16,16,8,128]{3,2,1,0:T(8,128)S(1)} %shard_map.143.refs_0_, f32[16,16,8,128]{3,2,1,0:T(8,128)S(1)} %all-to-all-done.refs_1_), custom_call_target="tpu_custom_call" | custom-call | tf_op jit(solution)/shard_map/images/pallas_call | solution.py:435
  (111 shorter events, 14.4 us)
Async XLA Ops:
  0.6 13.9 %collective-permute-start.2 = (f32[8,128,128]{2,1,0:T(8,128)}, f32[8,128,128]{2,1,0:T(8,128)S(1)}, u32[]{:S(2)}, u32[]{:S(2)}) collective-permute-start(f32[8,128,128]{2,1,0:T(8,128)} %param.16), channel_id=1, source_target_pairs={{0,0},{1,2},{2,1},{3,3},{4,4},{5,6},{6,5},{7,7},{8,8},{9,10},{10,9... | collective-permute-start | bytes 1572872 | tf_op jit(solution)/shard_map/ppermute | solution.py:492
  4.3 1.0 copy-start.3
  5.4 1.0 copy-start.4
  6.4 18.3 %copy-start.7 = (f32[12,8,8,128]{3,2,1,0:T(8,128)S(1)}, f32[12,8,8,128]{3,2,1,0:T(8,128)}, u32[]{:S(2)}) copy-start(f32[12,8,8,128]{3,2,1,0:T(8,128)} %param.17) | copy-start | bytes 1179652
  6.4 18.3 %copy-start.17 = (s32[12]{0:T(128)S(1)}, s32[12]{0:T(128)}, u32[]{:S(2)}) copy-start(s32[12]{0:T(128)} %face_steps.1) | copy-start | bytes 148
  6.4 18.3 %copy-start.18 = (s32[8]{0:T(128)S(1)}, s32[8]{0:T(128)}, u32[]{:S(2)}) copy-start(s32[8]{0:T(128)} %lags.1) | copy-start | bytes 100
  6.5 16.8 %collective-permute-start.6 = (f32[8,128,128]{2,1,0:T(8,128)S(1)}, f32[8,128,128]{2,1,0:T(8,128)S(1)}, u32[]{:S(2)}, u32[]{:S(2)}) collective-permute-start(f32[8,128,128]{2,1,0:T(8,128)S(1)} %get-tuple-element.157), channel_id=1, source_target_pairs={{0,0},{1,2},{2,1},{3,3},{4,4},{5,6},{6,5},{7,7},{8,8},{9,10},{10,9... | collective-permute-start | bytes 1572872 | tf_op jit(solution)/shard_map/ppermute | solution.py:476
  8.6 14.7 %collective-permute-start.7 = (f32[8,128,128]{2,1,0:T(8,128)S(1)}, f32[8,128,128]{2,1,0:T(8,128)S(1)}, u32[]{:S(2)}, u32[]{:S(2)}) collective-permute-start(f32[8,128,128]{2,1,0:T(8,128)S(1)} %get-tuple-element.158), channel_id=1, source_target_pairs={{0,2},{1,0},{2,3},{3,1},{4,6},{5,4},{6,7},{7,5},{8,10},{9,8},{10,1... | collective-permute-start | bytes 1572872 | tf_op jit(solution)/shard_map/ppermute | solution.py:476
  8.6 1.0 copy-start.5
  9.7 1.0 copy-start.6
  10.8 23.1 %collective-permute-start = (f32[8,128,128]{2,1,0:T(8,128)S(1)}, f32[8,128,128]{2,1,0:T(8,128)S(1)}, u32[]{:S(2)}, u32[]{:S(2)}) collective-permute-start(f32[8,128,128]{2,1,0:T(8,128)S(1)} %get-tuple-element.152), channel_id=1, source_target_pairs={{0,0},{1,2},{2,1},{3,3},{4,4},{5,6},{6,5},{7,7},{8,8},{9,10},{10,9... | collective-permute-start | bytes 1572872 | tf_op jit(solution)/shard_map/ppermute | solution.py:476
  14.5 25.7 %copy-start = (bf16[128,256]{1,0:T(8,128)(2,1)S(1)}, bf16[128,256]{1,0:T(8,128)(2,1)}, u32[]{:S(2)}) copy-start(bf16[128,256]{1,0:T(8,128)(2,1)} %constant.5.clone.along) | copy-start | bytes 196612
  14.5 25.7 %copy-start.1 = (bf16[256,128]{1,0:T(8,128)(2,1)S(1)}, bf16[256,128]{1,0:T(8,128)(2,1)}, u32[]{:S(2)}) copy-start(bf16[256,128]{1,0:T(8,128)(2,1)} %constant.4.clone.across) | copy-start | bytes 196612
  14.5 25.7 %copy-start.2 = (bf16[12,128,128]{2,1,0:T(8,128)(2,1)S(1)}, bf16[12,128,128]{2,1,0:T(8,128)(2,1)}, u32[]{:S(2)}) copy-start(bf16[12,128,128]{2,1,0:T(8,128)(2,1)} %traces.23) | copy-start | bytes 1179652
  14.5 19.4 %collective-permute-start.1 = (f32[8,128,128]{2,1,0:T(8,128)S(1)}, f32[8,128,128]{2,1,0:T(8,128)S(1)}, u32[]{:S(2)}, u32[]{:S(2)}) collective-permute-start(f32[8,128,128]{2,1,0:T(8,128)S(1)} %get-tuple-element.153), channel_id=1, source_target_pairs={{0,2},{1,0},{2,3},{3,1},{4,6},{5,4},{6,7},{7,5},{8,10},{9,8},{10,1... | collective-permute-start | bytes 1572872 | tf_op jit(solution)/shard_map/ppermute | solution.py:476
  14.5 23.0 %collective-permute-start.3 = (f32[8,128,128]{2,1,0:T(8,128)S(1)}, f32[8,128,128]{2,1,0:T(8,128)S(1)}, u32[]{:S(2)}, u32[]{:S(2)}) collective-permute-start(f32[8,128,128]{2,1,0:T(8,128)S(1)} %collective-permute-done.2.speed_a), channel_id=1, source_target_pairs={{0,16},{16,0},{1,17},{17,1},{2,18},{18,2},{3,19},{19,3},{4,20},{20... | collective-permute-start | bytes 1572872 | tf_op jit(solution)/shard_map/ppermute | solution.py:493
  23.7 16.4 %collective-permute-start.9 = (f32[4,128,128]{2,1,0:T(8,128)S(1)}, f32[4,128,128]{2,1,0:T(8,128)S(1)}, u32[]{:S(2)}, u32[]{:S(2)}) collective-permute-start(f32[4,128,128]{2,1,0:T(8,128)S(1)} %get-tuple-element.160), channel_id=1, source_target_pairs={{1,4},{4,1},{3,6},{6,3},{5,8},{8,5},{7,10},{10,7},{9,12},{12,9},{1... | collective-permute-start | bytes 786440 | tf_op jit(solution)/shard_map/ppermute | solution.py:501
  24.7 16.0 %collective-permute-start.8 = (f32[4,128,128]{2,1,0:T(8,128)S(1)}, f32[4,128,128]{2,1,0:T(8,128)S(1)}, u32[]{:S(2)}, u32[]{:S(2)}) collective-permute-start(f32[4,128,128]{2,1,0:T(8,128)S(1)} %get-tuple-element.159), channel_id=1, source_target_pairs={{0,1},{1,0},{2,3},{3,2},{4,5},{5,4},{6,7},{7,6},{8,9},{9,8},{10,11... | collective-permute-start | bytes 786440 | tf_op jit(solution)/shard_map/ppermute | solution.py:502
  33.9 4.2 %collective-permute-start.5 = (f32[2,128,128]{2,1,0:T(8,128)S(1)}, f32[2,128,128]{2,1,0:T(8,128)S(1)}, u32[]{:S(2)}, u32[]{:S(2)}) collective-permute-start(f32[2,128,128]{2,1,0:T(8,128)S(1)} %get-tuple-element.156), channel_id=1, source_target_pairs={{0,2},{1,0},{2,3},{3,1},{4,6},{5,4},{6,7},{7,5},{8,10},{9,8},{10,1... | collective-permute-start | bytes 393224 | tf_op jit(solution)/shard_map/ppermute | solution.py:476
  33.9 6.3 %collective-permute-start.4 = (f32[2,128,128]{2,1,0:T(8,128)S(1)}, f32[2,128,128]{2,1,0:T(8,128)S(1)}, u32[]{:S(2)}, u32[]{:S(2)}) collective-permute-start(f32[2,128,128]{2,1,0:T(8,128)S(1)} %get-tuple-element.156), channel_id=1, source_target_pairs={{0,0},{1,2},{2,1},{3,3},{4,4},{5,6},{6,5},{7,7},{8,8},{9,10},{10,9... | collective-permute-start | bytes 393224 | tf_op jit(solution)/shard_map/ppermute | solution.py:476
  40.6 5.9 %collective-permute-start.13 = (f32[4,128,128]{2,1,0:T(8,128)S(1)}, f32[4,128,128]{2,1,0:T(8,128)S(1)}, u32[]{:S(2)}, u32[]{:S(2)}) collective-permute-start(f32[4,128,128]{2,1,0:T(8,128)S(1)} %get-tuple-element.170), channel_id=1, source_target_pairs={{1,4},{4,1},{3,6},{6,3},{5,8},{8,5},{7,10},{10,7},{9,12},{12,9},{1... | collective-permute-start | bytes 786440 | tf_op jit(solution)/shard_map/ppermute | solution.py:535
  40.7 1.0 copy-start.16
  41.1 5.9 %collective-permute-start.12 = (f32[4,128,128]{2,1,0:T(8,128)S(1)}, f32[4,128,128]{2,1,0:T(8,128)S(1)}, u32[]{:S(2)}, u32[]{:S(2)}) collective-permute-start(f32[4,128,128]{2,1,0:T(8,128)S(1)} %get-tuple-element.169), channel_id=1, source_target_pairs={{0,1},{1,0},{2,3},{3,2},{4,5},{5,4},{6,7},{7,6},{8,9},{9,8},{10,11... | collective-permute-start | bytes 786440 | tf_op jit(solution)/shard_map/ppermute | solution.py:537
  46.9 5.9 %collective-permute-start.15 = (f32[4,128,128]{2,1,0:T(8,128)S(1)}, f32[4,128,128]{2,1,0:T(8,128)S(1)}, u32[]{:S(2)}, u32[]{:S(2)}) collective-permute-start(f32[4,128,128]{2,1,0:T(8,128)S(1)} %get-tuple-element.175), channel_id=1, source_target_pairs={{1,4},{4,1},{3,6},{6,3},{5,8},{8,5},{7,10},{10,7},{9,12},{12,9},{1... | collective-permute-start | bytes 786440 | tf_op jit(solution)/shard_map/ppermute | solution.py:535
  47.4 5.9 %collective-permute-start.14 = (f32[4,128,128]{2,1,0:T(8,128)S(1)}, f32[4,128,128]{2,1,0:T(8,128)S(1)}, u32[]{:S(2)}, u32[]{:S(2)}) collective-permute-start(f32[4,128,128]{2,1,0:T(8,128)S(1)} %get-tuple-element.174), channel_id=1, source_target_pairs={{0,1},{1,0},{2,3},{3,2},{4,5},{5,4},{6,7},{7,6},{8,9},{9,8},{10,11... | collective-permute-start | bytes 786440 | tf_op jit(solution)/shard_map/ppermute | solution.py:537
  53.2 5.9 %collective-permute-start.17 = (f32[4,128,128]{2,1,0:T(8,128)S(1)}, f32[4,128,128]{2,1,0:T(8,128)S(1)}, u32[]{:S(2)}, u32[]{:S(2)}) collective-permute-start(f32[4,128,128]{2,1,0:T(8,128)S(1)} %get-tuple-element.183), channel_id=1, source_target_pairs={{1,4},{4,1},{3,6},{6,3},{5,8},{8,5},{7,10},{10,7},{9,12},{12,9},{1... | collective-permute-start | bytes 786440 | tf_op jit(solution)/shard_map/ppermute | solution.py:535
  53.7 11.2 %collective-permute-start.16 = (f32[4,128,128]{2,1,0:T(8,128)S(1)}, f32[4,128,128]{2,1,0:T(8,128)S(1)}, u32[]{:S(2)}, u32[]{:S(2)}) collective-permute-start(f32[4,128,128]{2,1,0:T(8,128)S(1)} %get-tuple-element.182), channel_id=1, source_target_pairs={{0,1},{1,0},{2,3},{3,2},{4,5},{5,4},{6,7},{7,6},{8,9},{9,8},{10,11... | collective-permute-start | bytes 786440 | tf_op jit(solution)/shard_map/ppermute | solution.py:537
  59.5 7.2 %collective-permute-start.19 = (f32[4,128,128]{2,1,0:T(8,128)S(1)}, f32[4,128,128]{2,1,0:T(8,128)S(1)}, u32[]{:S(2)}, u32[]{:S(2)}) collective-permute-start(f32[4,128,128]{2,1,0:T(8,128)S(1)} %get-tuple-element.191), channel_id=1, source_target_pairs={{1,4},{4,1},{3,6},{6,3},{5,8},{8,5},{7,10},{10,7},{9,12},{12,9},{1... | collective-permute-start | bytes 786440 | tf_op jit(solution)/shard_map/ppermute | solution.py:535
  59.6 7.1 %collective-permute-start.11 = (f32[4,128,128]{2,1,0:T(8,128)S(1)}, f32[4,128,128]{2,1,0:T(8,128)S(1)}, u32[]{:S(2)}, u32[]{:S(2)}) collective-permute-start(f32[4,128,128]{2,1,0:T(8,128)S(1)} %get-tuple-element.168), channel_id=1, source_target_pairs={{0,2},{1,0},{2,3},{3,1},{4,6},{5,4},{6,7},{7,5},{8,10},{9,8},{10,1... | collective-permute-start | bytes 786440 | tf_op jit(solution)/shard_map/ppermute | solution.py:476
  60.1 9.0 %collective-permute-start.10 = (f32[4,128,128]{2,1,0:T(8,128)S(1)}, f32[4,128,128]{2,1,0:T(8,128)S(1)}, u32[]{:S(2)}, u32[]{:S(2)}) collective-permute-start(f32[4,128,128]{2,1,0:T(8,128)S(1)} %get-tuple-element.168), channel_id=1, source_target_pairs={{0,0},{1,2},{2,1},{3,3},{4,4},{5,6},{6,5},{7,7},{8,8},{9,10},{10,9... | collective-permute-start | bytes 786440 | tf_op jit(solution)/shard_map/ppermute | solution.py:476
  65.3 4.4 %collective-permute-start.18 = (f32[4,128,128]{2,1,0:T(8,128)S(1)}, f32[4,128,128]{2,1,0:T(8,128)S(1)}, u32[]{:S(2)}, u32[]{:S(2)}) collective-permute-start(f32[4,128,128]{2,1,0:T(8,128)S(1)} %get-tuple-element.190), channel_id=1, source_target_pairs={{0,1},{1,0},{2,3},{3,2},{4,5},{5,4},{6,7},{7,6},{8,9},{9,8},{10,11... | collective-permute-start | bytes 786440 | tf_op jit(solution)/shard_map/ppermute | solution.py:537
  69.6 6.2 %collective-permute-start.21 = (f32[4,128,128]{2,1,0:T(8,128)S(1)}, f32[4,128,128]{2,1,0:T(8,128)S(1)}, u32[]{:S(2)}, u32[]{:S(2)}) collective-permute-start(f32[4,128,128]{2,1,0:T(8,128)S(1)} %get-tuple-element.199), channel_id=1, source_target_pairs={{1,4},{4,1},{3,6},{6,3},{5,8},{8,5},{7,10},{10,7},{9,12},{12,9},{1... | collective-permute-start | bytes 786440 | tf_op jit(solution)/shard_map/ppermute | solution.py:535
  70.1 6.2 %collective-permute-start.20 = (f32[4,128,128]{2,1,0:T(8,128)S(1)}, f32[4,128,128]{2,1,0:T(8,128)S(1)}, u32[]{:S(2)}, u32[]{:S(2)}) collective-permute-start(f32[4,128,128]{2,1,0:T(8,128)S(1)} %get-tuple-element.198), channel_id=1, source_target_pairs={{0,1},{1,0},{2,3},{3,2},{4,5},{5,4},{6,7},{7,6},{8,9},{9,8},{10,11... | collective-permute-start | bytes 786440 | tf_op jit(solution)/shard_map/ppermute | solution.py:537
  76.2 6.2 %collective-permute-start.26 = (f32[4,128,128]{2,1,0:T(8,128)S(1)}, f32[4,128,128]{2,1,0:T(8,128)S(1)}, u32[]{:S(2)}, u32[]{:S(2)}) collective-permute-start(f32[4,128,128]{2,1,0:T(8,128)S(1)} %get-tuple-element.221), channel_id=1, source_target_pairs={{1,4},{4,1},{3,6},{6,3},{5,8},{8,5},{7,10},{10,7},{9,12},{12,9},{1... | collective-permute-start | bytes 786440 | tf_op jit(solution)/shard_map/ppermute | solution.py:535
  76.7 6.3 %collective-permute-start.25 = (f32[4,128,128]{2,1,0:T(8,128)S(1)}, f32[4,128,128]{2,1,0:T(8,128)S(1)}, u32[]{:S(2)}, u32[]{:S(2)}) collective-permute-start(f32[4,128,128]{2,1,0:T(8,128)S(1)} %get-tuple-element.220), channel_id=1, source_target_pairs={{0,1},{1,0},{2,3},{3,2},{4,5},{5,4},{6,7},{7,6},{8,9},{9,8},{10,11... | collective-permute-start | bytes 786440 | tf_op jit(solution)/shard_map/ppermute | solution.py:537
  83.0 6.6 %collective-permute-start.28 = (f32[4,128,128]{2,1,0:T(8,128)S(1)}, f32[4,128,128]{2,1,0:T(8,128)S(1)}, u32[]{:S(2)}, u32[]{:S(2)}) collective-permute-start(f32[4,128,128]{2,1,0:T(8,128)S(1)} %get-tuple-element.226), channel_id=1, source_target_pairs={{1,4},{4,1},{3,6},{6,3},{5,8},{8,5},{7,10},{10,7},{9,12},{12,9},{1... | collective-permute-start | bytes 786440 | tf_op jit(solution)/shard_map/ppermute | solution.py:535
  83.5 6.6 %collective-permute-start.27 = (f32[4,128,128]{2,1,0:T(8,128)S(1)}, f32[4,128,128]{2,1,0:T(8,128)S(1)}, u32[]{:S(2)}, u32[]{:S(2)}) collective-permute-start(f32[4,128,128]{2,1,0:T(8,128)S(1)} %get-tuple-element.225), channel_id=1, source_target_pairs={{0,1},{1,0},{2,3},{3,2},{4,5},{5,4},{6,7},{7,6},{8,9},{9,8},{10,11... | collective-permute-start | bytes 786440 | tf_op jit(solution)/shard_map/ppermute | solution.py:537
  86.1 8.9 %collective-permute-start.24 = (f32[4,16,8,128]{3,2,1,0:T(8,128)S(1)}, f32[4,16,8,128]{3,2,1,0:T(8,128)S(1)}, u32[]{:S(2)}, u32[]{:S(2)}) collective-permute-start(f32[4,16,8,128]{3,2,1,0:T(8,128)S(1)} %get-tuple-element.219), channel_id=1, source_target_pairs={{0,3},{1,2},{2,1},{3,0},{4,7},{5,6},{6,5},{7,4},{8,11},{9,10},{10,... | collective-permute-start | bytes 786440 | tf_op jit(solution)/shard_map/ppermute | solution.py:589
  86.1 13.3 %collective-permute-start.23 = (f32[4,16,8,128]{3,2,1,0:T(8,128)S(1)}, f32[4,16,8,128]{3,2,1,0:T(8,128)S(1)}, u32[]{:S(2)}, u32[]{:S(2)}) collective-permute-start(f32[4,16,8,128]{3,2,1,0:T(8,128)S(1)} %get-tuple-element.216), channel_id=1, source_target_pairs={{0,2},{1,3},{2,0},{3,1},{4,6},{5,7},{6,4},{7,5},{8,10},{9,11},{10,... | collective-permute-start | bytes 786440 | tf_op jit(solution)/shard_map/ppermute | solution.py:589
  87.5 11.9 %collective-permute-start.22 = (f32[4,16,8,128]{3,2,1,0:T(8,128)S(1)}, f32[4,16,8,128]{3,2,1,0:T(8,128)S(1)}, u32[]{:S(2)}, u32[]{:S(2)}) collective-permute-start(f32[4,16,8,128]{3,2,1,0:T(8,128)S(1)} %get-tuple-element.213), channel_id=1, source_target_pairs={{0,1},{1,0},{2,3},{3,2},{4,5},{5,4},{6,7},{7,6},{8,9},{9,8},{10,11... | collective-permute-start | bytes 786440 | tf_op jit(solution)/shard_map/ppermute | solution.py:589
  90.0 9.6 %collective-permute-start.29 = (f32[4,128,128]{2,1,0:T(8,128)S(1)}, f32[4,128,128]{2,1,0:T(8,128)S(1)}, u32[]{:S(2)}, u32[]{:S(2)}) collective-permute-start(f32[4,128,128]{2,1,0:T(8,128)S(1)} %get-tuple-element.240), channel_id=1, source_target_pairs={{1,4},{4,1},{3,6},{6,3},{5,8},{8,5},{7,10},{10,7},{9,12},{12,9},{1... | collective-permute-start | bytes 786440 | tf_op jit(solution)/shard_map/ppermute | solution.py:535
  90.5 10.0 %collective-permute-start.32 = (f32[4,128,128]{2,1,0:T(8,128)S(1)}, f32[4,128,128]{2,1,0:T(8,128)S(1)}, u32[]{:S(2)}, u32[]{:S(2)}) collective-permute-start(f32[4,128,128]{2,1,0:T(8,128)S(1)} %get-tuple-element.249), channel_id=1, source_target_pairs={{0,1},{1,0},{2,3},{3,2},{4,5},{5,4},{6,7},{7,6},{8,9},{9,8},{10,11... | collective-permute-start | bytes 786440 | tf_op jit(solution)/shard_map/ppermute | solution.py:537
  100.0 9.1 %collective-permute-start.30 = (f32[4,128,128]{2,1,0:T(8,128)S(1)}, f32[4,128,128]{2,1,0:T(8,128)S(1)}, u32[]{:S(2)}, u32[]{:S(2)}) collective-permute-start(f32[4,128,128]{2,1,0:T(8,128)S(1)} %get-tuple-element.244), channel_id=1, source_target_pairs={{1,4},{4,1},{3,6},{6,3},{5,8},{8,5},{7,10},{10,7},{9,12},{12,9},{1... | collective-permute-start | bytes 786440 | tf_op jit(solution)/shard_map/ppermute | solution.py:535
  100.9 11.6 %collective-permute-start.36 = (f32[4,128,128]{2,1,0:T(8,128)S(1)}, f32[4,128,128]{2,1,0:T(8,128)S(1)}, u32[]{:S(2)}, u32[]{:S(2)}) collective-permute-start(f32[4,128,128]{2,1,0:T(8,128)S(1)} %get-tuple-element.265), channel_id=1, source_target_pairs={{0,1},{1,0},{2,3},{3,2},{4,5},{5,4},{6,7},{7,6},{8,9},{9,8},{10,11... | collective-permute-start | bytes 786440 | tf_op jit(solution)/shard_map/ppermute | solution.py:537
  103.2 5.9 %collective-permute-start.31 = (f32[2,16,8,128]{3,2,1,0:T(8,128)S(1)}, f32[2,16,8,128]{3,2,1,0:T(8,128)S(1)}, u32[]{:S(2)}, u32[]{:S(2)}) collective-permute-start(f32[2,16,8,128]{3,2,1,0:T(8,128)S(1)} %get-tuple-element.245), channel_id=1, source_target_pairs={{0,8},{1,9},{2,10},{3,11},{4,12},{5,13},{6,14},{7,15},{8,0},{9,1},... | collective-permute-start | bytes 393224 | tf_op jit(solution)/shard_map/ppermute | solution.py:612
  109.6 13.0 %collective-permute-start.33 = (f32[4,128,128]{2,1,0:T(8,128)S(1)}, f32[4,128,128]{2,1,0:T(8,128)S(1)}, u32[]{:S(2)}, u32[]{:S(2)}) collective-permute-start(f32[4,128,128]{2,1,0:T(8,128)S(1)} %get-tuple-element.258), channel_id=1, source_target_pairs={{1,4},{4,1},{3,6},{6,3},{5,8},{8,5},{7,10},{10,7},{9,12},{12,9},{1... | collective-permute-start | bytes 786440 | tf_op jit(solution)/shard_map/ppermute | solution.py:535
  113.0 12.9 %collective-permute-start.40 = (f32[4,128,128]{2,1,0:T(8,128)S(1)}, f32[4,128,128]{2,1,0:T(8,128)S(1)}, u32[]{:S(2)}, u32[]{:S(2)}) collective-permute-start(f32[4,128,128]{2,1,0:T(8,128)S(1)} %get-tuple-element.282), channel_id=1, source_target_pairs={{0,1},{1,0},{2,3},{3,2},{4,5},{5,4},{6,7},{7,6},{8,9},{9,8},{10,11... | collective-permute-start | bytes 786440 | tf_op jit(solution)/shard_map/ppermute | solution.py:537
  115.0 6.5 %collective-permute-start.35 = (f32[2,16,8,128]{3,2,1,0:T(8,128)S(1)}, f32[2,16,8,128]{3,2,1,0:T(8,128)S(1)}, u32[]{:S(2)}, u32[]{:S(2)}) collective-permute-start(f32[2,16,8,128]{3,2,1,0:T(8,128)S(1)} %get-tuple-element.260), channel_id=1, source_target_pairs={{0,4},{1,5},{2,6},{3,7},{4,0},{5,1},{6,2},{7,3},{8,12},{9,13},{10,... | collective-permute-start | bytes 393224 | tf_op jit(solution)/shard_map/ppermute | solution.py:612
  116.1 6.4 %collective-permute-start.34 = (f32[2,16,8,128]{3,2,1,0:T(8,128)S(1)}, f32[2,16,8,128]{3,2,1,0:T(8,128)S(1)}, u32[]{:S(2)}, u32[]{:S(2)}) collective-permute-start(f32[2,16,8,128]{3,2,1,0:T(8,128)S(1)} %get-tuple-element.259), channel_id=1, source_target_pairs={{0,8},{1,9},{2,10},{3,11},{4,12},{5,13},{6,14},{7,15},{8,0},{9,1},... | collective-permute-start | bytes 393224 | tf_op jit(solution)/shard_map/ppermute | solution.py:612
  121.5 1.5 copy-start.8
  122.5 0.7 copy-start.10
  123.2 11.1 %collective-permute-start.37 = (f32[4,128,128]{2,1,0:T(8,128)S(1)}, f32[4,128,128]{2,1,0:T(8,128)S(1)}, u32[]{:S(2)}, u32[]{:S(2)}) collective-permute-start(f32[4,128,128]{2,1,0:T(8,128)S(1)} %get-tuple-element.274), channel_id=1, source_target_pairs={{1,4},{4,1},{3,6},{6,3},{5,8},{8,5},{7,10},{10,7},{9,12},{12,9},{1... | collective-permute-start | bytes 786440 | tf_op jit(solution)/shard_map/ppermute | solution.py:535
  126.3 8.0 %collective-permute-start.42 = (f32[4,128,128]{2,1,0:T(8,128)S(1)}, f32[4,128,128]{2,1,0:T(8,128)S(1)}, u32[]{:S(2)}, u32[]{:S(2)}) collective-permute-start(f32[4,128,128]{2,1,0:T(8,128)S(1)} %get-tuple-element.291), channel_id=1, source_target_pairs={{0,1},{1,0},{2,3},{3,2},{4,5},{5,4},{6,7},{7,6},{8,9},{9,8},{10,11... | collective-permute-start | bytes 786440 | tf_op jit(solution)/shard_map/ppermute | solution.py:537
  126.4 6.7 %collective-permute-start.39 = (f32[2,16,8,128]{3,2,1,0:T(8,128)S(1)}, f32[2,16,8,128]{3,2,1,0:T(8,128)S(1)}, u32[]{:S(2)}, u32[]{:S(2)}) collective-permute-start(f32[2,16,8,128]{3,2,1,0:T(8,128)S(1)} %get-tuple-element.276), channel_id=1, source_target_pairs={{0,4},{1,5},{2,6},{3,7},{4,0},{5,1},{6,2},{7,3},{8,12},{9,13},{10,... | collective-permute-start | bytes 393224 | tf_op jit(solution)/shard_map/ppermute | solution.py:612
  128.0 5.7 %collective-permute-start.38 = (f32[2,16,8,128]{3,2,1,0:T(8,128)S(1)}, f32[2,16,8,128]{3,2,1,0:T(8,128)S(1)}, u32[]{:S(2)}, u32[]{:S(2)}) collective-permute-start(f32[2,16,8,128]{3,2,1,0:T(8,128)S(1)} %get-tuple-element.275), channel_id=1, source_target_pairs={{0,12},{1,13},{2,14},{3,15},{4,8},{5,9},{6,10},{7,11},{8,4},{9,5},... | collective-permute-start | bytes 393224 | tf_op jit(solution)/shard_map/ppermute | solution.py:612
  133.1 4.2 %copy-start.12 = (f32[2,16,8,128]{3,2,1,0:T(8,128)}, f32[2,16,8,128]{3,2,1,0:T(8,128)S(1)}, u32[]{:S(2)}) copy-start(f32[2,16,8,128]{3,2,1,0:T(8,128)S(1)} %collective-permute-done.39.refs_1_) | copy-start | bytes 393220
  137.3 43.3 %all-to-all-start = ((f32[16,16,8,128]{3,2,1,0:T(8,128)}), f32[16,16,8,128]{3,2,1,0:T(8,128)S(1)}, u32[]{:S(2)}, u32[]{:S(2)}) async-start(f32[16,16,8,128]{3,2,1,0:T(8,128)} %get-tuple-element.294), calls=%async_computation | async-start | bytes 2097152 | tf_op jit(solution)/shard_map/all_to_all | solution.py:618
  145.5 33.9 %collective-permute-start.43 = (f32[8,128,128]{2,1,0:T(8,128)}, f32[8,128,128]{2,1,0:T(8,128)S(1)}, u32[]{:S(2)}, u32[]{:S(2)}) collective-permute-start(f32[8,128,128]{2,1,0:T(8,128)} %get-tuple-element.295), channel_id=1, source_target_pairs={{0,0},{1,2},{2,1},{3,3},{4,4},{5,6},{6,5},{7,7},{8,8},{9,10},{10,9... | collective-permute-start | bytes 1572872 | tf_op jit(solution)/shard_map/ppermute | solution.py:619
  148.9 30.6 %collective-permute-start.44 = (f32[8,128,128]{2,1,0:T(8,128)}, f32[8,128,128]{2,1,0:T(8,128)S(1)}, u32[]{:S(2)}, u32[]{:S(2)}) collective-permute-start(f32[8,128,128]{2,1,0:T(8,128)} %get-tuple-element.296), channel_id=1, source_target_pairs={{2,0},{0,1},{3,2},{1,3},{6,4},{4,5},{7,6},{5,7},{10,8},{8,9},{11,1... | collective-permute-start | bytes 1572872 | tf_op jit(solution)/shard_map/ppermute | solution.py:620
  148.9 26.8 %collective-permute-start.41 = (f32[2,16,8,128]{3,2,1,0:T(8,128)S(1)}, f32[2,16,8,128]{3,2,1,0:T(8,128)S(1)}, u32[]{:S(2)}, u32[]{:S(2)}) collective-permute-start(f32[2,16,8,128]{3,2,1,0:T(8,128)S(1)} %get-tuple-element.289), channel_id=1, source_target_pairs={{0,12},{1,13},{2,14},{3,15},{4,8},{5,9},{6,10},{7,11},{8,4},{9,5},... | collective-permute-start | bytes 393224 | tf_op jit(solution)/shard_map/ppermute | solution.py:612
  175.8 0.9 copy-start.9
  176.7 0.9 copy-start.11
  177.6 0.9 copy-start.13
  178.5 0.9 copy-start.15
  (1 other events, 0.6 us)

commit v9 on v8

--- a/solution.py
+++ b/solution.py
@@ -368,12 +368,25 @@
 
 
 def image_kernel(shifts, *refs):
-    windows, (out, light, stage, sem) = refs[:-4], refs[-4:]
+    windows, (out, light, parts, stage, sem) = refs[:-5], refs[-5:]
     _, layers, rows, nx = windows[0].shape
     lags, depth = out.shape[:2]
     size = layers * rows
-    blocks = depth // layers
+    groups = depth // (2 * layers)
     table = sweep_table(depth)
+
+    def fill(group, carry):
+        for which in range(2):
+            for window in range(len(windows)):
+                for half in range(2):
+                    first = (2 * window + half) * size
+                    value = windows[window][4 * group + 2 * which + half].reshape(size, nx)
+                    high, low = split(value)
+                    parts[which, group, first : first + size, :nx] = high
+                    parts[which, group, first : first + size, nx:] = low
+        return carry
+
+    lax.fori_loop(0, groups, fill, 0)
 
     carried = jnp.zeros((rows, nx), jnp.float32)
     for d in range(depth):
@@ -387,38 +400,34 @@
         carried = light[d] + carried * (smoothing * table[d])
         light[d] = 1.0 / (carried + damping)
 
-    def put(block, slot):
-        return pltpu.make_async_copy(
-            stage.at[slot], out.at[:, pl.ds(block * layers, layers)], sem.at[slot]
-        )
-
-    def one_block(block, carry):
-        slot = lax.rem(block, 2)
-        device = (block // 2) * 4 + lax.rem(block, 2)
-        pl.when(block >= 2)(lambda: put(block - 2, slot).wait())
-
-        def both(device, window):
-            return jnp.concatenate(split(window[device].reshape(size, nx)), axis=1)
-
-        sources = [both(device, window) for window in windows]
-        receivers = [both(device + 2, window) for window in windows]
-        inverse = light[pl.ds(block * layers, layers)].reshape(size, nx)
-        for lag in range(0, lags, 2):
-            columns = slice(lag * nx, (lag + 2) * nx)
-            raw = 0.0
-            for window in range(len(windows)):
-                raw = raw + jnp.dot(
-                    sources[window], shifts[0, :, columns], preferred_element_type=jnp.float32
-                ) * jnp.dot(receivers[window], shifts[1, :, columns], preferred_element_type=jnp.float32)
+    def put(pair, slot):
+        return pltpu.make_async_copy(stage.at[slot], out.at[pl.ds(2 * pair, 2)], sem.at[slot])
+
+    def one_pair(pair, carry):
+        slot = lax.rem(pair, 2)
+        pl.when(pair >= 2)(lambda: put(pair - 2, slot).wait())
+        columns = pl.ds(pl.multiple_of(pair * 2 * nx, 2 * nx), 2 * nx)
+        toward, away = shifts[0, :, columns], shifts[1, :, columns]
+
+        def one_group(group, carry):
+            moved = jnp.dot(parts[0, group], toward, preferred_element_type=jnp.float32) * jnp.dot(
+                parts[1, group], away, preferred_element_type=jnp.float32
+            )
+            raw = sum(moved[2 * size * window : 2 * size * (window + 1)] for window in range(len(windows)))
+            where = pl.ds(2 * layers * group, 2 * layers)
+            inverse = light[where].reshape(2 * size, nx)
             for i in range(2):
                 value = (raw[:, i * nx : (i + 1) * nx] * inverse).astype(stage.dtype)
-                stage[slot, lag + i] = value.reshape(layers, rows, nx)
-        put(block, slot).start()
+                stage[slot, i, where] = value.reshape(2 * layers, rows, nx)
+            return carry
+
+        lax.fori_loop(0, groups, one_group, 0)
+        put(pair, slot).start()
         return carry
 
-    lax.fori_loop(0, blocks, one_block, 0)
-    for block in (blocks - 2, blocks - 1):
-        put(block, block % 2).wait()
+    lax.fori_loop(0, lags // 2, one_pair, 0)
+    for pair in (lags // 2 - 2, lags // 2 - 1):
+        put(pair, pair % 2).wait()
 
 
 def sweep_table(depth):
@@ -439,7 +448,8 @@
         out_specs=ANY,
         scratch_shapes=[
             pltpu.VMEM((depth, rows, nx), jnp.float32),
-            pltpu.VMEM((2, lags, layers, rows, nx), jnp.bfloat16),
+            pltpu.VMEM((2, count // 4, 2 * len(windows) * layers * rows, 2 * nx), jnp.bfloat16),
+            pltpu.VMEM((2, 2, depth, rows, nx), jnp.bfloat16),
             pltpu.SemaphoreType.DMA((2,)),
         ],
         compiler_params=PARAMS,

time: 187 us -> 189 us (1.011)
  no operation moved by 1% of the time
where the time goes in v9:
time: 189 us; the launch traced here: 188 us
  waiting for transfers between devices  78.5 us (42%)
  starting transfers between devices  61.4 us (32%)
  Pallas kernels  37.5 us (20%)
  local copies, waits for them, and re-layouts  8.67 us (5%)
    ppermute x6, waiting for transfers between devices, local(): under_way.append((which_part, lax.ppermute(payload, 'gz', pairs)))  38.8 us
    ppermute x4, waiting for transfers between devices, regroup(): lax.ppermute(a, 'gz', first_pairs)  21.4 us
    ppermute x12, starting transfers between devices, local(): high = lax.ppermute(high, 'gz', within)  17.4 us
    ppermute x4, starting transfers between devices, regroup(): lax.ppermute(a, 'gz', first_pairs)  14.1 us
    pallas_call x11, Pallas kernels, local(): inner(functools.partial(inner_kernel, step, wide, True), out_shape=(tall,...  14.1 us
    ppermute x12, waiting for transfers between devices, local(): low = lax.ppermute(low, ('shot', 'gz'), between)  12.8 us
    unnamed x38, local copies, waits for them, and re-layouts  8.67 us
    all_to_all x1, starting transfers between devices, local(): second = lax.all_to_all(send, 'gz', split_axis=0, concat_axis=0, tiled=True)  8.23 us
  transfers between devices with their start and end apart: 46, of which 17 were waited for; matrix products, arithmetic and copies ran while one was open for 0% of the time, Pallas kernels for 15%

profile of v9, /device:TPU:9, one launch (start us, length us, event | category | flops | bytes accessed | tf_op | source)
XLA Modules:
  0.0 187.6 jit_solution(8784317204837877457)
XLA Ops:
  0.6 3.7 %collective-permute-start.2 = (f32[8,128,128]{2,1,0:T(8,128)}, f32[8,128,128]{2,1,0:T(8,128)S(1)}, u32[]{:S(2)}, u32[]{:S(2)}) collective-permute-start(f32[8,128,128]{2,1,0:T(8,128)} %param.16), channel_id=1, source_target_pairs={{0,0},{1,2},{2,1},{3,3},{4,4},{5,6},{6,5},{7,7},{8,8},{9,10},{10,9... | collective-permute-start | bytes 1572872 | tf_op jit(solution)/shard_map/ppermute | solution.py:502
  4.4 1.0 copy-done.3
  5.4 1.0 copy-done.4
  6.5 2.1 %collective-permute-start.6 = (f32[8,128,128]{2,1,0:T(8,128)S(1)}, f32[8,128,128]{2,1,0:T(8,128)S(1)}, u32[]{:S(2)}, u32[]{:S(2)}) collective-permute-start(f32[8,128,128]{2,1,0:T(8,128)S(1)} %get-tuple-element.157), channel_id=1, source_target_pairs={{0,0},{1,2},{2,1},{3,3},{4,4},{5,6},{6,5},{7,7},{8,8},{9,10},{10,9... | collective-permute-start | bytes 1572872 | tf_op jit(solution)/shard_map/ppermute | solution.py:486
  8.6 1.0 copy-done.5
  9.7 1.0 copy-done.6
  10.8 3.6 %collective-permute-start = (f32[8,128,128]{2,1,0:T(8,128)S(1)}, f32[8,128,128]{2,1,0:T(8,128)S(1)}, u32[]{:S(2)}, u32[]{:S(2)}) collective-permute-start(f32[8,128,128]{2,1,0:T(8,128)S(1)} %get-tuple-element.152), channel_id=1, source_target_pairs={{0,0},{1,2},{2,1},{3,3},{4,4},{5,6},{6,5},{7,7},{8,8},{9,10},{10,9... | collective-permute-start | bytes 1572872 | tf_op jit(solution)/shard_map/ppermute | solution.py:486
  14.7 8.6 %collective-permute-done.6.now_a = f32[8,128,128]{2,1,0:T(8,128)S(1)} collective-permute-done((f32[8,128,128]{2,1,0:T(8,128)S(1)}, f32[8,128,128]{2,1,0:T(8,128)S(1)}, u32[]{:S(2)}, u32[]{:S(2)}) %collective-permute-start.6) | collective-permute-done | bytes 524320 | tf_op jit(solution)/shard_map/ppermute | solution.py:486
  23.7 1.0 collective-permute-start.9
  24.7 1.0 prepare.1
  25.7 8.2 %collective-permute-done.before_a = f32[8,128,128]{2,1,0:T(8,128)S(1)} collective-permute-done((f32[8,128,128]{2,1,0:T(8,128)S(1)}, f32[8,128,128]{2,1,0:T(8,128)S(1)}, u32[]{:S(2)}, u32[]{:S(2)}) %collective-permute-start) | collective-permute-done | bytes 524320 | tf_op jit(solution)/shard_map/ppermute | solution.py:486
  33.9 3.6 %collective-permute-start.4 = (f32[2,128,128]{2,1,0:T(8,128)S(1)}, f32[2,128,128]{2,1,0:T(8,128)S(1)}, u32[]{:S(2)}, u32[]{:S(2)}) collective-permute-start(f32[2,128,128]{2,1,0:T(8,128)S(1)} %get-tuple-element.156), channel_id=1, source_target_pairs={{0,0},{1,2},{2,1},{3,3},{4,4},{5,6},{6,5},{7,7},{8,8},{9,10},{10,9... | collective-permute-start | bytes 393224 | tf_op jit(solution)/shard_map/ppermute | solution.py:486
  38.1 2.1 %collective-permute-done.4.face_a.rest_0_ = f32[2,128,128]{2,1,0:T(8,128)S(1)} collective-permute-done((f32[2,128,128]{2,1,0:T(8,128)S(1)}, f32[2,128,128]{2,1,0:T(8,128)S(1)}, u32[]{:S(2)}, u32[]{:S(2)}) %collective-permute-start.4) | collective-permute-done | bytes 131104 | tf_op jit(solution)/shard_map/ppermute | solution.py:486
  41.7 1.3 inner.12
  43.0 3.5 %collective-permute-done.13.low = f32[4,128,128]{2,1,0:T(8,128)S(1)} collective-permute-done((f32[4,128,128]{2,1,0:T(8,128)S(1)}, f32[4,128,128]{2,1,0:T(8,128)S(1)}, u32[]{:S(2)}, u32[]{:S(2)}) %collective-permute-start.13) | collective-permute-done | bytes 262176 | tf_op jit(solution)/shard_map/ppermute | solution.py:545
  47.4 0.6 collective-permute-start.14
  48.0 1.3 inner.13
  49.3 3.5 %collective-permute-done.15.low = f32[4,128,128]{2,1,0:T(8,128)S(1)} collective-permute-done((f32[4,128,128]{2,1,0:T(8,128)S(1)}, f32[4,128,128]{2,1,0:T(8,128)S(1)}, u32[]{:S(2)}, u32[]{:S(2)}) %collective-permute-start.15) | collective-permute-done | bytes 262176 | tf_op jit(solution)/shard_map/ppermute | solution.py:545
  53.7 0.6 collective-permute-start.16
  54.3 1.3 inner.14
  55.6 3.5 %collective-permute-done.17.low = f32[4,128,128]{2,1,0:T(8,128)S(1)} collective-permute-done((f32[4,128,128]{2,1,0:T(8,128)S(1)}, f32[4,128,128]{2,1,0:T(8,128)S(1)}, u32[]{:S(2)}, u32[]{:S(2)}) %collective-permute-start.17) | collective-permute-done | bytes 262176 | tf_op jit(solution)/shard_map/ppermute | solution.py:545
  60.1 4.8 %collective-permute-start.10 = (f32[4,128,128]{2,1,0:T(8,128)S(1)}, f32[4,128,128]{2,1,0:T(8,128)S(1)}, u32[]{:S(2)}, u32[]{:S(2)}) collective-permute-start(f32[4,128,128]{2,1,0:T(8,128)S(1)} %get-tuple-element.168), channel_id=1, source_target_pairs={{0,0},{1,2},{2,1},{3,3},{4,4},{5,6},{6,5},{7,7},{8,8},{9,10},{10,9... | collective-permute-start | bytes 786440 | tf_op jit(solution)/shard_map/ppermute | solution.py:486
  65.4 1.3 inner.15
  66.7 2.5 %collective-permute-done.10.face_a.rest_0_ = f32[4,128,128]{2,1,0:T(8,128)S(1)} collective-permute-done((f32[4,128,128]{2,1,0:T(8,128)S(1)}, f32[4,128,128]{2,1,0:T(8,128)S(1)}, u32[]{:S(2)}, u32[]{:S(2)}) %collective-permute-start.10) | collective-permute-done | bytes 262176 | tf_op jit(solution)/shard_map/ppermute | solution.py:486
  70.1 3.2 %collective-permute-start.20 = (f32[4,128,128]{2,1,0:T(8,128)S(1)}, f32[4,128,128]{2,1,0:T(8,128)S(1)}, u32[]{:S(2)}, u32[]{:S(2)}) collective-permute-start(f32[4,128,128]{2,1,0:T(8,128)S(1)} %get-tuple-element.198), channel_id=1, source_target_pairs={{0,1},{1,0},{2,3},{3,2},{4,5},{5,4},{6,7},{7,6},{8,9},{9,8},{10,11... | collective-permute-start | bytes 786440 | tf_op jit(solution)/shard_map/ppermute | solution.py:547
  73.3 1.4 inner.16
  74.7 1.0 collective-permute-done.21.low
  76.7 2.9 %collective-permute-start.25 = (f32[4,128,128]{2,1,0:T(8,128)S(1)}, f32[4,128,128]{2,1,0:T(8,128)S(1)}, u32[]{:S(2)}, u32[]{:S(2)}) collective-permute-start(f32[4,128,128]{2,1,0:T(8,128)S(1)} %get-tuple-element.220), channel_id=1, source_target_pairs={{0,1},{1,0},{2,3},{3,2},{4,5},{5,4},{6,7},{7,6},{8,9},{9,8},{10,11... | collective-permute-start | bytes 786440 | tf_op jit(solution)/shard_map/ppermute | solution.py:547
  79.6 1.3 inner.17
  81.0 1.3 collective-permute-done.26.low
  83.5 2.6 %collective-permute-start.27 = (f32[4,128,128]{2,1,0:T(8,128)S(1)}, f32[4,128,128]{2,1,0:T(8,128)S(1)}, u32[]{:S(2)}, u32[]{:S(2)}) collective-permute-start(f32[4,128,128]{2,1,0:T(8,128)S(1)} %get-tuple-element.225), channel_id=1, source_target_pairs={{0,1},{1,0},{2,3},{3,2},{4,5},{5,4},{6,7},{7,6},{8,9},{9,8},{10,11... | collective-permute-start | bytes 786440 | tf_op jit(solution)/shard_map/ppermute | solution.py:547
  86.1 1.4 collective-permute-start.23
  87.5 0.7 collective-permute-start.22
  88.3 1.3 inner.18
  90.5 2.2 %collective-permute-start.32 = (f32[4,128,128]{2,1,0:T(8,128)S(1)}, f32[4,128,128]{2,1,0:T(8,128)S(1)}, u32[]{:S(2)}, u32[]{:S(2)}) collective-permute-start(f32[4,128,128]{2,1,0:T(8,128)S(1)} %get-tuple-element.249), channel_id=1, source_target_pairs={{0,1},{1,0},{2,3},{3,2},{4,5},{5,4},{6,7},{7,6},{8,9},{9,8},{10,11... | collective-permute-start | bytes 786440 | tf_op jit(solution)/shard_map/ppermute | solution.py:547
  92.7 1.3 inner.19
  94.0 1.0 collective-permute-done.24.refs_3_
  95.0 4.4 %collective-permute-done.23.refs_2_ = f32[4,16,8,128]{3,2,1,0:T(8,128)S(1)} collective-permute-done((f32[4,16,8,128]{3,2,1,0:T(8,128)S(1)}, f32[4,16,8,128]{3,2,1,0:T(8,128)S(1)}, u32[]{:S(2)}, u32[]{:S(2)}) %collective-permute-start.23) | collective-permute-done | bytes 262176 | tf_op jit(solution)/shard_map/ppermute | solution.py:599
  100.9 2.3 %collective-permute-start.36 = (f32[4,128,128]{2,1,0:T(8,128)S(1)}, f32[4,128,128]{2,1,0:T(8,128)S(1)}, u32[]{:S(2)}, u32[]{:S(2)}) collective-permute-start(f32[4,128,128]{2,1,0:T(8,128)S(1)} %get-tuple-element.265), channel_id=1, source_target_pairs={{0,1},{1,0},{2,3},{3,2},{4,5},{5,4},{6,7},{7,6},{8,9},{9,8},{10,11... | collective-permute-start | bytes 786440 | tf_op jit(solution)/shard_map/ppermute | solution.py:547
  103.2 1.4 inner.20
  104.6 4.5 %collective-permute-done.31.refs_2_ = f32[2,16,8,128]{3,2,1,0:T(8,128)S(1)} collective-permute-done((f32[2,16,8,128]{3,2,1,0:T(8,128)S(1)}, f32[2,16,8,128]{3,2,1,0:T(8,128)S(1)}, u32[]{:S(2)}, u32[]{:S(2)}) %collective-permute-start.31) | collective-permute-done | bytes 131104 | tf_op jit(solution)/shard_map/ppermute | solution.py:622
  109.6 3.0 %collective-permute-start.33 = (f32[4,128,128]{2,1,0:T(8,128)S(1)}, f32[4,128,128]{2,1,0:T(8,128)S(1)}, u32[]{:S(2)}, u32[]{:S(2)}) collective-permute-start(f32[4,128,128]{2,1,0:T(8,128)S(1)} %get-tuple-element.258), channel_id=1, source_target_pairs={{1,4},{4,1},{3,6},{6,3},{5,8},{8,5},{7,10},{10,7},{9,12},{12,9},{1... | collective-permute-start | bytes 786440 | tf_op jit(solution)/shard_map/ppermute | solution.py:545
  113.0 2.0 %collective-permute-start.40 = (f32[4,128,128]{2,1,0:T(8,128)S(1)}, f32[4,128,128]{2,1,0:T(8,128)S(1)}, u32[]{:S(2)}, u32[]{:S(2)}) collective-permute-start(f32[4,128,128]{2,1,0:T(8,128)S(1)} %get-tuple-element.282), channel_id=1, source_target_pairs={{0,1},{1,0},{2,3},{3,2},{4,5},{5,4},{6,7},{7,6},{8,9},{9,8},{10,11... | collective-permute-start | bytes 786440 | tf_op jit(solution)/shard_map/ppermute | solution.py:547
  115.0 1.1 collective-permute-start.35
  116.1 1.3 inner.21
  117.4 4.1 %collective-permute-done.35.refs_0_ = f32[2,16,8,128]{3,2,1,0:T(8,128)S(1)} collective-permute-done((f32[2,16,8,128]{3,2,1,0:T(8,128)S(1)}, f32[2,16,8,128]{3,2,1,0:T(8,128)S(1)}, u32[]{:S(2)}, u32[]{:S(2)}) %collective-permute-start.35) | collective-permute-done | bytes 131104 | tf_op jit(solution)/shard_map/ppermute | solution.py:622
  121.5 1.1 collective-permute-done.34.refs_3_
  123.2 2.7 %collective-permute-start.37 = (f32[4,128,128]{2,1,0:T(8,128)S(1)}, f32[4,128,128]{2,1,0:T(8,128)S(1)}, u32[]{:S(2)}, u32[]{:S(2)}) collective-permute-start(f32[4,128,128]{2,1,0:T(8,128)S(1)} %get-tuple-element.274), channel_id=1, source_target_pairs={{1,4},{4,1},{3,6},{6,3},{5,8},{8,5},{7,10},{10,7},{9,12},{12,9},{1... | collective-permute-start | bytes 786440 | tf_op jit(solution)/shard_map/ppermute | solution.py:545
  126.4 1.6 collective-permute-start.39
  128.0 1.3 inner.22
  129.3 0.7 inner.23.prev
  130.0 3.1 %collective-permute-done.39.refs_1_ = f32[2,16,8,128]{3,2,1,0:T(8,128)S(1)} collective-permute-done((f32[2,16,8,128]{3,2,1,0:T(8,128)S(1)}, f32[2,16,8,128]{3,2,1,0:T(8,128)S(1)}, u32[]{:S(2)}, u32[]{:S(2)}) %collective-permute-start.39) | collective-permute-done | bytes 131104 | tf_op jit(solution)/shard_map/ppermute | solution.py:622
  133.7 0.6 copy-done.14
  134.3 3.0 %last.1 = (f32[24,128,128]{2,1,0:T(8,128)S(1)}, f32[24,128,128]{2,1,0:T(8,128)S(1)}, f32[16,16,8,128]{3,2,1,0:T(8,128)S(1)}, f32[8,128,128]{2,1,0:T(8,128)}, f32...) custom-call(s32[2]{0:T(128)S(1)} %copy-done.16, ...), custom_call_target="tpu_custom_call", output_to_operand_aliasing={{0}: (9, {}), {1}: (10, {}), {2}: (11, {})} | custom-call | tf_op jit(solution)/shard_map/last/pallas_call | solution.py:591
  137.3 8.2 %all-to-all-start = ((f32[16,16,8,128]{3,2,1,0:T(8,128)}), f32[16,16,8,128]{3,2,1,0:T(8,128)S(1)}, u32[]{:S(2)}, u32[]{:S(2)}) async-start(f32[16,16,8,128]{3,2,1,0:T(8,128)} %get-tuple-element.294), calls=%async_computation | async-start | bytes 2097152 | tf_op jit(solution)/shard_map/all_to_all | solution.py:628
  145.5 3.4 %collective-permute-start.43 = (f32[8,128,128]{2,1,0:T(8,128)}, f32[8,128,128]{2,1,0:T(8,128)S(1)}, u32[]{:S(2)}, u32[]{:S(2)}) collective-permute-start(f32[8,128,128]{2,1,0:T(8,128)} %get-tuple-element.295), channel_id=1, source_target_pairs={{0,0},{1,2},{2,1},{3,3},{4,4},{5,6},{6,5},{7,7},{8,8},{9,10},{10,9... | collective-permute-start | bytes 1572872 | tf_op jit(solution)/shard_map/ppermute | solution.py:629
  148.9 1.3 collective-permute-start.41
  150.2 25.5 %collective-permute-done.41.refs_5_ = f32[2,16,8,128]{3,2,1,0:T(8,128)S(1)} collective-permute-done((f32[2,16,8,128]{3,2,1,0:T(8,128)S(1)}, f32[2,16,8,128]{3,2,1,0:T(8,128)S(1)}, u32[]{:S(2)}, u32[]{:S(2)}) %collective-permute-start.41) | collective-permute-done | bytes 131104 | tf_op jit(solution)/shard_map/ppermute | solution.py:622
  175.8 0.9 copy-done.9
  176.7 0.9 copy-done.11
  177.6 0.9 copy-done.13
  178.5 0.9 copy-done.15
  179.5 1.1 choose.5
  180.6 6.9 %images.1 = bf16[8,128,8,128]{3,2,1,0:T(8,128)(2,1)} custom-call(bf16[2,256,1024]{2,1,0:T(8,128)(2,1)S(1)} %get-tuple-element.151.shifts, f32[16,16,8,128]{3,2,1,0:T(8,128)S(1)} %shard_map.143.refs_0_, f32[16,16,8,128]{3,2,1,0:T(8,128)S(1)} %all-to-all-done.refs_1_), custom_call_target="tpu_custom_call" | custom-call | tf_op jit(solution)/shard_map/images/pallas_call | solution.py:444
  (111 shorter events, 14.4 us)
Async XLA Ops:
  0.6 13.9 %collective-permute-start.2 = (f32[8,128,128]{2,1,0:T(8,128)}, f32[8,128,128]{2,1,0:T(8,128)S(1)}, u32[]{:S(2)}, u32[]{:S(2)}) collective-permute-start(f32[8,128,128]{2,1,0:T(8,128)} %param.16), channel_id=1, source_target_pairs={{0,0},{1,2},{2,1},{3,3},{4,4},{5,6},{6,5},{7,7},{8,8},{9,10},{10,9... | collective-permute-start | bytes 1572872 | tf_op jit(solution)/shard_map/ppermute | solution.py:502
  4.3 1.0 copy-start.3
  5.4 1.0 copy-start.4
  6.4 18.3 %copy-start.7 = (f32[12,8,8,128]{3,2,1,0:T(8,128)S(1)}, f32[12,8,8,128]{3,2,1,0:T(8,128)}, u32[]{:S(2)}) copy-start(f32[12,8,8,128]{3,2,1,0:T(8,128)} %param.17) | copy-start | bytes 1179652
  6.4 18.3 %copy-start.17 = (s32[12]{0:T(128)S(1)}, s32[12]{0:T(128)}, u32[]{:S(2)}) copy-start(s32[12]{0:T(128)} %face_steps.1) | copy-start | bytes 148
  6.4 18.3 %copy-start.18 = (s32[8]{0:T(128)S(1)}, s32[8]{0:T(128)}, u32[]{:S(2)}) copy-start(s32[8]{0:T(128)} %lags.1) | copy-start | bytes 100
  6.5 16.8 %collective-permute-start.6 = (f32[8,128,128]{2,1,0:T(8,128)S(1)}, f32[8,128,128]{2,1,0:T(8,128)S(1)}, u32[]{:S(2)}, u32[]{:S(2)}) collective-permute-start(f32[8,128,128]{2,1,0:T(8,128)S(1)} %get-tuple-element.157), channel_id=1, source_target_pairs={{0,0},{1,2},{2,1},{3,3},{4,4},{5,6},{6,5},{7,7},{8,8},{9,10},{10,9... | collective-permute-start | bytes 1572872 | tf_op jit(solution)/shard_map/ppermute | solution.py:486
  8.6 14.7 %collective-permute-start.7 = (f32[8,128,128]{2,1,0:T(8,128)S(1)}, f32[8,128,128]{2,1,0:T(8,128)S(1)}, u32[]{:S(2)}, u32[]{:S(2)}) collective-permute-start(f32[8,128,128]{2,1,0:T(8,128)S(1)} %get-tuple-element.158), channel_id=1, source_target_pairs={{0,2},{1,0},{2,3},{3,1},{4,6},{5,4},{6,7},{7,5},{8,10},{9,8},{10,1... | collective-permute-start | bytes 1572872 | tf_op jit(solution)/shard_map/ppermute | solution.py:486
  8.6 1.0 copy-start.5
  9.7 1.0 copy-start.6
  10.8 23.1 %collective-permute-start = (f32[8,128,128]{2,1,0:T(8,128)S(1)}, f32[8,128,128]{2,1,0:T(8,128)S(1)}, u32[]{:S(2)}, u32[]{:S(2)}) collective-permute-start(f32[8,128,128]{2,1,0:T(8,128)S(1)} %get-tuple-element.152), channel_id=1, source_target_pairs={{0,0},{1,2},{2,1},{3,3},{4,4},{5,6},{6,5},{7,7},{8,8},{9,10},{10,9... | collective-permute-start | bytes 1572872 | tf_op jit(solution)/shard_map/ppermute | solution.py:486
  14.5 25.7 %copy-start = (bf16[128,256]{1,0:T(8,128)(2,1)S(1)}, bf16[128,256]{1,0:T(8,128)(2,1)}, u32[]{:S(2)}) copy-start(bf16[128,256]{1,0:T(8,128)(2,1)} %constant.5.clone.along) | copy-start | bytes 196612
  14.5 25.7 %copy-start.1 = (bf16[256,128]{1,0:T(8,128)(2,1)S(1)}, bf16[256,128]{1,0:T(8,128)(2,1)}, u32[]{:S(2)}) copy-start(bf16[256,128]{1,0:T(8,128)(2,1)} %constant.4.clone.across) | copy-start | bytes 196612
  14.5 25.7 %copy-start.2 = (bf16[12,128,128]{2,1,0:T(8,128)(2,1)S(1)}, bf16[12,128,128]{2,1,0:T(8,128)(2,1)}, u32[]{:S(2)}) copy-start(bf16[12,128,128]{2,1,0:T(8,128)(2,1)} %traces.23) | copy-start | bytes 1179652
  14.5 19.4 %collective-permute-start.1 = (f32[8,128,128]{2,1,0:T(8,128)S(1)}, f32[8,128,128]{2,1,0:T(8,128)S(1)}, u32[]{:S(2)}, u32[]{:S(2)}) collective-permute-start(f32[8,128,128]{2,1,0:T(8,128)S(1)} %get-tuple-element.153), channel_id=1, source_target_pairs={{0,2},{1,0},{2,3},{3,1},{4,6},{5,4},{6,7},{7,5},{8,10},{9,8},{10,1... | collective-permute-start | bytes 1572872 | tf_op jit(solution)/shard_map/ppermute | solution.py:486
  14.5 23.0 %collective-permute-start.3 = (f32[8,128,128]{2,1,0:T(8,128)S(1)}, f32[8,128,128]{2,1,0:T(8,128)S(1)}, u32[]{:S(2)}, u32[]{:S(2)}) collective-permute-start(f32[8,128,128]{2,1,0:T(8,128)S(1)} %collective-permute-done.2.speed_a), channel_id=1, source_target_pairs={{0,16},{16,0},{1,17},{17,1},{2,18},{18,2},{3,19},{19,3},{4,20},{20... | collective-permute-start | bytes 1572872 | tf_op jit(solution)/shard_map/ppermute | solution.py:503
  23.7 16.4 %collective-permute-start.9 = (f32[4,128,128]{2,1,0:T(8,128)S(1)}, f32[4,128,128]{2,1,0:T(8,128)S(1)}, u32[]{:S(2)}, u32[]{:S(2)}) collective-permute-start(f32[4,128,128]{2,1,0:T(8,128)S(1)} %get-tuple-element.160), channel_id=1, source_target_pairs={{1,4},{4,1},{3,6},{6,3},{5,8},{8,5},{7,10},{10,7},{9,12},{12,9},{1... | collective-permute-start | bytes 786440 | tf_op jit(solution)/shard_map/ppermute | solution.py:511
  24.7 16.0 %collective-permute-start.8 = (f32[4,128,128]{2,1,0:T(8,128)S(1)}, f32[4,128,128]{2,1,0:T(8,128)S(1)}, u32[]{:S(2)}, u32[]{:S(2)}) collective-permute-start(f32[4,128,128]{2,1,0:T(8,128)S(1)} %get-tuple-element.159), channel_id=1, source_target_pairs={{0,1},{1,0},{2,3},{3,2},{4,5},{5,4},{6,7},{7,6},{8,9},{9,8},{10,11... | collective-permute-start | bytes 786440 | tf_op jit(solution)/shard_map/ppermute | solution.py:512
  33.9 4.2 %collective-permute-start.5 = (f32[2,128,128]{2,1,0:T(8,128)S(1)}, f32[2,128,128]{2,1,0:T(8,128)S(1)}, u32[]{:S(2)}, u32[]{:S(2)}) collective-permute-start(f32[2,128,128]{2,1,0:T(8,128)S(1)} %get-tuple-element.156), channel_id=1, source_target_pairs={{0,2},{1,0},{2,3},{3,1},{4,6},{5,4},{6,7},{7,5},{8,10},{9,8},{10,1... | collective-permute-start | bytes 393224 | tf_op jit(solution)/shard_map/ppermute | solution.py:486
  33.9 6.3 %collective-permute-start.4 = (f32[2,128,128]{2,1,0:T(8,128)S(1)}, f32[2,128,128]{2,1,0:T(8,128)S(1)}, u32[]{:S(2)}, u32[]{:S(2)}) collective-permute-start(f32[2,128,128]{2,1,0:T(8,128)S(1)} %get-tuple-element.156), channel_id=1, source_target_pairs={{0,0},{1,2},{2,1},{3,3},{4,4},{5,6},{6,5},{7,7},{8,8},{9,10},{10,9... | collective-permute-start | bytes 393224 | tf_op jit(solution)/shard_map/ppermute | solution.py:486
  40.6 5.9 %collective-permute-start.13 = (f32[4,128,128]{2,1,0:T(8,128)S(1)}, f32[4,128,128]{2,1,0:T(8,128)S(1)}, u32[]{:S(2)}, u32[]{:S(2)}) collective-permute-start(f32[4,128,128]{2,1,0:T(8,128)S(1)} %get-tuple-element.170), channel_id=1, source_target_pairs={{1,4},{4,1},{3,6},{6,3},{5,8},{8,5},{7,10},{10,7},{9,12},{12,9},{1... | collective-permute-start | bytes 786440 | tf_op jit(solution)/shard_map/ppermute | solution.py:545
  40.7 1.0 copy-start.16
  41.1 5.9 %collective-permute-start.12 = (f32[4,128,128]{2,1,0:T(8,128)S(1)}, f32[4,128,128]{2,1,0:T(8,128)S(1)}, u32[]{:S(2)}, u32[]{:S(2)}) collective-permute-start(f32[4,128,128]{2,1,0:T(8,128)S(1)} %get-tuple-element.169), channel_id=1, source_target_pairs={{0,1},{1,0},{2,3},{3,2},{4,5},{5,4},{6,7},{7,6},{8,9},{9,8},{10,11... | collective-permute-start | bytes 786440 | tf_op jit(solution)/shard_map/ppermute | solution.py:547
  46.9 5.9 %collective-permute-start.15 = (f32[4,128,128]{2,1,0:T(8,128)S(1)}, f32[4,128,128]{2,1,0:T(8,128)S(1)}, u32[]{:S(2)}, u32[]{:S(2)}) collective-permute-start(f32[4,128,128]{2,1,0:T(8,128)S(1)} %get-tuple-element.175), channel_id=1, source_target_pairs={{1,4},{4,1},{3,6},{6,3},{5,8},{8,5},{7,10},{10,7},{9,12},{12,9},{1... | collective-permute-start | bytes 786440 | tf_op jit(solution)/shard_map/ppermute | solution.py:545
  47.4 5.9 %collective-permute-start.14 = (f32[4,128,128]{2,1,0:T(8,128)S(1)}, f32[4,128,128]{2,1,0:T(8,128)S(1)}, u32[]{:S(2)}, u32[]{:S(2)}) collective-permute-start(f32[4,128,128]{2,1,0:T(8,128)S(1)} %get-tuple-element.174), channel_id=1, source_target_pairs={{0,1},{1,0},{2,3},{3,2},{4,5},{5,4},{6,7},{7,6},{8,9},{9,8},{10,11... | collective-permute-start | bytes 786440 | tf_op jit(solution)/shard_map/ppermute | solution.py:547
  53.2 5.9 %collective-permute-start.17 = (f32[4,128,128]{2,1,0:T(8,128)S(1)}, f32[4,128,128]{2,1,0:T(8,128)S(1)}, u32[]{:S(2)}, u32[]{:S(2)}) collective-permute-start(f32[4,128,128]{2,1,0:T(8,128)S(1)} %get-tuple-element.183), channel_id=1, source_target_pairs={{1,4},{4,1},{3,6},{6,3},{5,8},{8,5},{7,10},{10,7},{9,12},{12,9},{1... | collective-permute-start | bytes 786440 | tf_op jit(solution)/shard_map/ppermute | solution.py:545
  53.7 11.2 %collective-permute-start.16 = (f32[4,128,128]{2,1,0:T(8,128)S(1)}, f32[4,128,128]{2,1,0:T(8,128)S(1)}, u32[]{:S(2)}, u32[]{:S(2)}) collective-permute-start(f32[4,128,128]{2,1,0:T(8,128)S(1)} %get-tuple-element.182), channel_id=1, source_target_pairs={{0,1},{1,0},{2,3},{3,2},{4,5},{5,4},{6,7},{7,6},{8,9},{9,8},{10,11... | collective-permute-start | bytes 786440 | tf_op jit(solution)/shard_map/ppermute | solution.py:547
  59.5 7.2 %collective-permute-start.19 = (f32[4,128,128]{2,1,0:T(8,128)S(1)}, f32[4,128,128]{2,1,0:T(8,128)S(1)}, u32[]{:S(2)}, u32[]{:S(2)}) collective-permute-start(f32[4,128,128]{2,1,0:T(8,128)S(1)} %get-tuple-element.191), channel_id=1, source_target_pairs={{1,4},{4,1},{3,6},{6,3},{5,8},{8,5},{7,10},{10,7},{9,12},{12,9},{1... | collective-permute-start | bytes 786440 | tf_op jit(solution)/shard_map/ppermute | solution.py:545
  59.6 7.1 %collective-permute-start.11 = (f32[4,128,128]{2,1,0:T(8,128)S(1)}, f32[4,128,128]{2,1,0:T(8,128)S(1)}, u32[]{:S(2)}, u32[]{:S(2)}) collective-permute-start(f32[4,128,128]{2,1,0:T(8,128)S(1)} %get-tuple-element.168), channel_id=1, source_target_pairs={{0,2},{1,0},{2,3},{3,1},{4,6},{5,4},{6,7},{7,5},{8,10},{9,8},{10,1... | collective-permute-start | bytes 786440 | tf_op jit(solution)/shard_map/ppermute | solution.py:486
  60.1 9.0 %collective-permute-start.10 = (f32[4,128,128]{2,1,0:T(8,128)S(1)}, f32[4,128,128]{2,1,0:T(8,128)S(1)}, u32[]{:S(2)}, u32[]{:S(2)}) collective-permute-start(f32[4,128,128]{2,1,0:T(8,128)S(1)} %get-tuple-element.168), channel_id=1, source_target_pairs={{0,0},{1,2},{2,1},{3,3},{4,4},{5,6},{6,5},{7,7},{8,8},{9,10},{10,9... | collective-permute-start | bytes 786440 | tf_op jit(solution)/shard_map/ppermute | solution.py:486
  65.3 4.4 %collective-permute-start.18 = (f32[4,128,128]{2,1,0:T(8,128)S(1)}, f32[4,128,128]{2,1,0:T(8,128)S(1)}, u32[]{:S(2)}, u32[]{:S(2)}) collective-permute-start(f32[4,128,128]{2,1,0:T(8,128)S(1)} %get-tuple-element.190), channel_id=1, source_target_pairs={{0,1},{1,0},{2,3},{3,2},{4,5},{5,4},{6,7},{7,6},{8,9},{9,8},{10,11... | collective-permute-start | bytes 786440 | tf_op jit(solution)/shard_map/ppermute | solution.py:547
  69.6 6.2 %collective-permute-start.21 = (f32[4,128,128]{2,1,0:T(8,128)S(1)}, f32[4,128,128]{2,1,0:T(8,128)S(1)}, u32[]{:S(2)}, u32[]{:S(2)}) collective-permute-start(f32[4,128,128]{2,1,0:T(8,128)S(1)} %get-tuple-element.199), channel_id=1, source_target_pairs={{1,4},{4,1},{3,6},{6,3},{5,8},{8,5},{7,10},{10,7},{9,12},{12,9},{1... | collective-permute-start | bytes 786440 | tf_op jit(solution)/shard_map/ppermute | solution.py:545
  70.1 6.2 %collective-permute-start.20 = (f32[4,128,128]{2,1,0:T(8,128)S(1)}, f32[4,128,128]{2,1,0:T(8,128)S(1)}, u32[]{:S(2)}, u32[]{:S(2)}) collective-permute-start(f32[4,128,128]{2,1,0:T(8,128)S(1)} %get-tuple-element.198), channel_id=1, source_target_pairs={{0,1},{1,0},{2,3},{3,2},{4,5},{5,4},{6,7},{7,6},{8,9},{9,8},{10,11... | collective-permute-start | bytes 786440 | tf_op jit(solution)/shard_map/ppermute | solution.py:547
  76.2 6.2 %collective-permute-start.26 = (f32[4,128,128]{2,1,0:T(8,128)S(1)}, f32[4,128,128]{2,1,0:T(8,128)S(1)}, u32[]{:S(2)}, u32[]{:S(2)}) collective-permute-start(f32[4,128,128]{2,1,0:T(8,128)S(1)} %get-tuple-element.221), channel_id=1, source_target_pairs={{1,4},{4,1},{3,6},{6,3},{5,8},{8,5},{7,10},{10,7},{9,12},{12,9},{1... | collective-permute-start | bytes 786440 | tf_op jit(solution)/shard_map/ppermute | solution.py:545
  76.7 6.3 %collective-permute-start.25 = (f32[4,128,128]{2,1,0:T(8,128)S(1)}, f32[4,128,128]{2,1,0:T(8,128)S(1)}, u32[]{:S(2)}, u32[]{:S(2)}) collective-permute-start(f32[4,128,128]{2,1,0:T(8,128)S(1)} %get-tuple-element.220), channel_id=1, source_target_pairs={{0,1},{1,0},{2,3},{3,2},{4,5},{5,4},{6,7},{7,6},{8,9},{9,8},{10,11... | collective-permute-start | bytes 786440 | tf_op jit(solution)/shard_map/ppermute | solution.py:547
  83.0 6.6 %collective-permute-start.28 = (f32[4,128,128]{2,1,0:T(8,128)S(1)}, f32[4,128,128]{2,1,0:T(8,128)S(1)}, u32[]{:S(2)}, u32[]{:S(2)}) collective-permute-start(f32[4,128,128]{2,1,0:T(8,128)S(1)} %get-tuple-element.226), channel_id=1, source_target_pairs={{1,4},{4,1},{3,6},{6,3},{5,8},{8,5},{7,10},{10,7},{9,12},{12,9},{1... | collective-permute-start | bytes 786440 | tf_op jit(solution)/shard_map/ppermute | solution.py:545
  83.5 6.6 %collective-permute-start.27 = (f32[4,128,128]{2,1,0:T(8,128)S(1)}, f32[4,128,128]{2,1,0:T(8,128)S(1)}, u32[]{:S(2)}, u32[]{:S(2)}) collective-permute-start(f32[4,128,128]{2,1,0:T(8,128)S(1)} %get-tuple-element.225), channel_id=1, source_target_pairs={{0,1},{1,0},{2,3},{3,2},{4,5},{5,4},{6,7},{7,6},{8,9},{9,8},{10,11... | collective-permute-start | bytes 786440 | tf_op jit(solution)/shard_map/ppermute | solution.py:547
  86.1 8.9 %collective-permute-start.24 = (f32[4,16,8,128]{3,2,1,0:T(8,128)S(1)}, f32[4,16,8,128]{3,2,1,0:T(8,128)S(1)}, u32[]{:S(2)}, u32[]{:S(2)}) collective-permute-start(f32[4,16,8,128]{3,2,1,0:T(8,128)S(1)} %get-tuple-element.219), channel_id=1, source_target_pairs={{0,3},{1,2},{2,1},{3,0},{4,7},{5,6},{6,5},{7,4},{8,11},{9,10},{10,... | collective-permute-start | bytes 786440 | tf_op jit(solution)/shard_map/ppermute | solution.py:599
  86.1 13.3 %collective-permute-start.23 = (f32[4,16,8,128]{3,2,1,0:T(8,128)S(1)}, f32[4,16,8,128]{3,2,1,0:T(8,128)S(1)}, u32[]{:S(2)}, u32[]{:S(2)}) collective-permute-start(f32[4,16,8,128]{3,2,1,0:T(8,128)S(1)} %get-tuple-element.216), channel_id=1, source_target_pairs={{0,2},{1,3},{2,0},{3,1},{4,6},{5,7},{6,4},{7,5},{8,10},{9,11},{10,... | collective-permute-start | bytes 786440 | tf_op jit(solution)/shard_map/ppermute | solution.py:599
  87.5 11.9 %collective-permute-start.22 = (f32[4,16,8,128]{3,2,1,0:T(8,128)S(1)}, f32[4,16,8,128]{3,2,1,0:T(8,128)S(1)}, u32[]{:S(2)}, u32[]{:S(2)}) collective-permute-start(f32[4,16,8,128]{3,2,1,0:T(8,128)S(1)} %get-tuple-element.213), channel_id=1, source_target_pairs={{0,1},{1,0},{2,3},{3,2},{4,5},{5,4},{6,7},{7,6},{8,9},{9,8},{10,11... | collective-permute-start | bytes 786440 | tf_op jit(solution)/shard_map/ppermute | solution.py:599
  90.0 9.6 %collective-permute-start.29 = (f32[4,128,128]{2,1,0:T(8,128)S(1)}, f32[4,128,128]{2,1,0:T(8,128)S(1)}, u32[]{:S(2)}, u32[]{:S(2)}) collective-permute-start(f32[4,128,128]{2,1,0:T(8,128)S(1)} %get-tuple-element.240), channel_id=1, source_target_pairs={{1,4},{4,1},{3,6},{6,3},{5,8},{8,5},{7,10},{10,7},{9,12},{12,9},{1... | collective-permute-start | bytes 786440 | tf_op jit(solution)/shard_map/ppermute | solution.py:545
  90.5 10.0 %collective-permute-start.32 = (f32[4,128,128]{2,1,0:T(8,128)S(1)}, f32[4,128,128]{2,1,0:T(8,128)S(1)}, u32[]{:S(2)}, u32[]{:S(2)}) collective-permute-start(f32[4,128,128]{2,1,0:T(8,128)S(1)} %get-tuple-element.249), channel_id=1, source_target_pairs={{0,1},{1,0},{2,3},{3,2},{4,5},{5,4},{6,7},{7,6},{8,9},{9,8},{10,11... | collective-permute-start | bytes 786440 | tf_op jit(solution)/shard_map/ppermute | solution.py:547
  100.0 9.1 %collective-permute-start.30 = (f32[4,128,128]{2,1,0:T(8,128)S(1)}, f32[4,128,128]{2,1,0:T(8,128)S(1)}, u32[]{:S(2)}, u32[]{:S(2)}) collective-permute-start(f32[4,128,128]{2,1,0:T(8,128)S(1)} %get-tuple-element.244), channel_id=1, source_target_pairs={{1,4},{4,1},{3,6},{6,3},{5,8},{8,5},{7,10},{10,7},{9,12},{12,9},{1... | collective-permute-start | bytes 786440 | tf_op jit(solution)/shard_map/ppermute | solution.py:545
  100.9 11.6 %collective-permute-start.36 = (f32[4,128,128]{2,1,0:T(8,128)S(1)}, f32[4,128,128]{2,1,0:T(8,128)S(1)}, u32[]{:S(2)}, u32[]{:S(2)}) collective-permute-start(f32[4,128,128]{2,1,0:T(8,128)S(1)} %get-tuple-element.265), channel_id=1, source_target_pairs={{0,1},{1,0},{2,3},{3,2},{4,5},{5,4},{6,7},{7,6},{8,9},{9,8},{10,11... | collective-permute-start | bytes 786440 | tf_op jit(solution)/shard_map/ppermute | solution.py:547
  103.2 5.9 %collective-permute-start.31 = (f32[2,16,8,128]{3,2,1,0:T(8,128)S(1)}, f32[2,16,8,128]{3,2,1,0:T(8,128)S(1)}, u32[]{:S(2)}, u32[]{:S(2)}) collective-permute-start(f32[2,16,8,128]{3,2,1,0:T(8,128)S(1)} %get-tuple-element.245), channel_id=1, source_target_pairs={{0,8},{1,9},{2,10},{3,11},{4,12},{5,13},{6,14},{7,15},{8,0},{9,1},... | collective-permute-start | bytes 393224 | tf_op jit(solution)/shard_map/ppermute | solution.py:622
  109.6 13.0 %collective-permute-start.33 = (f32[4,128,128]{2,1,0:T(8,128)S(1)}, f32[4,128,128]{2,1,0:T(8,128)S(1)}, u32[]{:S(2)}, u32[]{:S(2)}) collective-permute-start(f32[4,128,128]{2,1,0:T(8,128)S(1)} %get-tuple-element.258), channel_id=1, source_target_pairs={{1,4},{4,1},{3,6},{6,3},{5,8},{8,5},{7,10},{10,7},{9,12},{12,9},{1... | collective-permute-start | bytes 786440 | tf_op jit(solution)/shard_map/ppermute | solution.py:545
  113.0 12.9 %collective-permute-start.40 = (f32[4,128,128]{2,1,0:T(8,128)S(1)}, f32[4,128,128]{2,1,0:T(8,128)S(1)}, u32[]{:S(2)}, u32[]{:S(2)}) collective-permute-start(f32[4,128,128]{2,1,0:T(8,128)S(1)} %get-tuple-element.282), channel_id=1, source_target_pairs={{0,1},{1,0},{2,3},{3,2},{4,5},{5,4},{6,7},{7,6},{8,9},{9,8},{10,11... | collective-permute-start | bytes 786440 | tf_op jit(solution)/shard_map/ppermute | solution.py:547
  115.0 6.5 %collective-permute-start.35 = (f32[2,16,8,128]{3,2,1,0:T(8,128)S(1)}, f32[2,16,8,128]{3,2,1,0:T(8,128)S(1)}, u32[]{:S(2)}, u32[]{:S(2)}) collective-permute-start(f32[2,16,8,128]{3,2,1,0:T(8,128)S(1)} %get-tuple-element.260), channel_id=1, source_target_pairs={{0,4},{1,5},{2,6},{3,7},{4,0},{5,1},{6,2},{7,3},{8,12},{9,13},{10,... | collective-permute-start | bytes 393224 | tf_op jit(solution)/shard_map/ppermute | solution.py:622
  116.1 6.4 %collective-permute-start.34 = (f32[2,16,8,128]{3,2,1,0:T(8,128)S(1)}, f32[2,16,8,128]{3,2,1,0:T(8,128)S(1)}, u32[]{:S(2)}, u32[]{:S(2)}) collective-permute-start(f32[2,16,8,128]{3,2,1,0:T(8,128)S(1)} %get-tuple-element.259), channel_id=1, source_target_pairs={{0,8},{1,9},{2,10},{3,11},{4,12},{5,13},{6,14},{7,15},{8,0},{9,1},... | collective-permute-start | bytes 393224 | tf_op jit(solution)/shard_map/ppermute | solution.py:622
  121.5 1.5 copy-start.8
  122.5 0.7 copy-start.10
  123.2 11.1 %collective-permute-start.37 = (f32[4,128,128]{2,1,0:T(8,128)S(1)}, f32[4,128,128]{2,1,0:T(8,128)S(1)}, u32[]{:S(2)}, u32[]{:S(2)}) collective-permute-start(f32[4,128,128]{2,1,0:T(8,128)S(1)} %get-tuple-element.274), channel_id=1, source_target_pairs={{1,4},{4,1},{3,6},{6,3},{5,8},{8,5},{7,10},{10,7},{9,12},{12,9},{1... | collective-permute-start | bytes 786440 | tf_op jit(solution)/shard_map/ppermute | solution.py:545
  126.3 8.0 %collective-permute-start.42 = (f32[4,128,128]{2,1,0:T(8,128)S(1)}, f32[4,128,128]{2,1,0:T(8,128)S(1)}, u32[]{:S(2)}, u32[]{:S(2)}) collective-permute-start(f32[4,128,128]{2,1,0:T(8,128)S(1)} %get-tuple-element.291), channel_id=1, source_target_pairs={{0,1},{1,0},{2,3},{3,2},{4,5},{5,4},{6,7},{7,6},{8,9},{9,8},{10,11... | collective-permute-start | bytes 786440 | tf_op jit(solution)/shard_map/ppermute | solution.py:547
  126.4 6.7 %collective-permute-start.39 = (f32[2,16,8,128]{3,2,1,0:T(8,128)S(1)}, f32[2,16,8,128]{3,2,1,0:T(8,128)S(1)}, u32[]{:S(2)}, u32[]{:S(2)}) collective-permute-start(f32[2,16,8,128]{3,2,1,0:T(8,128)S(1)} %get-tuple-element.276), channel_id=1, source_target_pairs={{0,4},{1,5},{2,6},{3,7},{4,0},{5,1},{6,2},{7,3},{8,12},{9,13},{10,... | collective-permute-start | bytes 393224 | tf_op jit(solution)/shard_map/ppermute | solution.py:622
  128.0 5.7 %collective-permute-start.38 = (f32[2,16,8,128]{3,2,1,0:T(8,128)S(1)}, f32[2,16,8,128]{3,2,1,0:T(8,128)S(1)}, u32[]{:S(2)}, u32[]{:S(2)}) collective-permute-start(f32[2,16,8,128]{3,2,1,0:T(8,128)S(1)} %get-tuple-element.275), channel_id=1, source_target_pairs={{0,12},{1,13},{2,14},{3,15},{4,8},{5,9},{6,10},{7,11},{8,4},{9,5},... | collective-permute-start | bytes 393224 | tf_op jit(solution)/shard_map/ppermute | solution.py:622
  133.1 4.2 %copy-start.12 = (f32[2,16,8,128]{3,2,1,0:T(8,128)}, f32[2,16,8,128]{3,2,1,0:T(8,128)S(1)}, u32[]{:S(2)}) copy-start(f32[2,16,8,128]{3,2,1,0:T(8,128)S(1)} %collective-permute-done.39.refs_1_) | copy-start | bytes 393220
  137.3 43.3 %all-to-all-start = ((f32[16,16,8,128]{3,2,1,0:T(8,128)}), f32[16,16,8,128]{3,2,1,0:T(8,128)S(1)}, u32[]{:S(2)}, u32[]{:S(2)}) async-start(f32[16,16,8,128]{3,2,1,0:T(8,128)} %get-tuple-element.294), calls=%async_computation | async-start | bytes 2097152 | tf_op jit(solution)/shard_map/all_to_all | solution.py:628
  145.5 33.9 %collective-permute-start.43 = (f32[8,128,128]{2,1,0:T(8,128)}, f32[8,128,128]{2,1,0:T(8,128)S(1)}, u32[]{:S(2)}, u32[]{:S(2)}) collective-permute-start(f32[8,128,128]{2,1,0:T(8,128)} %get-tuple-element.295), channel_id=1, source_target_pairs={{0,0},{1,2},{2,1},{3,3},{4,4},{5,6},{6,5},{7,7},{8,8},{9,10},{10,9... | collective-permute-start | bytes 1572872 | tf_op jit(solution)/shard_map/ppermute | solution.py:629
  148.9 30.6 %collective-permute-start.44 = (f32[8,128,128]{2,1,0:T(8,128)}, f32[8,128,128]{2,1,0:T(8,128)S(1)}, u32[]{:S(2)}, u32[]{:S(2)}) collective-permute-start(f32[8,128,128]{2,1,0:T(8,128)} %get-tuple-element.296), channel_id=1, source_target_pairs={{2,0},{0,1},{3,2},{1,3},{6,4},{4,5},{7,6},{5,7},{10,8},{8,9},{11,1... | collective-permute-start | bytes 1572872 | tf_op jit(solution)/shard_map/ppermute | solution.py:630
  148.9 26.8 %collective-permute-start.41 = (f32[2,16,8,128]{3,2,1,0:T(8,128)S(1)}, f32[2,16,8,128]{3,2,1,0:T(8,128)S(1)}, u32[]{:S(2)}, u32[]{:S(2)}) collective-permute-start(f32[2,16,8,128]{3,2,1,0:T(8,128)S(1)} %get-tuple-element.289), channel_id=1, source_target_pairs={{0,12},{1,13},{2,14},{3,15},{4,8},{5,9},{6,10},{7,11},{8,4},{9,5},... | collective-permute-start | bytes 393224 | tf_op jit(solution)/shard_map/ppermute | solution.py:622
  175.8 0.9 copy-start.9
  176.7 0.9 copy-start.11
  177.6 0.9 copy-start.13
  178.5 0.9 copy-start.15
  (1 other events, 0.6 us)

commit v10 on v8

--- a/solution.py
+++ b/solution.py
@@ -337,34 +337,22 @@
 
 
 def regather_kernel(*refs):
-    held_by, (own, *parts) = refs[:4], refs[4:]
-    groups = held_by[0].shape[0]
-    pieces = len(parts) // (groups - 1)
-    size = 4 // pieces
+    held_by, (own, *parts) = refs[:2], refs[2:]
+    group = lax.axis_index("gz") // 4
+    for i, strips in enumerate(held_by):
+        own[i] = strips[group]
+        for distance, part in enumerate(parts):
+            part[i] = strips[jnp.bitwise_xor(group, distance + 1)]
+
+
+def collect_kernel(*refs):
+    parts, out = refs[:-1], refs[-1]
     group = lax.axis_index("gz") // 4
     mine = lax.rem(lax.axis_index("gz"), 4)
-    for which, strips in enumerate(held_by):
-        source = jnp.bitwise_xor(mine, which)
-        own[source] = strips[group]
-        for i, part in enumerate(parts):
-            first = (i % pieces) * size
-
-            @pl.when((source >= first) & (source < first + size))
-            def _(i=i, part=part, first=first, source=source, strips=strips):
-                part[source - first] = strips[jnp.bitwise_xor(group, i // pieces + 1)]
-
-
-def collect_kernel(own, *refs):
-    parts, out = refs[:-1], refs[-1]
-    pieces = len(parts) // (out.shape[0] // 4 - 1)
-    size = 4 // pieces
-    group = lax.axis_index("gz") // 4
-    for i in range(4):
-        out[4 * group + i] = own[i]
     for i, part in enumerate(parts):
-        first = 4 * jnp.bitwise_xor(group, i // pieces + 1) + (i % pieces) * size
-        for j in range(size):
-            out[first + j] = part[j]
+        first = 4 * jnp.bitwise_xor(group, i // 2)
+        for j in range(2):
+            out[first + jnp.bitwise_xor(mine, 2 * (i % 2) + j)] = part[j]
 
 
 def image_kernel(shifts, *refs):
@@ -503,8 +491,7 @@
     prev, speed = merge(functools.partial(merge_rest_kernel, shared), (tall, whole), *before, *speed_parts)
 
     groups = count // 4
-    pieces = max(1, 8 // groups)
-    waiting, under_way, arrived = [], [], []
+    near, far, under_way, arrived = [], [], [], []
 
     snap = None
     for step in range(steps):
@@ -535,10 +522,8 @@
             low = lax.ppermute(low, ("shot", "gz"), between)
             cur, new, high = upper(across, along, high, speed, *faces, cur, new)
             high = lax.ppermute(high, "gz", within)
-            landed = []
-            if step not in (SNAP_EVERY, SNAP_EVERY + 1):
+            if step > SNAP_EVERY:
                 low, *landed = lax.optimization_barrier((low, *[array for _, array in under_way]))
-            if step not in (SNAP_EVERY, SNAP_EVERY + 1):
                 arrived += [(part, array) for (part, _), array in zip(under_way, landed)]
                 under_way = []
         else:
@@ -584,36 +569,33 @@
             late = regroup(late, late)
         if step == SNAP_EVERY - 1:
             strip_parts = merge(spread_kernel, (f32(groups, layers, rows, nx),) * 4, snap)
+            held_by = [strip_parts[0]]
             for which in (1, 2, 3):
                 payload, new = lax.optimization_barrier((strip_parts[which], new))
-                under_way.append((which, lax.ppermute(payload, "gz", [(i, i ^ which) for i in range(count)])))
+                held_by.append(lax.ppermute(payload, "gz", [(i, i ^ which) for i in range(count)]))
             snap = None
-        if step == SNAP_EVERY + 1:
-            *landed, new = lax.optimization_barrier((*[array for _, array in under_way], new))
-            own_strips, *sent = merge(
-                regather_kernel,
-                (f32(4, layers, rows, nx), *[f32(4 // pieces, layers, rows, nx)] * (pieces * (groups - 1))),
-                strip_parts[0],
-                *landed,
-            )
-            waiting = [
-                (j < pieces, j, [(i, 4 * ((i // 4) ^ (j // pieces + 1)) + i % 4) for i in range(count)])
-                for j in range(len(sent))
-            ]
-            under_way = []
-        slots = max(1, steps - 1 - step)
-        far = [item for item in waiting if not item[0]]
-        near = [item for item in waiting if item[0]]
-        chosen = far[: -(-len(far) // slots)] + (near[: -(-len(near) // slots)] if step > SNAP_EVERY + 1 or not far else [])
-        waiting = [item for item in waiting if item not in chosen]
-        for _, which_part, pairs in chosen:
-            payload = sent[which_part]
-            payload, new = lax.optimization_barrier((payload, new))
-            under_way.append((which_part, lax.ppermute(payload, "gz", pairs)))
+        if step in (SNAP_EVERY, SNAP_EVERY + 1):
+            side = step - SNAP_EVERY
+            *landed, new = lax.optimization_barrier((*held_by[2 * side : 2 * side + 2], new))
+            own, *sent = merge(regather_kernel, (f32(2, layers, rows, nx),) * groups, *landed)
+            arrived.append((side, own))
+            for distance in range(1, groups):
+                (near if distance == 1 else far).append((2 * distance + side, sent[distance - 1]))
+        if step >= SNAP_EVERY:
+            slots = max(1, steps - 2 - step)
+            total = len(far) + (groups - 2 if step == SNAP_EVERY else 0)
+            many = min(len(far), -(-total // slots))
+            chosen, far = far[:many], far[many:]
+            if step > SNAP_EVERY + 1:
+                chosen, near = chosen + near[:1], near[1:]
+            for part, payload in chosen:
+                payload, new = lax.optimization_barrier((payload, new))
+                pairs = [(i, 4 * ((i // 4) ^ (part // 2)) + i % 4) for i in range(count)]
+                under_way.append((part, lax.ppermute(payload, "gz", pairs)))
         prev, cur = cur, new
 
     (first,) = merge(
-        collect_kernel, (f32(count, layers, rows, nx),), own_strips, *[array for _, array in sorted(arrived + under_way, key=lambda item: item[0])]
+        collect_kernel, (f32(count, layers, rows, nx),), *[array for _, array in sorted(arrived + under_way, key=lambda item: item[0])]
     )
     second = lax.all_to_all(send, "gz", split_axis=0, concat_axis=0, tiled=True)
     back_a = lax.ppermute(out_a, "gz", first_pairs)

time: 187 us -> 176 us (0.941); the launches traced: 186 us -> 173 us
  waiting for transfers between devices: 78.5 us -> 68.1 us
  starting transfers between devices: 61.4 us -> 58.2 us
    ppermute x6, waiting for transfers between devices: 38.8 us -> 15.4 us  [local(): under_way.append((part, lax.ppermute(payload, 'gz', pairs)))]
    ppermute x1, waiting for transfers between devices: 0.01 us -> 7.97 us  [local(): back_a = lax.ppermute(out_a, 'gz', first_pairs)]
    ppermute x1, waiting for transfers between devices: 0.01 us -> 5.91 us  [local(): back_b = lax.ppermute(out_b, 'gz', back_pairs)]
    ppermute x4, waiting for transfers between devices: 21.4 us -> 18.9 us  [regroup(): lax.ppermute(a, 'gz', first_pairs)]
    ppermute x12, starting transfers between devices: 17.4 us -> 15.1 us  [local(): high = lax.ppermute(high, 'gz', within)]
    all_to_all x1, waiting for transfers between devices: 0.01 us -> 1.97 us  [local(): second = lax.all_to_all(send, 'gz', split_axis=0, concat_axis=0, tiled=True)]
    unnamed x38 -> x42, local copies, waits for them, and re-layouts: 8.67 us -> 8.93 us
  transfers between devices with their start and end apart: 46 -> 46, of which waited for: 17 -> 18; matrix products, arithmetic and copies ran while one was open for 0% -> 0% of each run, Pallas kernels for 15% -> 16%
where the time goes in v10:
time: 176 us; the launch traced here: 173 us
  waiting for transfers between devices  68.1 us (39%)
  starting transfers between devices  58.2 us (33%)
  Pallas kernels  36.3 us (21%)
  local copies, waits for them, and re-layouts  8.93 us (5%)
    ppermute x4, waiting for transfers between devices, regroup(): lax.ppermute(a, 'gz', first_pairs)  18.9 us
    ppermute x6, waiting for transfers between devices, local(): under_way.append((part, lax.ppermute(payload, 'gz', pairs)))  15.4 us
    ppermute x12, starting transfers between devices, local(): high = lax.ppermute(high, 'gz', within)  15.1 us
    pallas_call x11, Pallas kernels, local(): inner(functools.partial(inner_kernel, step, wide, True), out_shape=(tall,...  14.2 us
    ppermute x4, starting transfers between devices, regroup(): lax.ppermute(a, 'gz', first_pairs)  14.1 us
    ppermute x12, waiting for transfers between devices, local(): low = lax.ppermute(low, ('shot', 'gz'), between)  12.8 us
    ppermute x12, starting transfers between devices, local(): low = lax.ppermute(low, ('shot', 'gz'), between)  9.41 us
    unnamed x42, local copies, waits for them, and re-layouts  8.93 us
  transfers between devices with their start and end apart: 46, of which 18 were waited for; matrix products, arithmetic and copies ran while one was open for 0% of the time, Pallas kernels for 16%

profile of v10, /device:TPU:9, one launch (start us, length us, event | category | flops | bytes accessed | tf_op | source)
XLA Modules:
  0.0 173.0 jit_solution(12312243375284233640)
XLA Ops:
  0.6 3.7 %collective-permute-start.2 = (f32[8,128,128]{2,1,0:T(8,128)}, f32[8,128,128]{2,1,0:T(8,128)S(1)}, u32[]{:S(2)}, u32[]{:S(2)}) collective-permute-start(f32[8,128,128]{2,1,0:T(8,128)} %param.16), channel_id=1, source_target_pairs={{0,0},{1,2},{2,1},{3,3},{4,4},{5,6},{6,5},{7,7},{8,8},{9,10},{10,9... | collective-permute-start | bytes 1572872 | tf_op jit(solution)/shard_map/ppermute | solution.py:480
  4.4 1.0 copy-done.3
  5.4 1.0 copy-done.4
  6.5 2.1 %collective-permute-start.6 = (f32[8,128,128]{2,1,0:T(8,128)S(1)}, f32[8,128,128]{2,1,0:T(8,128)S(1)}, u32[]{:S(2)}, u32[]{:S(2)}) collective-permute-start(f32[8,128,128]{2,1,0:T(8,128)S(1)} %get-tuple-element.162), channel_id=1, source_target_pairs={{0,0},{1,2},{2,1},{3,3},{4,4},{5,6},{6,5},{7,7},{8,8},{9,10},{10,9... | collective-permute-start | bytes 1572872 | tf_op jit(solution)/shard_map/ppermute | solution.py:464
  8.6 1.0 copy-done.5
  9.7 1.0 copy-done.6
  10.8 3.6 %collective-permute-start = (f32[8,128,128]{2,1,0:T(8,128)S(1)}, f32[8,128,128]{2,1,0:T(8,128)S(1)}, u32[]{:S(2)}, u32[]{:S(2)}) collective-permute-start(f32[8,128,128]{2,1,0:T(8,128)S(1)} %get-tuple-element.157), channel_id=1, source_target_pairs={{0,0},{1,2},{2,1},{3,3},{4,4},{5,6},{6,5},{7,7},{8,8},{9,10},{10,9... | collective-permute-start | bytes 1572872 | tf_op jit(solution)/shard_map/ppermute | solution.py:464
  14.7 8.6 %collective-permute-done.6.now_a = f32[8,128,128]{2,1,0:T(8,128)S(1)} collective-permute-done((f32[8,128,128]{2,1,0:T(8,128)S(1)}, f32[8,128,128]{2,1,0:T(8,128)S(1)}, u32[]{:S(2)}, u32[]{:S(2)}) %collective-permute-start.6) | collective-permute-done | bytes 524320 | tf_op jit(solution)/shard_map/ppermute | solution.py:464
  23.7 1.0 collective-permute-start.9
  24.7 1.0 prepare.1
  25.7 8.2 %collective-permute-done.before_a = f32[8,128,128]{2,1,0:T(8,128)S(1)} collective-permute-done((f32[8,128,128]{2,1,0:T(8,128)S(1)}, f32[8,128,128]{2,1,0:T(8,128)S(1)}, u32[]{:S(2)}, u32[]{:S(2)}) %collective-permute-start) | collective-permute-done | bytes 524320 | tf_op jit(solution)/shard_map/ppermute | solution.py:464
  33.9 3.6 %collective-permute-start.4 = (f32[2,128,128]{2,1,0:T(8,128)S(1)}, f32[2,128,128]{2,1,0:T(8,128)S(1)}, u32[]{:S(2)}, u32[]{:S(2)}) collective-permute-start(f32[2,128,128]{2,1,0:T(8,128)S(1)} %get-tuple-element.161), channel_id=1, source_target_pairs={{0,0},{1,2},{2,1},{3,3},{4,4},{5,6},{6,5},{7,7},{8,8},{9,10},{10,9... | collective-permute-start | bytes 393224 | tf_op jit(solution)/shard_map/ppermute | solution.py:464
  38.1 2.1 %collective-permute-done.4.face_a.rest_0_ = f32[2,128,128]{2,1,0:T(8,128)S(1)} collective-permute-done((f32[2,128,128]{2,1,0:T(8,128)S(1)}, f32[2,128,128]{2,1,0:T(8,128)S(1)}, u32[]{:S(2)}, u32[]{:S(2)}) %collective-permute-start.4) | collective-permute-done | bytes 131104 | tf_op jit(solution)/shard_map/ppermute | solution.py:464
  41.7 1.3 inner.12
  43.0 3.5 %collective-permute-done.13.low = f32[4,128,128]{2,1,0:T(8,128)S(1)} collective-permute-done((f32[4,128,128]{2,1,0:T(8,128)S(1)}, f32[4,128,128]{2,1,0:T(8,128)S(1)}, u32[]{:S(2)}, u32[]{:S(2)}) %collective-permute-start.13) | collective-permute-done | bytes 262176 | tf_op jit(solution)/shard_map/ppermute | solution.py:522
  47.4 0.6 collective-permute-start.14
  48.0 1.3 inner.13
  49.3 3.5 %collective-permute-done.15.low = f32[4,128,128]{2,1,0:T(8,128)S(1)} collective-permute-done((f32[4,128,128]{2,1,0:T(8,128)S(1)}, f32[4,128,128]{2,1,0:T(8,128)S(1)}, u32[]{:S(2)}, u32[]{:S(2)}) %collective-permute-start.15) | collective-permute-done | bytes 262176 | tf_op jit(solution)/shard_map/ppermute | solution.py:522
  53.7 0.6 collective-permute-start.16
  54.4 4.8 %collective-permute-start.10 = (f32[4,128,128]{2,1,0:T(8,128)S(1)}, f32[4,128,128]{2,1,0:T(8,128)S(1)}, u32[]{:S(2)}, u32[]{:S(2)}) collective-permute-start(f32[4,128,128]{2,1,0:T(8,128)S(1)} %get-tuple-element.173), channel_id=1, source_target_pairs={{0,0},{1,2},{2,1},{3,3},{4,4},{5,6},{6,5},{7,7},{8,8},{9,10},{10,9... | collective-permute-start | bytes 786440 | tf_op jit(solution)/shard_map/ppermute | solution.py:464
  59.1 1.3 inner.14
  61.6 2.3 %collective-permute-start.18 = (f32[4,128,128]{2,1,0:T(8,128)S(1)}, f32[4,128,128]{2,1,0:T(8,128)S(1)}, u32[]{:S(2)}, u32[]{:S(2)}) collective-permute-start(f32[4,128,128]{2,1,0:T(8,128)S(1)} %get-tuple-element.195), channel_id=1, source_target_pairs={{0,1},{1,0},{2,3},{3,2},{4,5},{5,4},{6,7},{7,6},{8,9},{9,8},{10,11... | collective-permute-start | bytes 786440 | tf_op jit(solution)/shard_map/ppermute | solution.py:524
  64.0 1.3 inner.15
  65.2 1.8 %collective-permute-done.19.low = f32[4,128,128]{2,1,0:T(8,128)S(1)} collective-permute-done((f32[4,128,128]{2,1,0:T(8,128)S(1)}, f32[4,128,128]{2,1,0:T(8,128)S(1)}, u32[]{:S(2)}, u32[]{:S(2)}) %collective-permute-start.19) | collective-permute-done | bytes 262176 | tf_op jit(solution)/shard_map/ppermute | solution.py:522
  67.9 2.3 %collective-permute-start.20 = (f32[4,128,128]{2,1,0:T(8,128)S(1)}, f32[4,128,128]{2,1,0:T(8,128)S(1)}, u32[]{:S(2)}, u32[]{:S(2)}) collective-permute-start(f32[4,128,128]{2,1,0:T(8,128)S(1)} %get-tuple-element.203), channel_id=1, source_target_pairs={{0,1},{1,0},{2,3},{3,2},{4,5},{5,4},{6,7},{7,6},{8,9},{9,8},{10,11... | collective-permute-start | bytes 786440 | tf_op jit(solution)/shard_map/ppermute | solution.py:524
  70.2 1.4 inner.16
  71.6 1.8 %collective-permute-done.21.low = f32[4,128,128]{2,1,0:T(8,128)S(1)} collective-permute-done((f32[4,128,128]{2,1,0:T(8,128)S(1)}, f32[4,128,128]{2,1,0:T(8,128)S(1)}, u32[]{:S(2)}, u32[]{:S(2)}) %collective-permute-start.21) | collective-permute-done | bytes 262176 | tf_op jit(solution)/shard_map/ppermute | solution.py:522
  74.4 2.2 %collective-permute-start.23 = (f32[4,128,128]{2,1,0:T(8,128)S(1)}, f32[4,128,128]{2,1,0:T(8,128)S(1)}, u32[]{:S(2)}, u32[]{:S(2)}) collective-permute-start(f32[4,128,128]{2,1,0:T(8,128)S(1)} %get-tuple-element.219), channel_id=1, source_target_pairs={{0,1},{1,0},{2,3},{3,2},{4,5},{5,4},{6,7},{7,6},{8,9},{9,8},{10,11... | collective-permute-start | bytes 786440 | tf_op jit(solution)/shard_map/ppermute | solution.py:524
  76.5 1.4 inner.17
  78.2 1.5 collective-permute-done.24.low
  80.7 2.2 %collective-permute-start.27 = (f32[4,128,128]{2,1,0:T(8,128)S(1)}, f32[4,128,128]{2,1,0:T(8,128)S(1)}, u32[]{:S(2)}, u32[]{:S(2)}) collective-permute-start(f32[4,128,128]{2,1,0:T(8,128)S(1)} %get-tuple-element.236), channel_id=1, source_target_pairs={{0,1},{1,0},{2,3},{3,2},{4,5},{5,4},{6,7},{7,6},{8,9},{9,8},{10,11... | collective-permute-start | bytes 786440 | tf_op jit(solution)/shard_map/ppermute | solution.py:524
  82.8 1.4 collective-permute-start.25
  84.3 1.3 inner.18
  85.6 0.7 collective-permute-done.28.low
  87.3 2.2 %collective-permute-start.33 = (f32[4,128,128]{2,1,0:T(8,128)S(1)}, f32[4,128,128]{2,1,0:T(8,128)S(1)}, u32[]{:S(2)}, u32[]{:S(2)}) collective-permute-start(f32[4,128,128]{2,1,0:T(8,128)S(1)} %get-tuple-element.261), channel_id=1, source_target_pairs={{0,1},{1,0},{2,3},{3,2},{4,5},{5,4},{6,7},{7,6},{8,9},{9,8},{10,11... | collective-permute-start | bytes 786440 | tf_op jit(solution)/shard_map/ppermute | solution.py:524
  89.7 1.3 inner.19
  91.0 0.7 collective-permute-done.26.refs_1_
  91.7 4.4 %collective-permute-done.25.refs_0_ = f32[4,16,8,128]{3,2,1,0:T(8,128)S(1)} collective-permute-done((f32[4,16,8,128]{3,2,1,0:T(8,128)S(1)}, f32[4,16,8,128]{3,2,1,0:T(8,128)S(1)}, u32[]{:S(2)}, u32[]{:S(2)}) %collective-permute-start.25) | collective-permute-done | bytes 262176 | tf_op jit(solution)/shard_map/ppermute | solution.py:575
  96.6 2.0 %collective-permute-start.31 = (f32[4,128,128]{2,1,0:T(8,128)S(1)}, f32[4,128,128]{2,1,0:T(8,128)S(1)}, u32[]{:S(2)}, u32[]{:S(2)}) collective-permute-start(f32[4,128,128]{2,1,0:T(8,128)S(1)} %get-tuple-element.256), channel_id=1, source_target_pairs={{1,4},{4,1},{3,6},{6,3},{5,8},{8,5},{7,10},{10,7},{9,12},{12,9},{1... | collective-permute-start | bytes 786440 | tf_op jit(solution)/shard_map/ppermute | solution.py:522
  99.0 1.8 %collective-permute-start.37 = (f32[4,128,128]{2,1,0:T(8,128)S(1)}, f32[4,128,128]{2,1,0:T(8,128)S(1)}, u32[]{:S(2)}, u32[]{:S(2)}) collective-permute-start(f32[4,128,128]{2,1,0:T(8,128)S(1)} %get-tuple-element.277), channel_id=1, source_target_pairs={{0,1},{1,0},{2,3},{3,2},{4,5},{5,4},{6,7},{7,6},{8,9},{9,8},{10,11... | collective-permute-start | bytes 786440 | tf_op jit(solution)/shard_map/ppermute | solution.py:524
  100.9 1.4 inner.20
  102.3 5.2 %collective-permute-done.32.refs_6_ = f32[2,16,8,128]{3,2,1,0:T(8,128)S(1)} collective-permute-done((f32[2,16,8,128]{3,2,1,0:T(8,128)S(1)}, f32[2,16,8,128]{3,2,1,0:T(8,128)S(1)}, u32[]{:S(2)}, u32[]{:S(2)}) %collective-permute-start.32) | collective-permute-done | bytes 131104 | tf_op jit(solution)/shard_map/ppermute | solution.py:594
  107.9 2.6 %collective-permute-start.34 = (f32[4,128,128]{2,1,0:T(8,128)S(1)}, f32[4,128,128]{2,1,0:T(8,128)S(1)}, u32[]{:S(2)}, u32[]{:S(2)}) collective-permute-start(f32[4,128,128]{2,1,0:T(8,128)S(1)} %get-tuple-element.270), channel_id=1, source_target_pairs={{1,4},{4,1},{3,6},{6,3},{5,8},{8,5},{7,10},{10,7},{9,12},{12,9},{1... | collective-permute-start | bytes 786440 | tf_op jit(solution)/shard_map/ppermute | solution.py:522
  111.0 1.0 collective-permute-start.36
  112.3 1.3 inner.21
  113.6 5.2 %collective-permute-done.36.refs_2_ = f32[2,16,8,128]{3,2,1,0:T(8,128)S(1)} collective-permute-done((f32[2,16,8,128]{3,2,1,0:T(8,128)S(1)}, f32[2,16,8,128]{3,2,1,0:T(8,128)S(1)}, u32[]{:S(2)}, u32[]{:S(2)}) %collective-permute-start.36) | collective-permute-done | bytes 131104 | tf_op jit(solution)/shard_map/ppermute | solution.py:594
  119.5 2.9 %collective-permute-start.38 = (f32[4,128,128]{2,1,0:T(8,128)S(1)}, f32[4,128,128]{2,1,0:T(8,128)S(1)}, u32[]{:S(2)}, u32[]{:S(2)}) collective-permute-start(f32[4,128,128]{2,1,0:T(8,128)S(1)} %get-tuple-element.286), channel_id=1, source_target_pairs={{1,4},{4,1},{3,6},{6,3},{5,8},{8,5},{7,10},{10,7},{9,12},{12,9},{1... | collective-permute-start | bytes 786440 | tf_op jit(solution)/shard_map/ppermute | solution.py:522
  123.1 1.4 collective-permute-start.40
  124.9 1.3 inner.22
  126.2 0.7 inner.23.prev
  127.0 5.0 %collective-permute-done.40.refs_3_ = f32[2,16,8,128]{3,2,1,0:T(8,128)S(1)} collective-permute-done((f32[2,16,8,128]{3,2,1,0:T(8,128)S(1)}, f32[2,16,8,128]{3,2,1,0:T(8,128)S(1)}, u32[]{:S(2)}, u32[]{:S(2)}) %collective-permute-start.40) | collective-permute-done | bytes 131104 | tf_op jit(solution)/shard_map/ppermute | solution.py:594
  131.9 3.0 %last.1 = (f32[24,128,128]{2,1,0:T(8,128)S(1)}, f32[24,128,128]{2,1,0:T(8,128)S(1)}, f32[16,16,8,128]{3,2,1,0:T(8,128)S(1)}, f32[8,128,128]{2,1,0:T(8,128)}, f32...) custom-call(s32[2]{0:T(128)S(1)} %copy-done.18, ...), custom_call_target="tpu_custom_call", output_to_operand_aliasing={{0}: (9, {}), {1}: (10, {}), {2}: (11, {})} | custom-call | tf_op jit(solution)/shard_map/last/pallas_call | solution.py:566
  134.9 7.3 %all-to-all-start = ((f32[16,16,8,128]{3,2,1,0:T(8,128)}), f32[16,16,8,128]{3,2,1,0:T(8,128)S(1)}, u32[]{:S(2)}, u32[]{:S(2)}) async-start(f32[16,16,8,128]{3,2,1,0:T(8,128)} %get-tuple-element.304), calls=%async_computation | async-start | bytes 2097152 | tf_op jit(solution)/shard_map/all_to_all | solution.py:600
  142.2 3.4 %collective-permute-start.43 = (f32[8,128,128]{2,1,0:T(8,128)}, f32[8,128,128]{2,1,0:T(8,128)S(1)}, u32[]{:S(2)}, u32[]{:S(2)}) collective-permute-start(f32[8,128,128]{2,1,0:T(8,128)} %get-tuple-element.305), channel_id=1, source_target_pairs={{0,0},{1,2},{2,1},{3,3},{4,4},{5,6},{6,5},{7,7},{8,8},{9,10},{10,9... | collective-permute-start | bytes 1572872 | tf_op jit(solution)/shard_map/ppermute | solution.py:601
  145.6 0.9 copy-done.9
  146.5 0.9 copy-done.11
  147.4 0.9 copy-done.13
  148.3 0.9 copy-done.15
  149.2 0.9 copy-done.17
  150.2 8.0 %collective-permute-done.43.here = f32[8,128,128]{2,1,0:T(8,128)S(1)} collective-permute-done((f32[8,128,128]{2,1,0:T(8,128)}, f32[8,128,128]{2,1,0:T(8,128)S(1)}, u32[]{:S(2)}, u32[]{:S(2)}) %collective-permute-start.43) | collective-permute-done | bytes 524320 | tf_op jit(solution)/shard_map/ppermute | solution.py:601
  158.2 5.9 %collective-permute-done.44.there = f32[8,128,128]{2,1,0:T(8,128)S(1)} collective-permute-done((f32[8,128,128]{2,1,0:T(8,128)}, f32[8,128,128]{2,1,0:T(8,128)S(1)}, u32[]{:S(2)}, u32[]{:S(2)}) %collective-permute-start.44) | collective-permute-done | bytes 524320 | tf_op jit(solution)/shard_map/ppermute | solution.py:602
  164.1 1.1 choose.5
  165.2 2.0 %all-to-all-done.refs_1_ = f32[16,16,8,128]{3,2,1,0:T(8,128)S(1)} async-done(((f32[16,16,8,128]{3,2,1,0:T(8,128)}), f32[16,16,8,128]{3,2,1,0:T(8,128)S(1)}, u32[]{:S(2)}, u32[]{:S(2)}) %all-to-all-start) | async-done | bytes 1048608 | tf_op jit(solution)/shard_map/all_to_all | solution.py:600
  167.1 5.7 %images.1 = bf16[8,128,8,128]{3,2,1,0:T(8,128)(2,1)} custom-call(bf16[2,256,1024]{2,1,0:T(8,128)(2,1)S(1)} %get-tuple-element.156.shifts, f32[16,16,8,128]{3,2,1,0:T(8,128)S(1)} %shard_map.144.refs_0_, f32[16,16,8,128]{3,2,1,0:T(8,128)S(1)} %all-to-all-done.refs_1_), custom_call_target="tpu_custom_call" | custom-call | tf_op jit(solution)/shard_map/images/pallas_call | solution.py:423
  (116 shorter events, 14.3 us)
Async XLA Ops:
  0.6 13.9 %collective-permute-start.2 = (f32[8,128,128]{2,1,0:T(8,128)}, f32[8,128,128]{2,1,0:T(8,128)S(1)}, u32[]{:S(2)}, u32[]{:S(2)}) collective-permute-start(f32[8,128,128]{2,1,0:T(8,128)} %param.16), channel_id=1, source_target_pairs={{0,0},{1,2},{2,1},{3,3},{4,4},{5,6},{6,5},{7,7},{8,8},{9,10},{10,9... | collective-permute-start | bytes 1572872 | tf_op jit(solution)/shard_map/ppermute | solution.py:480
  4.3 1.0 copy-start.3
  5.4 1.0 copy-start.4
  6.4 18.3 %copy-start.7 = (f32[12,8,8,128]{3,2,1,0:T(8,128)S(1)}, f32[12,8,8,128]{3,2,1,0:T(8,128)}, u32[]{:S(2)}) copy-start(f32[12,8,8,128]{3,2,1,0:T(8,128)} %param.17) | copy-start | bytes 1179652
  6.4 18.3 %copy-start.19 = (s32[12]{0:T(128)S(1)}, s32[12]{0:T(128)}, u32[]{:S(2)}) copy-start(s32[12]{0:T(128)} %face_steps.1) | copy-start | bytes 148
  6.4 18.3 %copy-start.20 = (s32[8]{0:T(128)S(1)}, s32[8]{0:T(128)}, u32[]{:S(2)}) copy-start(s32[8]{0:T(128)} %lags.1) | copy-start | bytes 100
  6.5 16.8 %collective-permute-start.6 = (f32[8,128,128]{2,1,0:T(8,128)S(1)}, f32[8,128,128]{2,1,0:T(8,128)S(1)}, u32[]{:S(2)}, u32[]{:S(2)}) collective-permute-start(f32[8,128,128]{2,1,0:T(8,128)S(1)} %get-tuple-element.162), channel_id=1, source_target_pairs={{0,0},{1,2},{2,1},{3,3},{4,4},{5,6},{6,5},{7,7},{8,8},{9,10},{10,9... | collective-permute-start | bytes 1572872 | tf_op jit(solution)/shard_map/ppermute | solution.py:464
  8.6 14.7 %collective-permute-start.7 = (f32[8,128,128]{2,1,0:T(8,128)S(1)}, f32[8,128,128]{2,1,0:T(8,128)S(1)}, u32[]{:S(2)}, u32[]{:S(2)}) collective-permute-start(f32[8,128,128]{2,1,0:T(8,128)S(1)} %get-tuple-element.163), channel_id=1, source_target_pairs={{0,2},{1,0},{2,3},{3,1},{4,6},{5,4},{6,7},{7,5},{8,10},{9,8},{10,1... | collective-permute-start | bytes 1572872 | tf_op jit(solution)/shard_map/ppermute | solution.py:464
  8.6 1.0 copy-start.5
  9.7 1.0 copy-start.6
  10.8 23.1 %collective-permute-start = (f32[8,128,128]{2,1,0:T(8,128)S(1)}, f32[8,128,128]{2,1,0:T(8,128)S(1)}, u32[]{:S(2)}, u32[]{:S(2)}) collective-permute-start(f32[8,128,128]{2,1,0:T(8,128)S(1)} %get-tuple-element.157), channel_id=1, source_target_pairs={{0,0},{1,2},{2,1},{3,3},{4,4},{5,6},{6,5},{7,7},{8,8},{9,10},{10,9... | collective-permute-start | bytes 1572872 | tf_op jit(solution)/shard_map/ppermute | solution.py:464
  14.5 25.7 %copy-start = (bf16[128,256]{1,0:T(8,128)(2,1)S(1)}, bf16[128,256]{1,0:T(8,128)(2,1)}, u32[]{:S(2)}) copy-start(bf16[128,256]{1,0:T(8,128)(2,1)} %constant.5.clone.along) | copy-start | bytes 196612
  14.5 25.7 %copy-start.1 = (bf16[256,128]{1,0:T(8,128)(2,1)S(1)}, bf16[256,128]{1,0:T(8,128)(2,1)}, u32[]{:S(2)}) copy-start(bf16[256,128]{1,0:T(8,128)(2,1)} %constant.4.clone.across) | copy-start | bytes 196612
  14.5 25.7 %copy-start.2 = (bf16[12,128,128]{2,1,0:T(8,128)(2,1)S(1)}, bf16[12,128,128]{2,1,0:T(8,128)(2,1)}, u32[]{:S(2)}) copy-start(bf16[12,128,128]{2,1,0:T(8,128)(2,1)} %traces.23) | copy-start | bytes 1179652
  14.5 19.4 %collective-permute-start.1 = (f32[8,128,128]{2,1,0:T(8,128)S(1)}, f32[8,128,128]{2,1,0:T(8,128)S(1)}, u32[]{:S(2)}, u32[]{:S(2)}) collective-permute-start(f32[8,128,128]{2,1,0:T(8,128)S(1)} %get-tuple-element.158), channel_id=1, source_target_pairs={{0,2},{1,0},{2,3},{3,1},{4,6},{5,4},{6,7},{7,5},{8,10},{9,8},{10,1... | collective-permute-start | bytes 1572872 | tf_op jit(solution)/shard_map/ppermute | solution.py:464
  14.5 23.0 %collective-permute-start.3 = (f32[8,128,128]{2,1,0:T(8,128)S(1)}, f32[8,128,128]{2,1,0:T(8,128)S(1)}, u32[]{:S(2)}, u32[]{:S(2)}) collective-permute-start(f32[8,128,128]{2,1,0:T(8,128)S(1)} %collective-permute-done.2.speed_a), channel_id=1, source_target_pairs={{0,16},{16,0},{1,17},{17,1},{2,18},{18,2},{3,19},{19,3},{4,20},{20... | collective-permute-start | bytes 1572872 | tf_op jit(solution)/shard_map/ppermute | solution.py:481
  23.7 16.4 %collective-permute-start.9 = (f32[4,128,128]{2,1,0:T(8,128)S(1)}, f32[4,128,128]{2,1,0:T(8,128)S(1)}, u32[]{:S(2)}, u32[]{:S(2)}) collective-permute-start(f32[4,128,128]{2,1,0:T(8,128)S(1)} %get-tuple-element.165), channel_id=1, source_target_pairs={{1,4},{4,1},{3,6},{6,3},{5,8},{8,5},{7,10},{10,7},{9,12},{12,9},{1... | collective-permute-start | bytes 786440 | tf_op jit(solution)/shard_map/ppermute | solution.py:489
  24.7 16.0 %collective-permute-start.8 = (f32[4,128,128]{2,1,0:T(8,128)S(1)}, f32[4,128,128]{2,1,0:T(8,128)S(1)}, u32[]{:S(2)}, u32[]{:S(2)}) collective-permute-start(f32[4,128,128]{2,1,0:T(8,128)S(1)} %get-tuple-element.164), channel_id=1, source_target_pairs={{0,1},{1,0},{2,3},{3,2},{4,5},{5,4},{6,7},{7,6},{8,9},{9,8},{10,11... | collective-permute-start | bytes 786440 | tf_op jit(solution)/shard_map/ppermute | solution.py:490
  33.9 4.2 %collective-permute-start.5 = (f32[2,128,128]{2,1,0:T(8,128)S(1)}, f32[2,128,128]{2,1,0:T(8,128)S(1)}, u32[]{:S(2)}, u32[]{:S(2)}) collective-permute-start(f32[2,128,128]{2,1,0:T(8,128)S(1)} %get-tuple-element.161), channel_id=1, source_target_pairs={{0,2},{1,0},{2,3},{3,1},{4,6},{5,4},{6,7},{7,5},{8,10},{9,8},{10,1... | collective-permute-start | bytes 393224 | tf_op jit(solution)/shard_map/ppermute | solution.py:464
  33.9 6.3 %collective-permute-start.4 = (f32[2,128,128]{2,1,0:T(8,128)S(1)}, f32[2,128,128]{2,1,0:T(8,128)S(1)}, u32[]{:S(2)}, u32[]{:S(2)}) collective-permute-start(f32[2,128,128]{2,1,0:T(8,128)S(1)} %get-tuple-element.161), channel_id=1, source_target_pairs={{0,0},{1,2},{2,1},{3,3},{4,4},{5,6},{6,5},{7,7},{8,8},{9,10},{10,9... | collective-permute-start | bytes 393224 | tf_op jit(solution)/shard_map/ppermute | solution.py:464
  40.6 5.9 %collective-permute-start.13 = (f32[4,128,128]{2,1,0:T(8,128)S(1)}, f32[4,128,128]{2,1,0:T(8,128)S(1)}, u32[]{:S(2)}, u32[]{:S(2)}) collective-permute-start(f32[4,128,128]{2,1,0:T(8,128)S(1)} %get-tuple-element.175), channel_id=1, source_target_pairs={{1,4},{4,1},{3,6},{6,3},{5,8},{8,5},{7,10},{10,7},{9,12},{12,9},{1... | collective-permute-start | bytes 786440 | tf_op jit(solution)/shard_map/ppermute | solution.py:522
  40.7 1.0 copy-start.18
  41.1 5.9 %collective-permute-start.12 = (f32[4,128,128]{2,1,0:T(8,128)S(1)}, f32[4,128,128]{2,1,0:T(8,128)S(1)}, u32[]{:S(2)}, u32[]{:S(2)}) collective-permute-start(f32[4,128,128]{2,1,0:T(8,128)S(1)} %get-tuple-element.174), channel_id=1, source_target_pairs={{0,1},{1,0},{2,3},{3,2},{4,5},{5,4},{6,7},{7,6},{8,9},{9,8},{10,11... | collective-permute-start | bytes 786440 | tf_op jit(solution)/shard_map/ppermute | solution.py:524
  46.9 5.9 %collective-permute-start.15 = (f32[4,128,128]{2,1,0:T(8,128)S(1)}, f32[4,128,128]{2,1,0:T(8,128)S(1)}, u32[]{:S(2)}, u32[]{:S(2)}) collective-permute-start(f32[4,128,128]{2,1,0:T(8,128)S(1)} %get-tuple-element.180), channel_id=1, source_target_pairs={{1,4},{4,1},{3,6},{6,3},{5,8},{8,5},{7,10},{10,7},{9,12},{12,9},{1... | collective-permute-start | bytes 786440 | tf_op jit(solution)/shard_map/ppermute | solution.py:522
  47.4 5.9 %collective-permute-start.14 = (f32[4,128,128]{2,1,0:T(8,128)S(1)}, f32[4,128,128]{2,1,0:T(8,128)S(1)}, u32[]{:S(2)}, u32[]{:S(2)}) collective-permute-start(f32[4,128,128]{2,1,0:T(8,128)S(1)} %get-tuple-element.179), channel_id=1, source_target_pairs={{0,1},{1,0},{2,3},{3,2},{4,5},{5,4},{6,7},{7,6},{8,9},{9,8},{10,11... | collective-permute-start | bytes 786440 | tf_op jit(solution)/shard_map/ppermute | solution.py:524
  53.2 7.2 %collective-permute-start.17 = (f32[4,128,128]{2,1,0:T(8,128)S(1)}, f32[4,128,128]{2,1,0:T(8,128)S(1)}, u32[]{:S(2)}, u32[]{:S(2)}) collective-permute-start(f32[4,128,128]{2,1,0:T(8,128)S(1)} %get-tuple-element.188), channel_id=1, source_target_pairs={{1,4},{4,1},{3,6},{6,3},{5,8},{8,5},{7,10},{10,7},{9,12},{12,9},{1... | collective-permute-start | bytes 786440 | tf_op jit(solution)/shard_map/ppermute | solution.py:522
  53.7 7.5 %collective-permute-start.16 = (f32[4,128,128]{2,1,0:T(8,128)S(1)}, f32[4,128,128]{2,1,0:T(8,128)S(1)}, u32[]{:S(2)}, u32[]{:S(2)}) collective-permute-start(f32[4,128,128]{2,1,0:T(8,128)S(1)} %get-tuple-element.187), channel_id=1, source_target_pairs={{0,1},{1,0},{2,3},{3,2},{4,5},{5,4},{6,7},{7,6},{8,9},{9,8},{10,11... | collective-permute-start | bytes 786440 | tf_op jit(solution)/shard_map/ppermute | solution.py:524
  54.3 10.9 %collective-permute-start.11 = (f32[4,128,128]{2,1,0:T(8,128)S(1)}, f32[4,128,128]{2,1,0:T(8,128)S(1)}, u32[]{:S(2)}, u32[]{:S(2)}) collective-permute-start(f32[4,128,128]{2,1,0:T(8,128)S(1)} %get-tuple-element.173), channel_id=1, source_target_pairs={{0,2},{1,0},{2,3},{3,1},{4,6},{5,4},{6,7},{7,5},{8,10},{9,8},{10,1... | collective-permute-start | bytes 786440 | tf_op jit(solution)/shard_map/ppermute | solution.py:464
  54.4 10.9 %collective-permute-start.10 = (f32[4,128,128]{2,1,0:T(8,128)S(1)}, f32[4,128,128]{2,1,0:T(8,128)S(1)}, u32[]{:S(2)}, u32[]{:S(2)}) collective-permute-start(f32[4,128,128]{2,1,0:T(8,128)S(1)} %get-tuple-element.173), channel_id=1, source_target_pairs={{0,0},{1,2},{2,1},{3,3},{4,4},{5,6},{6,5},{7,7},{8,8},{9,10},{10,9... | collective-permute-start | bytes 786440 | tf_op jit(solution)/shard_map/ppermute | solution.py:464
  60.8 6.2 %collective-permute-start.19 = (f32[4,128,128]{2,1,0:T(8,128)S(1)}, f32[4,128,128]{2,1,0:T(8,128)S(1)}, u32[]{:S(2)}, u32[]{:S(2)}) collective-permute-start(f32[4,128,128]{2,1,0:T(8,128)S(1)} %get-tuple-element.196), channel_id=1, source_target_pairs={{1,4},{4,1},{3,6},{6,3},{5,8},{8,5},{7,10},{10,7},{9,12},{12,9},{1... | collective-permute-start | bytes 786440 | tf_op jit(solution)/shard_map/ppermute | solution.py:522
  61.6 5.9 %collective-permute-start.18 = (f32[4,128,128]{2,1,0:T(8,128)S(1)}, f32[4,128,128]{2,1,0:T(8,128)S(1)}, u32[]{:S(2)}, u32[]{:S(2)}) collective-permute-start(f32[4,128,128]{2,1,0:T(8,128)S(1)} %get-tuple-element.195), channel_id=1, source_target_pairs={{0,1},{1,0},{2,3},{3,2},{4,5},{5,4},{6,7},{7,6},{8,9},{9,8},{10,11... | collective-permute-start | bytes 786440 | tf_op jit(solution)/shard_map/ppermute | solution.py:524
  67.4 6.0 %collective-permute-start.21 = (f32[4,128,128]{2,1,0:T(8,128)S(1)}, f32[4,128,128]{2,1,0:T(8,128)S(1)}, u32[]{:S(2)}, u32[]{:S(2)}) collective-permute-start(f32[4,128,128]{2,1,0:T(8,128)S(1)} %get-tuple-element.204), channel_id=1, source_target_pairs={{1,4},{4,1},{3,6},{6,3},{5,8},{8,5},{7,10},{10,7},{9,12},{12,9},{1... | collective-permute-start | bytes 786440 | tf_op jit(solution)/shard_map/ppermute | solution.py:522
  67.9 6.0 %collective-permute-start.20 = (f32[4,128,128]{2,1,0:T(8,128)S(1)}, f32[4,128,128]{2,1,0:T(8,128)S(1)}, u32[]{:S(2)}, u32[]{:S(2)}) collective-permute-start(f32[4,128,128]{2,1,0:T(8,128)S(1)} %get-tuple-element.203), channel_id=1, source_target_pairs={{0,1},{1,0},{2,3},{3,2},{4,5},{5,4},{6,7},{7,6},{8,9},{9,8},{10,11... | collective-permute-start | bytes 786440 | tf_op jit(solution)/shard_map/ppermute | solution.py:524
  73.9 5.9 %collective-permute-start.24 = (f32[4,128,128]{2,1,0:T(8,128)S(1)}, f32[4,128,128]{2,1,0:T(8,128)S(1)}, u32[]{:S(2)}, u32[]{:S(2)}) collective-permute-start(f32[4,128,128]{2,1,0:T(8,128)S(1)} %get-tuple-element.220), channel_id=1, source_target_pairs={{1,4},{4,1},{3,6},{6,3},{5,8},{8,5},{7,10},{10,7},{9,12},{12,9},{1... | collective-permute-start | bytes 786440 | tf_op jit(solution)/shard_map/ppermute | solution.py:522
  74.4 5.9 %collective-permute-start.23 = (f32[4,128,128]{2,1,0:T(8,128)S(1)}, f32[4,128,128]{2,1,0:T(8,128)S(1)}, u32[]{:S(2)}, u32[]{:S(2)}) collective-permute-start(f32[4,128,128]{2,1,0:T(8,128)S(1)} %get-tuple-element.219), channel_id=1, source_target_pairs={{0,1},{1,0},{2,3},{3,2},{4,5},{5,4},{6,7},{7,6},{8,9},{9,8},{10,11... | collective-permute-start | bytes 786440 | tf_op jit(solution)/shard_map/ppermute | solution.py:524
  78.1 7.4 %collective-permute-start.22 = (f32[4,16,8,128]{3,2,1,0:T(8,128)S(1)}, f32[4,16,8,128]{3,2,1,0:T(8,128)S(1)}, u32[]{:S(2)}, u32[]{:S(2)}) collective-permute-start(f32[4,16,8,128]{3,2,1,0:T(8,128)S(1)} %get-tuple-element.218), channel_id=1, source_target_pairs={{0,1},{1,0},{2,3},{3,2},{4,5},{5,4},{6,7},{7,6},{8,9},{9,8},{10,11... | collective-permute-start | bytes 786440 | tf_op jit(solution)/shard_map/ppermute | solution.py:575
  80.2 6.2 %collective-permute-start.28 = (f32[4,128,128]{2,1,0:T(8,128)S(1)}, f32[4,128,128]{2,1,0:T(8,128)S(1)}, u32[]{:S(2)}, u32[]{:S(2)}) collective-permute-start(f32[4,128,128]{2,1,0:T(8,128)S(1)} %get-tuple-element.237), channel_id=1, source_target_pairs={{1,4},{4,1},{3,6},{6,3},{5,8},{8,5},{7,10},{10,7},{9,12},{12,9},{1... | collective-permute-start | bytes 786440 | tf_op jit(solution)/shard_map/ppermute | solution.py:522
  80.7 6.2 %collective-permute-start.27 = (f32[4,128,128]{2,1,0:T(8,128)S(1)}, f32[4,128,128]{2,1,0:T(8,128)S(1)}, u32[]{:S(2)}, u32[]{:S(2)}) collective-permute-start(f32[4,128,128]{2,1,0:T(8,128)S(1)} %get-tuple-element.236), channel_id=1, source_target_pairs={{0,1},{1,0},{2,3},{3,2},{4,5},{5,4},{6,7},{7,6},{8,9},{9,8},{10,11... | collective-permute-start | bytes 786440 | tf_op jit(solution)/shard_map/ppermute | solution.py:524
  82.8 8.9 %collective-permute-start.26 = (f32[4,16,8,128]{3,2,1,0:T(8,128)S(1)}, f32[4,16,8,128]{3,2,1,0:T(8,128)S(1)}, u32[]{:S(2)}, u32[]{:S(2)}) collective-permute-start(f32[4,16,8,128]{3,2,1,0:T(8,128)S(1)} %get-tuple-element.235), channel_id=1, source_target_pairs={{0,3},{1,2},{2,1},{3,0},{4,7},{5,6},{6,5},{7,4},{8,11},{9,10},{10,... | collective-permute-start | bytes 786440 | tf_op jit(solution)/shard_map/ppermute | solution.py:575
  82.8 13.3 %collective-permute-start.25 = (f32[4,16,8,128]{3,2,1,0:T(8,128)S(1)}, f32[4,16,8,128]{3,2,1,0:T(8,128)S(1)}, u32[]{:S(2)}, u32[]{:S(2)}) collective-permute-start(f32[4,16,8,128]{3,2,1,0:T(8,128)S(1)} %get-tuple-element.234), channel_id=1, source_target_pairs={{0,2},{1,3},{2,0},{3,1},{4,6},{5,7},{6,4},{7,5},{8,10},{9,11},{10,... | collective-permute-start | bytes 786440 | tf_op jit(solution)/shard_map/ppermute | solution.py:575
  86.8 9.4 %collective-permute-start.29 = (f32[4,128,128]{2,1,0:T(8,128)S(1)}, f32[4,128,128]{2,1,0:T(8,128)S(1)}, u32[]{:S(2)}, u32[]{:S(2)}) collective-permute-start(f32[4,128,128]{2,1,0:T(8,128)S(1)} %get-tuple-element.250), channel_id=1, source_target_pairs={{1,4},{4,1},{3,6},{6,3},{5,8},{8,5},{7,10},{10,7},{9,12},{12,9},{1... | collective-permute-start | bytes 786440 | tf_op jit(solution)/shard_map/ppermute | solution.py:522
  87.3 11.3 %collective-permute-start.33 = (f32[4,128,128]{2,1,0:T(8,128)S(1)}, f32[4,128,128]{2,1,0:T(8,128)S(1)}, u32[]{:S(2)}, u32[]{:S(2)}) collective-permute-start(f32[4,128,128]{2,1,0:T(8,128)S(1)} %get-tuple-element.261), channel_id=1, source_target_pairs={{0,1},{1,0},{2,3},{3,2},{4,5},{5,4},{6,7},{7,6},{8,9},{9,8},{10,11... | collective-permute-start | bytes 786440 | tf_op jit(solution)/shard_map/ppermute | solution.py:524
  89.4 6.7 %collective-permute-start.30 = (f32[2,16,8,128]{3,2,1,0:T(8,128)S(1)}, f32[2,16,8,128]{3,2,1,0:T(8,128)S(1)}, u32[]{:S(2)}, u32[]{:S(2)}) collective-permute-start(f32[2,16,8,128]{3,2,1,0:T(8,128)S(1)} %get-tuple-element.251), channel_id=1, source_target_pairs={{0,8},{1,9},{2,10},{3,11},{4,12},{5,13},{6,14},{7,15},{8,0},{9,1},... | collective-permute-start | bytes 393224 | tf_op jit(solution)/shard_map/ppermute | solution.py:594
  96.6 10.9 %collective-permute-start.31 = (f32[4,128,128]{2,1,0:T(8,128)S(1)}, f32[4,128,128]{2,1,0:T(8,128)S(1)}, u32[]{:S(2)}, u32[]{:S(2)}) collective-permute-start(f32[4,128,128]{2,1,0:T(8,128)S(1)} %get-tuple-element.256), channel_id=1, source_target_pairs={{1,4},{4,1},{3,6},{6,3},{5,8},{8,5},{7,10},{10,7},{9,12},{12,9},{1... | collective-permute-start | bytes 786440 | tf_op jit(solution)/shard_map/ppermute | solution.py:522
  99.0 11.5 %collective-permute-start.37 = (f32[4,128,128]{2,1,0:T(8,128)S(1)}, f32[4,128,128]{2,1,0:T(8,128)S(1)}, u32[]{:S(2)}, u32[]{:S(2)}) collective-permute-start(f32[4,128,128]{2,1,0:T(8,128)S(1)} %get-tuple-element.277), channel_id=1, source_target_pairs={{0,1},{1,0},{2,3},{3,2},{4,5},{5,4},{6,7},{7,6},{8,9},{9,8},{10,11... | collective-permute-start | bytes 786440 | tf_op jit(solution)/shard_map/ppermute | solution.py:524
  100.8 6.6 %collective-permute-start.32 = (f32[2,16,8,128]{3,2,1,0:T(8,128)S(1)}, f32[2,16,8,128]{3,2,1,0:T(8,128)S(1)}, u32[]{:S(2)}, u32[]{:S(2)}) collective-permute-start(f32[2,16,8,128]{3,2,1,0:T(8,128)S(1)} %get-tuple-element.257), channel_id=1, source_target_pairs={{0,12},{1,13},{2,14},{3,15},{4,8},{5,9},{6,10},{7,11},{8,4},{9,5},... | collective-permute-start | bytes 393224 | tf_op jit(solution)/shard_map/ppermute | solution.py:594
  100.8 1.4 copy-start.8
  107.9 11.0 %collective-permute-start.34 = (f32[4,128,128]{2,1,0:T(8,128)S(1)}, f32[4,128,128]{2,1,0:T(8,128)S(1)}, u32[]{:S(2)}, u32[]{:S(2)}) collective-permute-start(f32[4,128,128]{2,1,0:T(8,128)S(1)} %get-tuple-element.270), channel_id=1, source_target_pairs={{1,4},{4,1},{3,6},{6,3},{5,8},{8,5},{7,10},{10,7},{9,12},{12,9},{1... | collective-permute-start | bytes 786440 | tf_op jit(solution)/shard_map/ppermute | solution.py:522
  110.9 11.5 %collective-permute-start.41 = (f32[4,128,128]{2,1,0:T(8,128)S(1)}, f32[4,128,128]{2,1,0:T(8,128)S(1)}, u32[]{:S(2)}, u32[]{:S(2)}) collective-permute-start(f32[4,128,128]{2,1,0:T(8,128)S(1)} %get-tuple-element.295), channel_id=1, source_target_pairs={{0,1},{1,0},{2,3},{3,2},{4,5},{5,4},{6,7},{7,6},{8,9},{9,8},{10,11... | collective-permute-start | bytes 786440 | tf_op jit(solution)/shard_map/ppermute | solution.py:524
  111.0 7.8 %collective-permute-start.36 = (f32[2,16,8,128]{3,2,1,0:T(8,128)S(1)}, f32[2,16,8,128]{3,2,1,0:T(8,128)S(1)}, u32[]{:S(2)}, u32[]{:S(2)}) collective-permute-start(f32[2,16,8,128]{3,2,1,0:T(8,128)S(1)} %get-tuple-element.272), channel_id=1, source_target_pairs={{0,4},{1,5},{2,6},{3,7},{4,0},{5,1},{6,2},{7,3},{8,12},{9,13},{10,... | collective-permute-start | bytes 393224 | tf_op jit(solution)/shard_map/ppermute | solution.py:594
  112.0 6.9 %collective-permute-start.35 = (f32[2,16,8,128]{3,2,1,0:T(8,128)S(1)}, f32[2,16,8,128]{3,2,1,0:T(8,128)S(1)}, u32[]{:S(2)}, u32[]{:S(2)}) collective-permute-start(f32[2,16,8,128]{3,2,1,0:T(8,128)S(1)} %get-tuple-element.271), channel_id=1, source_target_pairs={{0,8},{1,9},{2,10},{3,11},{4,12},{5,13},{6,14},{7,15},{8,0},{9,1},... | collective-permute-start | bytes 393224 | tf_op jit(solution)/shard_map/ppermute | solution.py:594
  119.5 12.4 %collective-permute-start.38 = (f32[4,128,128]{2,1,0:T(8,128)S(1)}, f32[4,128,128]{2,1,0:T(8,128)S(1)}, u32[]{:S(2)}, u32[]{:S(2)}) collective-permute-start(f32[4,128,128]{2,1,0:T(8,128)S(1)} %get-tuple-element.286), channel_id=1, source_target_pairs={{1,4},{4,1},{3,6},{6,3},{5,8},{8,5},{7,10},{10,7},{9,12},{12,9},{1... | collective-permute-start | bytes 786440 | tf_op jit(solution)/shard_map/ppermute | solution.py:522
  122.8 9.1 %collective-permute-start.42 = (f32[4,128,128]{2,1,0:T(8,128)S(1)}, f32[4,128,128]{2,1,0:T(8,128)S(1)}, u32[]{:S(2)}, u32[]{:S(2)}) collective-permute-start(f32[4,128,128]{2,1,0:T(8,128)S(1)} %get-tuple-element.298), channel_id=1, source_target_pairs={{0,1},{1,0},{2,3},{3,2},{4,5},{5,4},{6,7},{7,6},{8,9},{9,8},{10,11... | collective-permute-start | bytes 786440 | tf_op jit(solution)/shard_map/ppermute | solution.py:524
  123.1 8.8 %collective-permute-start.40 = (f32[2,16,8,128]{3,2,1,0:T(8,128)S(1)}, f32[2,16,8,128]{3,2,1,0:T(8,128)S(1)}, u32[]{:S(2)}, u32[]{:S(2)}) collective-permute-start(f32[2,16,8,128]{3,2,1,0:T(8,128)S(1)} %get-tuple-element.288), channel_id=1, source_target_pairs={{0,4},{1,5},{2,6},{3,7},{4,0},{5,1},{6,2},{7,3},{8,12},{9,13},{10,... | collective-permute-start | bytes 393224 | tf_op jit(solution)/shard_map/ppermute | solution.py:594
  124.5 7.4 %collective-permute-start.39 = (f32[2,16,8,128]{3,2,1,0:T(8,128)S(1)}, f32[2,16,8,128]{3,2,1,0:T(8,128)S(1)}, u32[]{:S(2)}, u32[]{:S(2)}) collective-permute-start(f32[2,16,8,128]{3,2,1,0:T(8,128)S(1)} %get-tuple-element.287), channel_id=1, source_target_pairs={{0,12},{1,13},{2,14},{3,15},{4,8},{5,9},{6,10},{7,11},{8,4},{9,5},... | collective-permute-start | bytes 393224 | tf_op jit(solution)/shard_map/ppermute | solution.py:594
  131.9 3.0 %copy-start.14 = (f32[2,16,8,128]{3,2,1,0:T(8,128)}, f32[2,16,8,128]{3,2,1,0:T(8,128)S(1)}, u32[]{:S(2)}) copy-start(f32[2,16,8,128]{3,2,1,0:T(8,128)S(1)} %collective-permute-done.40.refs_3_) | copy-start | bytes 393220
  131.9 3.0 %copy-start.16 = (f32[2,16,8,128]{3,2,1,0:T(8,128)}, f32[2,16,8,128]{3,2,1,0:T(8,128)S(1)}, u32[]{:S(2)}) copy-start(f32[2,16,8,128]{3,2,1,0:T(8,128)S(1)} %collective-permute-done.39.refs_7_) | copy-start | bytes 393220
  134.9 32.2 %all-to-all-start = ((f32[16,16,8,128]{3,2,1,0:T(8,128)}), f32[16,16,8,128]{3,2,1,0:T(8,128)S(1)}, u32[]{:S(2)}, u32[]{:S(2)}) async-start(f32[16,16,8,128]{3,2,1,0:T(8,128)} %get-tuple-element.304), calls=%async_computation | async-start | bytes 2097152 | tf_op jit(solution)/shard_map/all_to_all | solution.py:600
  142.2 16.0 %collective-permute-start.43 = (f32[8,128,128]{2,1,0:T(8,128)}, f32[8,128,128]{2,1,0:T(8,128)S(1)}, u32[]{:S(2)}, u32[]{:S(2)}) collective-permute-start(f32[8,128,128]{2,1,0:T(8,128)} %get-tuple-element.305), channel_id=1, source_target_pairs={{0,0},{1,2},{2,1},{3,3},{4,4},{5,6},{6,5},{7,7},{8,8},{9,10},{10,9... | collective-permute-start | bytes 1572872 | tf_op jit(solution)/shard_map/ppermute | solution.py:601
  145.6 18.5 %collective-permute-start.44 = (f32[8,128,128]{2,1,0:T(8,128)}, f32[8,128,128]{2,1,0:T(8,128)S(1)}, u32[]{:S(2)}, u32[]{:S(2)}) collective-permute-start(f32[8,128,128]{2,1,0:T(8,128)} %get-tuple-element.306), channel_id=1, source_target_pairs={{2,0},{0,1},{3,2},{1,3},{6,4},{4,5},{7,6},{5,7},{10,8},{8,9},{11,1... | collective-permute-start | bytes 1572872 | tf_op jit(solution)/shard_map/ppermute | solution.py:602
  145.6 0.9 copy-start.9
  146.5 0.9 copy-start.11
  148.3 0.9 copy-start.15
  149.2 0.9 copy-start.17
  (3 other events, 2.2 us)

commit v11 on v8

--- a/solution.py
+++ b/solution.py
@@ -293,24 +293,33 @@
     high_out[...] = new[layers : layers + REACH]
 
 
-def inner_kernel(step, faces, keep, phase, across, along, speed, *rest):
+def inner_kernel(step, faces, keep, phase_in, across, along, speed, *rest):
+    if keep:
+        rest, (phase, sem) = rest[:-2], rest[-2:]
+        fetch = pltpu.make_async_copy(phase_in, phase, sem)
+        fetch.start()
     face, rest = rest[:faces], rest[faces:]
     cur, prev, new = rest[0], rest[1], rest[-2] if keep else rest[-1]
     layers = speed.shape[0]
     advance(step, across, along, cur, prev, speed, face, new, list(range(REACH, layers - REACH)))
     if keep:
+        fetch.wait()
         keep_snapshot(step, phase, new, rest[-1])
 
 
 def last_kernel(
-    step, phase, across, along, low, high, traces, speed, face_a, face_b, cur_in, prev, snap_in, cur, new, snap, out_a, out_b, send
+    step, phase_in, across, along, low, high, traces, speed, face_a, face_b, cur_in, prev, snap_in,
+    cur, new, snap, out_a, out_b, send, phase, sem,
 ):
+    fetch = pltpu.make_async_copy(phase_in, phase, sem)
+    fetch.start()
     layers = speed.shape[0]
     fill_low(low, cur)
     fill_high(high, cur)
     outer = [*range(REACH), *range(layers - REACH, layers)]
     advance(step, across, along, cur, prev, speed, (face_a, face_b), new, outer)
     add_trace(step, traces, new)
+    fetch.wait()
     keep_snapshot(step, phase, new, snap)
 
     def run(j, q, which):
@@ -557,8 +566,9 @@
             new, snap = inner(
                 functools.partial(inner_kernel, step, wide, True),
                 out_shape=(tall, strips),
-                in_specs=[SMEM] + [VMEM] * (len(operands) - 1),
+                in_specs=[ANY] + [VMEM] * (len(operands) - 1),
                 out_specs=(VMEM,) * 2,
+                scratch_shapes=[pltpu.SMEM(snap_phase.shape, jnp.int32), pltpu.SemaphoreType.DMA],
                 input_output_aliases=alias,
             )(*operands)
         else:
@@ -572,8 +582,9 @@
             last = pl.pallas_call(
                 functools.partial(last_kernel, step),
                 out_shape=(tall, tall, strips, half, half, f32(*strips.shape)),
-                in_specs=[SMEM] + [VMEM] * 11,
+                in_specs=[ANY] + [VMEM] * 11,
                 out_specs=(VMEM,) * 6,
+                scratch_shapes=[pltpu.SMEM(snap_phase.shape, jnp.int32), pltpu.SemaphoreType.DMA],
                 input_output_aliases={9: 0, 10: 1, 11: 2},
                 compiler_params=PARAMS,
                 name="last",

time: 187 us -> 187 us (level)
  Pallas kernels: 36.4 us -> 32 us
  waiting for transfers between devices: 78.5 us -> 81.9 us
    pallas_call x11, Pallas kernels: 14.1 us -> 10.3 us  [local(): inner(functools.partial(inner_kernel, step, wide, True), out_shape=(tall,...]
  transfers between devices with their start and end apart: 46 -> 46, of which waited for: 17 -> 18; matrix products, arithmetic and copies ran while one was open for 0% -> 0% of each run, Pallas kernels for 15% -> 13%
where the time goes in v11:
time: 187 us; the launch traced here: 186 us
  waiting for transfers between devices  81.9 us (44%)
  starting transfers between devices  61.8 us (33%)
  Pallas kernels  32 us (17%)
  local copies, waits for them, and re-layouts  8.67 us (5%)
    ppermute x6, waiting for transfers between devices, local(): under_way.append((which_part, lax.ppermute(payload, 'gz', pairs)))  39.8 us
    ppermute x4, waiting for transfers between devices, regroup(): lax.ppermute(a, 'gz', first_pairs)  21.5 us
    ppermute x12, starting transfers between devices, local(): high = lax.ppermute(high, 'gz', within)  17.7 us
    ppermute x12, waiting for transfers between devices, local(): low = lax.ppermute(low, ('shot', 'gz'), between)  14.4 us
    ppermute x4, starting transfers between devices, regroup(): lax.ppermute(a, 'gz', first_pairs)  14.1 us
    pallas_call x11, Pallas kernels, local(): inner(functools.partial(inner_kernel, step, wide, True), out_shape=(tall,...  10.3 us
    unnamed x38, local copies, waits for them, and re-layouts  8.67 us
    all_to_all x1, starting transfers between devices, local(): second = lax.all_to_all(send, 'gz', split_axis=0, concat_axis=0, tiled=True)  8.26 us
  transfers between devices with their start and end apart: 46, of which 18 were waited for; matrix products, arithmetic and copies ran while one was open for 0% of the time, Pallas kernels for 13%

profile of v11, /device:TPU:9, one launch (start us, length us, event | category | flops | bytes accessed | tf_op | source)
XLA Modules:
  0.0 185.9 jit_solution(3924325326982229878)
XLA Ops:
  0.6 3.7 %collective-permute-start.2 = (f32[8,128,128]{2,1,0:T(8,128)}, f32[8,128,128]{2,1,0:T(8,128)S(1)}, u32[]{:S(2)}, u32[]{:S(2)}) collective-permute-start(f32[8,128,128]{2,1,0:T(8,128)} %param.16), channel_id=1, source_target_pairs={{0,0},{1,2},{2,1},{3,3},{4,4},{5,6},{6,5},{7,7},{8,8},{9,10},{10,9... | collective-permute-start | bytes 1572872 | tf_op jit(solution)/shard_map/ppermute | solution.py:501
  4.4 1.0 copy-done.3
  5.4 1.0 copy-done.4
  6.5 2.1 %collective-permute-start.6 = (f32[8,128,128]{2,1,0:T(8,128)S(1)}, f32[8,128,128]{2,1,0:T(8,128)S(1)}, u32[]{:S(2)}, u32[]{:S(2)}) collective-permute-start(f32[8,128,128]{2,1,0:T(8,128)S(1)} %get-tuple-element.157), channel_id=1, source_target_pairs={{0,0},{1,2},{2,1},{3,3},{4,4},{5,6},{6,5},{7,7},{8,8},{9,10},{10,9... | collective-permute-start | bytes 1572872 | tf_op jit(solution)/shard_map/ppermute | solution.py:485
  8.6 1.0 copy-done.5
  9.7 1.0 copy-done.6
  10.8 3.6 %collective-permute-start = (f32[8,128,128]{2,1,0:T(8,128)S(1)}, f32[8,128,128]{2,1,0:T(8,128)S(1)}, u32[]{:S(2)}, u32[]{:S(2)}) collective-permute-start(f32[8,128,128]{2,1,0:T(8,128)S(1)} %get-tuple-element.152), channel_id=1, source_target_pairs={{0,0},{1,2},{2,1},{3,3},{4,4},{5,6},{6,5},{7,7},{8,8},{9,10},{10,9... | collective-permute-start | bytes 1572872 | tf_op jit(solution)/shard_map/ppermute | solution.py:485
  14.7 8.6 %collective-permute-done.6.now_a = f32[8,128,128]{2,1,0:T(8,128)S(1)} collective-permute-done((f32[8,128,128]{2,1,0:T(8,128)S(1)}, f32[8,128,128]{2,1,0:T(8,128)S(1)}, u32[]{:S(2)}, u32[]{:S(2)}) %collective-permute-start.6) | collective-permute-done | bytes 524320 | tf_op jit(solution)/shard_map/ppermute | solution.py:485
  23.7 1.0 collective-permute-start.9
  24.7 1.0 prepare.1
  25.7 8.2 %collective-permute-done.before_a = f32[8,128,128]{2,1,0:T(8,128)S(1)} collective-permute-done((f32[8,128,128]{2,1,0:T(8,128)S(1)}, f32[8,128,128]{2,1,0:T(8,128)S(1)}, u32[]{:S(2)}, u32[]{:S(2)}) %collective-permute-start) | collective-permute-done | bytes 524320 | tf_op jit(solution)/shard_map/ppermute | solution.py:485
  33.9 3.6 %collective-permute-start.4 = (f32[2,128,128]{2,1,0:T(8,128)S(1)}, f32[2,128,128]{2,1,0:T(8,128)S(1)}, u32[]{:S(2)}, u32[]{:S(2)}) collective-permute-start(f32[2,128,128]{2,1,0:T(8,128)S(1)} %get-tuple-element.156), channel_id=1, source_target_pairs={{0,0},{1,2},{2,1},{3,3},{4,4},{5,6},{6,5},{7,7},{8,8},{9,10},{10,9... | collective-permute-start | bytes 393224 | tf_op jit(solution)/shard_map/ppermute | solution.py:485
  38.1 2.1 %collective-permute-done.4.face_a.rest_0_ = f32[2,128,128]{2,1,0:T(8,128)S(1)} collective-permute-done((f32[2,128,128]{2,1,0:T(8,128)S(1)}, f32[2,128,128]{2,1,0:T(8,128)S(1)}, u32[]{:S(2)}, u32[]{:S(2)}) %collective-permute-start.4) | collective-permute-done | bytes 131104 | tf_op jit(solution)/shard_map/ppermute | solution.py:485
  41.7 0.9 inner.12
  42.7 3.8 %collective-permute-done.13.low = f32[4,128,128]{2,1,0:T(8,128)S(1)} collective-permute-done((f32[4,128,128]{2,1,0:T(8,128)S(1)}, f32[4,128,128]{2,1,0:T(8,128)S(1)}, u32[]{:S(2)}, u32[]{:S(2)}) %collective-permute-start.13) | collective-permute-done | bytes 262176 | tf_op jit(solution)/shard_map/ppermute | solution.py:544
  47.4 0.6 collective-permute-start.14
  48.0 0.8 inner.13
  48.9 3.9 %collective-permute-done.15.low = f32[4,128,128]{2,1,0:T(8,128)S(1)} collective-permute-done((f32[4,128,128]{2,1,0:T(8,128)S(1)}, f32[4,128,128]{2,1,0:T(8,128)S(1)}, u32[]{:S(2)}, u32[]{:S(2)}) %collective-permute-start.15) | collective-permute-done | bytes 262176 | tf_op jit(solution)/shard_map/ppermute | solution.py:544
  53.7 0.6 collective-permute-start.16
  54.3 0.9 inner.14
  55.3 3.8 %collective-permute-done.17.low = f32[4,128,128]{2,1,0:T(8,128)S(1)} collective-permute-done((f32[4,128,128]{2,1,0:T(8,128)S(1)}, f32[4,128,128]{2,1,0:T(8,128)S(1)}, u32[]{:S(2)}, u32[]{:S(2)}) %collective-permute-start.17) | collective-permute-done | bytes 262176 | tf_op jit(solution)/shard_map/ppermute | solution.py:544
  60.1 4.8 %collective-permute-start.10 = (f32[4,128,128]{2,1,0:T(8,128)S(1)}, f32[4,128,128]{2,1,0:T(8,128)S(1)}, u32[]{:S(2)}, u32[]{:S(2)}) collective-permute-start(f32[4,128,128]{2,1,0:T(8,128)S(1)} %get-tuple-element.168), channel_id=1, source_target_pairs={{0,0},{1,2},{2,1},{3,3},{4,4},{5,6},{6,5},{7,7},{8,8},{9,10},{10,9... | collective-permute-start | bytes 786440 | tf_op jit(solution)/shard_map/ppermute | solution.py:485
  65.4 0.8 inner.15
  66.6 2.6 %collective-permute-done.10.face_a.rest_0_ = f32[4,128,128]{2,1,0:T(8,128)S(1)} collective-permute-done((f32[4,128,128]{2,1,0:T(8,128)S(1)}, f32[4,128,128]{2,1,0:T(8,128)S(1)}, u32[]{:S(2)}, u32[]{:S(2)}) %collective-permute-start.10) | collective-permute-done | bytes 262176 | tf_op jit(solution)/shard_map/ppermute | solution.py:485
  70.1 3.2 %collective-permute-start.20 = (f32[4,128,128]{2,1,0:T(8,128)S(1)}, f32[4,128,128]{2,1,0:T(8,128)S(1)}, u32[]{:S(2)}, u32[]{:S(2)}) collective-permute-start(f32[4,128,128]{2,1,0:T(8,128)S(1)} %get-tuple-element.198), channel_id=1, source_target_pairs={{0,1},{1,0},{2,3},{3,2},{4,5},{5,4},{6,7},{7,6},{8,9},{9,8},{10,11... | collective-permute-start | bytes 786440 | tf_op jit(solution)/shard_map/ppermute | solution.py:546
  73.3 1.1 inner.16
  74.4 1.3 collective-permute-done.21.low
  76.7 2.9 %collective-permute-start.25 = (f32[4,128,128]{2,1,0:T(8,128)S(1)}, f32[4,128,128]{2,1,0:T(8,128)S(1)}, u32[]{:S(2)}, u32[]{:S(2)}) collective-permute-start(f32[4,128,128]{2,1,0:T(8,128)S(1)} %get-tuple-element.220), channel_id=1, source_target_pairs={{0,1},{1,0},{2,3},{3,2},{4,5},{5,4},{6,7},{7,6},{8,9},{9,8},{10,11... | collective-permute-start | bytes 786440 | tf_op jit(solution)/shard_map/ppermute | solution.py:546
  79.6 1.0 inner.17
  80.8 1.6 collective-permute-done.26.low
  83.3 2.6 %collective-permute-start.27 = (f32[4,128,128]{2,1,0:T(8,128)S(1)}, f32[4,128,128]{2,1,0:T(8,128)S(1)}, u32[]{:S(2)}, u32[]{:S(2)}) collective-permute-start(f32[4,128,128]{2,1,0:T(8,128)S(1)} %get-tuple-element.225), channel_id=1, source_target_pairs={{0,1},{1,0},{2,3},{3,2},{4,5},{5,4},{6,7},{7,6},{8,9},{9,8},{10,11... | collective-permute-start | bytes 786440 | tf_op jit(solution)/shard_map/ppermute | solution.py:546
  85.9 1.4 collective-permute-start.23
  87.4 0.7 collective-permute-start.22
  88.1 0.9 inner.18
  90.0 2.5 %collective-permute-start.32 = (f32[4,128,128]{2,1,0:T(8,128)S(1)}, f32[4,128,128]{2,1,0:T(8,128)S(1)}, u32[]{:S(2)}, u32[]{:S(2)}) collective-permute-start(f32[4,128,128]{2,1,0:T(8,128)S(1)} %get-tuple-element.249), channel_id=1, source_target_pairs={{0,1},{1,0},{2,3},{3,2},{4,5},{5,4},{6,7},{7,6},{8,9},{9,8},{10,11... | collective-permute-start | bytes 786440 | tf_op jit(solution)/shard_map/ppermute | solution.py:546
  92.5 0.8 inner.19
  93.4 1.5 collective-permute-done.24.refs_3_
  94.8 4.4 %collective-permute-done.23.refs_2_ = f32[4,16,8,128]{3,2,1,0:T(8,128)S(1)} collective-permute-done((f32[4,16,8,128]{3,2,1,0:T(8,128)S(1)}, f32[4,16,8,128]{3,2,1,0:T(8,128)S(1)}, u32[]{:S(2)}, u32[]{:S(2)}) %collective-permute-start.23) | collective-permute-done | bytes 262176 | tf_op jit(solution)/shard_map/ppermute | solution.py:600
  100.7 2.3 %collective-permute-start.36 = (f32[4,128,128]{2,1,0:T(8,128)S(1)}, f32[4,128,128]{2,1,0:T(8,128)S(1)}, u32[]{:S(2)}, u32[]{:S(2)}) collective-permute-start(f32[4,128,128]{2,1,0:T(8,128)S(1)} %get-tuple-element.265), channel_id=1, source_target_pairs={{0,1},{1,0},{2,3},{3,2},{4,5},{5,4},{6,7},{7,6},{8,9},{9,8},{10,11... | collective-permute-start | bytes 786440 | tf_op jit(solution)/shard_map/ppermute | solution.py:546
  103.1 1.1 inner.20
  104.1 4.8 %collective-permute-done.31.refs_2_ = f32[2,16,8,128]{3,2,1,0:T(8,128)S(1)} collective-permute-done((f32[2,16,8,128]{3,2,1,0:T(8,128)S(1)}, f32[2,16,8,128]{3,2,1,0:T(8,128)S(1)}, u32[]{:S(2)}, u32[]{:S(2)}) %collective-permute-start.31) | collective-permute-done | bytes 131104 | tf_op jit(solution)/shard_map/ppermute | solution.py:623
  109.4 3.0 %collective-permute-start.33 = (f32[4,128,128]{2,1,0:T(8,128)S(1)}, f32[4,128,128]{2,1,0:T(8,128)S(1)}, u32[]{:S(2)}, u32[]{:S(2)}) collective-permute-start(f32[4,128,128]{2,1,0:T(8,128)S(1)} %get-tuple-element.258), channel_id=1, source_target_pairs={{1,4},{4,1},{3,6},{6,3},{5,8},{8,5},{7,10},{10,7},{9,12},{12,9},{1... | collective-permute-start | bytes 786440 | tf_op jit(solution)/shard_map/ppermute | solution.py:544
  112.8 2.0 %collective-permute-start.40 = (f32[4,128,128]{2,1,0:T(8,128)S(1)}, f32[4,128,128]{2,1,0:T(8,128)S(1)}, u32[]{:S(2)}, u32[]{:S(2)}) collective-permute-start(f32[4,128,128]{2,1,0:T(8,128)S(1)} %get-tuple-element.282), channel_id=1, source_target_pairs={{0,1},{1,0},{2,3},{3,2},{4,5},{5,4},{6,7},{7,6},{8,9},{9,8},{10,11... | collective-permute-start | bytes 786440 | tf_op jit(solution)/shard_map/ppermute | solution.py:546
  114.8 1.2 collective-permute-start.35
  116.0 0.8 inner.21
  116.8 4.5 %collective-permute-done.35.refs_0_ = f32[2,16,8,128]{3,2,1,0:T(8,128)S(1)} collective-permute-done((f32[2,16,8,128]{3,2,1,0:T(8,128)S(1)}, f32[2,16,8,128]{3,2,1,0:T(8,128)S(1)}, u32[]{:S(2)}, u32[]{:S(2)}) %collective-permute-start.35) | collective-permute-done | bytes 131104 | tf_op jit(solution)/shard_map/ppermute | solution.py:623
  121.3 1.1 collective-permute-done.34.refs_3_
  123.0 2.7 %collective-permute-start.37 = (f32[4,128,128]{2,1,0:T(8,128)S(1)}, f32[4,128,128]{2,1,0:T(8,128)S(1)}, u32[]{:S(2)}, u32[]{:S(2)}) collective-permute-start(f32[4,128,128]{2,1,0:T(8,128)S(1)} %get-tuple-element.274), channel_id=1, source_target_pairs={{1,4},{4,1},{3,6},{6,3},{5,8},{8,5},{7,10},{10,7},{9,12},{12,9},{1... | collective-permute-start | bytes 786440 | tf_op jit(solution)/shard_map/ppermute | solution.py:544
  126.2 1.6 collective-permute-start.39
  127.8 0.9 inner.22
  128.8 0.7 inner.23.prev
  129.5 3.4 %collective-permute-done.39.refs_1_ = f32[2,16,8,128]{3,2,1,0:T(8,128)S(1)} collective-permute-done((f32[2,16,8,128]{3,2,1,0:T(8,128)S(1)}, f32[2,16,8,128]{3,2,1,0:T(8,128)S(1)}, u32[]{:S(2)}, u32[]{:S(2)}) %collective-permute-start.39) | collective-permute-done | bytes 131104 | tf_op jit(solution)/shard_map/ppermute | solution.py:623
  133.5 0.6 copy-done.14
  134.1 2.6 %last.1 = (f32[24,128,128]{2,1,0:T(8,128)S(1)}, f32[24,128,128]{2,1,0:T(8,128)S(1)}, f32[16,16,8,128]{3,2,1,0:T(8,128)S(1)}, f32[8,128,128]{2,1,0:T(8,128)}, f32...) custom-call(s32[2]{0:T(128)S(1)} %copy-done.16, ...), custom_call_target="tpu_custom_call", output_to_operand_aliasing={{0}: (9, {}), {1}: (10, {}), {2}: (11, {})} | custom-call | tf_op jit(solution)/shard_map/last/pallas_call | solution.py:592
  136.7 8.3 %all-to-all-start = ((f32[16,16,8,128]{3,2,1,0:T(8,128)}), f32[16,16,8,128]{3,2,1,0:T(8,128)S(1)}, u32[]{:S(2)}, u32[]{:S(2)}) async-start(f32[16,16,8,128]{3,2,1,0:T(8,128)} %get-tuple-element.294), calls=%async_computation | async-start | bytes 2097152 | tf_op jit(solution)/shard_map/all_to_all | solution.py:629
  145.0 3.4 %collective-permute-start.43 = (f32[8,128,128]{2,1,0:T(8,128)}, f32[8,128,128]{2,1,0:T(8,128)S(1)}, u32[]{:S(2)}, u32[]{:S(2)}) collective-permute-start(f32[8,128,128]{2,1,0:T(8,128)} %get-tuple-element.295), channel_id=1, source_target_pairs={{0,0},{1,2},{2,1},{3,3},{4,4},{5,6},{6,5},{7,7},{8,8},{9,10},{10,9... | collective-permute-start | bytes 1572872 | tf_op jit(solution)/shard_map/ppermute | solution.py:630
  148.4 1.3 collective-permute-start.41
  149.7 25.5 %collective-permute-done.41.refs_5_ = f32[2,16,8,128]{3,2,1,0:T(8,128)S(1)} collective-permute-done((f32[2,16,8,128]{3,2,1,0:T(8,128)S(1)}, f32[2,16,8,128]{3,2,1,0:T(8,128)S(1)}, u32[]{:S(2)}, u32[]{:S(2)}) %collective-permute-start.41) | collective-permute-done | bytes 131104 | tf_op jit(solution)/shard_map/ppermute | solution.py:623
  175.2 0.9 copy-done.9
  176.1 0.9 copy-done.11
  177.0 0.9 copy-done.13
  177.9 0.9 copy-done.15
  179.0 1.1 choose.5
  180.0 5.7 %images.1 = bf16[8,128,8,128]{3,2,1,0:T(8,128)(2,1)} custom-call(bf16[2,256,1024]{2,1,0:T(8,128)(2,1)S(1)} %get-tuple-element.151.shifts, f32[16,16,8,128]{3,2,1,0:T(8,128)S(1)} %shard_map.143.refs_0_, f32[16,16,8,128]{3,2,1,0:T(8,128)S(1)} %all-to-all-done.refs_1_), custom_call_target="tpu_custom_call" | custom-call | tf_op jit(solution)/shard_map/images/pallas_call | solution.py:444
  (111 shorter events, 14.5 us)
Async XLA Ops:
  0.6 13.9 %collective-permute-start.2 = (f32[8,128,128]{2,1,0:T(8,128)}, f32[8,128,128]{2,1,0:T(8,128)S(1)}, u32[]{:S(2)}, u32[]{:S(2)}) collective-permute-start(f32[8,128,128]{2,1,0:T(8,128)} %param.16), channel_id=1, source_target_pairs={{0,0},{1,2},{2,1},{3,3},{4,4},{5,6},{6,5},{7,7},{8,8},{9,10},{10,9... | collective-permute-start | bytes 1572872 | tf_op jit(solution)/shard_map/ppermute | solution.py:501
  4.3 1.0 copy-start.3
  5.4 1.0 copy-start.4
  6.4 18.3 %copy-start.7 = (f32[12,8,8,128]{3,2,1,0:T(8,128)S(1)}, f32[12,8,8,128]{3,2,1,0:T(8,128)}, u32[]{:S(2)}) copy-start(f32[12,8,8,128]{3,2,1,0:T(8,128)} %param.17) | copy-start | bytes 1179652
  6.4 18.3 %copy-start.17 = (s32[12]{0:T(128)S(1)}, s32[12]{0:T(128)}, u32[]{:S(2)}) copy-start(s32[12]{0:T(128)} %face_steps.1) | copy-start | bytes 148
  6.4 18.3 %copy-start.18 = (s32[8]{0:T(128)S(1)}, s32[8]{0:T(128)}, u32[]{:S(2)}) copy-start(s32[8]{0:T(128)} %lags.1) | copy-start | bytes 100
  6.5 16.8 %collective-permute-start.6 = (f32[8,128,128]{2,1,0:T(8,128)S(1)}, f32[8,128,128]{2,1,0:T(8,128)S(1)}, u32[]{:S(2)}, u32[]{:S(2)}) collective-permute-start(f32[8,128,128]{2,1,0:T(8,128)S(1)} %get-tuple-element.157), channel_id=1, source_target_pairs={{0,0},{1,2},{2,1},{3,3},{4,4},{5,6},{6,5},{7,7},{8,8},{9,10},{10,9... | collective-permute-start | bytes 1572872 | tf_op jit(solution)/shard_map/ppermute | solution.py:485
  8.6 14.7 %collective-permute-start.7 = (f32[8,128,128]{2,1,0:T(8,128)S(1)}, f32[8,128,128]{2,1,0:T(8,128)S(1)}, u32[]{:S(2)}, u32[]{:S(2)}) collective-permute-start(f32[8,128,128]{2,1,0:T(8,128)S(1)} %get-tuple-element.158), channel_id=1, source_target_pairs={{0,2},{1,0},{2,3},{3,1},{4,6},{5,4},{6,7},{7,5},{8,10},{9,8},{10,1... | collective-permute-start | bytes 1572872 | tf_op jit(solution)/shard_map/ppermute | solution.py:485
  8.6 1.0 copy-start.5
  9.7 1.0 copy-start.6
  10.8 23.1 %collective-permute-start = (f32[8,128,128]{2,1,0:T(8,128)S(1)}, f32[8,128,128]{2,1,0:T(8,128)S(1)}, u32[]{:S(2)}, u32[]{:S(2)}) collective-permute-start(f32[8,128,128]{2,1,0:T(8,128)S(1)} %get-tuple-element.152), channel_id=1, source_target_pairs={{0,0},{1,2},{2,1},{3,3},{4,4},{5,6},{6,5},{7,7},{8,8},{9,10},{10,9... | collective-permute-start | bytes 1572872 | tf_op jit(solution)/shard_map/ppermute | solution.py:485
  14.5 25.7 %copy-start = (bf16[128,256]{1,0:T(8,128)(2,1)S(1)}, bf16[128,256]{1,0:T(8,128)(2,1)}, u32[]{:S(2)}) copy-start(bf16[128,256]{1,0:T(8,128)(2,1)} %constant.5.clone.along) | copy-start | bytes 196612
  14.5 25.7 %copy-start.1 = (bf16[256,128]{1,0:T(8,128)(2,1)S(1)}, bf16[256,128]{1,0:T(8,128)(2,1)}, u32[]{:S(2)}) copy-start(bf16[256,128]{1,0:T(8,128)(2,1)} %constant.4.clone.across) | copy-start | bytes 196612
  14.5 25.7 %copy-start.2 = (bf16[12,128,128]{2,1,0:T(8,128)(2,1)S(1)}, bf16[12,128,128]{2,1,0:T(8,128)(2,1)}, u32[]{:S(2)}) copy-start(bf16[12,128,128]{2,1,0:T(8,128)(2,1)} %traces.23) | copy-start | bytes 1179652
  14.5 19.4 %collective-permute-start.1 = (f32[8,128,128]{2,1,0:T(8,128)S(1)}, f32[8,128,128]{2,1,0:T(8,128)S(1)}, u32[]{:S(2)}, u32[]{:S(2)}) collective-permute-start(f32[8,128,128]{2,1,0:T(8,128)S(1)} %get-tuple-element.153), channel_id=1, source_target_pairs={{0,2},{1,0},{2,3},{3,1},{4,6},{5,4},{6,7},{7,5},{8,10},{9,8},{10,1... | collective-permute-start | bytes 1572872 | tf_op jit(solution)/shard_map/ppermute | solution.py:485
  14.5 23.0 %collective-permute-start.3 = (f32[8,128,128]{2,1,0:T(8,128)S(1)}, f32[8,128,128]{2,1,0:T(8,128)S(1)}, u32[]{:S(2)}, u32[]{:S(2)}) collective-permute-start(f32[8,128,128]{2,1,0:T(8,128)S(1)} %collective-permute-done.2.speed_a), channel_id=1, source_target_pairs={{0,16},{16,0},{1,17},{17,1},{2,18},{18,2},{3,19},{19,3},{4,20},{20... | collective-permute-start | bytes 1572872 | tf_op jit(solution)/shard_map/ppermute | solution.py:502
  23.7 16.4 %collective-permute-start.9 = (f32[4,128,128]{2,1,0:T(8,128)S(1)}, f32[4,128,128]{2,1,0:T(8,128)S(1)}, u32[]{:S(2)}, u32[]{:S(2)}) collective-permute-start(f32[4,128,128]{2,1,0:T(8,128)S(1)} %get-tuple-element.160), channel_id=1, source_target_pairs={{1,4},{4,1},{3,6},{6,3},{5,8},{8,5},{7,10},{10,7},{9,12},{12,9},{1... | collective-permute-start | bytes 786440 | tf_op jit(solution)/shard_map/ppermute | solution.py:510
  24.7 16.0 %collective-permute-start.8 = (f32[4,128,128]{2,1,0:T(8,128)S(1)}, f32[4,128,128]{2,1,0:T(8,128)S(1)}, u32[]{:S(2)}, u32[]{:S(2)}) collective-permute-start(f32[4,128,128]{2,1,0:T(8,128)S(1)} %get-tuple-element.159), channel_id=1, source_target_pairs={{0,1},{1,0},{2,3},{3,2},{4,5},{5,4},{6,7},{7,6},{8,9},{9,8},{10,11... | collective-permute-start | bytes 786440 | tf_op jit(solution)/shard_map/ppermute | solution.py:511
  33.9 4.2 %collective-permute-start.5 = (f32[2,128,128]{2,1,0:T(8,128)S(1)}, f32[2,128,128]{2,1,0:T(8,128)S(1)}, u32[]{:S(2)}, u32[]{:S(2)}) collective-permute-start(f32[2,128,128]{2,1,0:T(8,128)S(1)} %get-tuple-element.156), channel_id=1, source_target_pairs={{0,2},{1,0},{2,3},{3,1},{4,6},{5,4},{6,7},{7,5},{8,10},{9,8},{10,1... | collective-permute-start | bytes 393224 | tf_op jit(solution)/shard_map/ppermute | solution.py:485
  33.9 6.3 %collective-permute-start.4 = (f32[2,128,128]{2,1,0:T(8,128)S(1)}, f32[2,128,128]{2,1,0:T(8,128)S(1)}, u32[]{:S(2)}, u32[]{:S(2)}) collective-permute-start(f32[2,128,128]{2,1,0:T(8,128)S(1)} %get-tuple-element.156), channel_id=1, source_target_pairs={{0,0},{1,2},{2,1},{3,3},{4,4},{5,6},{6,5},{7,7},{8,8},{9,10},{10,9... | collective-permute-start | bytes 393224 | tf_op jit(solution)/shard_map/ppermute | solution.py:485
  40.6 5.9 %collective-permute-start.13 = (f32[4,128,128]{2,1,0:T(8,128)S(1)}, f32[4,128,128]{2,1,0:T(8,128)S(1)}, u32[]{:S(2)}, u32[]{:S(2)}) collective-permute-start(f32[4,128,128]{2,1,0:T(8,128)S(1)} %get-tuple-element.170), channel_id=1, source_target_pairs={{1,4},{4,1},{3,6},{6,3},{5,8},{8,5},{7,10},{10,7},{9,12},{12,9},{1... | collective-permute-start | bytes 786440 | tf_op jit(solution)/shard_map/ppermute | solution.py:544
  40.7 1.0 copy-start.16
  41.1 5.9 %collective-permute-start.12 = (f32[4,128,128]{2,1,0:T(8,128)S(1)}, f32[4,128,128]{2,1,0:T(8,128)S(1)}, u32[]{:S(2)}, u32[]{:S(2)}) collective-permute-start(f32[4,128,128]{2,1,0:T(8,128)S(1)} %get-tuple-element.169), channel_id=1, source_target_pairs={{0,1},{1,0},{2,3},{3,2},{4,5},{5,4},{6,7},{7,6},{8,9},{9,8},{10,11... | collective-permute-start | bytes 786440 | tf_op jit(solution)/shard_map/ppermute | solution.py:546
  46.9 5.9 %collective-permute-start.15 = (f32[4,128,128]{2,1,0:T(8,128)S(1)}, f32[4,128,128]{2,1,0:T(8,128)S(1)}, u32[]{:S(2)}, u32[]{:S(2)}) collective-permute-start(f32[4,128,128]{2,1,0:T(8,128)S(1)} %get-tuple-element.175), channel_id=1, source_target_pairs={{1,4},{4,1},{3,6},{6,3},{5,8},{8,5},{7,10},{10,7},{9,12},{12,9},{1... | collective-permute-start | bytes 786440 | tf_op jit(solution)/shard_map/ppermute | solution.py:544
  47.4 5.9 %collective-permute-start.14 = (f32[4,128,128]{2,1,0:T(8,128)S(1)}, f32[4,128,128]{2,1,0:T(8,128)S(1)}, u32[]{:S(2)}, u32[]{:S(2)}) collective-permute-start(f32[4,128,128]{2,1,0:T(8,128)S(1)} %get-tuple-element.174), channel_id=1, source_target_pairs={{0,1},{1,0},{2,3},{3,2},{4,5},{5,4},{6,7},{7,6},{8,9},{9,8},{10,11... | collective-permute-start | bytes 786440 | tf_op jit(solution)/shard_map/ppermute | solution.py:546
  53.2 5.9 %collective-permute-start.17 = (f32[4,128,128]{2,1,0:T(8,128)S(1)}, f32[4,128,128]{2,1,0:T(8,128)S(1)}, u32[]{:S(2)}, u32[]{:S(2)}) collective-permute-start(f32[4,128,128]{2,1,0:T(8,128)S(1)} %get-tuple-element.183), channel_id=1, source_target_pairs={{1,4},{4,1},{3,6},{6,3},{5,8},{8,5},{7,10},{10,7},{9,12},{12,9},{1... | collective-permute-start | bytes 786440 | tf_op jit(solution)/shard_map/ppermute | solution.py:544
  53.7 11.2 %collective-permute-start.16 = (f32[4,128,128]{2,1,0:T(8,128)S(1)}, f32[4,128,128]{2,1,0:T(8,128)S(1)}, u32[]{:S(2)}, u32[]{:S(2)}) collective-permute-start(f32[4,128,128]{2,1,0:T(8,128)S(1)} %get-tuple-element.182), channel_id=1, source_target_pairs={{0,1},{1,0},{2,3},{3,2},{4,5},{5,4},{6,7},{7,6},{8,9},{9,8},{10,11... | collective-permute-start | bytes 786440 | tf_op jit(solution)/shard_map/ppermute | solution.py:546
  59.5 6.7 %collective-permute-start.19 = (f32[4,128,128]{2,1,0:T(8,128)S(1)}, f32[4,128,128]{2,1,0:T(8,128)S(1)}, u32[]{:S(2)}, u32[]{:S(2)}) collective-permute-start(f32[4,128,128]{2,1,0:T(8,128)S(1)} %get-tuple-element.191), channel_id=1, source_target_pairs={{1,4},{4,1},{3,6},{6,3},{5,8},{8,5},{7,10},{10,7},{9,12},{12,9},{1... | collective-permute-start | bytes 786440 | tf_op jit(solution)/shard_map/ppermute | solution.py:544
  59.6 7.0 %collective-permute-start.11 = (f32[4,128,128]{2,1,0:T(8,128)S(1)}, f32[4,128,128]{2,1,0:T(8,128)S(1)}, u32[]{:S(2)}, u32[]{:S(2)}) collective-permute-start(f32[4,128,128]{2,1,0:T(8,128)S(1)} %get-tuple-element.168), channel_id=1, source_target_pairs={{0,2},{1,0},{2,3},{3,1},{4,6},{5,4},{6,7},{7,5},{8,10},{9,8},{10,1... | collective-permute-start | bytes 786440 | tf_op jit(solution)/shard_map/ppermute | solution.py:485
  60.1 9.0 %collective-permute-start.10 = (f32[4,128,128]{2,1,0:T(8,128)S(1)}, f32[4,128,128]{2,1,0:T(8,128)S(1)}, u32[]{:S(2)}, u32[]{:S(2)}) collective-permute-start(f32[4,128,128]{2,1,0:T(8,128)S(1)} %get-tuple-element.168), channel_id=1, source_target_pairs={{0,0},{1,2},{2,1},{3,3},{4,4},{5,6},{6,5},{7,7},{8,8},{9,10},{10,9... | collective-permute-start | bytes 786440 | tf_op jit(solution)/shard_map/ppermute | solution.py:485
  65.3 4.4 %collective-permute-start.18 = (f32[4,128,128]{2,1,0:T(8,128)S(1)}, f32[4,128,128]{2,1,0:T(8,128)S(1)}, u32[]{:S(2)}, u32[]{:S(2)}) collective-permute-start(f32[4,128,128]{2,1,0:T(8,128)S(1)} %get-tuple-element.190), channel_id=1, source_target_pairs={{0,1},{1,0},{2,3},{3,2},{4,5},{5,4},{6,7},{7,6},{8,9},{9,8},{10,11... | collective-permute-start | bytes 786440 | tf_op jit(solution)/shard_map/ppermute | solution.py:546
  69.6 6.2 %collective-permute-start.21 = (f32[4,128,128]{2,1,0:T(8,128)S(1)}, f32[4,128,128]{2,1,0:T(8,128)S(1)}, u32[]{:S(2)}, u32[]{:S(2)}) collective-permute-start(f32[4,128,128]{2,1,0:T(8,128)S(1)} %get-tuple-element.199), channel_id=1, source_target_pairs={{1,4},{4,1},{3,6},{6,3},{5,8},{8,5},{7,10},{10,7},{9,12},{12,9},{1... | collective-permute-start | bytes 786440 | tf_op jit(solution)/shard_map/ppermute | solution.py:544
  70.1 6.2 %collective-permute-start.20 = (f32[4,128,128]{2,1,0:T(8,128)S(1)}, f32[4,128,128]{2,1,0:T(8,128)S(1)}, u32[]{:S(2)}, u32[]{:S(2)}) collective-permute-start(f32[4,128,128]{2,1,0:T(8,128)S(1)} %get-tuple-element.198), channel_id=1, source_target_pairs={{0,1},{1,0},{2,3},{3,2},{4,5},{5,4},{6,7},{7,6},{8,9},{9,8},{10,11... | collective-permute-start | bytes 786440 | tf_op jit(solution)/shard_map/ppermute | solution.py:546
  76.2 6.2 %collective-permute-start.26 = (f32[4,128,128]{2,1,0:T(8,128)S(1)}, f32[4,128,128]{2,1,0:T(8,128)S(1)}, u32[]{:S(2)}, u32[]{:S(2)}) collective-permute-start(f32[4,128,128]{2,1,0:T(8,128)S(1)} %get-tuple-element.221), channel_id=1, source_target_pairs={{1,4},{4,1},{3,6},{6,3},{5,8},{8,5},{7,10},{10,7},{9,12},{12,9},{1... | collective-permute-start | bytes 786440 | tf_op jit(solution)/shard_map/ppermute | solution.py:544
  76.7 6.2 %collective-permute-start.25 = (f32[4,128,128]{2,1,0:T(8,128)S(1)}, f32[4,128,128]{2,1,0:T(8,128)S(1)}, u32[]{:S(2)}, u32[]{:S(2)}) collective-permute-start(f32[4,128,128]{2,1,0:T(8,128)S(1)} %get-tuple-element.220), channel_id=1, source_target_pairs={{0,1},{1,0},{2,3},{3,2},{4,5},{5,4},{6,7},{7,6},{8,9},{9,8},{10,11... | collective-permute-start | bytes 786440 | tf_op jit(solution)/shard_map/ppermute | solution.py:546
  82.8 6.3 %collective-permute-start.28 = (f32[4,128,128]{2,1,0:T(8,128)S(1)}, f32[4,128,128]{2,1,0:T(8,128)S(1)}, u32[]{:S(2)}, u32[]{:S(2)}) collective-permute-start(f32[4,128,128]{2,1,0:T(8,128)S(1)} %get-tuple-element.226), channel_id=1, source_target_pairs={{1,4},{4,1},{3,6},{6,3},{5,8},{8,5},{7,10},{10,7},{9,12},{12,9},{1... | collective-permute-start | bytes 786440 | tf_op jit(solution)/shard_map/ppermute | solution.py:544
  83.3 6.3 %collective-permute-start.27 = (f32[4,128,128]{2,1,0:T(8,128)S(1)}, f32[4,128,128]{2,1,0:T(8,128)S(1)}, u32[]{:S(2)}, u32[]{:S(2)}) collective-permute-start(f32[4,128,128]{2,1,0:T(8,128)S(1)} %get-tuple-element.225), channel_id=1, source_target_pairs={{0,1},{1,0},{2,3},{3,2},{4,5},{5,4},{6,7},{7,6},{8,9},{9,8},{10,11... | collective-permute-start | bytes 786440 | tf_op jit(solution)/shard_map/ppermute | solution.py:546
  85.9 8.9 %collective-permute-start.24 = (f32[4,16,8,128]{3,2,1,0:T(8,128)S(1)}, f32[4,16,8,128]{3,2,1,0:T(8,128)S(1)}, u32[]{:S(2)}, u32[]{:S(2)}) collective-permute-start(f32[4,16,8,128]{3,2,1,0:T(8,128)S(1)} %get-tuple-element.219), channel_id=1, source_target_pairs={{0,3},{1,2},{2,1},{3,0},{4,7},{5,6},{6,5},{7,4},{8,11},{9,10},{10,... | collective-permute-start | bytes 786440 | tf_op jit(solution)/shard_map/ppermute | solution.py:600
  85.9 13.3 %collective-permute-start.23 = (f32[4,16,8,128]{3,2,1,0:T(8,128)S(1)}, f32[4,16,8,128]{3,2,1,0:T(8,128)S(1)}, u32[]{:S(2)}, u32[]{:S(2)}) collective-permute-start(f32[4,16,8,128]{3,2,1,0:T(8,128)S(1)} %get-tuple-element.216), channel_id=1, source_target_pairs={{0,2},{1,3},{2,0},{3,1},{4,6},{5,7},{6,4},{7,5},{8,10},{9,11},{10,... | collective-permute-start | bytes 786440 | tf_op jit(solution)/shard_map/ppermute | solution.py:600
  87.4 11.9 %collective-permute-start.22 = (f32[4,16,8,128]{3,2,1,0:T(8,128)S(1)}, f32[4,16,8,128]{3,2,1,0:T(8,128)S(1)}, u32[]{:S(2)}, u32[]{:S(2)}) collective-permute-start(f32[4,16,8,128]{3,2,1,0:T(8,128)S(1)} %get-tuple-element.213), channel_id=1, source_target_pairs={{0,1},{1,0},{2,3},{3,2},{4,5},{5,4},{6,7},{7,6},{8,9},{9,8},{10,11... | collective-permute-start | bytes 786440 | tf_op jit(solution)/shard_map/ppermute | solution.py:600
  89.5 9.9 %collective-permute-start.29 = (f32[4,128,128]{2,1,0:T(8,128)S(1)}, f32[4,128,128]{2,1,0:T(8,128)S(1)}, u32[]{:S(2)}, u32[]{:S(2)}) collective-permute-start(f32[4,128,128]{2,1,0:T(8,128)S(1)} %get-tuple-element.240), channel_id=1, source_target_pairs={{1,4},{4,1},{3,6},{6,3},{5,8},{8,5},{7,10},{10,7},{9,12},{12,9},{1... | collective-permute-start | bytes 786440 | tf_op jit(solution)/shard_map/ppermute | solution.py:544
  90.0 10.3 %collective-permute-start.32 = (f32[4,128,128]{2,1,0:T(8,128)S(1)}, f32[4,128,128]{2,1,0:T(8,128)S(1)}, u32[]{:S(2)}, u32[]{:S(2)}) collective-permute-start(f32[4,128,128]{2,1,0:T(8,128)S(1)} %get-tuple-element.249), channel_id=1, source_target_pairs={{0,1},{1,0},{2,3},{3,2},{4,5},{5,4},{6,7},{7,6},{8,9},{9,8},{10,11... | collective-permute-start | bytes 786440 | tf_op jit(solution)/shard_map/ppermute | solution.py:546
  99.8 9.1 %collective-permute-start.30 = (f32[4,128,128]{2,1,0:T(8,128)S(1)}, f32[4,128,128]{2,1,0:T(8,128)S(1)}, u32[]{:S(2)}, u32[]{:S(2)}) collective-permute-start(f32[4,128,128]{2,1,0:T(8,128)S(1)} %get-tuple-element.244), channel_id=1, source_target_pairs={{1,4},{4,1},{3,6},{6,3},{5,8},{8,5},{7,10},{10,7},{9,12},{12,9},{1... | collective-permute-start | bytes 786440 | tf_op jit(solution)/shard_map/ppermute | solution.py:544
  100.7 11.6 %collective-permute-start.36 = (f32[4,128,128]{2,1,0:T(8,128)S(1)}, f32[4,128,128]{2,1,0:T(8,128)S(1)}, u32[]{:S(2)}, u32[]{:S(2)}) collective-permute-start(f32[4,128,128]{2,1,0:T(8,128)S(1)} %get-tuple-element.265), channel_id=1, source_target_pairs={{0,1},{1,0},{2,3},{3,2},{4,5},{5,4},{6,7},{7,6},{8,9},{9,8},{10,11... | collective-permute-start | bytes 786440 | tf_op jit(solution)/shard_map/ppermute | solution.py:546
  103.1 5.9 %collective-permute-start.31 = (f32[2,16,8,128]{3,2,1,0:T(8,128)S(1)}, f32[2,16,8,128]{3,2,1,0:T(8,128)S(1)}, u32[]{:S(2)}, u32[]{:S(2)}) collective-permute-start(f32[2,16,8,128]{3,2,1,0:T(8,128)S(1)} %get-tuple-element.245), channel_id=1, source_target_pairs={{0,8},{1,9},{2,10},{3,11},{4,12},{5,13},{6,14},{7,15},{8,0},{9,1},... | collective-permute-start | bytes 393224 | tf_op jit(solution)/shard_map/ppermute | solution.py:623
  109.4 13.0 %collective-permute-start.33 = (f32[4,128,128]{2,1,0:T(8,128)S(1)}, f32[4,128,128]{2,1,0:T(8,128)S(1)}, u32[]{:S(2)}, u32[]{:S(2)}) collective-permute-start(f32[4,128,128]{2,1,0:T(8,128)S(1)} %get-tuple-element.258), channel_id=1, source_target_pairs={{1,4},{4,1},{3,6},{6,3},{5,8},{8,5},{7,10},{10,7},{9,12},{12,9},{1... | collective-permute-start | bytes 786440 | tf_op jit(solution)/shard_map/ppermute | solution.py:544
  112.8 13.0 %collective-permute-start.40 = (f32[4,128,128]{2,1,0:T(8,128)S(1)}, f32[4,128,128]{2,1,0:T(8,128)S(1)}, u32[]{:S(2)}, u32[]{:S(2)}) collective-permute-start(f32[4,128,128]{2,1,0:T(8,128)S(1)} %get-tuple-element.282), channel_id=1, source_target_pairs={{0,1},{1,0},{2,3},{3,2},{4,5},{5,4},{6,7},{7,6},{8,9},{9,8},{10,11... | collective-permute-start | bytes 786440 | tf_op jit(solution)/shard_map/ppermute | solution.py:546
  114.8 6.5 %collective-permute-start.35 = (f32[2,16,8,128]{3,2,1,0:T(8,128)S(1)}, f32[2,16,8,128]{3,2,1,0:T(8,128)S(1)}, u32[]{:S(2)}, u32[]{:S(2)}) collective-permute-start(f32[2,16,8,128]{3,2,1,0:T(8,128)S(1)} %get-tuple-element.260), channel_id=1, source_target_pairs={{0,4},{1,5},{2,6},{3,7},{4,0},{5,1},{6,2},{7,3},{8,12},{9,13},{10,... | collective-permute-start | bytes 393224 | tf_op jit(solution)/shard_map/ppermute | solution.py:623
  116.0 6.4 %collective-permute-start.34 = (f32[2,16,8,128]{3,2,1,0:T(8,128)S(1)}, f32[2,16,8,128]{3,2,1,0:T(8,128)S(1)}, u32[]{:S(2)}, u32[]{:S(2)}) collective-permute-start(f32[2,16,8,128]{3,2,1,0:T(8,128)S(1)} %get-tuple-element.259), channel_id=1, source_target_pairs={{0,8},{1,9},{2,10},{3,11},{4,12},{5,13},{6,14},{7,15},{8,0},{9,1},... | collective-permute-start | bytes 393224 | tf_op jit(solution)/shard_map/ppermute | solution.py:623
  121.3 1.5 copy-start.8
  122.4 0.7 copy-start.10
  123.0 11.1 %collective-permute-start.37 = (f32[4,128,128]{2,1,0:T(8,128)S(1)}, f32[4,128,128]{2,1,0:T(8,128)S(1)}, u32[]{:S(2)}, u32[]{:S(2)}) collective-permute-start(f32[4,128,128]{2,1,0:T(8,128)S(1)} %get-tuple-element.274), channel_id=1, source_target_pairs={{1,4},{4,1},{3,6},{6,3},{5,8},{8,5},{7,10},{10,7},{9,12},{12,9},{1... | collective-permute-start | bytes 786440 | tf_op jit(solution)/shard_map/ppermute | solution.py:544
  126.1 8.0 %collective-permute-start.42 = (f32[4,128,128]{2,1,0:T(8,128)S(1)}, f32[4,128,128]{2,1,0:T(8,128)S(1)}, u32[]{:S(2)}, u32[]{:S(2)}) collective-permute-start(f32[4,128,128]{2,1,0:T(8,128)S(1)} %get-tuple-element.291), channel_id=1, source_target_pairs={{0,1},{1,0},{2,3},{3,2},{4,5},{5,4},{6,7},{7,6},{8,9},{9,8},{10,11... | collective-permute-start | bytes 786440 | tf_op jit(solution)/shard_map/ppermute | solution.py:546
  126.2 6.7 %collective-permute-start.39 = (f32[2,16,8,128]{3,2,1,0:T(8,128)S(1)}, f32[2,16,8,128]{3,2,1,0:T(8,128)S(1)}, u32[]{:S(2)}, u32[]{:S(2)}) collective-permute-start(f32[2,16,8,128]{3,2,1,0:T(8,128)S(1)} %get-tuple-element.276), channel_id=1, source_target_pairs={{0,4},{1,5},{2,6},{3,7},{4,0},{5,1},{6,2},{7,3},{8,12},{9,13},{10,... | collective-permute-start | bytes 393224 | tf_op jit(solution)/shard_map/ppermute | solution.py:623
  127.8 5.7 %collective-permute-start.38 = (f32[2,16,8,128]{3,2,1,0:T(8,128)S(1)}, f32[2,16,8,128]{3,2,1,0:T(8,128)S(1)}, u32[]{:S(2)}, u32[]{:S(2)}) collective-permute-start(f32[2,16,8,128]{3,2,1,0:T(8,128)S(1)} %get-tuple-element.275), channel_id=1, source_target_pairs={{0,12},{1,13},{2,14},{3,15},{4,8},{5,9},{6,10},{7,11},{8,4},{9,5},... | collective-permute-start | bytes 393224 | tf_op jit(solution)/shard_map/ppermute | solution.py:623
  132.9 3.8 %copy-start.12 = (f32[2,16,8,128]{3,2,1,0:T(8,128)}, f32[2,16,8,128]{3,2,1,0:T(8,128)S(1)}, u32[]{:S(2)}) copy-start(f32[2,16,8,128]{3,2,1,0:T(8,128)S(1)} %collective-permute-done.39.refs_1_) | copy-start | bytes 393220
  136.7 43.3 %all-to-all-start = ((f32[16,16,8,128]{3,2,1,0:T(8,128)}), f32[16,16,8,128]{3,2,1,0:T(8,128)S(1)}, u32[]{:S(2)}, u32[]{:S(2)}) async-start(f32[16,16,8,128]{3,2,1,0:T(8,128)} %get-tuple-element.294), calls=%async_computation | async-start | bytes 2097152 | tf_op jit(solution)/shard_map/all_to_all | solution.py:629
  145.0 33.9 %collective-permute-start.43 = (f32[8,128,128]{2,1,0:T(8,128)}, f32[8,128,128]{2,1,0:T(8,128)S(1)}, u32[]{:S(2)}, u32[]{:S(2)}) collective-permute-start(f32[8,128,128]{2,1,0:T(8,128)} %get-tuple-element.295), channel_id=1, source_target_pairs={{0,0},{1,2},{2,1},{3,3},{4,4},{5,6},{6,5},{7,7},{8,8},{9,10},{10,9... | collective-permute-start | bytes 1572872 | tf_op jit(solution)/shard_map/ppermute | solution.py:630
  148.4 30.6 %collective-permute-start.44 = (f32[8,128,128]{2,1,0:T(8,128)}, f32[8,128,128]{2,1,0:T(8,128)S(1)}, u32[]{:S(2)}, u32[]{:S(2)}) collective-permute-start(f32[8,128,128]{2,1,0:T(8,128)} %get-tuple-element.296), channel_id=1, source_target_pairs={{2,0},{0,1},{3,2},{1,3},{6,4},{4,5},{7,6},{5,7},{10,8},{8,9},{11,1... | collective-permute-start | bytes 1572872 | tf_op jit(solution)/shard_map/ppermute | solution.py:631
  148.4 26.8 %collective-permute-start.41 = (f32[2,16,8,128]{3,2,1,0:T(8,128)S(1)}, f32[2,16,8,128]{3,2,1,0:T(8,128)S(1)}, u32[]{:S(2)}, u32[]{:S(2)}) collective-permute-start(f32[2,16,8,128]{3,2,1,0:T(8,128)S(1)} %get-tuple-element.289), channel_id=1, source_target_pairs={{0,12},{1,13},{2,14},{3,15},{4,8},{5,9},{6,10},{7,11},{8,4},{9,5},... | collective-permute-start | bytes 393224 | tf_op jit(solution)/shard_map/ppermute | solution.py:623
  175.2 0.9 copy-start.9
  176.1 0.9 copy-start.11
  177.0 0.9 copy-start.13
  177.9 0.9 copy-start.15
  (1 other events, 0.6 us)
